TPU v7x, 32 devices: a whole 2x2x4 slice. The times are simulated.
32 devices in a mesh: seq: 16 (over z, x, core), head: 2 (over y).
Axes of the slice: x: 2, y: 2, z: 4, core: 2. Of those that a mesh axis runs over, the one named last changes fastest.
Arguments:
- tokens: bfloat16 [2048, 768], P('seq'), may hold values from -6 to 6
- cotangent: bfloat16 [2048, 768], P('seq'), may hold values from -6 to 6
- doc_lengths: int32 [2], replicated, may hold values from 1 to 1600, 2048 in all
- plane_bits: int32 [64, 7, 12, 64], P(None, None, 'head'), may hold values from 0 to 1
- qkv_weight: float32 [3, 768, 768], P(None, 'seq', 'head'), may hold values from -0.21875 to 0.21875
- qkv_first: float32 [3, 768, 768], P(None, 'seq', 'head'), may hold values from -16 to 16
- qkv_second: float32 [3, 768, 768], P(None, 'seq', 'head'), may hold values from 0.256 to 4.096
- out_weight: float32 [768, 768], P('head', 'seq'), may hold values from -0.21875 to 0.21875
- out_first: float32 [768, 768], P('head', 'seq'), may hold values from -16 to 16
- out_second: float32 [768, 768], P('head', 'seq'), may hold values from 0.256 to 4.096
- up_weight: float32 [768, 3072], P('seq', 'head'), may hold values from -0.21875 to 0.21875
- up_first: float32 [768, 3072], P('seq', 'head'), may hold values from -16 to 16
- up_second: float32 [768, 3072], P('seq', 'head'), may hold values from 0.256 to 4.096
- down_weight: float32 [3072, 768], P('head', 'seq'), may hold values from -0.109375 to 0.109375
- down_first: float32 [3072, 768], P('head', 'seq'), may hold values from -16 to 16
- down_second: float32 [3072, 768], P('head', 'seq'), may hold values from 0.256 to 4.096
- norm_params: float32 [4, 768], replicated, may hold values from -1 to 1.65, as said below
- norm_first: float32 [4, 768], replicated, may hold values from -24 to 24
- norm_second: float32 [4, 768], replicated, may hold values from 0.6144 to 10.24
- conv_taps: float32 [12, 33], P('head'), may hold values from -1 to 1
- conv_first: float32 [12, 33], P('head'), may hold values from -160 to 160
- conv_second: float32 [12, 33], P('head'), may hold values from 32.768 to 524.288
Outputs:
- block_out: float32 [2048, 768], P('seq')
- tokens_grad: float32 [2048, 768], P('seq')
- occupancy: float32 [2, 64, 12, 128], P(None, None, 'head', 'seq')
- qkv_new: float32 [3, 768, 768], P(None, 'seq', 'head')
- qkv_first_new: float32 [3, 768, 768], P(None, 'seq', 'head')
- qkv_second_new: float32 [3, 768, 768], P(None, 'seq', 'head')
- qkv_copy: bfloat16 [3, 768, 768], P(None, 'seq', 'head')
- out_new: float32 [768, 768], P('head', 'seq')
- out_first_new: float32 [768, 768], P('head', 'seq')
- out_second_new: float32 [768, 768], P('head', 'seq')
- out_copy: bfloat16 [768, 768], P('head', 'seq')
- up_new: float32 [768, 3072], P('seq', 'head')
- up_first_new: float32 [768, 3072], P('seq', 'head')
- up_second_new: float32 [768, 3072], P('seq', 'head')
- up_copy: bfloat16 [768, 3072], P('seq', 'head')
- down_new: float32 [3072, 768], P('head', 'seq')
- down_first_new: float32 [3072, 768], P('head', 'seq')
- down_second_new: float32 [3072, 768], P('head', 'seq')
- down_copy: bfloat16 [3072, 768], P('head', 'seq')
- norm_new: float32 [4, 768], replicated
- norm_first_new: float32 [4, 768], replicated
- norm_second_new: float32 [4, 768], replicated
- conv_new: float32 [12, 33], P('head')
- conv_first_new: float32 [12, 33], P('head')
- conv_second_new: float32 [12, 33], P('head')
Inputs may be any that keep to these rules, and one draw needn't show every extreme that they name: `doc_lengths`: the documents lie end to end in the stream; the longest has at most 1600 tokens. `norm_params`: rows 0 and 2 are gains, rows 1 and 3 offsets.
All inputs are finite; a program needn't handle non-finite values.
Results may differ from a plain program's by a relative error of at most 0.015.
Values may be sent and summed in bfloat16 or wider, within the bound.
No kernel may reach another device: no remote copies, remote signals or barrier semaphores. Data moves between devices by JAX's collectives and lax.ppermute only.
A program may use at most 128 MiB of HBM per device.

v0:
```python
from functools import partial
import math

import jax
import jax.numpy as jnp
from jax import lax
from jax.sharding import PartitionSpec as P

D = 768
FF = 3072
CONV = 33
STEP = 7


sharpness = 4.0
norm_eps = 1e-06
layer_eps = 1e-05
beta_one = 0.9
beta_two = 0.999
adam_eps = 1e-08
decay_rate = 0.01
highest = lax.Precision.HIGHEST


def padded(value, sides, width):
    for axis, dim in sides:
        size, length = (lax.axis_size(axis), value.shape[dim])
        up = [(i, (i + 1) % size) for i in range(size - 1)]
        down = [(j, i) for i, j in up]
        last = lax.slice_in_dim(value, length - width, length, axis=dim)
        initial = lax.slice_in_dim(value, 0, width, axis=dim)
        before = lax.ppermute(last, axis, up)
        after = lax.ppermute(initial, axis, down)
        value = jnp.concatenate([before, value, after], axis=dim)
    return value


def bit_table(bit_count):
    all_codes = jnp.arange(2**bit_count, dtype=jnp.int32)
    places = 2 ** jnp.arange(bit_count, dtype=jnp.int32)
    return (all_codes[None, :] // places[:, None] % 2).astype(jnp.float32)


def soft_codes(unit_vals, planes):
    scaled = jnp.einsum("thd,rjhd->rhjt", unit_vals, planes, precision=highest) * (
        sharpness / math.sqrt(unit_vals.shape[2])
    )
    selector = bit_table(planes.shape[1])
    logits = jnp.einsum("rhjt,jb->rhtb", jax.nn.log_sigmoid(scaled), selector, precision=highest)
    logits = logits + jnp.einsum(
        "rhjt,jb->rhtb", jax.nn.log_sigmoid(-scaled), 1.0 - selector, precision=highest
    )
    return jnp.exp(logits)


def unit_rows(source):
    return source * lax.rsqrt(jnp.mean(source * source, axis=-1, keepdims=True) + norm_eps)


def normalize(source):
    centered = source - jnp.mean(source, axis=-1, keepdims=True)
    inverse = lax.rsqrt(jnp.mean(centered * centered, axis=-1, keepdims=True) + layer_eps)
    return (centered * inverse, inverse)


def norm_back(grad, normed, inverse, gain):
    scaled = grad * gain
    inner = (
        scaled
        - jnp.mean(scaled, axis=-1, keepdims=True)
        - normed * jnp.mean(scaled * normed, axis=-1, keepdims=True)
    )
    return (inverse * inner, jnp.sum(grad * normed, axis=0), jnp.sum(grad, axis=0))


def segment_masks(positions, doc_lengths):
    bounds = jnp.cumsum(doc_lengths)[:-1]
    seg_ids = jnp.sum((positions[:, None] >= bounds[None, :]).astype(jnp.int32), axis=1)
    seg_mask = (
        seg_ids[:, None] == jnp.arange(doc_lengths.shape[0], dtype=jnp.int32)[None, :]
    ).astype(jnp.float32)
    return (seg_ids, seg_mask)


def conv_values(ext_rows, seg_ext, seg_own, tap_weights):
    tok_rows = seg_own.shape[0]
    running = jnp.zeros((tok_rows, tap_weights.shape[0], ext_rows.shape[2]), jnp.float32)
    for offset in range(tap_weights.shape[1]):
        same_doc = (seg_ext[offset : offset + tok_rows] == seg_own).astype(jnp.float32)
        running = (
            running
            + tap_weights[:, offset][None, :, None]
            * ext_rows[offset : offset + tok_rows].astype(jnp.float32)
            * same_doc[:, None, None]
        )
    return running


def conv_back(grad_ext, grad_own, value_ext, seg_ext, seg_own, tap_weights):
    tok_rows = seg_own.shape[0]
    rim_width = tap_weights.shape[1] // 2
    value_grad = jnp.zeros(grad_own.shape, jnp.float32)
    tap_grads = []
    for offset in range(tap_weights.shape[1]):
        mirror = 2 * rim_width - offset
        back_same = (seg_ext[mirror : mirror + tok_rows] == seg_own).astype(jnp.float32)
        value_grad = (
            value_grad
            + tap_weights[:, offset][None, :, None]
            * grad_ext[mirror : mirror + tok_rows]
            * back_same[:, None, None]
        )
        fore_same = (seg_ext[offset : offset + tok_rows] == seg_own).astype(jnp.float32)
        product = (
            grad_own
            * value_ext[offset : offset + tok_rows].astype(jnp.float32)
            * fore_same[:, None, None]
        )
        tap_grads.append(jnp.sum(product, axis=(0, 2)))
    return (value_grad, jnp.stack(tap_grads, axis=1))


def adam_step(weight, first, second, grad, rate):
    first_new = beta_one * first + (1.0 - beta_one) * grad
    second_new = beta_two * second + (1.0 - beta_two) * grad * grad
    fix_one = 1.0 - beta_one**STEP
    fix_two = 1.0 - beta_two**STEP
    update = first_new / fix_one / (jnp.sqrt(second_new / fix_two) + adam_eps) + decay_rate * weight
    return (weight - rate * update, first_new, second_new)


def on_device(
    tokens,
    cotangent,
    doc_lengths,
    plane_bits,
    qkv_weight,
    qkv_first,
    qkv_second,
    out_weight,
    out_first,
    out_second,
    up_weight,
    up_first,
    up_second,
    down_weight,
    down_first,
    down_second,
    norm_params,
    norm_first,
    norm_second,
    conv_taps,
    conv_first,
    conv_second,
):
    tok_rows, feat_width = tokens.shape
    hash_count, bit_count, head_count, head_dim = plane_bits.shape
    bucket_count = 2**bit_count
    seg_count = doc_lengths.shape[0]
    rim_width = conv_taps.shape[1] // 2
    local_width = head_count * head_dim
    table_width = seg_count * head_dim
    seq_count = lax.axis_size("seq")
    row_start = lax.axis_index("seq") * tok_rows
    positions = row_start + jnp.arange(tok_rows, dtype=jnp.int32)
    seg_own, seg_mask = segment_masks(positions, doc_lengths)
    seg_ext, unused_mask = segment_masks(
        row_start - rim_width + jnp.arange(tok_rows + 2 * rim_width, dtype=jnp.int32), doc_lengths
    )
    mask_low = seg_mask.astype(jnp.bfloat16)
    planes = (2 * plane_bits - 1).astype(jnp.float32)
    hash_block = math.gcd(hash_count, 4)
    group_count = hash_count // hash_block
    plane_groups = planes.reshape(group_count, hash_block, bit_count, head_count, head_dim)
    qkv_w, out_w, up_w, down_w = (
        lax.all_gather(qkv_weight.astype(jnp.bfloat16), "seq", axis=1, tiled=True),
        lax.all_gather(out_weight.astype(jnp.bfloat16), "seq", axis=1, tiled=True),
        lax.all_gather(up_weight.astype(jnp.bfloat16), "seq", axis=0, tiled=True),
        lax.all_gather(down_weight.astype(jnp.bfloat16), "seq", axis=1, tiled=True),
    )
    proj = jnp.einsum("tc,pcf->ptf", tokens, qkv_w, preferred_element_type=jnp.float32)
    queries = proj[0].reshape(tok_rows, head_count, head_dim)
    key_proj = proj[1].reshape(tok_rows, head_count, head_dim)
    values = proj[2].astype(jnp.bfloat16).reshape(tok_rows, head_count, head_dim)
    query_norm, query_pull = jax.vjp(unit_rows, queries)
    key_norm, key_pull = jax.vjp(unit_rows, key_proj)
    query_unit = lax.optimization_barrier(query_norm.astype(jnp.bfloat16)).astype(jnp.float32)
    key_unit = lax.optimization_barrier(key_norm.astype(jnp.bfloat16)).astype(jnp.float32)
    masked = (values[:, :, None, :] * mask_low[:, None, :, None]).reshape(
        tok_rows, head_count, table_width
    )

    def fill_tables(carry, plane_set):
        hash_codes = soft_codes(key_unit, plane_set)
        table_set = jnp.einsum(
            "rhtb,thf->rhbf",
            hash_codes.astype(jnp.bfloat16),
            masked,
            preferred_element_type=jnp.float32,
        )
        count_set = jnp.einsum("rhtb,ts->srhb", hash_codes, seg_mask, precision=highest)
        return (carry, (table_set, count_set))

    unused, (tables, counts) = lax.scan(fill_tables, None, plane_groups)
    tables = tables.reshape(hash_count, head_count, bucket_count, table_width)
    counts = jnp.transpose(counts, (1, 0, 2, 3, 4)).reshape(
        seg_count, hash_count, head_count, bucket_count
    )
    slice_width = bucket_count // seq_count
    summed, totals = lax.psum((tables, counts), "seq")
    table_low = summed.astype(jnp.bfloat16)
    own_counts = lax.dynamic_slice_in_dim(
        totals, lax.axis_index("seq") * slice_width, slice_width, 3
    )
    occupancy = own_counts * (bucket_count / (tok_rows * seq_count))
    table_groups = table_low.reshape(group_count, hash_block, head_count, bucket_count, table_width)

    def read_tables(running, step_items):
        hash_codes = soft_codes(query_unit, step_items[0]).astype(jnp.bfloat16)
        return (
            running
            + jnp.einsum(
                "rhtb,rhbf->thf", hash_codes, step_items[1], preferred_element_type=jnp.float32
            ),
            None,
        )

    gathered, unused = lax.scan(
        read_tables,
        jnp.zeros((tok_rows, head_count, table_width), jnp.float32),
        (plane_groups, table_groups),
    )
    numerator = jnp.sum(
        gathered.reshape(tok_rows, head_count, seg_count, head_dim) * seg_mask[:, None, :, None],
        axis=2,
    )
    attention, attention_pull = jax.vjp(unit_rows, numerator)
    value_ext = padded(values, (("seq", 0),), rim_width)
    mixed_rows = attention + conv_values(value_ext, seg_ext, seg_own, conv_taps)
    context = mixed_rows.reshape(tok_rows, local_width).astype(jnp.bfloat16)
    mixer_out = lax.psum(
        jnp.dot(context, out_w, preferred_element_type=jnp.float32).astype(jnp.bfloat16), "head"
    ).astype(jnp.float32)
    first_hat, first_inverse = normalize(tokens.astype(jnp.float32) + mixer_out)
    first_out = first_hat * norm_params[0] + norm_params[1]
    first_low = first_out.astype(jnp.bfloat16)
    hidden = jnp.dot(first_low, up_w, preferred_element_type=jnp.float32)
    gelu_out, gelu_pull = jax.vjp(partial(jax.nn.gelu, approximate=False), hidden)
    active = gelu_out.astype(jnp.bfloat16)
    feed_out = lax.psum(
        jnp.dot(active, down_w, preferred_element_type=jnp.float32).astype(jnp.bfloat16), "head"
    ).astype(jnp.float32)
    second_hat, second_inverse = normalize(first_out + feed_out)
    block_out = second_hat * norm_params[2] + norm_params[3]
    grad_out = cotangent.astype(jnp.float32)
    grad_second, gain_two, offset_two = norm_back(
        grad_out, second_hat, second_inverse, norm_params[2]
    )
    grad_feed_low = grad_second.astype(jnp.bfloat16)
    down_grad = jnp.einsum("tf,tc->fc", active, grad_feed_low, preferred_element_type=jnp.float32)
    grad_active = jnp.einsum("tc,fc->tf", grad_feed_low, down_w, preferred_element_type=jnp.float32)
    grad_hidden_low = gelu_pull(grad_active)[0].astype(jnp.bfloat16)
    up_grad = jnp.einsum(
        "tc,tf->cf", first_low, grad_hidden_low, preferred_element_type=jnp.float32
    )
    grad_first = grad_second + lax.psum(
        jnp.einsum("tf,cf->tc", grad_hidden_low, up_w, preferred_element_type=jnp.float32).astype(
            jnp.bfloat16
        ),
        "head",
    ).astype(jnp.float32)
    grad_mixer, gain_one, offset_one = norm_back(
        grad_first, first_hat, first_inverse, norm_params[0]
    )
    grad_mixer_low = grad_mixer.astype(jnp.bfloat16)
    out_grad = jnp.einsum("tf,tc->fc", context, grad_mixer_low, preferred_element_type=jnp.float32)
    grad_context = jnp.einsum(
        "tc,fc->tf", grad_mixer_low, out_w, preferred_element_type=jnp.float32
    ).reshape(tok_rows, head_count, head_dim)
    grad_numerator_low = attention_pull(grad_context)[0].astype(jnp.bfloat16)
    grad_ext = padded(grad_context.astype(jnp.bfloat16), (("seq", 0),), rim_width).astype(
        grad_context.dtype
    )
    grad_conv, taps_grad = conv_back(grad_ext, grad_context, value_ext, seg_ext, seg_own, conv_taps)
    grad_masked = (grad_numerator_low[:, :, None, :] * mask_low[:, None, :, None]).reshape(
        tok_rows, head_count, table_width
    )

    def query_back(running, step_items):
        hash_codes, code_pull = jax.vjp(lambda point: soft_codes(point, step_items[0]), query_unit)
        codes_low = hash_codes.astype(jnp.bfloat16)
        table_grad = jnp.einsum(
            "rhtb,thf->rhbf", codes_low, grad_masked, preferred_element_type=jnp.float32
        )
        code_grad = jnp.einsum(
            "thf,rhbf->rhtb", grad_masked, step_items[1], preferred_element_type=jnp.float32
        )
        return (running + code_pull(code_grad)[0], table_grad)

    grad_query_unit, table_grads = lax.scan(
        query_back, jnp.zeros_like(query_unit), (plane_groups, table_groups)
    )
    grad_share = lax.psum_scatter(
        table_grads.reshape(hash_count * head_count * bucket_count, table_width),
        "seq",
        scatter_dimension=0,
        tiled=True,
    )
    grad_tables = lax.all_gather(
        grad_share.astype(jnp.bfloat16), "seq", axis=0, tiled=True
    ).reshape(group_count, hash_block, head_count, bucket_count, table_width)

    def key_back(carry, step_items):
        hash_codes, code_pull = jax.vjp(lambda point: soft_codes(point, step_items[0]), key_unit)
        codes_low = hash_codes.astype(jnp.bfloat16)
        value_part = jnp.einsum(
            "rhtb,rhbf->thf", codes_low, step_items[1], preferred_element_type=jnp.float32
        )
        code_grad = jnp.einsum(
            "thf,rhbf->rhtb", masked, step_items[1], preferred_element_type=jnp.float32
        )
        return ((carry[0] + code_pull(code_grad)[0], carry[1] + value_part), None)

    (grad_key_unit, grad_value_sets), unused = lax.scan(
        key_back,
        (jnp.zeros_like(key_unit), jnp.zeros((tok_rows, head_count, table_width), jnp.float32)),
        (plane_groups, grad_tables),
    )
    grad_values = (
        jnp.sum(
            grad_value_sets.reshape(tok_rows, head_count, seg_count, head_dim)
            * seg_mask[:, None, :, None],
            axis=2,
        )
        + grad_conv
    )
    grad_queries = query_pull(grad_query_unit)[0]
    grad_keys = key_pull(grad_key_unit)[0]
    grad_proj_low = jnp.stack(
        [
            grad_queries.reshape(tok_rows, local_width),
            grad_keys.reshape(tok_rows, local_width),
            grad_values.reshape(tok_rows, local_width),
        ]
    ).astype(jnp.bfloat16)
    qkv_grad = jnp.einsum("tc,ptf->pcf", tokens, grad_proj_low, preferred_element_type=jnp.float32)
    tokens_grad = grad_mixer + lax.psum(
        jnp.einsum("ptf,pcf->tc", grad_proj_low, qkv_w, preferred_element_type=jnp.float32).astype(
            jnp.bfloat16
        ),
        "head",
    ).astype(jnp.float32)
    qkv_owned, out_owned, up_owned, down_owned = (
        lax.psum_scatter(qkv_grad, "seq", scatter_dimension=1, tiled=True),
        lax.psum_scatter(out_grad, "seq", scatter_dimension=1, tiled=True),
        lax.psum_scatter(up_grad, "seq", scatter_dimension=0, tiled=True),
        lax.psum_scatter(down_grad, "seq", scatter_dimension=1, tiled=True),
    )
    norm_grad, conv_grad = lax.psum(
        (jnp.stack([gain_one, offset_one, gain_two, offset_two]), taps_grad), "seq"
    )
    qkv_new, qkv_first_new, qkv_second_new = adam_step(
        qkv_weight, qkv_first, qkv_second, qkv_owned, D ** (-0.5)
    )
    out_new, out_first_new, out_second_new = adam_step(
        out_weight, out_first, out_second, out_owned, D ** (-0.5)
    )
    up_new, up_first_new, up_second_new = adam_step(
        up_weight, up_first, up_second, up_owned, D ** (-0.5)
    )
    down_new, down_first_new, down_second_new = adam_step(
        down_weight, down_first, down_second, down_owned, FF ** (-0.5)
    )
    norm_new, norm_first_new, norm_second_new = adam_step(
        norm_params, norm_first, norm_second, norm_grad, 0.3
    )
    conv_new, conv_first_new, conv_second_new = adam_step(
        conv_taps, conv_first, conv_second, conv_grad, CONV ** (-0.5)
    )
    return (
        block_out,
        tokens_grad,
        occupancy,
        qkv_new,
        qkv_first_new,
        qkv_second_new,
        qkv_new.astype(jnp.bfloat16),
        out_new,
        out_first_new,
        out_second_new,
        out_new.astype(jnp.bfloat16),
        up_new,
        up_first_new,
        up_second_new,
        up_new.astype(jnp.bfloat16),
        down_new,
        down_first_new,
        down_second_new,
        down_new.astype(jnp.bfloat16),
        norm_new,
        norm_first_new,
        norm_second_new,
        conv_new,
        conv_first_new,
        conv_second_new,
    )


def solution(mesh):
    in_specs = (
        P("seq", None),
        P("seq", None),
        P(),
        P(None, None, "head", None),
        P(None, "seq", "head"),
        P(None, "seq", "head"),
        P(None, "seq", "head"),
        P("head", "seq"),
        P("head", "seq"),
        P("head", "seq"),
        P("seq", "head"),
        P("seq", "head"),
        P("seq", "head"),
        P("head", "seq"),
        P("head", "seq"),
        P("head", "seq"),
        P(),
        P(),
        P(),
        P("head", None),
        P("head", None),
        P("head", None),
    )
    out_specs = (
        P("seq", None),
        P("seq", None),
        P(None, None, "head", "seq"),
        P(None, "seq", "head"),
        P(None, "seq", "head"),
        P(None, "seq", "head"),
        P(None, "seq", "head"),
        P("head", "seq"),
        P("head", "seq"),
        P("head", "seq"),
        P("head", "seq"),
        P("seq", "head"),
        P("seq", "head"),
        P("seq", "head"),
        P("seq", "head"),
        P("head", "seq"),
        P("head", "seq"),
        P("head", "seq"),
        P("head", "seq"),
        P(),
        P(),
        P(),
        P("head", None),
        P("head", None),
        P("head", None),
    )
    return jax.shard_map(
        on_device, mesh=mesh, in_specs=in_specs, out_specs=out_specs, check_vma=False
    )
```

profile of v0, /device:TPU:0, one launch (start us, length us, event | category | flops | bytes accessed | tf_op | source)
XLA Modules:
  0.0 2002.9 jit_solution(10850809910898238564)
XLA Ops:
  16.7 26.2 %all_gather.16 = bf16[384,768]{0,1:T(8,128)(2,1)} all-gather(bf16[384,48]{0,1:T(8,128)(2,1)S(1)} %convert_element_type.842), channel_id=1, replica_groups=mesh['seq'=16,'head'=2] {'seq'}, dimensions={1}, use_global_device_ids=true | all-gather | bytes 626688 | tf_op jit(solution)/shard_map/all_gather | solution.py:177
  42.9 11.7 all-gather.5.cloned.1.call-done
  59.0 11.5 broadcast.1638.clone2
  70.6 160.0 %while.58 = (s32[]{:T(128)}, f32[16,4,6,128,128]{4,3,2,1,0:T(8,128)}, f32[16,2,4,6,128]{4,1,3,2,0:T(2,128)}, f32[16,4,7,6,64]{4,2,1,3,0:T(8,128)}, f32[128,6,64]...) while((s32[]{:T(128)}, ...), condition=%wide.region_3.5_spmd.clone, body=%wide.region_2.4_spmd.clone.sunk | while | flops 193940416 | bytes 13773081 | solution.py:204
  230.6 517.3 %all-reduce.19 = bf16[64,6,128,128]{3,2,1,0:T(8,128)(2,1)} all-reduce(f32[64,6,128,128]{3,2,1,0:T(8,128)} %bitcast.594), channel_id=1, replica_groups=mesh['seq'=16,'head'=2] {'seq'}, use_global_device_ids=true, to_apply=%region_4.6 | all-reduce | flops 6291456 | bytes 37748736 | tf_op jit(solution)/shard_map/psum | solution.py:210
  748.0 137.2 %while.59 = (s32[]{:T(128)}, f32[128,6,128]{0,2,1:T(8,128)S(1)}, bf16[16,4,6,128,128]{4,3,2,1,0:T(8,128)(2,1)}, f32[16,4,7,6,64]{4,2,1,3,0:T(8,128)}, f32[128,6,64]{0,2,1:T(8,128)S(1)}, /*index=5*/s32[]{:T(128)}, s32[]{:T(128)}) while((s32[]{:T(128)}, f32[128,6,128]{0,2,1:T(8,128)S(1)}, bf16[16,4,6,128,128]{4,3,2,1,0:T(8,128)(2,1)}, ...), condition=%wide.region_7.9_spmd.clone, body=%wide.region_6.8_spmd.clone.sunk | while | flops 184601024 | bytes 9991951 | solution.py:228
  769.1 2.7 exponential_convert_fusion.2
  777.7 2.7 exponential_convert_fusion.2
  885.3 9.5 collective-permute-start
  898.2 3.9 fusion.363
  904.8 26.8 %all-reduce.10.cloned.1.call-done = bf16[128,768]{1,0:T(8,128)(2,1)} async-done(((bf16[128,768]{1,0:T(8,128)(2,1)}), bf16[128,768]{1,0:T(8,128)(2,1)}) %all-reduce.10.cloned.1.call-update) | async-done | bytes 196624 | tf_op jit(solution)/shard_map/psum | solution.py:241
  933.8 43.0 %all-gather.7.cloned.1.call-done = bf16[768,1536]{1,0:T(8,128)(2,1)} async-done(((bf16[48,1536]{1,0:T(8,128)(2,1)}), bf16[768,1536]{1,0:T(8,128)(2,1)}) %all-gather.7.cloned.1.call-update) | async-done | bytes 2359312 | tf_op jit(solution)/shard_map/all_gather | solution.py:178
  976.8 4.6 multiply_convert_fusion
  981.4 39.2 %all-gather.9.cloned.1.call-done = bf16[1536,768]{0,1:T(8,128)(2,1)} async-done(((bf16[1536,48]{0,1:T(8,128)(2,1)}), bf16[1536,768]{0,1:T(8,128)(2,1)}) %all-gather.9.cloned.1.call-update) | async-done | bytes 2359312 | tf_op jit(solution)/shard_map/all_gather | solution.py:179
  1020.6 3.3 convolution_convert_fusion.1
  1024.0 21.2 %all-reduce.12.cloned.1.call-done = bf16[128,768]{1,0:T(8,128)(2,1)} async-done(((bf16[128,768]{1,0:T(8,128)(2,1)}), bf16[128,768]{1,0:T(8,128)(2,1)}) %all-reduce.12.cloned.1.call-update) | async-done | bytes 196624 | tf_op jit(solution)/shard_map/psum | solution.py:250
  1047.9 3.4 add_convert_fusion.1
  1053.2 22.2 %all-reduce.14.cloned.1.call-done = bf16[128,768]{1,0:T(8,128)(2,1)} async-done(((bf16[128,768]{1,0:T(8,128)(2,1)}), bf16[128,768]{1,0:T(8,128)(2,1)}) %all-reduce.14.cloned.1.call-update) | async-done | bytes 196624 | tf_op jit(solution)/shard_map/psum | solution.py:266
  1083.2 11.5 broadcast.1638.clone
  1094.7 181.0 %while.60 = (s32[]{:T(128)}, f32[128,6,64]{0,2,1:T(8,128)S(1)}, f32[16,4,6,128,128]{4,3,2,1,0:T(8,128)}, bf16[16,4,6,128,128]{4,3,2,1,0:T(8,128)(2,1)}, f32[16,4...) while((s32[]{:T(128)}, f32[128,6,64]{0,2,1:T(8,128)S(1)}, ...), condition=%wide.region_23.26_spmd.clone, body=%wide.region_22.25_spmd.clone.sunk | while | flops 368912960 | bytes 20765636 | solution.py:300
  1275.8 243.9 %reduce-scatter.5.cloned.1.call-done = f32[3072,128]{1,0:T(8,128)} async-done(((f32[49152,128]{1,0:T(8,128)}), f32[3072,128]{1,0:T(8,128)}) %reduce-scatter.5.cloned.1.call-update) | async-done | bytes 1572880 | tf_op jit(solution)/shard_map/reduce_scatter | solution.py:303
  1523.7 3.0 fusion.502
  1529.5 3.0 fusion.495
  1534.3 3.2 collective-permute-start.2
  1544.4 61.2 %all-reduce.1 = (f32[4,768]{1,0:T(4,128)}, f32[6,33]{1,0:T(8,128)}) all-reduce(f32[4,768]{1,0:T(4,128)S(1)} %pad_maximum_fusion.5, f32[6,33]{1,0:T(8,128)S(1)} %stack.160), channel_id=1, replica_groups=mesh['seq'=16,'head'=2] {'seq'}, use_global_device_ids=true, to_apply=%region_40.43 | all-reduce | flops 3270 | bytes 26160 | tf_op jit(solution)/shard_map/psum | solution.py:359
  1605.8 18.3 all-gather.11.cloned.1.call-done
  1624.1 181.2 %while.61 = (s32[]{:T(128)}, f32[128,6,64]{0,2,1:T(8,128)}, f32[128,6,128]{0,2,1:T(8,128)S(1)}, bf16[16,4,6,128,128]{4,3,2,1,0:T(8,128)(2,1)}, f32[16,4,7,6,64]{...) while((s32[]{:T(128)}, f32[128,6,64]{0,2,1:T(8,128)}, ...), condition=%wide.region_27.30_spmd.clone, body=%wide.region_26.29_spmd.clone.sunk | while | flops 369109568 | bytes 18865108 | solution.py:324
  1805.4 3.6 fusion.393
  1813.5 6.3 copy.370
  1825.4 16.1 reduce-scatter.11.cloned.1.call-done
  1843.6 22.1 %all-reduce.16.cloned.1.call-done = bf16[128,768]{1,0:T(8,128)(2,1)} async-done(((bf16[128,768]{1,0:T(8,128)(2,1)}), bf16[128,768]{1,0:T(8,128)(2,1)}) %all-reduce.16.cloned.1.call-update) | async-done | bytes 196624 | tf_op jit(solution)/shard_map/psum | solution.py:347
  1867.4 124.5 %all-reduce.18.cloned.1.call-done = (f32[2,64,6,128]{3,1,2,0:T(8,128)}, f32[3,768,384]{2,0,1:T(4,128)}) async-done(((f32[2,64,6,128]{3,1,2,0:T(8,128)}, f32[3,768,384]{2,0,1:T(4,128)}), (f32[2,64,6,128]{3,1,2,0:T(8,128)}, f32[3,768,384]{2,0,1:T(4,128)})) %all-reduce.18.cloned.1.call-update) | async-done | bytes 3932176 | tf_op jit(solution)/shard_map/psum | solution.py:210
  (1143 shorter events, 715.9 us)
Async XLA Ops:
  7.2 47.4 %all-gather.5.cloned.1.call-start = ((), (), s32[]{:S(2)}) async-start(), calls=%async_computation.4 | async-start | bytes 1880064 | tf_op jit(solution)/shard_map/all_gather | solution.py:176
  8.9 922.7 %all-reduce.10.cloned.1.call-start = ((), (), s32[]{:S(2)}) async-start(), calls=%async_computation.5 | async-start | bytes 393216 | tf_op jit(solution)/shard_map/psum | solution.py:241
  16.6 881.5 %copy-start.62 = (f32[128]{0:T(128)}, f32[128]{0:T(128)S(1)}, u32[]{:S(2)}) copy-start(f32[128]{0:T(128)S(1)} %get-tuple-element.941) | copy-start | bytes 1540
  16.6 881.5 %copy-start.64 = (f32[128]{0:T(128)}, f32[128]{0:T(128)S(1)}, u32[]{:S(2)}) copy-start(f32[128]{0:T(128)S(1)} %get-tuple-element.942) | copy-start | bytes 1540
  16.6 881.5 %copy-start.66 = (f32[128]{0:T(128)}, f32[128]{0:T(128)S(1)}, u32[]{:S(2)}) copy-start(f32[128]{0:T(128)S(1)} %get-tuple-element.943) | copy-start | bytes 1540
  16.6 881.5 %copy-start.68 = (f32[128]{0:T(128)}, f32[128]{0:T(128)S(1)}, u32[]{:S(2)}) copy-start(f32[128]{0:T(128)S(1)} %get-tuple-element.944) | copy-start | bytes 1540
  16.6 881.5 %copy-start.70 = (f32[128]{0:T(128)}, f32[128]{0:T(128)S(1)}, u32[]{:S(2)}) copy-start(f32[128]{0:T(128)S(1)} %get-tuple-element.945) | copy-start | bytes 1540
  16.6 881.5 %copy-start.72 = (f32[128]{0:T(128)}, f32[128]{0:T(128)S(1)}, u32[]{:S(2)}) copy-start(f32[128]{0:T(128)S(1)} %get-tuple-element.946) | copy-start | bytes 1540
  16.6 881.5 %copy-start.74 = (f32[128]{0:T(128)}, f32[128]{0:T(128)S(1)}, u32[]{:S(2)}) copy-start(f32[128]{0:T(128)S(1)} %get-tuple-element.947) | copy-start | bytes 1540
  16.6 881.5 %copy-start.76 = (f32[128]{0:T(128)}, f32[128]{0:T(128)S(1)}, u32[]{:S(2)}) copy-start(f32[128]{0:T(128)S(1)} %get-tuple-element.948) | copy-start | bytes 1540
  16.6 881.5 %copy-start.78 = (f32[128]{0:T(128)}, f32[128]{0:T(128)S(1)}, u32[]{:S(2)}) copy-start(f32[128]{0:T(128)S(1)} %get-tuple-element.949) | copy-start | bytes 1540
  16.6 881.5 %copy-start.80 = (f32[128]{0:T(128)}, f32[128]{0:T(128)S(1)}, u32[]{:S(2)}) copy-start(f32[128]{0:T(128)S(1)} %get-tuple-element.950) | copy-start | bytes 1540
  16.7 1061.2 %copy-start.60 = (f32[128]{0:T(128)}, f32[128]{0:T(128)S(1)}, u32[]{:S(2)}) copy-start(f32[128]{0:T(128)S(1)} %get-tuple-element.956) | copy-start | bytes 1540
  16.7 1523.0 %copy-start.61 = (f32[128]{0:T(128)}, f32[128]{0:T(128)S(1)}, u32[]{:S(2)}) copy-start(f32[128]{0:T(128)S(1)} %get-tuple-element.940) | copy-start | bytes 1540
  56.8 691.1 %copy-start.12 = (f32[1,128,384]{1,2,0:T(8,128)}, f32[1,128,384]{1,2,0:T(8,128)S(1)}, u32[]{:S(2)}) copy-start(f32[1,128,384]{1,2,0:T(8,128)S(1)} %get-tuple-element.930) | copy-start | bytes 589828
  885.3 10.9 collective-permute-start
  894.9 3.2 collective-permute-start.1
  903.2 73.6 %all-gather.7.cloned.1.call-start = ((), (), s32[]{:S(2)}) async-start(), calls=%async_computation.6 | async-start | bytes 2506752 | tf_op jit(solution)/shard_map/all_gather | solution.py:178
  903.9 116.7 %all-gather.9.cloned.1.call-start = ((), (), s32[]{:S(2)}) async-start(), calls=%async_computation.7 | async-start | bytes 2506752 | tf_op jit(solution)/shard_map/all_gather | solution.py:179
  904.7 140.5 %all-reduce.12.cloned.1.call-start = ((), (), s32[]{:S(2)}) async-start(), calls=%async_computation.8 | async-start | bytes 393216 | tf_op jit(solution)/shard_map/psum | solution.py:250
  1023.9 51.5 %all-reduce.14.cloned.1.call-start = ((), (), s32[]{:S(2)}) async-start(), calls=%async_computation.9 | async-start | bytes 393216 | tf_op jit(solution)/shard_map/psum | solution.py:266
  1053.0 466.8 %reduce-scatter.5.cloned.1.call-start = ((), (), s32[]{:S(2)}) async-start(), calls=%async_computation.10 | async-start | bytes 26738688 | tf_op jit(solution)/shard_map/reduce_scatter | solution.py:303
  1275.7 246.5 %copy-start.7 = (f32[128,768]{1,0:T(8,128)S(1)}, f32[128,768]{1,0:T(8,128)}, u32[]{:S(2)}) copy-start(f32[128,768]{1,0:T(8,128)} %copy-done.6) | copy-start | bytes 1179652
  1275.8 246.5 %copy-start.35 = (bf16[128,6,64]{0,2,1:T(8,128)(2,1)S(1)}, bf16[128,6,64]{0,2,1:T(8,128)(2,1)}, u32[]{:S(2)}) copy-start(bf16[128,6,64]{0,2,1:T(8,128)(2,1)} %copy-done.34) | copy-start | bytes 294916
  1275.8 348.3 %all-gather.11.cloned.1.call-start = ((), (), s32[]{:S(2)}) async-start(), calls=%async_computation.11 | async-start | bytes 13369344 | tf_op jit(solution)/shard_map/all_gather | solution.py:309
  1522.1 299.6 %reduce-scatter.7.cloned.1.call-start = ((), (), s32[]{:S(2)}) async-start(), calls=%async_computation.13 | async-start | bytes 1253376 | tf_op jit(solution)/shard_map/reduce_scatter | solution.py:355
  1523.6 299.7 %reduce-scatter.9.cloned.1.call-start = ((), (), s32[]{:S(2)}) async-start(), calls=%async_computation.14 | async-start | bytes 5013504 | tf_op jit(solution)/shard_map/reduce_scatter | solution.py:356
  1526.7 314.8 %reduce-scatter.11.cloned.1.call-start = ((), (), s32[]{:S(2)}) async-start(), calls=%async_computation.15 | async-start | bytes 5013504 | tf_op jit(solution)/shard_map/reduce_scatter | solution.py:357
  1532.7 333.0 %all-reduce.16.cloned.1.call-start = ((), (), s32[]{:S(2)}) async-start(), calls=%async_computation.12 | async-start | bytes 393216 | tf_op jit(solution)/shard_map/psum | solution.py:347
  1533.0 72.7 %collective-permute-start.3 = (bf16[16,6,64]{0,2,1:T(8,128)(2,1)S(1)}, bf16[16,6,64]{0,2,1:T(8,128)(2,1)S(1)}, u32[]{:S(2)}, u32[]{:S(2)}) collective-permute-start(bf16[16,6,64]{0,2,1:T(8,128)(2,1)S(1)} %get-tuple-element.936), channel_id=1, source_target_pairs={{2,0},{4,2},{6,4},{8,6},{10,8},{12,10},{14,12},{16,14},{18,16},{20... | collective-permute-start | bytes 36872 | tf_op jit(solution)/shard_map/ppermute | solution.py:33
  1534.3 71.4 %collective-permute-start.2 = (bf16[16,6,64]{0,2,1:T(8,128)(2,1)S(1)}, bf16[16,6,64]{0,2,1:T(8,128)(2,1)S(1)}, u32[]{:S(2)}, u32[]{:S(2)}) collective-permute-start(bf16[16,6,64]{0,2,1:T(8,128)(2,1)S(1)} %get-tuple-element.935), channel_id=1, source_target_pairs={{0,2},{2,4},{4,6},{6,8},{8,10},{10,12},{12,14},{14,16},{16,18},{18... | collective-permute-start | bytes 36872 | tf_op jit(solution)/shard_map/ppermute | solution.py:32
  1810.7 181.2 %all-reduce.18.cloned.1.call-start = ((), (), s32[]{:S(2)}) async-start(), calls=%async_computation.16 | async-start | bytes 10223616 | tf_op jit(solution)/shard_map/psum | solution.py:210
  (147 other events, 2025.9 us)
Sparse Core Ops, SparseCore 0:
  10.9 43.6 all-gather.4
  903.3 28.2 all-reduce.9
  934.4 42.3 all-gather.6
  979.5 41.0 all-gather.8
  1024.1 21.0 all-reduce.11
  1053.1 22.2 all-reduce.13
  1275.9 243.8 reduce-scatter.4
  1522.3 101.7 all-gather.10
  1627.7 56.1 reduce-scatter.6
  1687.7 74.8 reduce-scatter.8
  1766.9 74.5 reduce-scatter.10
  1844.3 21.3 all-reduce.15
  1869.5 122.3 all-reduce.17
where the time goes:
time: 2020 us; the launch traced here: 2000 us
  blocking collectives  605 us (30%)
  matrix products  594 us (29%)
  waiting for transfers between devices  591 us (29%)
  local copies, waits for them, and re-layouts  133 us (7%)
  other arithmetic  42.7 us (2%)
    psum x1, blocking collectives, on_device(): summed, totals = lax.psum((tables, counts), 'seq')  517 us
    reduce_scatter x1, waiting for transfers between devices, on_device(): lax.psum_scatter(table_grads.reshape(hash_count * head_count * bucket_cou...  244 us
    dot_general x96, matrix products, soft_codes(): jnp.einsum('rhjt,jb->rhtb', jax.nn.log_sigmoid(-scaled), 1.0 - selector,...  173 us
    dot_general x96, matrix products, soft_codes(): jnp.einsum('rhjt,jb->rhtb', jax.nn.log_sigmoid(scaled), selector, precisi...  170 us
    dot_general x96, matrix products, soft_codes(): jnp.einsum('thd,rjhd->rhjt', unit_vals, planes, precision=highest)  140 us
    psum x1, waiting for transfers between devices, on_device(): summed, totals = lax.psum((tables, counts), 'seq')  125 us
    psum x1, blocking collectives, on_device(): lax.psum((jnp.stack([gain_one, offset_one, gain_two, offset_two]), taps_g...  61.2 us
    dynamic_slice x48, local copies, waits for them, and re-layouts, on_device(): lax.scan(read_tables, jnp.zeros((tok_rows, head_count, table_width), jnp....  44.4 us
  transfers between devices with their start and end apart: 17, of which 12 were waited for; matrix products, arithmetic and copies ran while one was open for 12% of the time, Pallas kernels for 0%

commit v1 on v0

v1 whole, which is shorter than its diff:
```python
from functools import partial
import math

import jax
import jax.numpy as jnp
from jax import lax
from jax.experimental import pallas as pl
from jax.experimental.pallas import tpu as pltpu
from jax.sharding import PartitionSpec as P

D = 768
FF = 3072
CONV = 33
STEP = 7
CORES = 2

sharpness = 4.0
norm_eps = 1e-06
layer_eps = 1e-05
beta_one = 0.9
beta_two = 0.999
adam_eps = 1e-08
decay_rate = 0.01
highest = lax.Precision.HIGHEST
f32 = jnp.float32
bf16 = jnp.bfloat16
VMEM_LIMIT = 56 * 1024 * 1024


def nn(a, b):
    return lax.dot_general(a, b, (((1,), (0,)), ((), ())), preferred_element_type=f32)


def nt(a, b):
    return lax.dot_general(a, b, (((1,), (1,)), ((), ())), preferred_element_type=f32)


def swap_sum(value):
    own = lax.optimization_barrier(value.astype(bf16))
    other = lax.ppermute(own, "head", [(0, 1), (1, 0)])
    return own.astype(f32) + other.astype(f32)


def normalize(source):
    centered = source - jnp.mean(source, axis=-1, keepdims=True)
    inverse = lax.rsqrt(jnp.mean(centered * centered, axis=-1, keepdims=True) + layer_eps)
    return (centered * inverse, inverse)


def norm_back(grad, normed, inverse, gain):
    scaled = grad * gain
    inner = (
        scaled
        - jnp.mean(scaled, axis=-1, keepdims=True)
        - normed * jnp.mean(scaled * normed, axis=-1, keepdims=True)
    )
    return (inverse * inner, jnp.sum(grad * normed, axis=0), jnp.sum(grad, axis=0))


def adam_step(weight, first, second, grad, rate):
    first_new = beta_one * first + (1.0 - beta_one) * grad
    second_new = beta_two * second + (1.0 - beta_two) * grad * grad
    fix_one = 1.0 - beta_one**STEP
    fix_two = 1.0 - beta_two**STEP
    update = first_new / fix_one / (jnp.sqrt(second_new / fix_two) + adam_eps) + decay_rate * weight
    return (weight - rate * update, first_new, second_new)


def head_units(source):
    inverse = lax.rsqrt(jnp.mean(source * source, axis=0, keepdims=True) + norm_eps)
    return source * inverse, inverse


def log_norms(unit, bit_planes, bits, rows):
    z = jnp.abs(nn(bit_planes, unit))
    parts = 0.5 * z + jnp.log1p(jnp.exp(-z))
    total = parts[0:rows]
    for j in range(1, bits):
        total = total + parts[j * rows : (j + 1) * rows]
    return total


def seg_rows(limit, start, width):
    pos = start + lax.broadcasted_iota(jnp.int32, (1, width), 1)
    late = (pos >= limit).astype(f32)
    return 1.0 - late, late


def masked_pair(rows, early, late):
    return jnp.concatenate([rows * early, rows * late], axis=0).astype(bf16)


def forward_kernel(
    hashes, bits, rows, tile, tiles,
    limit_ref, tok_ref, w_ref, code_ref, bit_ref,
    num_ref, qu_ref, ku_ref, v_ref, inv_ref, table_ref, count_ref,
    acc_ref, codes_ref,
):
    buckets = 2**bits
    limit = limit_ref[0]
    acc_ref[...] = jnp.zeros_like(acc_ref)

    def fill(i, carry):
        start = pl.multiple_of(i * tile, tile)
        span = pl.ds(start, tile)
        proj = nt(w_ref[0], tok_ref[span, :])
        q_unit, q_inv = head_units(proj[0:64])
        k_unit, k_inv = head_units(proj[64:128])
        q_low = q_unit.astype(bf16)
        k_low = k_unit.astype(bf16)
        values = proj[128:192].astype(bf16)
        qu_ref[:, span] = q_low
        ku_ref[:, span] = k_low
        v_ref[:, span] = values
        inv_ref[0, 0:1, span] = q_inv
        inv_ref[0, 1:2, span] = k_inv
        norms = log_norms(k_low, bit_ref[0], bits, rows)
        logits = nn(code_ref[0], k_low)
        for r in range(hashes):
            part = slice(r * buckets, (r + 1) * buckets)
            codes_ref[part, :] = jnp.exp(logits[part] - norms[r : r + 1]).astype(bf16)
        early, late = seg_rows(limit, start, tile)
        marks = jnp.concatenate([early, late, jnp.zeros((14, tile), f32)], axis=0).astype(bf16)
        pair = jnp.concatenate([masked_pair(values.astype(f32), early, late), marks], axis=0)
        acc_ref[...] += nt(codes_ref[...], pair)
        return carry

    lax.fori_loop(0, tiles, fill, 0)
    table = acc_ref[:, 0:128].astype(bf16)
    table_ref[0] = table
    table_t = jnp.transpose(table.astype(f32)).astype(bf16)
    counts = jnp.concatenate(
        [acc_ref[:, 128:144], jnp.zeros((hashes * buckets, 112), f32)], axis=1
    )
    count_ref[0] = jnp.transpose(counts)[0:8]

    def read(i, carry):
        start = pl.multiple_of(i * tile, tile)
        span = pl.ds(start, tile)
        q_low = qu_ref[:, span]
        norms = log_norms(q_low, bit_ref[0], bits, rows)
        logits = nn(code_ref[0], q_low)
        for r in range(hashes):
            part = slice(r * buckets, (r + 1) * buckets)
            codes_ref[part, :] = jnp.exp(logits[part] - norms[r : r + 1]).astype(bf16)
        both = nn(table_t, codes_ref[...])
        early, late = seg_rows(limit, start, tile)
        num_ref[i] = (both[0:64] * early + both[64:128] * late).astype(bf16)
        return carry

    lax.fori_loop(0, tiles, read, 0)


def backward_kernel(
    hashes, bits, rows, tile, tiles, heads,
    limit_ref, spot_ref, tok_ref, w_ref, code_ref, code_t_ref, bit_ref,
    qu_ref, ku_ref, v_ref, inv_ref, table_ref, gnum_ref, conv_ref,
    grad_ref, back_ref,
    acc_ref, codes_ref, slopes_ref, proj_ref,
):
    buckets = 2**bits
    limit = limit_ref[0]
    spot = spot_ref[0]
    head = pl.program_id(0)
    acc_ref[...] = jnp.zeros_like(acc_ref)

    def soften(unit, slopes, span):
        norms = log_norms(unit, bit_ref[0], bits, rows)
        logits = nn(code_ref[0], unit)
        for r in range(hashes):
            part = slice(r * buckets, (r + 1) * buckets)
            codes = jnp.exp(logits[part] - norms[r : r + 1])
            weighted = codes * slopes[part]
            total = jnp.sum(weighted, axis=0, keepdims=True)
            codes_ref[part, :] = codes.astype(bf16)
            slopes_ref[part, :] = (weighted - codes * total).astype(bf16)
        return nn(code_t_ref[0], slopes_ref[...])

    def unit_back(grad, unit, inverse):
        unit = unit.astype(f32)
        inner = jnp.mean(grad * unit, axis=0, keepdims=True)
        return inverse * (grad - unit * inner)

    def queries(i, carry):
        start = pl.multiple_of(i * tile, tile)
        span = pl.ds(start, tile)
        early, late = seg_rows(limit, start, tile)
        pair = masked_pair(gnum_ref[i].astype(f32), early, late)
        unit = qu_ref[:, span]
        grad = soften(unit, nn(table_ref[0], pair), span)
        acc_ref[...] += nt(codes_ref[...], pair)
        proj_ref[head, 0:64, span] = unit_back(grad, unit, inv_ref[0, 0:1, span]).astype(bf16)
        return carry

    lax.fori_loop(0, tiles, queries, 0)
    table_grad = acc_ref[...].astype(bf16)
    table_grad_t = jnp.transpose(table_grad.astype(f32)).astype(bf16)

    def keys(i, carry):
        start = pl.multiple_of(i * tile, tile)
        span = pl.ds(start, tile)
        early, late = seg_rows(limit, start, tile)
        pair = masked_pair(v_ref[:, span].astype(f32), early, late)
        unit = ku_ref[:, span]
        grad = soften(unit, nn(table_grad, pair), span)
        both = nn(table_grad_t, codes_ref[...])
        here = (spot == i).astype(f32)
        value_grad = both[0:64] * early + both[64:128] * late + conv_ref[...] * here
        proj_ref[head, 64:128, span] = unit_back(grad, unit, inv_ref[0, 1:2, span]).astype(bf16)
        proj_ref[head, 128:192, span] = value_grad.astype(bf16)
        return carry

    lax.fori_loop(0, tiles, keys, 0)
    grad_ref[...] = nn(proj_ref[head], tok_ref[...])

    @pl.when(head == heads - 1)
    def _():
        def inputs(i, carry):
            span = pl.ds(pl.multiple_of(i * tile, tile), tile)
            part = nn(w_ref[0], proj_ref[0, :, span])
            for h in range(1, heads):
                part = part + nn(w_ref[h], proj_ref[h, :, span])
            half = tile // CORES
            for k in range(CORES):
                back_ref[k, i] = part[:, k * half : (k + 1) * half].astype(bf16)
            return carry

        lax.fori_loop(0, tiles, inputs, 0)


def on_device(
    tokens,
    cotangent,
    doc_lengths,
    plane_bits,
    qkv_weight,
    qkv_first,
    qkv_second,
    out_weight,
    out_first,
    out_second,
    up_weight,
    up_first,
    up_second,
    down_weight,
    down_first,
    down_second,
    norm_params,
    norm_first,
    norm_second,
    conv_taps,
    conv_first,
    conv_second,
):
    tok_rows, width = tokens.shape
    hash_count, bits, group_heads, head_dim = plane_bits.shape
    buckets = 2**bits
    taps = conv_taps.shape[1]
    rim = taps // 2
    seq_count = lax.axis_size("seq")
    chips = seq_count // CORES
    place = lax.axis_index("seq")
    spot, core = place // CORES, place % CORES
    heads = group_heads // CORES
    feats = heads * head_dim
    group_feats = group_heads * head_dim
    hashes = hash_count // chips
    rows = -(-hashes // 8) * 8
    tile = CORES * tok_rows
    total = chips * tile
    own_rows = width // seq_count
    ff = up_weight.shape[1]
    pairs = [[CORES * c + k for k in range(CORES)] for c in range(chips)]
    planes_of = [[CORES * c + k for c in range(chips)] for k in range(CORES)]
    across = partial(
        lax.all_to_all, axis_name="seq", split_axis=0, concat_axis=0, tiled=True,
        axis_index_groups=planes_of,
    )
    within = partial(
        lax.all_to_all, axis_name="seq", split_axis=0, concat_axis=0, tiled=True,
        axis_index_groups=pairs,
    )
    limit = doc_lengths[0:1]

    qkv_rows = jnp.transpose(qkv_weight, (1, 0, 2)).astype(bf16)
    qkv_extra = qkv_rows.size // width
    first_send = jnp.concatenate([tokens, qkv_rows.reshape(qkv_extra, width)], axis=0)
    first_got = lax.all_gather(first_send, "seq", axis=0, tiled=False)
    all_tokens = first_got[:, :tok_rows].reshape(total, width)
    qkv_all = first_got[:, tok_rows:].reshape(width, 3, group_feats)
    second_send = jnp.concatenate(
        [out_weight.T.astype(bf16), up_weight.astype(bf16), down_weight.T.astype(bf16)], axis=1
    )
    second_send, first_got_tie = lax.optimization_barrier((second_send, first_got[0, 0, 0:1]))
    weights = lax.all_gather(second_send, "seq", axis=0, tiled=True)
    out_wt = weights[:, :group_feats]
    up_w = weights[:, group_feats : group_feats + ff]
    down_wt = weights[:, group_feats + ff :]

    own_planes = lax.dynamic_slice(
        plane_bits, (spot * hashes, 0, core * heads, 0), (hashes, bits, heads, head_dim)
    )
    signs = (2 * own_planes - 1).astype(f32)
    scale = sharpness / math.sqrt(head_dim)
    table_bits = (
        jnp.arange(buckets, dtype=jnp.int32)[None, :] // (2 ** jnp.arange(bits, dtype=jnp.int32))[:, None] % 2
    ).astype(f32) - 0.5
    code_w = scale * sum(
        table_bits[j][None, None, :, None] * jnp.transpose(signs[:, j], (1, 0, 2))[:, :, None, :]
        for j in range(bits)
    )
    code_w = code_w.reshape(heads, hashes * buckets, head_dim).astype(bf16)
    code_wt = jnp.transpose(code_w, (0, 2, 1))
    bit_w = scale * jnp.pad(
        jnp.transpose(signs, (2, 1, 0, 3)), ((0, 0), (0, 0), (0, rows - hashes), (0, 0))
    )
    bit_w = bit_w.reshape(heads, bits * rows, head_dim).astype(bf16)

    own_w = lax.dynamic_slice(qkv_all, (0, 0, core * feats), (width, 3, feats))
    own_w = own_w.reshape(width, 3, heads, head_dim)
    w_rows = jnp.transpose(own_w, (2, 1, 3, 0)).reshape(heads, 3 * head_dim, width)
    w_cols = jnp.transpose(own_w, (2, 0, 1, 3)).reshape(heads, width, 3 * head_dim)

    smem = pl.BlockSpec(memory_space=pltpu.SMEM)
    whole = lambda shape: pl.BlockSpec(
        shape, lambda h: (0,) * len(shape), pipeline_mode=pl.Buffered(1)
    )
    by_head = lambda *shape: pl.BlockSpec((1,) + shape, lambda h: (h,) + (0,) * len(shape))
    head_rows = pl.BlockSpec((head_dim, total), lambda h: (h, 0))
    code_rows = hashes * buckets
    params = pltpu.CompilerParams(
        dimension_semantics=("arbitrary",), vmem_limit_bytes=VMEM_LIMIT
    )
    num_parts, q_unit, k_unit, values, inverses, tables, counts = pl.pallas_call(
        partial(forward_kernel, hashes, bits, rows, tile, chips),
        grid=(heads,),
        in_specs=[
            smem,
            whole((total, width)),
            by_head(3 * head_dim, width),
            by_head(code_rows, head_dim),
            by_head(bits * rows, head_dim),
        ],
        out_specs=[
            pl.BlockSpec((chips, head_dim, tile), lambda h: (0, h, 0)),
            head_rows,
            head_rows,
            head_rows,
            by_head(8, total),
            by_head(code_rows, 2 * head_dim),
            by_head(8, code_rows),
        ],
        out_shape=[
            jax.ShapeDtypeStruct((chips, feats, tile), bf16),
            jax.ShapeDtypeStruct((feats, total), bf16),
            jax.ShapeDtypeStruct((feats, total), bf16),
            jax.ShapeDtypeStruct((feats, total), bf16),
            jax.ShapeDtypeStruct((heads, 8, total), f32),
            jax.ShapeDtypeStruct((heads, code_rows, 2 * head_dim), bf16),
            jax.ShapeDtypeStruct((heads, 8, code_rows), f32),
        ],
        scratch_shapes=[
            pltpu.VMEM((code_rows, 2 * head_dim + 16), f32),
            pltpu.VMEM((code_rows, tile), bf16),
        ],
        compiler_params=params,
        name="hash_forward",
    )(limit, all_tokens, w_rows, code_w, bit_w)

    slice_width = buckets // seq_count
    count_send = counts[:, 0:2].reshape(heads, 2, hashes, seq_count, slice_width)
    count_got = lax.all_to_all(
        jnp.transpose(count_send, (3, 1, 2, 0, 4)), "seq", 0, 0, tiled=True
    ).reshape(chips, CORES, 2, hashes, heads, slice_width)
    occupancy = jnp.transpose(count_got, (2, 0, 3, 1, 4, 5)).reshape(
        2, hash_count, group_heads, slice_width
    ) * (buckets / (tok_rows * seq_count))

    ext = tile + 2 * rim
    chip_start = spot * tile
    tok_pos = chip_start + jnp.arange(tile, dtype=jnp.int32)
    ext_pos = chip_start - rim + jnp.arange(ext, dtype=jnp.int32)
    same = ((tok_pos >= limit[0])[None, :] == (ext_pos >= limit[0])[:, None]).astype(f32)
    apart = jnp.arange(ext, dtype=jnp.int32)[:, None] - jnp.arange(tile, dtype=jnp.int32)[None, :]
    own_taps = lax.dynamic_slice(conv_taps, (core * heads, 0), (heads, taps))
    spread = jnp.zeros((heads, ext, tile), f32)
    gather_back = jnp.zeros((heads, ext, tile), f32)
    for o in range(taps):
        spread = spread + own_taps[:, o][:, None, None] * (apart == o)
        gather_back = gather_back + own_taps[:, o][:, None, None] * (apart == 2 * rim - o)
    spread = spread * same
    gather_back = gather_back * same

    num_got = across(num_parts)
    numerator = jnp.sum(num_got.astype(f32), axis=0).reshape(heads, head_dim, tile)
    mean_sq = jnp.mean(numerator * numerator, axis=1, keepdims=True)
    att_inv = lax.rsqrt(mean_sq + norm_eps)
    attention = numerator * att_inv
    value_ext = lax.dynamic_slice(
        jnp.pad(values, ((0, 0), (rim, rim))), (0, chip_start), (feats, ext)
    ).reshape(heads, head_dim, ext)
    conv = jnp.einsum("hfe,het->hft", value_ext.astype(f32), spread, precision=highest)
    context = (attention + conv).astype(bf16).reshape(feats, CORES, tok_rows)
    context = within(jnp.transpose(context, (1, 0, 2))).reshape(group_feats, tok_rows)

    mixer_out = swap_sum(jnp.einsum("ft,cf->tc", context, out_wt, preferred_element_type=f32))
    first_hat, first_inverse = normalize(tokens.astype(f32) + mixer_out)
    first_out = first_hat * norm_params[0] + norm_params[1]
    first_low = first_out.astype(bf16)
    hidden = jnp.dot(first_low, up_w, preferred_element_type=f32)
    gelu_out, gelu_pull = jax.vjp(partial(jax.nn.gelu, approximate=False), hidden)
    active = gelu_out.astype(bf16)
    feed_out = swap_sum(jnp.einsum("tf,cf->tc", active, down_wt, preferred_element_type=f32))
    second_hat, second_inverse = normalize(first_out + feed_out)
    block_out = second_hat * norm_params[2] + norm_params[3]
    grad_out = cotangent.astype(f32)
    grad_second, gain_two, offset_two = norm_back(
        grad_out, second_hat, second_inverse, norm_params[2]
    )
    grad_feed_low = grad_second.astype(bf16)
    grad_active = jnp.dot(grad_feed_low, down_wt, preferred_element_type=f32)
    grad_hidden_low = gelu_pull(grad_active)[0].astype(bf16)
    grad_first = grad_second + swap_sum(
        jnp.einsum("tf,cf->tc", grad_hidden_low, up_w, preferred_element_type=f32)
    )
    grad_mixer, gain_one, offset_one = norm_back(
        grad_first, first_hat, first_inverse, norm_params[0]
    )
    grad_mixer_low = grad_mixer.astype(bf16)
    grad_context = jnp.einsum("tc,cf->ft", grad_mixer_low, out_wt, preferred_element_type=f32)
    grad_context = within(grad_context.reshape(CORES, feats, tok_rows))
    grad_context = jnp.transpose(grad_context, (1, 0, 2)).reshape(heads, head_dim, tile)
    att_grad = att_inv * (
        grad_context - attention * jnp.mean(grad_context * attention, axis=1, keepdims=True)
    )
    gnum = att_grad.astype(bf16).reshape(feats, tile)
    gnum_all = across(jnp.broadcast_to(gnum[None], (chips, feats, tile)))

    big_grad = jnp.concatenate(
        [
            jnp.einsum("tc,ft->cf", grad_mixer_low, context, preferred_element_type=f32).astype(bf16),
            jnp.einsum("tc,tf->cf", first_low, grad_hidden_low, preferred_element_type=f32).astype(bf16),
            jnp.einsum("tc,tf->cf", grad_feed_low, active, preferred_element_type=f32).astype(bf16),
        ],
        axis=1,
    )
    big_owned = lax.psum_scatter(big_grad, "seq", scatter_dimension=0, tiled=True).astype(f32)

    low_context = grad_context.astype(bf16).reshape(feats, tile)
    up_moves = [(i, i + CORES) for i in range(seq_count - CORES)]
    down_moves = [(j, i) for i, j in up_moves]
    before = lax.ppermute(low_context[:, tile - rim :], "seq", up_moves)
    after = lax.ppermute(low_context[:, :rim], "seq", down_moves)
    context_ext = jnp.concatenate([before, low_context, after], axis=1).reshape(
        heads, head_dim, ext
    )
    conv_grad = jnp.einsum(
        "hfe,het->hft", context_ext.astype(f32), gather_back, precision=highest
    ).reshape(feats, tile)
    crossed = jnp.einsum(
        "hfe,hft->het", value_ext.astype(f32), grad_context, precision=highest
    ) * same
    tap_grad = jnp.stack(
        [jnp.sum(crossed * (apart == o), axis=(1, 2)) for o in range(taps)], axis=1
    )
    tap_rows = lax.dynamic_update_slice(
        jnp.zeros((group_heads, taps), f32), tap_grad, (core * heads, 0)
    )
    small = jnp.concatenate(
        [
            jnp.stack([gain_one, offset_one, gain_two, offset_two]),
            jnp.pad(tap_rows, ((0, 8 - group_heads), (0, width - taps))),
        ],
        axis=0,
    )
    small_got = lax.all_to_all(
        jnp.broadcast_to(small[None], (seq_count,) + small.shape), "seq", 0, 0, tiled=True
    )
    small_sum = jnp.sum(small_got, axis=0)
    norm_grad = small_sum[:4]
    conv_tap_grad = small_sum[4 : 4 + group_heads, :taps]

    grad_parts, back_parts = pl.pallas_call(
        partial(backward_kernel, hashes, bits, rows, tile, chips, heads),
        grid=(heads,),
        in_specs=[
            smem,
            smem,
            whole((total, width)),
            whole((heads, width, 3 * head_dim)),
            by_head(code_rows, head_dim),
            by_head(head_dim, code_rows),
            by_head(bits * rows, head_dim),
            head_rows,
            head_rows,
            head_rows,
            by_head(8, total),
            by_head(code_rows, 2 * head_dim),
            pl.BlockSpec((chips, head_dim, tile), lambda h: (0, h, 0)),
            pl.BlockSpec((head_dim, tile), lambda h: (h, 0)),
        ],
        out_specs=[
            pl.BlockSpec((3 * head_dim, width), lambda h: (h, 0)),
            pl.BlockSpec(
                (CORES, chips, width, tok_rows), lambda h: (0, 0, 0, 0),
                pipeline_mode=pl.Buffered(1),
            ),
        ],
        out_shape=[
            jax.ShapeDtypeStruct((3 * feats, width), f32),
            jax.ShapeDtypeStruct((CORES, chips, width, tok_rows), bf16),
        ],
        scratch_shapes=[
            pltpu.VMEM((code_rows, 2 * head_dim), f32),
            pltpu.VMEM((code_rows, tile), bf16),
            pltpu.VMEM((code_rows, tile), bf16),
            pltpu.VMEM((heads, 3 * head_dim, total), bf16),
        ],
        compiler_params=params,
        name="hash_backward",
    )(
        limit, spot[None], all_tokens, w_cols, code_w, code_wt, bit_w,
        q_unit, k_unit, values, inverses, tables, gnum_all, conv_grad,
    )

    qkv_send = grad_parts.T.astype(bf16).reshape(chips, CORES * own_rows, 3 * feats)
    qkv_half = jnp.sum(across(qkv_send).astype(f32), axis=0)
    qkv_half = within(qkv_half.reshape(CORES, own_rows, 3 * feats))
    qkv_owned = jnp.transpose(
        qkv_half.reshape(CORES, own_rows, heads, 3, head_dim), (3, 1, 0, 2, 4)
    ).reshape(3, own_rows, group_feats)

    mine = lax.dynamic_index_in_dim(back_parts, core, 0, keepdims=False)
    theirs = lax.dynamic_index_in_dim(back_parts, 1 - core, 0, keepdims=False)
    swap = [(i, i ^ 1) for i in range(seq_count)]
    chip_sum = mine.astype(f32) + lax.ppermute(theirs, "seq", swap).astype(f32)
    side = lax.axis_index("head")
    half = width // 2
    chip_sum = chip_sum.astype(bf16).reshape(chips, 2, half, tok_rows)
    keep = lax.dynamic_index_in_dim(chip_sum, side, 1, keepdims=False)
    give = lax.dynamic_index_in_dim(chip_sum, 1 - side, 1, keepdims=False)
    pair_sum = keep.astype(f32) + lax.ppermute(give, "head", [(0, 1), (1, 0)]).astype(f32)
    back_half = jnp.sum(across(pair_sum.astype(bf16)).astype(f32), axis=0)
    back_other = lax.ppermute(back_half, "head", [(0, 1), (1, 0)])
    upper = jnp.where(side == 0, back_half, back_other)
    lower = jnp.where(side == 0, back_other, back_half)
    tokens_grad = grad_mixer + jnp.concatenate([upper, lower], axis=0).T

    out_owned = big_owned[:, :group_feats].T
    up_owned = big_owned[:, group_feats : group_feats + ff]
    down_owned = big_owned[:, group_feats + ff :].T
    qkv_new, qkv_first_new, qkv_second_new = adam_step(
        qkv_weight, qkv_first, qkv_second, qkv_owned, D ** (-0.5)
    )
    out_new, out_first_new, out_second_new = adam_step(
        out_weight, out_first, out_second, out_owned, D ** (-0.5)
    )
    up_new, up_first_new, up_second_new = adam_step(
        up_weight, up_first, up_second, up_owned, D ** (-0.5)
    )
    down_new, down_first_new, down_second_new = adam_step(
        down_weight, down_first, down_second, down_owned, FF ** (-0.5)
    )
    norm_new, norm_first_new, norm_second_new = adam_step(
        norm_params, norm_first, norm_second, norm_grad, 0.3
    )
    conv_new, conv_first_new, conv_second_new = adam_step(
        conv_taps, conv_first, conv_second, conv_tap_grad, CONV ** (-0.5)
    )
    return (
        block_out,
        tokens_grad,
        occupancy,
        qkv_new,
        qkv_first_new,
        qkv_second_new,
        qkv_new.astype(jnp.bfloat16),
        out_new,
        out_first_new,
        out_second_new,
        out_new.astype(jnp.bfloat16),
        up_new,
        up_first_new,
        up_second_new,
        up_new.astype(jnp.bfloat16),
        down_new,
        down_first_new,
        down_second_new,
        down_new.astype(jnp.bfloat16),
        norm_new,
        norm_first_new,
        norm_second_new,
        conv_new,
        conv_first_new,
        conv_second_new,
    )


def solution(mesh):
    in_specs = (
        P("seq", None),
        P("seq", None),
        P(),
        P(None, None, "head", None),
        P(None, "seq", "head"),
        P(None, "seq", "head"),
        P(None, "seq", "head"),
        P("head", "seq"),
        P("head", "seq"),
        P("head", "seq"),
        P("seq", "head"),
        P("seq", "head"),
        P("seq", "head"),
        P("head", "seq"),
        P("head", "seq"),
        P("head", "seq"),
        P(),
        P(),
        P(),
        P("head", None),
        P("head", None),
        P("head", None),
    )
    out_specs = (
        P("seq", None),
        P("seq", None),
        P(None, None, "head", "seq"),
        P(None, "seq", "head"),
        P(None, "seq", "head"),
        P(None, "seq", "head"),
        P(None, "seq", "head"),
        P("head", "seq"),
        P("head", "seq"),
        P("head", "seq"),
        P("head", "seq"),
        P("seq", "head"),
        P("seq", "head"),
        P("seq", "head"),
        P("seq", "head"),
        P("head", "seq"),
        P("head", "seq"),
        P("head", "seq"),
        P("head", "seq"),
        P(),
        P(),
        P(),
        P("head", None),
        P("head", None),
        P("head", None),
    )
    return jax.shard_map(
        on_device, mesh=mesh, in_specs=in_specs, out_specs=out_specs, check_vma=False
    )
```

time: 2020 us -> 424 us (0.21)
  blocking collectives: 605 us -> 7.8 us
  matrix products: 594 us -> 34.1 us
  waiting for transfers between devices: 591 us -> 112 us
  Pallas kernels: 0 us -> 88.7 us
  local copies, waits for them, and re-layouts: 133 us -> 55 us
  starting transfers between devices: 16.3 us -> 52.7 us
    psum x2 -> x0, blocking collectives: 579 us -> none  [the longest x1 517 us: on_device(): summed, totals = lax.psum((tables, counts), 'seq')]
    dot_general x411 -> x11, matrix products: 591 us -> 31.8 us  [the longest x1 7.8 us: on_device(): jnp.einsum('hfe,het->hft', context_ext.astype(f32), gather_back, precisio...]
    reduce_scatter x4 -> x1, waiting for transfers between devices: 260 us -> 0.01 us  [on_device(): lax.psum_scatter(big_grad, 'seq', scatter_dimension=0, tiled=True)]
    psum x5 -> x0, waiting for transfers between devices: 217 us -> none  [the longest x1 125 us: on_device(): summed, totals = lax.psum((tables, counts), 'seq')]
    pallas_call x0 -> x2, Pallas kernels: none -> 88.7 us  [the longest x1 49 us: on_device(): pl.pallas_call(partial(backward_kernel, hashes, bits, rows, tile, chips,...]
    all_gather x4 -> x2, waiting for transfers between devices: 112 us -> 26.4 us  [the longest x1 26.4 us: on_device(): first_got = lax.all_gather(first_send, 'seq', axis=0, tiled=False)]
    all_to_all x0 -> x7, waiting for transfers between devices: none -> 48.7 us  [the longest x1 14.7 us: on_device(): back_half = jnp.sum(across(pair_sum.astype(bf16)).astype(f32), axis=0)]
    dynamic_update_slice x32 -> x1, local copies, waits for them, and re-layouts: 40.7 us -> 0.12 us  [on_device(): lax.dynamic_update_slice(jnp.zeros((group_heads, taps), f32), tap_grad, (...]
  transfers between devices with their start and end apart: 17 -> 18, of which waited for: 12 -> 13; matrix products, arithmetic and copies ran while one was open for 12% -> 26% of each run, Pallas kernels for 0% -> 21%
where the time goes in v1:
time: 424 us; the launch traced here: 416 us
  waiting for transfers between devices  112 us (26%)
  Pallas kernels  88.7 us (21%)
  local copies, waits for them, and re-layouts  55 us (13%)
  starting transfers between devices  52.7 us (12%)
  other arithmetic  49.7 us (12%)
  matrix products  34.1 us (8%)
  between operations  16.4 us (4%)
  blocking collectives  7.8 us (2%)
    pallas_call x1, Pallas kernels, on_device(): pl.pallas_call(partial(backward_kernel, hashes, bits, rows, tile, chips,...  49 us
    pallas_call x1, Pallas kernels, on_device(): pl.pallas_call(partial(forward_kernel, hashes, bits, rows, tile, chips),...  39.7 us
    all_gather x1, waiting for transfers between devices, on_device(): first_got = lax.all_gather(first_send, 'seq', axis=0, tiled=False)  26.4 us
    ppermute x1, waiting for transfers between devices, on_device(): lax.ppermute(give, 'head', [(0, 1), (1, 0)]).astype(f32)  18.1 us
    all_to_all x1, waiting for transfers between devices, on_device(): back_half = jnp.sum(across(pair_sum.astype(bf16)).astype(f32), axis=0)  14.7 us
    mul x22, local copies, waits for them, and re-layouts, on_device(): table_bits[j][None, None, :, None]  14.5 us
    convert_element_type x17, other arithmetic, on_device(): spread = spread + own_taps[:, o][:, None, None] * (apart == o)  14 us
    all_to_all x1, starting transfers between devices, on_device(): lax.all_to_all(jnp.transpose(count_send, (3, 1, 2, 0, 4)), 'seq', 0, 0, t...  13.1 us
  transfers between devices with their start and end apart: 18, of which 13 were waited for; matrix products, arithmetic and copies ran while one was open for 26% of the time, Pallas kernels for 21%

profile of v1, /device:TPU:0, one launch (start us, length us, event | category | flops | bytes accessed | tf_op | source)
XLA Modules:
  0.0 415.9 jit_solution(2847175397687835317)
XLA Ops:
  41.6 26.4 %all-gather.6.cloned.1.call-done = bf16[3200,768]{1,0:T(8,128)(2,1)} async-done(((bf16[200,768]{1,0:T(8,128)(2,1)}), bf16[3200,768]{1,0:T(8,128)(2,1)}) %all-gather.6.cloned.1.call-update) | async-done | bytes 4915216 | tf_op jit(solution)/shard_map/all_gather | solution.py:288
  69.6 3.9 slice.296
  73.5 3.0 reshape.718
  76.5 3.0 constant_dynamic-slice_fusion.1
  81.4 39.7 %hash_forward.1 = (bf16[8,192,256]{2,1,0:T(8,128)(2,1)}, bf16[192,2048]{1,0:T(8,128)(2,1)}, bf16[192,2048]{1,0:T(8,128)(2,1)}, bf16[192,2048]{1,0:T(8,128)(2,1)}...) custom-call(s32[1]{0:T(128)} %bitcast.263, bf16[2048,768]{1,0:T(8,128)(2,1)} %bitcast.233, ...), custom_call_target="tpu_custom_call" | custom-call | tf_op jit(solution)/shard_map/hash_forward/pallas_call | solution.py:334
  121.1 3.7 all-to-all-start
  132.8 12.4 %all-to-all-done = bf16[8,192,256]{2,1,0:T(8,128)(2,1)S(1)} async-done(((bf16[8,192,256]{2,1,0:T(8,128)(2,1)}), bf16[8,192,256]{2,1,0:T(8,128)(2,1)S(1)}, u32[]{:S(2)}, u32[]{:S(2)}) %all-to-all-start) | async-done | bytes 786464 | tf_op jit(solution)/shard_map/all_to_all | solution.py:394
  145.8 6.4 %fusion.16 = bf16[3,64,256]{2,1,0:T(8,128)(2,1)S(1)} fusion(bf16[3,64,288]{2,1,0:T(8,128)(2,1)S(1)} %bitcast.261, f32[288,256]{1,0:T(8,128)} %get-tuple-element.209, f32[288,256]{1,0:T(8,128)} %get-tuple-element.208, f32[3]{0:T(128)S(1)} %get-tuple-element.89, f32[288,256]{1,0:T(8,128)S(1)} %get-tuple-element.207, f32[3]{0:T(128)S(1)} %get-tuple-element.90, ...), kind=kOutput, calls=%fused_computation.28 | convolution fusion | flops 184614912 | bytes 10435980 | tf_op jit(solution)/shard_map/hfe,het->hft/dot_general | solution.py:402
  152.9 3.3 all-to-all-start.1
  160.7 5.5 %collective-permute-done = bf16[128,768]{1,0:T(8,128)(2,1)S(1)} collective-permute-done((bf16[128,768]{1,0:T(8,128)(2,1)S(1)}, bf16[128,768]{1,0:T(8,128)(2,1)S(1)}, u32[]{:S(2)}, u32[]{:S(2)}) %collective-permute-start) | collective-permute-done | bytes 196640 | tf_op jit(solution)/shard_map/ppermute | solution.py:40
  166.5 3.8 multiply_convert_fusion
  172.8 4.7 %collective-permute-done.1 = bf16[128,768]{1,0:T(8,128)(2,1)S(1)} collective-permute-done((bf16[128,768]{1,0:T(8,128)(2,1)S(1)}, bf16[128,768]{1,0:T(8,128)(2,1)S(1)}, u32[]{:S(2)}, u32[]{:S(2)}) %collective-permute-start.1) | collective-permute-done | bytes 196640 | tf_op jit(solution)/shard_map/ppermute | solution.py:40
  194.4 4.6 %pad_maximum_fusion = bf16[768,3456]{1,0:T(8,128)(2,1)} fusion(bf16[768,1536]{1,0:T(8,128)(2,1)S(1)} %convolution_convert_fusion, bf16[768,1536]{1,0:T(8,128)(2,1)} %convolution_convert_fusion.1, bf16[768,384]{1,0:T(8,128)(2,1)} %copy.289), kind=kLoop, calls=%fused_computation | loop fusion | flops 15925248 | bytes 10616832 | tf_op jit(solution)/shard_map/concatenate | solution.py:439
  201.4 3.9 all_to_all.45
  206.7 4.2 %all-to-all-start.3 = ((bf16[8,192,256]{2,1,0:T(8,128)(2,1)}), bf16[8,192,256]{2,1,0:T(8,128)(2,1)}, u32[]{:S(2)}, u32[]{:S(2)}) async-start(bf16[8,192,256]{2,1,0:T(8,128)(2,1)} %broadcast_in_dim.13), calls=%async_computation.3 | async-start | bytes 1572864 | tf_op jit(solution)/shard_map/all_to_all | solution.py:437
  211.3 4.5 %collective-permute-start.3 = (bf16[192,16]{1,0:T(8,128)(2,1)S(1)}, bf16[192,16]{1,0:T(8,128)(2,1)}, u32[]{:S(2)}, u32[]{:S(2)}) collective-permute-start(bf16[192,16]{1,0:T(8,128)(2,1)S(1)} %get-tuple-element.155), channel_id=1, source_target_pairs={{0,4},{2,6},{4,8},{6,10},{8,12},{10,14},{12,16},{14,18},{16,20},{1... | collective-permute-start | bytes 18440 | tf_op jit(solution)/shard_map/ppermute | solution.py:452
  218.9 3.3 collective-permute-done.4
  222.4 7.8 %fusion.49 = f32[3,64,256]{2,1,0:T(8,128)} fusion(f32[288,256]{1,0:T(8,128)} %get-tuple-element.209, f32[288,256]{1,0:T(8,128)} %get-tuple-element.208, f32[3]{0:T(128)S(1)} %copy-done.77, f32[288,256]{1,0:T(8,128)S(1)} %copy-done.11, f32[3]{0:T(128)S(1)} %copy-done.79, f32[288,256]{1,0:T(8,128)S(1)} %copy-done.9, f32[3]{0:T(128)S(1)} %copy-done.81, ...), kind=kOutput, calls=%fused_computation.95 | convolution fusion | flops 184799232 | bytes 10334604 | tf_op jit(solution)/shard_map/hfe,het->hft/dot_general | solution.py:457
  230.2 7.3 %all-to-all-done.3.gnum_ref = bf16[8,192,256]{2,1,0:T(8,128)(2,1)} async-done(((bf16[8,192,256]{2,1,0:T(8,128)(2,1)}), bf16[8,192,256]{2,1,0:T(8,128)(2,1)}, u32[]{:S(2)}, u32[]{:S(2)}) %all-to-all-start.3) | async-done | bytes 786464 | tf_op jit(solution)/shard_map/all_to_all | solution.py:437
  237.6 49.0 %hash_backward.1 = (f32[576,768]{1,0:T(8,128)}, bf16[2,8,768,128]{3,2,1,0:T(8,128)(2,1)}) custom-call(s32[1]{0:T(128)} %bitcast.264, s32[1]{0:T(128)} %bitcast.43.spot_ref, bf16[2048,768]{1,0:T(8,128)(2,1)} %bitcast.234, bf16[3,768,192]{2,1,0:T(8,128)(2,1)} %copy.279.w_ref, bf16[3,1024,64]{2,1,0:T(8,128)(2,1)} %copy.274.code_ref, ...), custom_call_target="tpu_custom_call" | custom-call | tf_op jit(solution)/shard_map/hash_backward/pallas_call | solution.py:483
  291.4 13.1 %all-to-all-start.5 = ((f32[16,1,384]{2,1,0:T(1,128)}), f32[16,1,384]{2,1,0:T(1,128)S(1)}, u32[]{:S(2)}, u32[]{:S(2)}) async-start(f32[16,1,384]{2,1,0:T(1,128)} %reshape.776), calls=%async_computation.5 | async-start | bytes 49152 | tf_op jit(solution)/shard_map/all_to_all | solution.py:372
  307.6 3.5 all-to-all-done.5
  311.2 3.8 all-to-all-start.6
  315.1 5.0 %multiply_reduce_fusion.18 = (f32[3]{0:T(128)}, f32[3]{0:T(128)S(1)}, f32[3]{0:T(128)}, f32[3]{0:T(128)}, f32[3]{0:T(128)}, /*index=5*/f32[3]{0:T(128)}, f32[3]{...) fusion(f32[288,256]{1,0:T(8,128)} %get-tuple-element.190, ...), kind=kOutput, calls=%fused_computation.79 | convolution fusion | flops 176725952 | bytes 5910708 | tf_op jit(solution)/shard_map/hfe,hft->het/dot_general | solution.py:460
  321.1 3.4 multiply_reduce_fusion
  330.1 9.3 %all-to-all-done.6 = bf16[8,96,576]{2,1,0:T(8,128)(2,1)S(1)} async-done(((bf16[8,96,576]{2,1,0:T(8,128)(2,1)}), bf16[8,96,576]{2,1,0:T(8,128)(2,1)S(1)}, u32[]{:S(2)}, u32[]{:S(2)}) %all-to-all-start.6) | async-done | bytes 884768 | tf_op jit(solution)/shard_map/all_to_all | solution.py:527
  340.4 4.3 %all-to-all-start.8 = ((f32[16,12,768]{2,1,0:T(8,128)}), f32[16,12,768]{2,1,0:T(8,128)}, u32[]{:S(2)}, u32[]{:S(2)}) async-start(f32[16,12,768]{2,1,0:T(8,128)} %broadcast_in_dim.15), calls=%async_computation.9 | async-start | bytes 1572864 | tf_op jit(solution)/shard_map/all_to_all | solution.py:476
  347.5 18.1 %collective-permute-done.6 = bf16[8,384,128]{2,1,0:T(8,128)(2,1)} collective-permute-done((bf16[8,384,128]{2,1,0:T(8,128)(2,1)}, bf16[8,384,128]{2,1,0:T(8,128)(2,1)}, u32[]{:S(2)}, u32[]{:S(2)}) %collective-permute-start.6) | collective-permute-done | bytes 786464 | tf_op jit(solution)/shard_map/ppermute | solution.py:542
  367.8 3.9 all_to_all.46
  371.7 5.9 %all-to-all-start.4 = ((bf16[8,384,128]{2,1,0:T(8,128)(2,1)}), bf16[8,384,128]{2,1,0:T(8,128)(2,1)S(1)}, u32[]{:S(2)}, u32[]{:S(2)}) async-start(bf16[8,384,128]{2,1,0:T(8,128)(2,1)} %fusion.9), calls=%async_computation.4 | async-start | bytes 1572864 | tf_op jit(solution)/shard_map/all_to_all | solution.py:543
  383.3 14.7 %all-to-all-done.4 = bf16[8,384,128]{2,1,0:T(8,128)(2,1)S(1)} async-done(((bf16[8,384,128]{2,1,0:T(8,128)(2,1)}), bf16[8,384,128]{2,1,0:T(8,128)(2,1)S(1)}, u32[]{:S(2)}, u32[]{:S(2)}) %all-to-all-start.4) | async-done | bytes 786464 | tf_op jit(solution)/shard_map/all_to_all | solution.py:543
  401.2 3.0 collective-permute-done.7
  (443 shorter events, 111.0 us)
Async XLA Ops:
  7.2 60.8 %all-gather.6.cloned.1.call-start = ((), (), s32[]{:S(2)}) async-start(), calls=%async_computation.12 | async-start | bytes 5222400 | tf_op jit(solution)/shard_map/all_gather | solution.py:288
  10.1 146.2 %all-gather.4.cloned.1.call-start = ((), (), s32[]{:S(2)}) async-start(), calls=%async_computation.10 | async-start | bytes 5640192 | tf_op jit(solution)/shard_map/all_gather | solution.py:295
  34.6 110.9 %copy-start.46 = (f32[3]{0:T(128)}, f32[3]{0:T(128)S(1)}, u32[]{:S(2)}) copy-start(f32[3]{0:T(128)S(1)} %get-tuple-element.107) | copy-start | bytes 40
  34.6 110.9 %copy-start.48 = (f32[3]{0:T(128)}, f32[3]{0:T(128)S(1)}, u32[]{:S(2)}) copy-start(f32[3]{0:T(128)S(1)} %get-tuple-element.108) | copy-start | bytes 40
  34.6 110.9 %copy-start.50 = (f32[3]{0:T(128)}, f32[3]{0:T(128)S(1)}, u32[]{:S(2)}) copy-start(f32[3]{0:T(128)S(1)} %get-tuple-element.109) | copy-start | bytes 40
  34.6 110.9 %copy-start.52 = (f32[3]{0:T(128)}, f32[3]{0:T(128)S(1)}, u32[]{:S(2)}) copy-start(f32[3]{0:T(128)S(1)} %get-tuple-element.110) | copy-start | bytes 40
  34.6 110.9 %copy-start.54 = (f32[3]{0:T(128)}, f32[3]{0:T(128)S(1)}, u32[]{:S(2)}) copy-start(f32[3]{0:T(128)S(1)} %get-tuple-element.111) | copy-start | bytes 40
  34.6 110.9 %copy-start.56 = (f32[3]{0:T(128)}, f32[3]{0:T(128)S(1)}, u32[]{:S(2)}) copy-start(f32[3]{0:T(128)S(1)} %get-tuple-element.112) | copy-start | bytes 40
  34.6 110.9 %copy-start.58 = (f32[3]{0:T(128)}, f32[3]{0:T(128)S(1)}, u32[]{:S(2)}) copy-start(f32[3]{0:T(128)S(1)} %get-tuple-element.113) | copy-start | bytes 40
  34.6 110.9 %copy-start.60 = (f32[3]{0:T(128)}, f32[3]{0:T(128)S(1)}, u32[]{:S(2)}) copy-start(f32[3]{0:T(128)S(1)} %get-tuple-element.114) | copy-start | bytes 40
  34.6 110.9 %copy-start.62 = (f32[3]{0:T(128)}, f32[3]{0:T(128)S(1)}, u32[]{:S(2)}) copy-start(f32[3]{0:T(128)S(1)} %get-tuple-element.115) | copy-start | bytes 40
  34.7 110.9 %copy-start.64 = (f32[3]{0:T(128)}, f32[3]{0:T(128)S(1)}, u32[]{:S(2)}) copy-start(f32[3]{0:T(128)S(1)} %get-tuple-element.116) | copy-start | bytes 40
  34.7 110.9 %copy-start.66 = (f32[3]{0:T(128)}, f32[3]{0:T(128)S(1)}, u32[]{:S(2)}) copy-start(f32[3]{0:T(128)S(1)} %get-tuple-element.117) | copy-start | bytes 40
  34.7 110.9 %copy-start.68 = (f32[3]{0:T(128)}, f32[3]{0:T(128)S(1)}, u32[]{:S(2)}) copy-start(f32[3]{0:T(128)S(1)} %get-tuple-element.118) | copy-start | bytes 40
  34.7 110.9 %copy-start.70 = (f32[3]{0:T(128)}, f32[3]{0:T(128)S(1)}, u32[]{:S(2)}) copy-start(f32[3]{0:T(128)S(1)} %get-tuple-element.119) | copy-start | bytes 40
  34.7 110.9 %copy-start.72 = (f32[3]{0:T(128)}, f32[3]{0:T(128)S(1)}, u32[]{:S(2)}) copy-start(f32[3]{0:T(128)S(1)} %get-tuple-element.120) | copy-start | bytes 40
  121.1 24.2 %all-to-all-start = ((bf16[8,192,256]{2,1,0:T(8,128)(2,1)}), bf16[8,192,256]{2,1,0:T(8,128)(2,1)S(1)}, u32[]{:S(2)}, u32[]{:S(2)}) async-start(bf16[8,192,256]{2,1,0:T(8,128)(2,1)} %get-tuple-element.34), calls=%async_computation | async-start | bytes 1572864 | tf_op jit(solution)/shard_map/all_to_all | solution.py:394
  152.9 4.8 %all-to-all-start.1 = ((bf16[2,192,128]{2,1,0:T(8,128)(2,1)}), bf16[2,192,128]{2,1,0:T(8,128)(2,1)S(1)}, u32[]{:S(2)}, u32[]{:S(2)}) async-start(bf16[2,192,128]{2,1,0:T(8,128)(2,1)} %bitcast.229), calls=%async_computation.1 | async-start | bytes 196608 | tf_op jit(solution)/shard_map/all_to_all | solution.py:404
  156.3 248.7 %reduce-scatter.2.cloned.1.call-start = ((), (), s32[]{:S(2)}) async-start(), calls=%async_computation.11 | async-start | bytes 5640192 | tf_op jit(solution)/shard_map/reduce_scatter | solution.py:447
  159.1 7.0 %collective-permute-start = (bf16[128,768]{1,0:T(8,128)(2,1)S(1)}, bf16[128,768]{1,0:T(8,128)(2,1)S(1)}, u32[]{:S(2)}, u32[]{:S(2)}) collective-permute-start(bf16[128,768]{1,0:T(8,128)(2,1)S(1)} %convolution_convert_fusion.3), channel_id=1, source_target_pairs={{0,1},{1,0},{2,3},{3,2},{4,5},{5,4},{6,7},{7,6},{8,9},{9,8},{10,11... | collective-permute-start | bytes 589832 | tf_op jit(solution)/shard_map/ppermute | solution.py:40
  171.3 6.2 %collective-permute-start.1 = (bf16[128,768]{1,0:T(8,128)(2,1)S(1)}, bf16[128,768]{1,0:T(8,128)(2,1)S(1)}, u32[]{:S(2)}, u32[]{:S(2)}) collective-permute-start(bf16[128,768]{1,0:T(8,128)(2,1)S(1)} %fusion.13), channel_id=1, source_target_pairs={{0,1},{1,0},{2,3},{3,2},{4,5},{5,4},{6,7},{7,6},{8,9},{9,8},{10,11... | collective-permute-start | bytes 589832 | tf_op jit(solution)/shard_map/ppermute | solution.py:40
  182.7 5.7 %collective-permute-start.2 = (bf16[128,768]{1,0:T(8,128)(2,1)S(1)}, bf16[128,768]{1,0:T(8,128)(2,1)S(1)}, u32[]{:S(2)}, u32[]{:S(2)}) collective-permute-start(bf16[128,768]{1,0:T(8,128)(2,1)S(1)} %fusion.10), channel_id=1, source_target_pairs={{0,1},{1,0},{2,3},{3,2},{4,5},{5,4},{6,7},{7,6},{8,9},{9,8},{10,11... | collective-permute-start | bytes 589832 | tf_op jit(solution)/shard_map/ppermute | solution.py:40
  206.7 30.9 %all-to-all-start.3 = ((bf16[8,192,256]{2,1,0:T(8,128)(2,1)}), bf16[8,192,256]{2,1,0:T(8,128)(2,1)}, u32[]{:S(2)}, u32[]{:S(2)}) async-start(bf16[8,192,256]{2,1,0:T(8,128)(2,1)} %broadcast_in_dim.13), calls=%async_computation.3 | async-start | bytes 1572864 | tf_op jit(solution)/shard_map/all_to_all | solution.py:437
  211.3 7.5 %collective-permute-start.3 = (bf16[192,16]{1,0:T(8,128)(2,1)S(1)}, bf16[192,16]{1,0:T(8,128)(2,1)}, u32[]{:S(2)}, u32[]{:S(2)}) collective-permute-start(bf16[192,16]{1,0:T(8,128)(2,1)S(1)} %get-tuple-element.155), channel_id=1, source_target_pairs={{0,4},{2,6},{4,8},{6,10},{8,12},{10,14},{12,16},{14,18},{16,20},{1... | collective-permute-start | bytes 18440 | tf_op jit(solution)/shard_map/ppermute | solution.py:452
  215.9 6.3 %collective-permute-start.4 = (bf16[192,16]{1,0:T(8,128)(2,1)S(1)}, bf16[192,16]{1,0:T(8,128)(2,1)}, u32[]{:S(2)}, u32[]{:S(2)}) collective-permute-start(bf16[192,16]{1,0:T(8,128)(2,1)S(1)} %get-tuple-element.156), channel_id=1, source_target_pairs={{4,0},{6,2},{8,4},{10,6},{12,8},{14,10},{16,12},{18,14},{20,16},{2... | collective-permute-start | bytes 18440 | tf_op jit(solution)/shard_map/ppermute | solution.py:453
  289.3 38.5 %collective-permute-start.5 = (bf16[8,768,128]{2,1,0:T(8,128)(2,1)}, bf16[8,768,128]{2,1,0:T(8,128)(2,1)}, u32[]{:S(2)}, u32[]{:S(2)}) collective-permute-start(bf16[8,768,128]{2,1,0:T(8,128)(2,1)} %dynamic-slice_bitcast_fusion), channel_id=1, source_target_pairs={{0,2},{2,0},{4,6},{6,4},{8,10},{10,8},{12,14},{14,12},{16,18},{18,... | collective-permute-start | bytes 4718600 | tf_op jit(solution)/shard_map/ppermute | solution.py:536
  291.4 19.7 %all-to-all-start.5 = ((f32[16,1,384]{2,1,0:T(1,128)}), f32[16,1,384]{2,1,0:T(1,128)S(1)}, u32[]{:S(2)}, u32[]{:S(2)}) async-start(f32[16,1,384]{2,1,0:T(1,128)} %reshape.776), calls=%async_computation.5 | async-start | bytes 49152 | tf_op jit(solution)/shard_map/all_to_all | solution.py:372
  311.2 28.2 %all-to-all-start.6 = ((bf16[8,96,576]{2,1,0:T(8,128)(2,1)}), bf16[8,96,576]{2,1,0:T(8,128)(2,1)S(1)}, u32[]{:S(2)}, u32[]{:S(2)}) async-start(bf16[8,96,576]{2,1,0:T(8,128)(2,1)} %bitcast.64), calls=%async_computation.6 | async-start | bytes 1966080 | tf_op jit(solution)/shard_map/all_to_all | solution.py:527
  340.4 27.4 %all-to-all-start.8 = ((f32[16,12,768]{2,1,0:T(8,128)}), f32[16,12,768]{2,1,0:T(8,128)}, u32[]{:S(2)}, u32[]{:S(2)}) async-start(f32[16,12,768]{2,1,0:T(8,128)} %broadcast_in_dim.15), calls=%async_computation.9 | async-start | bytes 1572864 | tf_op jit(solution)/shard_map/all_to_all | solution.py:476
  345.6 20.0 %collective-permute-start.6 = (bf16[8,384,128]{2,1,0:T(8,128)(2,1)}, bf16[8,384,128]{2,1,0:T(8,128)(2,1)}, u32[]{:S(2)}, u32[]{:S(2)}) collective-permute-start(bf16[8,384,128]{2,1,0:T(8,128)(2,1)} %dynamic-slice_bitcast_fusion.1), channel_id=1, source_target_pairs={{0,1},{1,0},{2,3},{3,2},{4,5},{5,4},{6,7},{7,6},{8,9},{9,8},{10,11... | collective-permute-start | bytes 2359304 | tf_op jit(solution)/shard_map/ppermute | solution.py:542
  371.7 26.3 %all-to-all-start.4 = ((bf16[8,384,128]{2,1,0:T(8,128)(2,1)}), bf16[8,384,128]{2,1,0:T(8,128)(2,1)S(1)}, u32[]{:S(2)}, u32[]{:S(2)}) async-start(bf16[8,384,128]{2,1,0:T(8,128)(2,1)} %fusion.9), calls=%async_computation.4 | async-start | bytes 1572864 | tf_op jit(solution)/shard_map/all_to_all | solution.py:543
  398.4 5.7 %collective-permute-start.7 = (f32[384,128]{0,1:T(8,128)S(1)}, f32[384,128]{0,1:T(8,128)S(1)}, u32[]{:S(2)}, u32[]{:S(2)}) collective-permute-start(f32[384,128]{0,1:T(8,128)S(1)} %copy.283), channel_id=1, source_target_pairs={{0,1},{1,0},{2,3},{3,2},{4,5},{5,4},{6,7},{7,6},{8,9},{9,8},{10,11... | collective-permute-start | bytes 589832 | tf_op jit(solution)/shard_map/ppermute | solution.py:544
  (104 other events, 3122.6 us)
Sparse Core Ops, SparseCore 0:
  10.8 57.1 all-gather.5
  70.7 55.0 all-gather.3
  199.1 79.3 reduce-scatter.1

commit v2 on v1

v2 whole, which is shorter than its diff:
```python
from functools import partial
import math

import jax
import jax.numpy as jnp
from jax import lax
from jax.experimental import pallas as pl
from jax.experimental.pallas import tpu as pltpu
from jax.sharding import PartitionSpec as P

D = 768
FF = 3072
CONV = 33
STEP = 7
CORES = 2

sharpness = 4.0
norm_eps = 1e-06
layer_eps = 1e-05
beta_one = 0.9
beta_two = 0.999
adam_eps = 1e-08
decay_rate = 0.01
highest = lax.Precision.HIGHEST
f32 = jnp.float32
bf16 = jnp.bfloat16
VMEM_LIMIT = 56 * 1024 * 1024


def nn(a, b):
    return lax.dot_general(a, b, (((1,), (0,)), ((), ())), preferred_element_type=f32)


def nt(a, b):
    return lax.dot_general(a, b, (((1,), (1,)), ((), ())), preferred_element_type=f32)


def normalize(source):
    centered = source - jnp.mean(source, axis=-1, keepdims=True)
    inverse = lax.rsqrt(jnp.mean(centered * centered, axis=-1, keepdims=True) + layer_eps)
    return (centered * inverse, inverse)


def norm_back(grad, normed, inverse, gain):
    scaled = grad * gain
    inner = (
        scaled
        - jnp.mean(scaled, axis=-1, keepdims=True)
        - normed * jnp.mean(scaled * normed, axis=-1, keepdims=True)
    )
    gains = jnp.sum(grad * normed, axis=0, keepdims=True)
    return (inverse * inner, gains, jnp.sum(grad, axis=0, keepdims=True))


def adam_step(weight, first, second, grad, rate):
    first_new = beta_one * first + (1.0 - beta_one) * grad
    second_new = beta_two * second + (1.0 - beta_two) * grad * grad
    fix_one = 1.0 - beta_one**STEP
    fix_two = 1.0 - beta_two**STEP
    update = first_new / fix_one / (jnp.sqrt(second_new / fix_two) + adam_eps) + decay_rate * weight
    return (weight - rate * update, first_new, second_new)


def head_units(source):
    inverse = lax.rsqrt(jnp.mean(source * source, axis=0, keepdims=True) + norm_eps)
    return source * inverse, inverse


def log_norms(unit, bit_planes, bits, rows):
    z = jnp.abs(nn(bit_planes, unit))
    parts = 0.5 * z + jnp.log(1.0 + jnp.exp(-z))
    total = parts[0:rows]
    for j in range(1, bits):
        total = total + parts[j * rows : (j + 1) * rows]
    return total


def seg_rows(limit, start, width):
    pos = start + lax.broadcasted_iota(jnp.int32, (1, width), 1)
    late = (pos >= limit).astype(f32)
    return 1.0 - late, late


def masked_pair(rows, early, late):
    return jnp.concatenate([rows * early, rows * late], axis=0).astype(bf16)


def flip(value):
    return jnp.transpose(value.astype(f32)).astype(bf16)


def bit_halves(buckets, bits):
    place = lax.broadcasted_iota(jnp.int32, (buckets, 8), 1)
    bucket = lax.broadcasted_iota(jnp.int32, (buckets, 8), 0)
    value = ((bucket >> place) & 1).astype(f32) - 0.5
    return jnp.where(place < bits, value, 0.0).astype(bf16)


def code_matrix(sign_ref, code_ref, hashes, bits):
    buckets = 2**bits
    halves = bit_halves(buckets, bits)
    for r in range(hashes):
        code_ref[r * buckets : (r + 1) * buckets, :] = nn(halves, sign_ref[0, r]).astype(bf16)


def forward_kernel(
    hashes, bits, rows, tile, tiles, heads, group_feats,
    spots_ref, got_ref, qk_ref, vo_ref, sign_ref, bit_ref,
    num_ref, qu_ref, ku_ref, v_ref, inv_ref, table_ref, count_ref, w_ref,
    acc_ref, codes_ref, code_ref, wt_ref,
):
    buckets = 2**bits
    limit = spots_ref[0]
    core = spots_ref[2]
    head = pl.program_id(0)
    feats = heads * 64
    tok_rows = tile // CORES

    for k in range(CORES):
        @pl.when((head == 0) & (core == k))
        def _():
            for h in range(heads):
                for p, (ref, base) in enumerate(((qk_ref, 0), (qk_ref, group_feats), (vo_ref, 0))):
                    start = base + k * feats + h * 64
                    part = ref[:, start : start + 64]
                    spot = (3 * h + p) * 64
                    w_ref[:, spot : spot + 64] = part
                    wt_ref[h, p * 64 : (p + 1) * 64, :] = flip(part)

    code_matrix(sign_ref, code_ref, hashes, bits)
    acc_ref[...] = jnp.zeros_like(acc_ref)
    v_ref[:, 0:128] = jnp.zeros((64, 128), bf16)
    v_ref[:, 128 + tiles * tile :] = jnp.zeros((64, 128), bf16)

    def fill(i, carry):
        start = pl.multiple_of(i * tile, tile)
        span = pl.ds(start, tile)
        toks = got_ref[pl.ds(i * CORES, CORES), 0:tok_rows, :].reshape(tile, got_ref.shape[2])
        proj = nt(wt_ref[head], toks)
        q_unit, q_inv = head_units(proj[0:64])
        k_unit, k_inv = head_units(proj[64:128])
        q_low = q_unit.astype(bf16)
        k_low = k_unit.astype(bf16)
        values = proj[128:192].astype(bf16)
        qu_ref[:, span] = q_low
        ku_ref[:, span] = k_low
        v_ref[:, pl.ds(pl.multiple_of(start + 128, 128), tile)] = values
        inv_ref[0, 0:1, span] = q_inv
        inv_ref[0, 1:2, span] = k_inv
        norms = log_norms(k_low, bit_ref[0], bits, rows)
        logits = nn(code_ref[...], k_low)
        for r in range(hashes):
            part = slice(r * buckets, (r + 1) * buckets)
            codes_ref[part, :] = jnp.exp(logits[part] - norms[r : r + 1]).astype(bf16)
        early, late = seg_rows(limit, start, tile)
        marks = jnp.concatenate([early, late, jnp.zeros((14, tile), f32)], axis=0).astype(bf16)
        pair = jnp.concatenate([masked_pair(values.astype(f32), early, late), marks], axis=0)
        acc_ref[...] += nt(codes_ref[...], pair)
        return carry

    lax.fori_loop(0, tiles, fill, 0)
    table = acc_ref[:, 0:128].astype(bf16)
    table_ref[0] = table
    table_t = flip(table)
    counts = jnp.concatenate(
        [acc_ref[:, 128:144], jnp.zeros((hashes * buckets, 112), f32)], axis=1
    )
    count_ref[0] = jnp.transpose(counts)[0:8]

    def read(i, carry):
        start = pl.multiple_of(i * tile, tile)
        span = pl.ds(start, tile)
        q_low = qu_ref[:, span]
        norms = log_norms(q_low, bit_ref[0], bits, rows)
        logits = nn(code_ref[...], q_low)
        for r in range(hashes):
            part = slice(r * buckets, (r + 1) * buckets)
            codes_ref[part, :] = jnp.exp(logits[part] - norms[r : r + 1]).astype(bf16)
        both = nn(table_t, codes_ref[...])
        early, late = seg_rows(limit, start, tile)
        num_ref[i] = (both[0:64] * early + both[64:128] * late).astype(bf16)
        return carry

    lax.fori_loop(0, tiles, read, 0)


def backward_kernel(
    hashes, bits, rows, tile, tiles, heads, own_rows,
    spots_ref, got_ref, w_ref, sign_ref, bit_ref,
    qu_ref, ku_ref, v_ref, inv_ref, table_ref, gnum_ref, conv_ref, tap_ref,
    grad_ref, keep_ref, give_ref,
    acc_ref, codes_ref, slopes_ref, proj_ref, code_ref, code_t_ref, sum_ref,
):
    buckets = 2**bits
    limit = spots_ref[0]
    spot = spots_ref[1]
    core = spots_ref[2]
    head = pl.program_id(0)
    width = got_ref.shape[2]
    tok_rows = tile // CORES
    code_matrix(sign_ref, code_ref, hashes, bits)
    code_t_ref[...] = flip(code_ref[...])
    acc_ref[...] = jnp.zeros_like(acc_ref)

    def soften(unit, slopes):
        norms = log_norms(unit, bit_ref[0], bits, rows)
        logits = nn(code_ref[...], unit)
        for r in range(hashes):
            part = slice(r * buckets, (r + 1) * buckets)
            codes = jnp.exp(logits[part] - norms[r : r + 1])
            weighted = codes * slopes[part]
            total = jnp.sum(weighted, axis=0, keepdims=True)
            codes_ref[part, :] = codes.astype(bf16)
            slopes_ref[part, :] = (weighted - codes * total).astype(bf16)
        return nn(code_t_ref[...], slopes_ref[...])

    def unit_back(grad, unit, inverse):
        unit = unit.astype(f32)
        inner = jnp.mean(grad * unit, axis=0, keepdims=True)
        return inverse * (grad - unit * inner)

    def queries(i, carry):
        start = pl.multiple_of(i * tile, tile)
        span = pl.ds(start, tile)
        early, late = seg_rows(limit, start, tile)
        pair = masked_pair(gnum_ref[i].astype(f32), early, late)
        unit = qu_ref[:, span]
        grad = soften(unit, nn(table_ref[0], pair))
        acc_ref[...] += nt(codes_ref[...], pair)
        proj_ref[head, 0:64, span] = unit_back(grad, unit, inv_ref[0, 0:1, span]).astype(bf16)
        return carry

    lax.fori_loop(0, tiles, queries, 0)
    table_grad = acc_ref[...].astype(bf16)
    table_grad_t = flip(table_grad)

    def keys(i, carry):
        start = pl.multiple_of(i * tile, tile)
        span = pl.ds(start, tile)
        early, late = seg_rows(limit, start, tile)
        values = v_ref[:, pl.ds(pl.multiple_of(start + 128, 128), tile)]
        pair = masked_pair(values.astype(f32), early, late)
        unit = ku_ref[:, span]
        grad = soften(unit, nn(table_grad, pair))
        both = nn(table_grad_t, codes_ref[...])
        here = (spot == i).astype(f32)
        value_grad = both[0:64] * early + both[64:128] * late + conv_ref[...] * here
        proj_ref[head, 64:128, span] = unit_back(grad, unit, inv_ref[0, 1:2, span]).astype(bf16)
        proj_ref[head, 128:192, span] = value_grad.astype(bf16)
        return carry

    lax.fori_loop(0, tiles, keys, 0)

    def weights(i, carry):
        span = pl.ds(pl.multiple_of(i * tile, tile), tile)
        toks = got_ref[pl.ds(i * CORES, CORES), 0:tok_rows, :].reshape(tile, width)
        sum_ref[head] += nn(proj_ref[head, :, span], toks)
        return carry

    sum_ref[head] = jnp.zeros((192, width), f32)
    lax.fori_loop(0, tiles, weights, 0)

    @pl.when(head == heads - 1)
    def _():
        def inputs(i, carry):
            span = pl.ds(pl.multiple_of(i * tile, tile), tile)
            part = nn(w_ref[...], proj_ref[:, :, span].reshape(heads * 192, tile))
            first, second = part[:, :tok_rows].astype(bf16), part[:, tok_rows:].astype(bf16)

            @pl.when(core == 0)
            def _():
                keep_ref[i] = first
                give_ref[i] = second

            @pl.when(core != 0)
            def _():
                keep_ref[i] = second
                give_ref[i] = first

            return carry

        lax.fori_loop(0, tiles, inputs, 0)
        grad = jnp.transpose(sum_ref[...].reshape(heads * 192, width))
        grad_ref[:, :, 0 : heads * 192] = grad.reshape(
            tiles, CORES * own_rows, heads * 192
        ).astype(bf16)
        grad_ref[:, :, heads * 192 :] = jnp.zeros((tiles, CORES * own_rows, 64), bf16)
        taps = jnp.concatenate([tap_ref[h, 0:1, 0:64] for h in range(heads)], axis=0)
        for c in range(tiles):
            grad_ref[c, 0:heads, heads * 192 :] = taps.astype(bf16)


def window_same(spots_ref, tile):
    start = spots_ref[1] * tile
    width = tile + 256
    edge = lax.broadcasted_iota(jnp.int32, (width, tile), 0) + (start - 128)
    own = lax.broadcasted_iota(jnp.int32, (width, tile), 1) + start
    return (edge >= spots_ref[0]) == (own >= spots_ref[0])


def banded(base, same, tile):
    width = tile + 256
    spread = jnp.broadcast_to(base, (width, width))
    spread = pltpu.roll(spread, 0, 1, stride=1, stride_axis=0)[:, :tile]
    matrix = jnp.where(same, spread, 0.0)
    upper = matrix.astype(bf16)
    return upper, (matrix - upper.astype(f32)).astype(bf16)


def conv_kernel(tile, spots_ref, left_ref, right_ref, base_ref, out_ref):
    upper, lower = banded(base_ref[0, 0:1], window_same(spots_ref, tile), tile)
    window = jnp.concatenate([left_ref[...], right_ref[...]], axis=1)
    out_ref[...] = nn(window, upper) + nn(window, lower)


def conv_back_kernel(
    tile, taps, spots_ref, left_ref, right_ref, before_ref, low_ref, high_ref, after_ref, base_ref,
    out_ref, tap_ref,
):
    upper, lower = banded(base_ref[0, 0:1], window_same(spots_ref, tile), tile)
    grads = jnp.concatenate([before_ref[...], low_ref[...], high_ref[...], after_ref[...]], axis=1)
    out_ref[...] = nn(grads, upper) + nn(grads, lower)
    width = tile + 256
    values = jnp.concatenate([left_ref[...], right_ref[...]], axis=1).astype(f32)
    own = jnp.concatenate([low_ref[...], high_ref[...]], axis=1).astype(f32)
    start = spots_ref[1] * tile
    limit = spots_ref[0]
    pos = lax.broadcasted_iota(jnp.int32, (1, tile), 1) + start
    lane = lax.broadcasted_iota(jnp.int32, (8, 128), 1)
    rim = taps // 2

    def one(o, total):
        moved = pltpu.roll(values, width - (128 - rim) - o, 1)[:, :tile]
        row = jnp.sum(moved * own, axis=0, keepdims=True)
        same = (pos >= limit) == (pos + (o - rim) >= limit)
        tap = jnp.sum(jnp.where(same, row, 0.0), axis=1, keepdims=True)
        return total + jnp.where(lane == o, tap, 0.0)

    tap_ref[0] = lax.fori_loop(0, taps, one, jnp.zeros((8, 128), f32))


def context_kernel(heads, spots_ref, got_ref, conv_ref, keep_ref, give_ref, num_ref):
    total = jnp.sum(got_ref[...].astype(f32), axis=0)
    num_ref[...] = total
    tile = total.shape[1]
    parts = [head_units(total[64 * h : 64 * (h + 1)])[0] for h in range(heads)]
    context = (jnp.concatenate(parts, axis=0) + conv_ref[...]).astype(bf16)
    first, second = context[:, : tile // CORES], context[:, tile // CORES :]

    @pl.when(spots_ref[2] == 0)
    def _():
        keep_ref[...] = first
        give_ref[...] = second

    @pl.when(spots_ref[2] != 0)
    def _():
        keep_ref[...] = second
        give_ref[...] = first


def mixer_kernel(spots_ref, keep_ref, other_ref, out_ref, context_ref, part_ref):
    keep, other = keep_ref[...].astype(f32), other_ref[...].astype(f32)
    zero = spots_ref[2] == 0
    pair = jnp.concatenate([jnp.where(zero, keep, other), jnp.where(zero, other, keep)], axis=0)
    context = jnp.transpose(pair).astype(bf16)
    context_ref[...] = context
    part_ref[...] = nt(context, out_ref[...]).astype(bf16)


def hidden_kernel(
    tok_ref, own_ref, other_ref, norm_ref, up_ref, down_ref,
    hat_ref, inv_ref, hidden_ref, active_ref, part_ref,
):
    mixed = own_ref[...].astype(f32) + other_ref[...].astype(f32)
    hat, inverse = normalize(tok_ref[...].astype(f32) + mixed)
    hat_ref[...] = hat
    inv_ref[...] = inverse
    low = (hat * norm_ref[0:1] + norm_ref[1:2]).astype(bf16)
    hidden = nn(low, up_ref[...])
    hidden_ref[...] = hidden
    active = (0.5 * hidden * (1.0 + lax.erf(hidden * math.sqrt(0.5)))).astype(bf16)
    active_ref[...] = active
    part_ref[...] = nt(active, down_ref[...]).astype(bf16)


def feed_kernel(
    hat_ref, hidden_ref, own_ref, other_ref, cot_ref, norm_ref, up_ref, down_ref,
    out_ref, second_ref, feed_ref, slope_ref, part_ref, sums_ref,
):
    first_out = hat_ref[...] * norm_ref[0:1] + norm_ref[1:2]
    fed = own_ref[...].astype(f32) + other_ref[...].astype(f32)
    hat, inverse = normalize(first_out + fed)
    out_ref[...] = hat * norm_ref[2:3] + norm_ref[3:4]
    grad, gains, offsets = norm_back(cot_ref[...].astype(f32), hat, inverse, norm_ref[2:3])
    second_ref[...] = grad
    sums_ref[0:1] = gains
    sums_ref[1:2] = offsets
    low = grad.astype(bf16)
    feed_ref[...] = low
    active_grad = nn(low, down_ref[...])
    hidden = hidden_ref[...]
    cdf = 0.5 * (1.0 + lax.erf(hidden * math.sqrt(0.5)))
    density = jnp.exp(-0.5 * hidden * hidden) * (1.0 / math.sqrt(2.0 * math.pi))
    slope = (active_grad * (cdf + hidden * density)).astype(bf16)
    slope_ref[...] = slope
    part_ref[...] = nt(slope, up_ref[...]).astype(bf16)


def mixer_back_kernel(
    spots_ref, second_ref, own_ref, other_ref, hat_ref, inv_ref, norm_ref, out_ref, sums_ref,
    grad_ref, low_ref, keep_ref, give_ref, all_sums_ref,
):
    first = second_ref[...] + (own_ref[...].astype(f32) + other_ref[...].astype(f32))
    grad, gains, offsets = norm_back(first, hat_ref[...], inv_ref[...], norm_ref[0:1])
    grad_ref[...] = grad
    all_sums_ref[0:1] = gains
    all_sums_ref[1:2] = offsets
    all_sums_ref[2:4] = sums_ref[...]
    low = grad.astype(bf16)
    low_ref[...] = low
    context = jnp.transpose(nn(low, out_ref[...]))
    half = context.shape[0] // CORES
    zero = spots_ref[2] == 0
    keep_ref[...] = jnp.where(zero, context[:half], context[half:])
    give_ref[...] = jnp.where(zero, context[half:], context[:half])


def attention_back_kernel(
    heads, spots_ref, keep_ref, other_ref, num_ref, sums_ref, count_ref,
    send_ref, low_ref, high_ref,
):
    zero = spots_ref[2] == 0
    keep, other = keep_ref[...], other_ref[...]
    grad = jnp.concatenate([jnp.where(zero, keep, other), jnp.where(zero, other, keep)], axis=1)
    half = keep.shape[1]
    low = grad.astype(bf16)
    low_ref[...] = low[:, :half]
    high_ref[...] = low[:, half:]
    parts = []
    for h in range(heads):
        span = slice(64 * h, 64 * (h + 1))
        attention, inverse = head_units(num_ref[span])
        inner = jnp.mean(grad[span] * attention, axis=0, keepdims=True)
        parts.append(inverse * (grad[span] - attention * inner))
    gnum = jnp.concatenate(parts, axis=0).astype(bf16)
    tile = gnum.shape[1]
    feats = 64 * heads
    pieces = sums_ref.shape[1] // tile
    sums = sums_ref[...].astype(bf16).astype(f32)
    sums = jnp.concatenate(
        [sums[:, tile * i : tile * (i + 1)] for i in range(pieces)], axis=0
    )
    for c in range(send_ref.shape[0]):
        send_ref[c, 0:feats, :] = gnum
        extra = jnp.concatenate([sums, count_ref[c]], axis=0)
        send_ref[c, feats:, :] = extra.astype(bf16)


def big_grad_kernel(
    mixer_ref, context_ref, hat_ref, norm_ref, slope_ref, feed_ref, active_ref, out_ref
):
    low = hat_ref[...] * norm_ref[0:1] + norm_ref[1:2]
    out_width, ff = context_ref.shape[1], slope_ref.shape[1]
    out_ref[:, :out_width] = nn(flip(mixer_ref[...]), context_ref[...]).astype(bf16)
    first = jnp.transpose(low.astype(bf16).astype(f32)).astype(bf16)
    out_ref[:, out_width : out_width + ff] = nn(first, slope_ref[...]).astype(bf16)
    out_ref[:, out_width + ff :] = nn(flip(feed_ref[...]), active_ref[...]).astype(bf16)


def on_device(
    tokens,
    cotangent,
    doc_lengths,
    plane_bits,
    qkv_weight,
    qkv_first,
    qkv_second,
    out_weight,
    out_first,
    out_second,
    up_weight,
    up_first,
    up_second,
    down_weight,
    down_first,
    down_second,
    norm_params,
    norm_first,
    norm_second,
    conv_taps,
    conv_first,
    conv_second,
):
    tok_rows, width = tokens.shape
    hash_count, bits, group_heads, head_dim = plane_bits.shape
    buckets = 2**bits
    taps = conv_taps.shape[1]
    rim = taps // 2
    seq_count = lax.axis_size("seq")
    chips = seq_count // CORES
    place = lax.axis_index("seq")
    side = lax.axis_index("head")
    spot, core = place // CORES, place % CORES
    heads = group_heads // CORES
    feats = heads * head_dim
    group_feats = group_heads * head_dim
    hashes = hash_count // chips
    rows = -(-hashes // 8) * 8
    tile = CORES * tok_rows
    total = chips * tile
    own_rows = width // seq_count
    ff = up_weight.shape[1]
    code_rows = hashes * buckets
    planes_of = [[CORES * c + k for c in range(chips)] for k in range(CORES)]
    across = partial(
        lax.all_to_all, axis_name="seq", split_axis=0, concat_axis=0, tiled=True,
        axis_index_groups=planes_of,
    )
    core_swap = partial(
        lax.ppermute, axis_name="seq", perm=[(i, i ^ 1) for i in range(seq_count)]
    )
    head_swap = partial(lax.ppermute, axis_name="head", perm=[(0, 1), (1, 0)])
    spots = jnp.stack([doc_lengths[0], spot.astype(jnp.int32), core.astype(jnp.int32)])

    smem = pl.BlockSpec(memory_space=pltpu.SMEM)
    params = pltpu.CompilerParams(
        dimension_semantics=("arbitrary",), vmem_limit_bytes=VMEM_LIMIT
    )
    shape = jax.ShapeDtypeStruct

    def whole(*dims):
        return pl.BlockSpec(dims, lambda h: (0,) * len(dims), pipeline_mode=pl.Buffered(1))

    def by_head(*dims):
        return pl.BlockSpec((1,) + dims, lambda h: (h,) + (0,) * len(dims))

    def head_rows(*dims):
        return pl.BlockSpec((head_dim,) + dims, lambda h: (h,) + (0,) * len(dims))

    def full(value):
        return pl.BlockSpec(value.shape, lambda i: (0,) * value.ndim)

    def columns(block, which):
        return pl.BlockSpec((width, block), lambda i: (0, which))

    def once(kernel, name, outs, args, specs=None):
        if specs is None:
            specs = [None] * len(args)
        specs = [
            (smem if arg is spots else full(arg)) if spec is None else spec
            for spec, arg in zip(specs, args)
        ]
        return pl.pallas_call(
            kernel,
            grid=(1,),
            in_specs=specs,
            out_specs=[full(o) for o in outs],
            out_shape=outs,
            compiler_params=params,
            name=name,
        )(*args)

    low_qkv = qkv_weight.astype(bf16)
    first_send = jnp.concatenate(
        [
            tokens,
            jnp.concatenate([low_qkv[0], low_qkv[1]], axis=1),
            jnp.concatenate([low_qkv[2], out_weight.T.astype(bf16)], axis=1),
        ],
        axis=0,
    )
    got = lax.all_gather(first_send, "seq", axis=0, tiled=False)
    qk_all = got[:, tok_rows : tok_rows + own_rows].reshape(width, 2 * group_feats)
    vo_all = got[:, tok_rows + own_rows :].reshape(width, 2 * group_feats)
    second_send = jnp.concatenate([up_weight.astype(bf16), down_weight.T.astype(bf16)], axis=1)
    second_send, unused = lax.optimization_barrier((second_send, got[0, 0, 0:1]))
    ff_all = lax.all_gather(second_send, "seq", axis=0, tiled=True)

    own_planes = lax.dynamic_slice(
        plane_bits, (spot * hashes, 0, core * heads, 0), (hashes, bits, heads, head_dim)
    )
    scale = sharpness / math.sqrt(head_dim)
    signs = scale * (2 * own_planes - 1).astype(f32)
    sign_w = jnp.pad(
        jnp.transpose(signs, (2, 0, 1, 3)), ((0, 0), (0, 0), (0, 8 - bits), (0, 0))
    ).astype(bf16)
    bit_w = jnp.pad(
        jnp.transpose(signs, (2, 1, 0, 3)), ((0, 0), (0, 0), (0, rows - hashes), (0, 0))
    )
    bit_w = bit_w.reshape(heads, bits * rows, head_dim).astype(bf16)

    num_parts, q_unit, k_unit, values, inverses, tables, counts, w_cols = pl.pallas_call(
        partial(forward_kernel, hashes, bits, rows, tile, chips, heads, group_feats),
        grid=(heads,),
        in_specs=[
            smem,
            whole(*got.shape),
            whole(*qk_all.shape),
            whole(*vo_all.shape),
            by_head(hashes, 8, head_dim),
            by_head(bits * rows, head_dim),
        ],
        out_specs=[
            pl.BlockSpec((chips, head_dim, tile), lambda h: (0, h, 0)),
            head_rows(total),
            head_rows(total),
            head_rows(total + 256),
            by_head(8, total),
            by_head(code_rows, 2 * head_dim),
            by_head(8, code_rows),
            whole(width, 3 * feats),
        ],
        out_shape=[
            shape((chips, feats, tile), bf16),
            shape((feats, total), bf16),
            shape((feats, total), bf16),
            shape((feats, total + 256), bf16),
            shape((heads, 8, total), f32),
            shape((heads, code_rows, 2 * head_dim), bf16),
            shape((heads, 8, code_rows), f32),
            shape((width, 3 * feats), bf16),
        ],
        scratch_shapes=[
            pltpu.VMEM((code_rows, 2 * head_dim + 16), f32),
            pltpu.VMEM((code_rows, tile), bf16),
            pltpu.VMEM((code_rows, head_dim), bf16),
            pltpu.VMEM((heads, 3 * head_dim, width), bf16),
        ],
        compiler_params=params,
        name="hash_forward",
    )(spots, got, qk_all, vo_all, sign_w, bit_w)
    num_got = across(num_parts)

    own_taps = lax.dynamic_slice(conv_taps, (core * heads, 0), (heads, taps))
    lead = tile + 128 - rim
    bases = jnp.zeros((heads, 16, tile + 256), f32)
    bases = bases.at[:, 0, lead : lead + taps].set(own_taps[:, ::-1])
    bases = bases.at[:, 8, lead : lead + taps].set(own_taps)
    window = [
        pl.BlockSpec((head_dim, tile), lambda h, s: (h, s[1])),
        pl.BlockSpec((head_dim, tile), lambda h, s: (h, s[1] + 1)),
    ]
    half_rows = pl.BlockSpec((head_dim, tok_rows), lambda h, s: (h, 0))
    conv = pl.pallas_call(
        partial(conv_kernel, tile),
        grid_spec=pltpu.PrefetchScalarGridSpec(
            num_scalar_prefetch=1,
            grid=(heads,),
            in_specs=window + [pl.BlockSpec((1, 8, tile + 256), lambda h, s: (h, 0, 0))],
            out_specs=pl.BlockSpec((head_dim, tile), lambda h, s: (h, 0)),
        ),
        out_shape=shape((feats, tile), f32),
        compiler_params=params,
        name="conv_forward",
    )(spots, values, values, bases)

    chip_buckets = buckets // chips
    count_rows = -(-2 * hashes * heads * chip_buckets // tile)
    sum_rows = 4 * width // tile
    extra_rows = -(-(sum_rows + count_rows) // 16) * 16
    count_send = counts[:, 0:2].reshape(heads, 2, hashes, chips, chip_buckets)
    count_send = jnp.transpose(count_send, (3, 1, 2, 0, 4)).reshape(chips, -1)
    count_send = jnp.pad(
        count_send, ((0, 0), (0, (extra_rows - sum_rows) * tile - count_send.shape[1]))
    ).reshape(chips, extra_rows - sum_rows, tile)

    keep, give, numerator = once(
        partial(context_kernel, heads), "context",
        [shape((feats, tok_rows), bf16), shape((feats, tok_rows), bf16), shape((feats, tile), f32)],
        [spots, num_got, conv],
    )
    context, mixer_part = once(
        mixer_kernel, "mixer",
        [shape((tok_rows, group_feats), bf16), shape((tok_rows, width), bf16)],
        [spots, keep, core_swap(give), vo_all],
        [None, None, None, columns(group_feats, 1)],
    )
    first_hat, first_inverse, hidden, active, feed_part = once(
        hidden_kernel, "feed_forward",
        [
            shape((tok_rows, width), f32),
            shape((tok_rows, 1), f32),
            shape((tok_rows, ff), f32),
            shape((tok_rows, ff), bf16),
            shape((tok_rows, width), bf16),
        ],
        [tokens, mixer_part, head_swap(mixer_part), norm_params, ff_all, ff_all],
        [None, None, None, None, columns(ff, 0), columns(ff, 1)],
    )
    block_out, grad_second, feed_low, slope_low, first_part, second_sums = once(
        feed_kernel, "feed_back",
        [
            shape((tok_rows, width), f32),
            shape((tok_rows, width), f32),
            shape((tok_rows, width), bf16),
            shape((tok_rows, ff), bf16),
            shape((tok_rows, width), bf16),
            shape((2, width), f32),
        ],
        [first_hat, hidden, feed_part, head_swap(feed_part), cotangent, norm_params, ff_all, ff_all],
        [None, None, None, None, None, None, columns(ff, 0), columns(ff, 1)],
    )
    grad_mixer, mixer_low, keep, give, norm_sums = once(
        mixer_back_kernel, "mixer_back",
        [
            shape((tok_rows, width), f32),
            shape((tok_rows, width), bf16),
            shape((feats, tok_rows), f32),
            shape((feats, tok_rows), f32),
            shape((4, width), f32),
        ],
        [
            spots, grad_second, first_part, head_swap(first_part), first_hat, first_inverse,
            norm_params, vo_all, second_sums,
        ],
        [None, None, None, None, None, None, None, columns(group_feats, 1), None],
    )
    gnum_send, grad_low, grad_high = once(
        partial(attention_back_kernel, heads), "attention_back",
        [
            shape((chips, feats + extra_rows, tile), bf16),
            shape((feats, tok_rows), bf16),
            shape((feats, tok_rows), bf16),
        ],
        [spots, keep, core_swap(give), numerator, norm_sums, count_send],
    )
    gnum_got = across(gnum_send)

    (big_grad,) = once(
        big_grad_kernel, "weight_grads",
        [shape((width, group_feats + 2 * ff), bf16)],
        [mixer_low, context, first_hat, norm_params, slope_low, feed_low, active],
    )
    big_owned = lax.psum_scatter(big_grad, "seq", scatter_dimension=0, tiled=True).astype(f32)

    up_moves = [(i, i + CORES) for i in range(seq_count - CORES)]
    down_moves = [(j, i) for i, j in up_moves]
    before = lax.ppermute(grad_high, "seq", up_moves)
    after = lax.ppermute(grad_low, "seq", down_moves)
    conv_grad, tap_parts = pl.pallas_call(
        partial(conv_back_kernel, tile, taps),
        grid_spec=pltpu.PrefetchScalarGridSpec(
            num_scalar_prefetch=1,
            grid=(heads,),
            in_specs=window
            + [half_rows] * 4
            + [pl.BlockSpec((1, 8, tile + 256), lambda h, s: (h, 1, 0))],
            out_specs=[
                pl.BlockSpec((head_dim, tile), lambda h, s: (h, 0)),
                pl.BlockSpec((1, 8, 128), lambda h, s: (h, 0, 0)),
            ],
        ),
        out_shape=[shape((feats, tile), f32), shape((heads, 8, 128), f32)],
        compiler_params=params,
        name="conv_backward",
    )(spots, values, values, before, grad_low, grad_high, after, bases)

    qkv_send, back_keep, back_give = pl.pallas_call(
        partial(backward_kernel, hashes, bits, rows, tile, chips, heads, own_rows),
        grid=(heads,),
        in_specs=[
            smem,
            whole(*got.shape),
            whole(*w_cols.shape),
            by_head(hashes, 8, head_dim),
            by_head(bits * rows, head_dim),
            head_rows(total),
            head_rows(total),
            head_rows(total + 256),
            by_head(8, total),
            by_head(code_rows, 2 * head_dim),
            pl.BlockSpec((chips, head_dim, tile), lambda h: (0, h, 0)),
            head_rows(tile),
            whole(*tap_parts.shape),
        ],
        out_specs=[
            whole(chips, CORES * own_rows, 3 * feats + 64),
            whole(chips, width, tok_rows),
            whole(chips, width, tok_rows),
        ],
        out_shape=[
            shape((chips, CORES * own_rows, 3 * feats + 64), bf16),
            shape((chips, width, tok_rows), bf16),
            shape((chips, width, tok_rows), bf16),
        ],
        scratch_shapes=[
            pltpu.VMEM((code_rows, 2 * head_dim), f32),
            pltpu.VMEM((code_rows, tile), bf16),
            pltpu.VMEM((code_rows, tile), bf16),
            pltpu.VMEM((heads, 3 * head_dim, total), bf16),
            pltpu.VMEM((code_rows, head_dim), bf16),
            pltpu.VMEM((head_dim, code_rows), bf16),
            pltpu.VMEM((heads, 3 * head_dim, width), f32),
        ],
        compiler_params=params,
        name="hash_backward",
    )(
        spots, got, w_cols, sign_w, bit_w,
        q_unit, k_unit, values, inverses, tables, gnum_got, conv_grad, tap_parts,
    )

    chip_sum = back_keep.astype(f32) + core_swap(back_give).astype(f32)
    half = width // 2
    chip_sum = chip_sum.astype(bf16).reshape(chips, 2, half, tok_rows)
    keep = lax.dynamic_index_in_dim(chip_sum, side, 1, keepdims=False)
    give = lax.dynamic_index_in_dim(chip_sum, 1 - side, 1, keepdims=False)
    pair_sum = keep.astype(f32) + head_swap(give).astype(f32)

    qkv_half = jnp.sum(across(qkv_send).astype(f32), axis=0)
    back_half = jnp.sum(across(pair_sum.astype(bf16)).astype(f32), axis=0)
    by_core = qkv_half.reshape(CORES, own_rows, 3 * feats + 64)
    qkv_mine = lax.dynamic_index_in_dim(by_core, core, 0, keepdims=False)[:, : 3 * feats]
    qkv_give = lax.dynamic_index_in_dim(by_core, 1 - core, 0, keepdims=False)[:, : 3 * feats]
    qkv_other = core_swap(qkv_give)

    extras = gnum_got[:, feats:].astype(f32)
    norm_half = jnp.sum(extras[:, :sum_rows], axis=0)
    count_half = extras[:, sum_rows:].reshape(chips, -1)[:, : 2 * hashes * heads * chip_buckets]
    count_half = count_half.reshape(chips, 2, hashes, heads, CORES, chip_buckets // CORES)
    count_mine = lax.dynamic_index_in_dim(count_half, core, 4, keepdims=False)
    count_give = lax.dynamic_index_in_dim(count_half, 1 - core, 4, keepdims=False)
    tap_half = qkv_half[:heads, 3 * feats : 3 * feats + taps]
    swapped = core_swap(
        jnp.concatenate([norm_half.reshape(-1), count_give.reshape(-1), tap_half.reshape(-1)])
    )
    norm_size, count_size = norm_half.size, count_give.size

    def in_order(mine, other, axis):
        first = jnp.where(core == 0, mine, other)
        return jnp.concatenate([first, jnp.where(core == 0, other, mine)], axis=axis)

    norm_grad = norm_half + swapped[:norm_size].reshape(norm_half.shape)
    norm_grad = jnp.transpose(
        norm_grad.reshape(width // tile, 4, tile), (1, 0, 2)
    ).reshape(4, width)
    count_other = swapped[norm_size : norm_size + count_size].reshape(count_mine.shape)
    occupancy = jnp.transpose(
        in_order(count_mine, count_other, 3), (1, 0, 2, 3, 4)
    ).reshape(2, hash_count, group_heads, buckets // seq_count)
    occupancy = occupancy * (buckets / (tok_rows * seq_count))
    conv_tap_grad = in_order(tap_half, swapped[norm_size + count_size :].reshape(heads, taps), 0)

    def weight_order(part):
        return jnp.transpose(part.reshape(own_rows, heads, 3, head_dim), (2, 0, 1, 3)).reshape(
            3, own_rows, feats
        )

    qkv_owned = in_order(weight_order(qkv_mine), weight_order(qkv_other), 2)
    back_low = lax.optimization_barrier(back_half.astype(bf16))
    back_other = head_swap(back_low)
    upper = jnp.where(side == 0, back_low, back_other)
    lower = jnp.where(side == 0, back_other, back_low)
    tokens_grad = grad_mixer + jnp.concatenate([upper, lower], axis=0).T.astype(f32)

    out_owned = big_owned[:, :group_feats].T
    up_owned = big_owned[:, group_feats : group_feats + ff]
    down_owned = big_owned[:, group_feats + ff :].T
    qkv_new, qkv_first_new, qkv_second_new = adam_step(
        qkv_weight, qkv_first, qkv_second, qkv_owned, D ** (-0.5)
    )
    out_new, out_first_new, out_second_new = adam_step(
        out_weight, out_first, out_second, out_owned, D ** (-0.5)
    )
    up_new, up_first_new, up_second_new = adam_step(
        up_weight, up_first, up_second, up_owned, D ** (-0.5)
    )
    down_new, down_first_new, down_second_new = adam_step(
        down_weight, down_first, down_second, down_owned, FF ** (-0.5)
    )
    norm_new, norm_first_new, norm_second_new = adam_step(
        norm_params, norm_first, norm_second, norm_grad, 0.3
    )
    conv_new, conv_first_new, conv_second_new = adam_step(
        conv_taps, conv_first, conv_second, conv_tap_grad, CONV ** (-0.5)
    )
    return (
        block_out,
        tokens_grad,
        occupancy,
        qkv_new,
        qkv_first_new,
        qkv_second_new,
        qkv_new.astype(jnp.bfloat16),
        out_new,
        out_first_new,
        out_second_new,
        out_new.astype(jnp.bfloat16),
        up_new,
        up_first_new,
        up_second_new,
        up_new.astype(jnp.bfloat16),
        down_new,
        down_first_new,
        down_second_new,
        down_new.astype(jnp.bfloat16),
        norm_new,
        norm_first_new,
        norm_second_new,
        conv_new,
        conv_first_new,
        conv_second_new,
    )


def solution(mesh):
    in_specs = (
        P("seq", None),
        P("seq", None),
        P(),
        P(None, None, "head", None),
        P(None, "seq", "head"),
        P(None, "seq", "head"),
        P(None, "seq", "head"),
        P("head", "seq"),
        P("head", "seq"),
        P("head", "seq"),
        P("seq", "head"),
        P("seq", "head"),
        P("seq", "head"),
        P("head", "seq"),
        P("head", "seq"),
        P("head", "seq"),
        P(),
        P(),
        P(),
        P("head", None),
        P("head", None),
        P("head", None),
    )
    out_specs = (
        P("seq", None),
        P("seq", None),
        P(None, None, "head", "seq"),
        P(None, "seq", "head"),
        P(None, "seq", "head"),
        P(None, "seq", "head"),
        P(None, "seq", "head"),
        P("head", "seq"),
        P("head", "seq"),
        P("head", "seq"),
        P("head", "seq"),
        P("seq", "head"),
        P("seq", "head"),
        P("seq", "head"),
        P("seq", "head"),
        P("head", "seq"),
        P("head", "seq"),
        P("head", "seq"),
        P("head", "seq"),
        P(),
        P(),
        P(),
        P("head", None),
        P("head", None),
        P("head", None),
    )
    return jax.shard_map(
        on_device, mesh=mesh, in_specs=in_specs, out_specs=out_specs, check_vma=False
    )
```

time: 424 us -> 382 us (0.901); the launches traced: 416 us -> 380 us
  Pallas kernels: 88.7 us -> 145 us
  matrix products: 34.1 us -> 0 us
  local copies, waits for them, and re-layouts: 55 us -> 26.6 us
  other arithmetic: 49.7 us -> 24.4 us
  waiting for transfers between devices: 112 us -> 124 us
  blocking collectives: 7.8 us -> 0 us
  starting transfers between devices: 52.7 us -> 45 us
    pallas_call x1 -> x10, Pallas kernels: 39.7 us -> 91 us  [the longest x1 41.6 us: on_device(): pl.pallas_call(partial(forward_kernel, hashes, bits, rows, tile, chips, h...]
    dot_general x12 -> x0, matrix products: 34.1 us -> none  [the longest x1 7.8 us: on_device(): jnp.einsum('hfe,het->hft', context_ext.astype(f32), gather_back, precisio...]
    all_gather x2, waiting for transfers between devices: 26.4 us -> 57.4 us  [the longest x1 57.4 us: on_device(): got = lax.all_gather(first_send, 'seq', axis=0, tiled=False)]
    all_to_all x4 -> x1, starting transfers between devices: 25 us -> 3.7 us  [on_device(): gnum_got = across(gnum_send)]
    convert_element_type x22 -> x2, other arithmetic: 18.9 us -> 1.8 us  [the longest x1 0.95 us: on_device(): low_qkv = qkv_weight.astype(bf16)]
    all_to_all x1, starting transfers between devices: 3.81 us -> 20.2 us  [on_device(): qkv_half = jnp.sum(across(qkv_send).astype(f32), axis=0)]
    mul x24 -> x2, local copies, waits for them, and re-layouts: 15.4 us -> 0.99 us  [on_device(): occupancy = occupancy * (buckets / (tok_rows * seq_count))]
    ppermute x8 -> x12, waiting for transfers between devices: 36.4 us -> 23.5 us  [the longest x1 5.7 us: on_device(): head_swap(mixer_part)]
  transfers between devices with their start and end apart: 18 -> 19, of which waited for: 13 -> 11; matrix products, arithmetic and copies ran while one was open for 26% -> 9% of each run, Pallas kernels for 21% -> 33%
where the time goes in v2:
time: 382 us; the launch traced here: 380 us
  Pallas kernels  145 us (38%)
  waiting for transfers between devices  124 us (32%)
  starting transfers between devices  45 us (12%)
  local copies, waits for them, and re-layouts  26.6 us (7%)
  other arithmetic  24.4 us (6%)
  between operations  14.4 us (4%)
    all_gather x1, waiting for transfers between devices, on_device(): got = lax.all_gather(first_send, 'seq', axis=0, tiled=False)  57.4 us
    pallas_call x1, Pallas kernels, on_device(): pl.pallas_call(partial(backward_kernel, hashes, bits, rows, tile, chips,...  54.3 us
    pallas_call x1, Pallas kernels, on_device(): pl.pallas_call(partial(forward_kernel, hashes, bits, rows, tile, chips, h...  41.6 us
    pallas_call x7, Pallas kernels, once(): pl.pallas_call(kernel, grid=(1,), in_specs=specs, out_specs=[full(o) for...  24.7 us
    pallas_call x1, Pallas kernels, on_device(): pl.pallas_call(partial(conv_back_kernel, tile, taps), grid_spec=pltpu.Pre...  21.1 us
    all_to_all x1, starting transfers between devices, on_device(): qkv_half = jnp.sum(across(qkv_send).astype(f32), axis=0)  20.2 us
    all_to_all x1, waiting for transfers between devices, on_device(): back_half = jnp.sum(across(pair_sum.astype(bf16)).astype(f32), axis=0)  15.7 us
    all_to_all x1, waiting for transfers between devices, on_device(): qkv_half = jnp.sum(across(qkv_send).astype(f32), axis=0)  14.9 us
  transfers between devices with their start and end apart: 19, of which 11 were waited for; matrix products, arithmetic and copies ran while one was open for 9% of the time, Pallas kernels for 33%

profile of v2, /device:TPU:0, one launch (start us, length us, event | category | flops | bytes accessed | tf_op | source)
XLA Modules:
  0.0 380.2 jit_solution(9403192764366535962)
XLA Ops:
  13.9 57.4 %all-gather.6.cloned.1.call-done = bf16[3584,768]{1,0:T(8,128)(2,1)} async-done(((bf16[224,768]{1,0:T(8,128)(2,1)}), bf16[3584,768]{1,0:T(8,128)(2,1)}) %all-gather.6.cloned.1.call-update) | async-done | bytes 5505040 | tf_op jit(solution)/shard_map/all_gather | solution.py:572
  71.2 3.3 fusion.26
  74.5 41.6 %hash_forward.1 = (bf16[8,192,256]{2,1,0:T(8,128)(2,1)}, bf16[192,2048]{1,0:T(8,128)(2,1)}, bf16[192,2048]{1,0:T(8,128)(2,1)}, bf16[192,2304]{1,0:T(8,128)(2,1)}...) custom-call(s32[3]{0:T(128)} %pad_add_fusion.spots_ref, ...), custom_call_target="tpu_custom_call" | custom-call | tf_op jit(solution)/shard_map/hash_forward/pallas_call | solution.py:592
  116.1 3.6 all-to-all-start
  121.9 1.9 scatter.6
  125.2 3.7 conv_forward.1.conv_ref
  128.8 12.9 %all-to-all-done.got_ref = bf16[8,192,256]{2,1,0:T(8,128)(2,1)S(1)} async-done(((bf16[8,192,256]{2,1,0:T(8,128)(2,1)}), bf16[8,192,256]{2,1,0:T(8,128)(2,1)S(1)}, u32[]{:S(2)}, u32[]{:S(2)}) %all-to-all-start) | async-done | bytes 786464 | tf_op jit(solution)/shard_map/all_to_all | solution.py:632
  142.7 2.0 context.1
  146.8 2.2 mixer.1
  150.4 5.7 %collective-permute-done.1.other_ref = bf16[128,768]{1,0:T(8,128)(2,1)S(1)} collective-permute-done((bf16[128,768]{1,0:T(8,128)(2,1)}, bf16[128,768]{1,0:T(8,128)(2,1)S(1)}, u32[]{:S(2)}, u32[]{:S(2)}) %collective-permute-start.1) | collective-permute-done | bytes 196640 | tf_op jit(solution)/shard_map/ppermute | solution.py:687
  156.8 4.8 %feed_forward.1 = (f32[128,768]{1,0:T(8,128)}, f32[128,1]{1,0:T(8,128)}, f32[128,1536]{1,0:T(8,128)}, bf16[128,1536]{1,0:T(8,128)(2,1)}, bf16[128,768]{1,0:T(8,128)(2,1)}) custom-call(bf16[128,768]{1,0:T(8,128)(2,1)} %tok_ref.1, bf16[128,768]{1,0:T(8,128)(2,1)} %get-tuple-element.90.own_ref, bf16[128,768]{1,0:T(8,128)(2,1)} %copy-done.19, ...), custom_call_target="tpu_custom_call" | custom-call | tf_op jit(solution)/shard_map/feed_forward/pallas_call | solution.py:553
  163.1 4.9 %collective-permute-done.2.other_ref = bf16[128,768]{1,0:T(8,128)(2,1)S(1)} collective-permute-done((bf16[128,768]{1,0:T(8,128)(2,1)}, bf16[128,768]{1,0:T(8,128)(2,1)S(1)}, u32[]{:S(2)}, u32[]{:S(2)}) %collective-permute-start.2) | collective-permute-done | bytes 196640 | tf_op jit(solution)/shard_map/ppermute | solution.py:700
  168.6 5.2 %feed_back.1 = (f32[128,768]{1,0:T(8,128)}, f32[128,768]{1,0:T(8,128)}, bf16[128,768]{1,0:T(8,128)(2,1)}, bf16[128,1536]{1,0:T(8,128)(2,1)}, bf16[128,768]{1,0:T(8,128)(2,1)}, /*index=5*/f32[2,768]{1,0:T(2,128)}) custom-call(f32[128,768]{1,0:T(8,128)} %get-tuple-element.91.hat_ref, f32[128,1536]{1,0:T(8,128)} %get-tuple-element.92.hidden_ref, ...), custom_call_target="tpu_custom_call" | custom-call | tf_op jit(solution)/shard_map/feed_back/pallas_call | solution.py:553
  175.3 4.4 %collective-permute-done.3.other_ref = bf16[128,768]{1,0:T(8,128)(2,1)S(1)} collective-permute-done((bf16[128,768]{1,0:T(8,128)(2,1)}, bf16[128,768]{1,0:T(8,128)(2,1)S(1)}, u32[]{:S(2)}, u32[]{:S(2)}) %collective-permute-start.3) | collective-permute-done | bytes 196640 | tf_op jit(solution)/shard_map/ppermute | solution.py:713
  180.4 2.8 mixer_back.1
  183.2 5.5 %weight_grads.1 = bf16[768,3456]{1,0:T(8,128)(2,1)} custom-call(bf16[128,768]{1,0:T(8,128)(2,1)} %get-tuple-element.118.mixer_ref, bf16[128,384]{1,0:T(8,128)(2,1)} %get-tuple-element.119.context_ref, f32[128,768]{1,0:T(8,128)} %get-tuple-element.91.hat_ref, f32[4,768]{1,0:T(4,128)} %norm_ref.7, bf16[128,1536]{1,0:T(8,128)(2,1)} %get-tuple-element.120.slope_ref, ...), custom_call_target="tpu_custom_call" | custom-call | tf_op jit(solution)/shard_map/weight_grads/pallas_call | solution.py:553
  192.3 2.1 attention_back.1
  194.4 3.7 all-to-all-start.1
  198.1 3.8 %collective-permute-start.5 = (bf16[192,128]{1,0:T(8,128)(2,1)S(1)}, bf16[192,128]{1,0:T(8,128)(2,1)S(1)}, u32[]{:S(2)}, u32[]{:S(2)}) collective-permute-start(bf16[192,128]{1,0:T(8,128)(2,1)S(1)} %copy-done.24), channel_id=1, source_target_pairs={{0,4},{2,6},{4,8},{6,10},{8,12},{10,14},{12,16},{14,18},{16,20},{1... | collective-permute-start | bytes 147464 | tf_op jit(solution)/shard_map/ppermute | solution.py:738
  203.4 2.5 collective-permute-done.5.before_ref
  205.9 3.8 %collective-permute-done.6.after_ref = bf16[192,128]{1,0:T(8,128)(2,1)S(1)} collective-permute-done((bf16[192,128]{1,0:T(8,128)(2,1)S(1)}, bf16[192,128]{1,0:T(8,128)(2,1)S(1)}, u32[]{:S(2)}, u32[]{:S(2)}) %collective-permute-start.6) | collective-permute-done | bytes 49184 | tf_op jit(solution)/shard_map/ppermute | solution.py:739
  210.4 21.1 %conv_backward.1 = (f32[192,256]{1,0:T(8,128)}, f32[3,8,128]{2,1,0:T(8,128)}) custom-call(s32[3]{0:T(128)} %pad_add_fusion.spots_ref, bf16[192,2304]{1,0:T(8,128)(2,1)} %get-tuple-element.87.left_ref.right_ref.v_ref, bf16[192,2304]{1,0:T(8,128)(2,1)} %get-tuple-element.87.left_ref.right_ref.v_ref, bf16[192,128]{1,0:T(8,128)(2,1)} %copy-done.25, ...), custom_call_target="tpu_custom_call" | custom-call | tf_op jit(solution)/shard_map/conv_backward/pallas_call | solution.py:740
  232.5 54.3 %hash_backward.1 = (bf16[8,96,640]{2,1,0:T(8,128)(2,1)}, bf16[8,768,128]{2,1,0:T(8,128)(2,1)}, bf16[8,768,128]{2,1,0:T(8,128)(2,1)}) custom-call(s32[3]{0:T(128)} %pad_add_fusion.spots_ref, bf16[16,224,768]{2,1,0:T(8,128)(2,1)} %bitcast.86, bf16[768,576]{1,0:T(8,128)(2,1)} %get-tuple-element.100.w_ref, bf16[3,8,8,64]{3,2,1,0:T(8,128)(2,1)} %pad.17.sign_ref, ...), custom_call_target="tpu_custom_call" | custom-call | tf_op jit(solution)/shard_map/hash_backward/pallas_call | solution.py:758
  286.9 20.2 %all-to-all-start.3 = ((bf16[8,96,640]{2,1,0:T(8,128)(2,1)}), bf16[8,96,640]{2,1,0:T(8,128)(2,1)}, u32[]{:S(2)}, u32[]{:S(2)}) async-start(bf16[8,96,640]{2,1,0:T(8,128)(2,1)} %get-tuple-element.117), calls=%async_computation.3 | async-start | bytes 1966080 | tf_op jit(solution)/shard_map/all_to_all | solution.py:809
  309.1 2.3 add_convert_fusion
  318.0 14.9 %all-to-all-done.3 = bf16[8,96,640]{2,1,0:T(8,128)(2,1)} async-done(((bf16[8,96,640]{2,1,0:T(8,128)(2,1)}), bf16[8,96,640]{2,1,0:T(8,128)(2,1)}, u32[]{:S(2)}, u32[]{:S(2)}) %all-to-all-start.3) | async-done | bytes 983072 | tf_op jit(solution)/shard_map/all_to_all | solution.py:809
  336.4 2.3 fusion
  338.7 3.7 all-to-all-start.2
  347.2 15.7 %all-to-all-done.2 = bf16[8,384,128]{2,1,0:T(8,128)(2,1)S(1)} async-done(((bf16[8,384,128]{2,1,0:T(8,128)(2,1)}), bf16[8,384,128]{2,1,0:T(8,128)(2,1)S(1)}, u32[]{:S(2)}, u32[]{:S(2)}) %all-to-all-start.2) | async-done | bytes 786464 | tf_op jit(solution)/shard_map/all_to_all | solution.py:810
  363.2 1.7 collective-permute-start.9
  364.9 2.1 fusion.24
  369.7 1.7 fusion.22
  (168 shorter events, 48.0 us)
Async XLA Ops:
  7.2 4.7 %copy-start = (s32[64,7,6,64]{3,0,2,1:T(8,128)S(1)}, s32[64,7,6,64]{3,0,2,1:T(8,128)}, u32[]{:S(2)}) copy-start(s32[64,7,6,64]{3,0,2,1:T(8,128)} %param.29) | copy-start | bytes 2064388
  7.2 64.0 %all-gather.6.cloned.1.call-start = ((), (), s32[]{:S(2)}) async-start(), calls=%async_computation.7 | async-start | bytes 5849088 | tf_op jit(solution)/shard_map/all_gather | solution.py:572
  9.3 4.0 %copy-start.32 = (s32[2]{0:T(128)S(1)}, s32[2]{0:T(128)}, u32[]{:S(2)}) copy-start(s32[2]{0:T(128)} %param.28) | copy-start | bytes 28
  11.0 139.4 %all-gather.4.cloned.1.call-start = ((), (), s32[]{:S(2)}) async-start(), calls=%async_computation.5 | async-start | bytes 5013504 | tf_op jit(solution)/shard_map/all_gather | solution.py:577
  116.1 25.6 %all-to-all-start = ((bf16[8,192,256]{2,1,0:T(8,128)(2,1)}), bf16[8,192,256]{2,1,0:T(8,128)(2,1)S(1)}, u32[]{:S(2)}, u32[]{:S(2)}) async-start(bf16[8,192,256]{2,1,0:T(8,128)(2,1)} %get-tuple-element.86), calls=%async_computation | async-start | bytes 1572864 | tf_op jit(solution)/shard_map/all_to_all | solution.py:632
  119.7 249.0 %reduce-scatter.2.cloned.1.call-start = ((), (), s32[]{:S(2)}) async-start(), calls=%async_computation.6 | async-start | bytes 5640192 | tf_op jit(solution)/shard_map/reduce_scatter | solution.py:734
  144.7 1.4 collective-permute-start
  148.9 7.2 %collective-permute-start.1 = (bf16[128,768]{1,0:T(8,128)(2,1)}, bf16[128,768]{1,0:T(8,128)(2,1)S(1)}, u32[]{:S(2)}, u32[]{:S(2)}) collective-permute-start(bf16[128,768]{1,0:T(8,128)(2,1)} %get-tuple-element.90.own_ref), channel_id=1, source_target_pairs={{0,1},{1,0},{2,3},{3,2},{4,5},{5,4},{6,7},{7,6},{8,9},{9,8},{10,11... | collective-permute-start | bytes 589832 | tf_op jit(solution)/shard_map/ppermute | solution.py:687
  161.6 6.3 %collective-permute-start.2 = (bf16[128,768]{1,0:T(8,128)(2,1)}, bf16[128,768]{1,0:T(8,128)(2,1)S(1)}, u32[]{:S(2)}, u32[]{:S(2)}) collective-permute-start(bf16[128,768]{1,0:T(8,128)(2,1)} %get-tuple-element.93.own_ref), channel_id=1, source_target_pairs={{0,1},{1,0},{2,3},{3,2},{4,5},{5,4},{6,7},{7,6},{8,9},{9,8},{10,11... | collective-permute-start | bytes 589832 | tf_op jit(solution)/shard_map/ppermute | solution.py:700
  173.9 5.9 %collective-permute-start.3 = (bf16[128,768]{1,0:T(8,128)(2,1)}, bf16[128,768]{1,0:T(8,128)(2,1)S(1)}, u32[]{:S(2)}, u32[]{:S(2)}) collective-permute-start(bf16[128,768]{1,0:T(8,128)(2,1)} %get-tuple-element.96.own_ref), channel_id=1, source_target_pairs={{0,1},{1,0},{2,3},{3,2},{4,5},{5,4},{6,7},{7,6},{8,9},{9,8},{10,11... | collective-permute-start | bytes 589832 | tf_op jit(solution)/shard_map/ppermute | solution.py:713
  189.6 2.0 collective-permute-start.4
  194.4 7.5 %copy-start.23 = (bf16[192,128]{1,0:T(8,128)(2,1)S(1)}, bf16[192,128]{1,0:T(8,128)(2,1)}, u32[]{:S(2)}) copy-start(bf16[192,128]{1,0:T(8,128)(2,1)} %get-tuple-element.112.low_ref) | copy-start | bytes 147460
  194.4 37.1 %all-to-all-start.1 = ((bf16[8,208,256]{2,1,0:T(8,128)(2,1)}), bf16[8,208,256]{2,1,0:T(8,128)(2,1)S(1)}, u32[]{:S(2)}, u32[]{:S(2)}) async-start(bf16[8,208,256]{2,1,0:T(8,128)(2,1)} %get-tuple-element.110), calls=%async_computation.1 | async-start | bytes 1703936 | tf_op jit(solution)/shard_map/all_to_all | solution.py:727
  198.1 7.8 %collective-permute-start.5 = (bf16[192,128]{1,0:T(8,128)(2,1)S(1)}, bf16[192,128]{1,0:T(8,128)(2,1)S(1)}, u32[]{:S(2)}, u32[]{:S(2)}) collective-permute-start(bf16[192,128]{1,0:T(8,128)(2,1)S(1)} %copy-done.24), channel_id=1, source_target_pairs={{0,4},{2,6},{4,8},{6,10},{8,12},{10,14},{12,16},{14,18},{16,20},{1... | collective-permute-start | bytes 147464 | tf_op jit(solution)/shard_map/ppermute | solution.py:738
  202.0 7.8 %collective-permute-start.6 = (bf16[192,128]{1,0:T(8,128)(2,1)S(1)}, bf16[192,128]{1,0:T(8,128)(2,1)S(1)}, u32[]{:S(2)}, u32[]{:S(2)}) collective-permute-start(bf16[192,128]{1,0:T(8,128)(2,1)S(1)} %copy-done.23), channel_id=1, source_target_pairs={{4,0},{6,2},{8,4},{10,6},{12,8},{14,10},{16,12},{18,14},{20,16},{2... | collective-permute-start | bytes 147464 | tf_op jit(solution)/shard_map/ppermute | solution.py:739
  286.8 21.1 %collective-permute-start.7 = (bf16[8,768,128]{2,1,0:T(8,128)(2,1)}, bf16[8,768,128]{2,1,0:T(8,128)(2,1)S(1)}, u32[]{:S(2)}, u32[]{:S(2)}) collective-permute-start(bf16[8,768,128]{2,1,0:T(8,128)(2,1)} %get-tuple-element.116), channel_id=1, source_target_pairs={{0,2},{2,0},{4,6},{6,4},{8,10},{10,8},{12,14},{14,12},{16,18},{18,... | collective-permute-start | bytes 4718600 | tf_op jit(solution)/shard_map/ppermute | solution.py:802
  286.9 46.1 %all-to-all-start.3 = ((bf16[8,96,640]{2,1,0:T(8,128)(2,1)}), bf16[8,96,640]{2,1,0:T(8,128)(2,1)}, u32[]{:S(2)}, u32[]{:S(2)}) async-start(bf16[8,96,640]{2,1,0:T(8,128)(2,1)} %get-tuple-element.117), calls=%async_computation.3 | async-start | bytes 1966080 | tf_op jit(solution)/shard_map/all_to_all | solution.py:809
  312.4 24.0 %collective-permute-start.8 = (bf16[8,384,128]{2,1,0:T(8,128)(2,1)}, bf16[8,384,128]{2,1,0:T(8,128)(2,1)}, u32[]{:S(2)}, u32[]{:S(2)}) collective-permute-start(bf16[8,384,128]{2,1,0:T(8,128)(2,1)} %dynamic-slice_bitcast_fusion), channel_id=1, source_target_pairs={{0,1},{1,0},{2,3},{3,2},{4,5},{5,4},{6,7},{7,6},{8,9},{9,8},{10,11... | collective-permute-start | bytes 2359304 | tf_op jit(solution)/shard_map/ppermute | solution.py:807
  335.2 10.2 %collective-permute-start.11 = (f32[48,576]{1,0:T(8,128)}, f32[48,576]{1,0:T(8,128)}, u32[]{:S(2)}, u32[]{:S(2)}) collective-permute-start(f32[48,576]{1,0:T(8,128)} %bitcast.83), channel_id=1, source_target_pairs={{0,2},{2,0},{4,6},{6,4},{8,10},{10,8},{12,14},{14,12},{16,18},{18,... | collective-permute-start | bytes 331784 | tf_op jit(solution)/shard_map/ppermute | solution.py:814
  335.9 6.5 %collective-permute-start.10 = (f32[6243]{0:T(1024)S(1)}, f32[6243]{0:T(1024)S(1)}, u32[]{:S(2)}, u32[]{:S(2)}) collective-permute-start(f32[6243]{0:T(1024)S(1)} %pad_maximum_fusion.2), channel_id=1, source_target_pairs={{0,2},{2,0},{4,6},{6,4},{8,10},{10,8},{12,14},{14,12},{16,18},{18,... | collective-permute-start | bytes 74924 | tf_op jit(solution)/shard_map/ppermute | solution.py:823
  338.7 4.1 %copy-start.30 = (f32[6,33]{1,0:T(8,128)S(1)}, f32[6,33]{1,0:T(8,128)}, u32[]{:S(2)}) copy-start(f32[6,33]{1,0:T(8,128)} %param.46) | copy-start | bytes 2380
  338.7 4.1 %copy-start.31 = (f32[6,33]{1,0:T(8,128)S(1)}, f32[6,33]{1,0:T(8,128)}, u32[]{:S(2)}) copy-start(f32[6,33]{1,0:T(8,128)} %param.47) | copy-start | bytes 2380
  338.7 4.8 %copy-start.12 = (f32[4,768]{1,0:T(4,128)S(1)}, f32[4,768]{1,0:T(4,128)}, u32[]{:S(2)}) copy-start(f32[4,768]{1,0:T(4,128)} %norm_ref.7) | copy-start | bytes 36868
  338.7 4.8 %copy-start.28 = (f32[4,768]{1,0:T(4,128)S(1)}, f32[4,768]{1,0:T(4,128)}, u32[]{:S(2)}) copy-start(f32[4,768]{1,0:T(4,128)} %param.43) | copy-start | bytes 36868
  338.7 4.8 %copy-start.29 = (f32[4,768]{1,0:T(4,128)S(1)}, f32[4,768]{1,0:T(4,128)}, u32[]{:S(2)}) copy-start(f32[4,768]{1,0:T(4,128)} %param.44) | copy-start | bytes 36868
  338.7 24.2 %all-to-all-start.2 = ((bf16[8,384,128]{2,1,0:T(8,128)(2,1)}), bf16[8,384,128]{2,1,0:T(8,128)(2,1)S(1)}, u32[]{:S(2)}, u32[]{:S(2)}) async-start(bf16[8,384,128]{2,1,0:T(8,128)(2,1)} %fusion), calls=%async_computation.2 | async-start | bytes 1572864 | tf_op jit(solution)/shard_map/all_to_all | solution.py:810
  346.6 18.3 %copy-start.9 = (f32[3,48,384]{2,1,0:T(8,128)S(1)}, f32[3,48,384]{2,1,0:T(8,128)}, u32[]{:S(2)}) copy-start(f32[3,48,384]{2,1,0:T(8,128)} %param.30) | copy-start | bytes 663556
  347.2 20.6 %copy-start.11 = (f32[128,768]{1,0:T(8,128)S(1)}, f32[128,768]{1,0:T(8,128)}, u32[]{:S(2)}) copy-start(f32[128,768]{1,0:T(8,128)} %get-tuple-element.99) | copy-start | bytes 1179652
  363.2 4.7 %collective-permute-start.9 = (bf16[384,128]{0,1:T(8,128)(2,1)S(1)}, bf16[384,128]{0,1:T(8,128)(2,1)S(1)}, u32[]{:S(2)}, u32[]{:S(2)}) collective-permute-start(bf16[384,128]{0,1:T(8,128)(2,1)S(1)} %copy.77), channel_id=1, source_target_pairs={{0,1},{1,0},{2,3},{3,2},{4,5},{5,4},{6,7},{7,6},{8,9},{9,8},{10,11... | collective-permute-start | bytes 294920 | tf_op jit(solution)/shard_map/ppermute | solution.py:850
  367.0 4.5 %copy-start.5 = (f32[1536,48]{0,1:T(8,128)S(1)}, f32[1536,48]{0,1:T(8,128)}, u32[]{:S(2)}) copy-start(f32[1536,48]{0,1:T(8,128)} %param.39) | copy-start | bytes 884740
  367.0 4.5 %copy-start.13 = (f32[1536,48]{0,1:T(8,128)S(1)}, f32[1536,48]{0,1:T(8,128)}, u32[]{:S(2)}) copy-start(f32[1536,48]{0,1:T(8,128)} %param.40) | copy-start | bytes 884740
  367.0 4.5 %copy-start.14 = (f32[1536,48]{0,1:T(8,128)S(1)}, f32[1536,48]{0,1:T(8,128)}, u32[]{:S(2)}) copy-start(f32[1536,48]{0,1:T(8,128)} %param.41) | copy-start | bytes 884740
  (22 other events, 43.7 us)
Sparse Core Ops, SparseCore 0:
  11.1 60.0 all-gather.5
  74.1 52.6 all-gather.3
  188.8 79.1 reduce-scatter.1

commit v3 on v2

--- a/solution.py
+++ b/solution.py
@@ -25,6 +25,7 @@
 f32 = jnp.float32
 bf16 = jnp.bfloat16
 VMEM_LIMIT = 56 * 1024 * 1024
+WORK = 2
 
 
 def nn(a, b):
@@ -66,15 +67,6 @@
     return source * inverse, inverse
 
 
-def log_norms(unit, bit_planes, bits, rows):
-    z = jnp.abs(nn(bit_planes, unit))
-    parts = 0.5 * z + jnp.log(1.0 + jnp.exp(-z))
-    total = parts[0:rows]
-    for j in range(1, bits):
-        total = total + parts[j * rows : (j + 1) * rows]
-    return total
-
-
 def seg_rows(limit, start, width):
     pos = start + lax.broadcasted_iota(jnp.int32, (1, width), 1)
     late = (pos >= limit).astype(f32)
@@ -89,204 +81,243 @@
     return jnp.transpose(value.astype(f32)).astype(bf16)
 
 
-def bit_halves(buckets, bits):
-    place = lax.broadcasted_iota(jnp.int32, (buckets, 8), 1)
-    bucket = lax.broadcasted_iota(jnp.int32, (buckets, 8), 0)
-    value = ((bucket >> place) & 1).astype(f32) - 0.5
-    return jnp.where(place < bits, value, 0.0).astype(bf16)
-
-
-def code_matrix(sign_ref, code_ref, hashes, bits):
-    buckets = 2**bits
-    halves = bit_halves(buckets, bits)
-    for r in range(hashes):
-        code_ref[r * buckets : (r + 1) * buckets, :] = nn(halves, sign_ref[0, r]).astype(bf16)
+def bit_factors(bit_planes, unit, bits, hashes, rows):
+    z = nn(bit_planes, unit)
+    decay = jnp.exp(-jnp.abs(z))
+    large = 1.0 / (1.0 + decay)
+    small = decay * large
+    ones = jnp.where(z >= 0.0, large, small)
+    zeros = jnp.where(z >= 0.0, small, large)
+    ones = [ones[j * rows : (j + 1) * rows] for j in range(bits)]
+    zeros = [zeros[j * rows : (j + 1) * rows] for j in range(bits)]
+    if rows != hashes:
+        live = lax.broadcasted_iota(jnp.int32, ones[0].shape, 0) < hashes
+        return ones, [jnp.where(live, ones[0], 0.0)] + ones[1:], [
+            jnp.where(live, zeros[0], 0.0)
+        ] + zeros[1:]
+    return ones, ones, zeros
+
+
+def products(ones, zeros, first, last):
+    found = [zeros[first], ones[first]]
+    for j in range(first + 1, last):
+        found = [part * zeros[j] for part in found] + [part * ones[j] for part in found]
+    return found
+
+
+def code_parts(bit_planes, unit, bits, hashes, rows):
+    plain, ones, zeros = bit_factors(bit_planes, unit, bits, hashes, rows)
+    return plain, products(ones, zeros, 0, 3), products(ones, zeros, 3, bits)
+
+
+def store_codes(codes_ref, head, lows, highs, rows):
+    for g, high in enumerate(highs):
+        for s in range(0, len(lows), 2):
+            spot = (g * len(lows) + s) * rows
+            pair = jnp.concatenate([lows[s] * high, lows[s + 1] * high], axis=0)
+            codes_ref[head, spot : spot + 2 * rows, :] = pair.astype(bf16)
 
 
 def forward_kernel(
-    hashes, bits, rows, tile, tiles, heads, group_feats,
-    spots_ref, got_ref, qk_ref, vo_ref, sign_ref, bit_ref,
-    num_ref, qu_ref, ku_ref, v_ref, inv_ref, table_ref, count_ref, w_ref,
-    acc_ref, codes_ref, code_ref, wt_ref,
+    hashes, bits, rows, tile, steps, heads,
+    spots_ref, got_ref, w_ref, bit_ref,
+    num_ref, qu_ref, ku_ref, v_ref, inv_ref, table_ref, count_ref,
+    acc_ref, codes_ref, wt_ref, table_t_ref,
 ):
-    buckets = 2**bits
     limit = spots_ref[0]
-    core = spots_ref[2]
-    head = pl.program_id(0)
+    phase, i = pl.program_id(0), pl.program_id(1)
     feats = heads * 64
-    tok_rows = tile // CORES
-
-    for k in range(CORES):
-        @pl.when((head == 0) & (core == k))
-        def _():
-            for h in range(heads):
-                for p, (ref, base) in enumerate(((qk_ref, 0), (qk_ref, group_feats), (vo_ref, 0))):
-                    start = base + k * feats + h * 64
-                    part = ref[:, start : start + 64]
-                    spot = (3 * h + p) * 64
-                    w_ref[:, spot : spot + 64] = part
-                    wt_ref[h, p * 64 : (p + 1) * 64, :] = flip(part)
-
-    code_matrix(sign_ref, code_ref, hashes, bits)
-    acc_ref[...] = jnp.zeros_like(acc_ref)
-    v_ref[:, 0:128] = jnp.zeros((64, 128), bf16)
-    v_ref[:, 128 + tiles * tile :] = jnp.zeros((64, 128), bf16)
-
-    def fill(i, carry):
-        start = pl.multiple_of(i * tile, tile)
-        span = pl.ds(start, tile)
-        toks = got_ref[pl.ds(i * CORES, CORES), 0:tok_rows, :].reshape(tile, got_ref.shape[2])
-        proj = nt(wt_ref[head], toks)
-        q_unit, q_inv = head_units(proj[0:64])
-        k_unit, k_inv = head_units(proj[64:128])
-        q_low = q_unit.astype(bf16)
-        k_low = k_unit.astype(bf16)
-        values = proj[128:192].astype(bf16)
-        qu_ref[:, span] = q_low
-        ku_ref[:, span] = k_low
+    chips = num_ref.shape[0]
+    block = tile // chips
+    start = pl.multiple_of(i * tile, tile)
+    span = pl.ds(start, tile)
+    early, late = seg_rows(limit, start, tile)
+
+    @pl.when((phase == 0) & (i == 0))
+    def _():
+        wt_ref[...] = flip(w_ref[...])
+        acc_ref[...] = jnp.zeros_like(acc_ref)
+        v_ref[:, 0:128] = jnp.zeros((feats, 128), bf16)
+        v_ref[:, 128 + steps * tile :] = jnp.zeros((feats, 128), bf16)
+        inv_ref[...] = jnp.zeros_like(inv_ref)
+
+    @pl.when(phase == 0)
+    def _():
+        proj = nt(wt_ref[...], got_ref[...].reshape(tile, got_ref.shape[2]))
+        values = proj[2 * feats :].astype(bf16)
         v_ref[:, pl.ds(pl.multiple_of(start + 128, 128), tile)] = values
-        inv_ref[0, 0:1, span] = q_inv
-        inv_ref[0, 1:2, span] = k_inv
-        norms = log_norms(k_low, bit_ref[0], bits, rows)
-        logits = nn(code_ref[...], k_low)
-        for r in range(hashes):
-            part = slice(r * buckets, (r + 1) * buckets)
-            codes_ref[part, :] = jnp.exp(logits[part] - norms[r : r + 1]).astype(bf16)
-        early, late = seg_rows(limit, start, tile)
         marks = jnp.concatenate([early, late, jnp.zeros((14, tile), f32)], axis=0).astype(bf16)
-        pair = jnp.concatenate([masked_pair(values.astype(f32), early, late), marks], axis=0)
-        acc_ref[...] += nt(codes_ref[...], pair)
-        return carry
-
-    lax.fori_loop(0, tiles, fill, 0)
-    table = acc_ref[:, 0:128].astype(bf16)
-    table_ref[0] = table
-    table_t = flip(table)
-    counts = jnp.concatenate(
-        [acc_ref[:, 128:144], jnp.zeros((hashes * buckets, 112), f32)], axis=1
-    )
-    count_ref[0] = jnp.transpose(counts)[0:8]
-
-    def read(i, carry):
-        start = pl.multiple_of(i * tile, tile)
-        span = pl.ds(start, tile)
-        q_low = qu_ref[:, span]
-        norms = log_norms(q_low, bit_ref[0], bits, rows)
-        logits = nn(code_ref[...], q_low)
-        for r in range(hashes):
-            part = slice(r * buckets, (r + 1) * buckets)
-            codes_ref[part, :] = jnp.exp(logits[part] - norms[r : r + 1]).astype(bf16)
-        both = nn(table_t, codes_ref[...])
-        early, late = seg_rows(limit, start, tile)
-        num_ref[i] = (both[0:64] * early + both[64:128] * late).astype(bf16)
-        return carry
-
-    lax.fori_loop(0, tiles, read, 0)
+        units = []
+        for h in range(heads):
+            mine = slice(64 * h, 64 * (h + 1))
+            q_unit, q_inv = head_units(proj[mine])
+            k_unit, k_inv = head_units(proj[feats + 64 * h : feats + 64 * (h + 1)])
+            units.append(k_unit.astype(bf16))
+            qu_ref[mine, span] = q_unit.astype(bf16)
+            ku_ref[mine, span] = units[h]
+            inv_ref[h : h + 1, span] = q_inv
+            inv_ref[8 + h : 9 + h, span] = k_inv
+        for h in range(heads):
+            plain, lows, highs = code_parts(bit_ref[h], units[h], bits, hashes, rows)
+            store_codes(codes_ref, h, lows, highs, rows)
+        for h in range(heads):
+            pair = masked_pair(values[64 * h : 64 * (h + 1)].astype(f32), early, late)
+            pair = jnp.concatenate([pair, marks], axis=0)
+            acc_ref[h] += nt(codes_ref[h], pair)
+
+    @pl.when((phase == 1) & (i == 0))
+    def _():
+        for h in range(heads):
+            table = acc_ref[h, :, 0:128].astype(bf16)
+            table_ref[h] = table
+            table_t_ref[h] = flip(table)
+            counts = jnp.concatenate(
+                [acc_ref[h, :, 128:144], jnp.zeros((acc_ref.shape[1], 112), f32)], axis=1
+            )
+            count_ref[h] = jnp.transpose(counts)[0:8]
+
+    @pl.when(phase == 1)
+    def _():
+        for h in range(heads):
+            unit = qu_ref[64 * h : 64 * (h + 1), span]
+            plain, lows, highs = code_parts(bit_ref[h], unit, bits, hashes, rows)
+            store_codes(codes_ref, h, lows, highs, rows)
+        for h in range(heads):
+            mine = slice(64 * h, 64 * (h + 1))
+            both = nn(table_t_ref[h], codes_ref[h])
+            low = (both[0:64] * early + both[64:128] * late).astype(bf16)
+            for c in range(chips):
+                num_ref[c, mine, :] = low[:, c * block : (c + 1) * block]
+
+
+def soften(bit_planes, unit, slopes, codes_ref, head, bits, hashes, rows):
+    plain, lows, highs = code_parts(bit_planes, unit, bits, hashes, rows)
+    by_low = [None] * len(lows)
+    by_bit = [None] * (bits - 3)
+    for g, high in enumerate(highs):
+        row = None
+        for s in range(0, len(lows), 2):
+            spot = (g * len(lows) + s) * rows
+            parts = [lows[s] * high, lows[s + 1] * high]
+            codes_ref[head, spot : spot + 2 * rows, :] = jnp.concatenate(parts, axis=0).astype(bf16)
+            for k in range(2):
+                term = parts[k] * slopes[spot + k * rows : spot + (k + 1) * rows]
+                by_low[s + k] = term if by_low[s + k] is None else by_low[s + k] + term
+                row = term if row is None else row + term
+        for j in range(bits - 3):
+            if (g >> j) & 1:
+                by_bit[j] = row if by_bit[j] is None else by_bit[j] + row
+    pairs = [sum(part for s, part in enumerate(by_low) if (s >> j) & 1) for j in range(3)]
+    whole = sum(by_low)
+    slopes = [part - plain[j] * whole for j, part in enumerate(pairs + by_bit)]
+    return jnp.concatenate(slopes, axis=0).astype(bf16)
+
+
+def unit_back(grad, unit, inverse):
+    unit = unit.astype(f32)
+    inner = jnp.mean(grad * unit, axis=0, keepdims=True)
+    return inverse * (grad - unit * inner)
 
 
 def backward_kernel(
-    hashes, bits, rows, tile, tiles, heads, own_rows,
-    spots_ref, got_ref, w_ref, sign_ref, bit_ref,
+    hashes, bits, rows, tile, steps, heads, own_rows,
+    spots_ref, got_ref, w_ref, bit_ref, bit_t_ref,
     qu_ref, ku_ref, v_ref, inv_ref, table_ref, gnum_ref, conv_ref, tap_ref,
     grad_ref, keep_ref, give_ref,
-    acc_ref, codes_ref, slopes_ref, proj_ref, code_ref, code_t_ref, sum_ref,
+    acc_ref, codes_ref, proj_ref, sum_ref, table_t_ref, table_g_ref,
 ):
-    buckets = 2**bits
     limit = spots_ref[0]
     spot = spots_ref[1]
     core = spots_ref[2]
-    head = pl.program_id(0)
+    phase, i = pl.program_id(0), pl.program_id(1)
     width = got_ref.shape[2]
-    tok_rows = tile // CORES
-    code_matrix(sign_ref, code_ref, hashes, bits)
-    code_t_ref[...] = flip(code_ref[...])
-    acc_ref[...] = jnp.zeros_like(acc_ref)
-
-    def soften(unit, slopes):
-        norms = log_norms(unit, bit_ref[0], bits, rows)
-        logits = nn(code_ref[...], unit)
-        for r in range(hashes):
-            part = slice(r * buckets, (r + 1) * buckets)
-            codes = jnp.exp(logits[part] - norms[r : r + 1])
-            weighted = codes * slopes[part]
-            total = jnp.sum(weighted, axis=0, keepdims=True)
-            codes_ref[part, :] = codes.astype(bf16)
-            slopes_ref[part, :] = (weighted - codes * total).astype(bf16)
-        return nn(code_t_ref[...], slopes_ref[...])
-
-    def unit_back(grad, unit, inverse):
-        unit = unit.astype(f32)
-        inner = jnp.mean(grad * unit, axis=0, keepdims=True)
-        return inverse * (grad - unit * inner)
-
-    def queries(i, carry):
-        start = pl.multiple_of(i * tile, tile)
-        span = pl.ds(start, tile)
-        early, late = seg_rows(limit, start, tile)
-        pair = masked_pair(gnum_ref[i].astype(f32), early, late)
-        unit = qu_ref[:, span]
-        grad = soften(unit, nn(table_ref[0], pair))
-        acc_ref[...] += nt(codes_ref[...], pair)
-        proj_ref[head, 0:64, span] = unit_back(grad, unit, inv_ref[0, 0:1, span]).astype(bf16)
-        return carry
-
-    lax.fori_loop(0, tiles, queries, 0)
-    table_grad = acc_ref[...].astype(bf16)
-    table_grad_t = flip(table_grad)
-
-    def keys(i, carry):
-        start = pl.multiple_of(i * tile, tile)
-        span = pl.ds(start, tile)
-        early, late = seg_rows(limit, start, tile)
-        values = v_ref[:, pl.ds(pl.multiple_of(start + 128, 128), tile)]
-        pair = masked_pair(values.astype(f32), early, late)
-        unit = ku_ref[:, span]
-        grad = soften(unit, nn(table_grad, pair))
-        both = nn(table_grad_t, codes_ref[...])
-        here = (spot == i).astype(f32)
-        value_grad = both[0:64] * early + both[64:128] * late + conv_ref[...] * here
-        proj_ref[head, 64:128, span] = unit_back(grad, unit, inv_ref[0, 1:2, span]).astype(bf16)
-        proj_ref[head, 128:192, span] = value_grad.astype(bf16)
-        return carry
-
-    lax.fori_loop(0, tiles, keys, 0)
-
-    def weights(i, carry):
-        span = pl.ds(pl.multiple_of(i * tile, tile), tile)
-        toks = got_ref[pl.ds(i * CORES, CORES), 0:tok_rows, :].reshape(tile, width)
-        sum_ref[head] += nn(proj_ref[head, :, span], toks)
-        return carry
-
-    sum_ref[head] = jnp.zeros((192, width), f32)
-    lax.fori_loop(0, tiles, weights, 0)
-
-    @pl.when(head == heads - 1)
-    def _():
-        def inputs(i, carry):
-            span = pl.ds(pl.multiple_of(i * tile, tile), tile)
-            part = nn(w_ref[...], proj_ref[:, :, span].reshape(heads * 192, tile))
-            first, second = part[:, :tok_rows].astype(bf16), part[:, tok_rows:].astype(bf16)
-
-            @pl.when(core == 0)
-            def _():
-                keep_ref[i] = first
-                give_ref[i] = second
-
-            @pl.when(core != 0)
-            def _():
-                keep_ref[i] = second
-                give_ref[i] = first
-
-            return carry
-
-        lax.fori_loop(0, tiles, inputs, 0)
-        grad = jnp.transpose(sum_ref[...].reshape(heads * 192, width))
+    feats = heads * 64
+    blocks = keep_ref.shape[0]
+    block = tile // blocks
+    tok_rows = block // CORES
+    start = pl.multiple_of(i * tile, tile)
+    span = pl.ds(start, tile)
+    early, late = seg_rows(limit, start, tile)
+
+    @pl.when((phase == 0) & (i == 0))
+    def _():
+        acc_ref[...] = jnp.zeros_like(acc_ref)
+        sum_ref[...] = jnp.zeros_like(sum_ref)
+
+    @pl.when(phase == 0)
+    def _():
+        spans = [slice(64 * h, 64 * (h + 1)) for h in range(heads)]
+        pairs, grads, slopes = [], [], []
+        for mine in spans:
+            gnum = jnp.concatenate([gnum_ref[c, mine, :] for c in range(blocks)], axis=1)
+            pairs.append(masked_pair(gnum.astype(f32), early, late))
+        for h, mine in enumerate(spans):
+            slopes.append(
+                soften(
+                    bit_ref[h], qu_ref[mine, span], nn(table_ref[h], pairs[h]), codes_ref, h,
+                    bits, hashes, rows,
+                )
+            )
+        for h in range(heads):
+            acc_ref[h] += nt(codes_ref[h], pairs[h])
+        for h, mine in enumerate(spans):
+            grad = nn(bit_t_ref[h], slopes[h])
+            grad = unit_back(grad, qu_ref[mine, span], inv_ref[h : h + 1, span])
+            proj_ref[mine, span] = grad.astype(bf16)
+
+    @pl.when((phase == 1) & (i == 0))
+    def _():
+        for h in range(heads):
+            table_g_ref[h] = acc_ref[h].astype(bf16)
+            table_t_ref[h] = flip(table_g_ref[h])
+
+    @pl.when(phase == 1)
+    def _():
+        conv = []
+        for c in range(blocks):
+            step = i * blocks + c - spot + 1
+            near = ((step >= 0) & (step <= 2)).astype(f32)
+            step = jnp.clip(step, 0, 2)
+            conv.append(conv_ref[:, pl.ds(pl.multiple_of(step * block, block), block)] * near)
+        conv = jnp.concatenate(conv, axis=1)
+        spans = [slice(64 * h, 64 * (h + 1)) for h in range(heads)]
+        slopes, parts = [], []
+        for h, mine in enumerate(spans):
+            values = v_ref[mine, pl.ds(pl.multiple_of(start + 128, 128), tile)]
+            pair = masked_pair(values.astype(f32), early, late)
+            slopes.append(
+                soften(
+                    bit_ref[h], ku_ref[mine, span], nn(table_g_ref[h], pair), codes_ref, h,
+                    bits, hashes, rows,
+                )
+            )
+        for h, mine in enumerate(spans):
+            both = nn(table_t_ref[h], codes_ref[h])
+            value_grad = both[0:64] * early + both[64:128] * late + conv[mine]
+            grad = nn(bit_t_ref[h], slopes[h])
+            grad = unit_back(grad, ku_ref[mine, span], inv_ref[8 + h : 9 + h, span])
+            parts.append((grad.astype(bf16), value_grad.astype(bf16)))
+        full = jnp.concatenate(
+            [proj_ref[:, span]] + [part[0] for part in parts] + [part[1] for part in parts], axis=0
+        )
+        sum_ref[...] += nn(full, got_ref[...].reshape(tile, width))
+        part = nn(w_ref[...], full)
+        for c in range(blocks):
+            first = part[:, c * block : c * block + tok_rows]
+            second = part[:, c * block + tok_rows : (c + 1) * block]
+            keep_ref[c] = jnp.where(core == 0, first, second).astype(bf16)
+            give_ref[c] = jnp.where(core == 0, second, first).astype(bf16)
+
+    @pl.when((phase == 1) & (i == steps - 1))
+    def _():
+        grad = jnp.transpose(sum_ref[...])
+        chips = grad_ref.shape[0]
         grad_ref[:, :, 0 : heads * 192] = grad.reshape(
-            tiles, CORES * own_rows, heads * 192
+            chips, CORES * own_rows, heads * 192
         ).astype(bf16)
-        grad_ref[:, :, heads * 192 :] = jnp.zeros((tiles, CORES * own_rows, 64), bf16)
+        grad_ref[:, :, heads * 192 :] = jnp.zeros((chips, CORES * own_rows, 64), bf16)
         taps = jnp.concatenate([tap_ref[h, 0:1, 0:64] for h in range(heads)], axis=0)
-        for c in range(tiles):
+        for c in range(chips):
             grad_ref[c, 0:heads, heads * 192 :] = taps.astype(bf16)
 
 
@@ -314,29 +345,26 @@
 
 
 def conv_back_kernel(
-    tile, taps, spots_ref, left_ref, right_ref, before_ref, low_ref, high_ref, after_ref, base_ref,
-    out_ref, tap_ref,
+    tile, taps, spots_ref, left_ref, right_ref, low_ref, high_ref, base_ref, out_ref, tap_ref
 ):
     upper, lower = banded(base_ref[0, 0:1], window_same(spots_ref, tile), tile)
-    grads = jnp.concatenate([before_ref[...], low_ref[...], high_ref[...], after_ref[...]], axis=1)
-    out_ref[...] = nn(grads, upper) + nn(grads, lower)
+    own = jnp.concatenate([low_ref[...], high_ref[...]], axis=1)
+    out_ref[...] = jnp.zeros_like(out_ref)
+    out_ref[:, 128 : 128 + tile + 256] = nt(own, upper) + nt(own, lower)
     width = tile + 256
+    rim = taps // 2
     values = jnp.concatenate([left_ref[...], right_ref[...]], axis=1).astype(f32)
-    own = jnp.concatenate([low_ref[...], high_ref[...]], axis=1).astype(f32)
-    start = spots_ref[1] * tile
-    limit = spots_ref[0]
-    pos = lax.broadcasted_iota(jnp.int32, (1, tile), 1) + start
-    lane = lax.broadcasted_iota(jnp.int32, (8, 128), 1)
-    rim = taps // 2
-
-    def one(o, total):
+    own = own.astype(f32)
+    sums = []
+    for o in range(taps):
         moved = pltpu.roll(values, width - (128 - rim) - o, 1)[:, :tile]
-        row = jnp.sum(moved * own, axis=0, keepdims=True)
-        same = (pos >= limit) == (pos + (o - rim) >= limit)
-        tap = jnp.sum(jnp.where(same, row, 0.0), axis=1, keepdims=True)
-        return total + jnp.where(lane == o, tap, 0.0)
-
-    tap_ref[0] = lax.fori_loop(0, taps, one, jnp.zeros((8, 128), f32))
+        sums.append(jnp.sum(moved * own, axis=0, keepdims=True))
+    sums = jnp.concatenate(sums + [jnp.zeros((128 - taps, tile), f32)], axis=0)
+    pos = lax.broadcasted_iota(jnp.int32, (128, tile), 1) + spots_ref[1] * tile
+    other = pos + lax.broadcasted_iota(jnp.int32, (128, tile), 0) - rim
+    same = (pos >= spots_ref[0]) == (other >= spots_ref[0])
+    total = jnp.sum(jnp.where(same, sums, 0.0), axis=1, keepdims=True)
+    tap_ref[0] = jnp.transpose(jnp.broadcast_to(total, (128, 128)))[0:8]
 
 
 def context_kernel(heads, spots_ref, got_ref, conv_ref, keep_ref, give_ref, num_ref):
@@ -460,11 +488,10 @@
     mixer_ref, context_ref, hat_ref, norm_ref, slope_ref, feed_ref, active_ref, out_ref
 ):
     low = hat_ref[...] * norm_ref[0:1] + norm_ref[1:2]
-    out_width, ff = context_ref.shape[1], slope_ref.shape[1]
-    out_ref[:, :out_width] = nn(flip(mixer_ref[...]), context_ref[...]).astype(bf16)
-    first = jnp.transpose(low.astype(bf16).astype(f32)).astype(bf16)
-    out_ref[:, out_width : out_width + ff] = nn(first, slope_ref[...]).astype(bf16)
-    out_ref[:, out_width + ff :] = nn(flip(feed_ref[...]), active_ref[...]).astype(bf16)
+    ff = slope_ref.shape[1]
+    out_ref[:, :ff] = nn(flip(low.astype(bf16)), slope_ref[...]).astype(bf16)
+    out_ref[:, ff : 2 * ff] = nn(flip(feed_ref[...]), active_ref[...]).astype(bf16)
+    out_ref[:, 2 * ff :] = nn(flip(mixer_ref[...]), context_ref[...]).astype(bf16)
 
 
 def on_device(
@@ -510,7 +537,10 @@
     total = chips * tile
     own_rows = width // seq_count
     ff = up_weight.shape[1]
-    code_rows = hashes * buckets
+    code_rows = rows * buckets
+    blocks = WORK if chips % WORK == 0 else 1
+    steps = chips // blocks
+    work = blocks * tile
     planes_of = [[CORES * c + k for c in range(chips)] for k in range(CORES)]
     across = partial(
         lax.all_to_all, axis_name="seq", split_axis=0, concat_axis=0, tiled=True,
@@ -527,15 +557,6 @@
         dimension_semantics=("arbitrary",), vmem_limit_bytes=VMEM_LIMIT
     )
     shape = jax.ShapeDtypeStruct
-
-    def whole(*dims):
-        return pl.BlockSpec(dims, lambda h: (0,) * len(dims), pipeline_mode=pl.Buffered(1))
-
-    def by_head(*dims):
-        return pl.BlockSpec((1,) + dims, lambda h: (h,) + (0,) * len(dims))
-
-    def head_rows(*dims):
-        return pl.BlockSpec((head_dim,) + dims, lambda h: (h,) + (0,) * len(dims))
 
     def full(value):
         return pl.BlockSpec(value.shape, lambda i: (0,) * value.ndim)
@@ -560,19 +581,23 @@
             name=name,
         )(*args)
 
-    low_qkv = qkv_weight.astype(bf16)
-    first_send = jnp.concatenate(
-        [
-            tokens,
-            jnp.concatenate([low_qkv[0], low_qkv[1]], axis=1),
-            jnp.concatenate([low_qkv[2], out_weight.T.astype(bf16)], axis=1),
-        ],
-        axis=0,
-    )
-    got = lax.all_gather(first_send, "seq", axis=0, tiled=False)
-    qk_all = got[:, tok_rows : tok_rows + own_rows].reshape(width, 2 * group_feats)
-    vo_all = got[:, tok_rows + own_rows :].reshape(width, 2 * group_feats)
-    second_send = jnp.concatenate([up_weight.astype(bf16), down_weight.T.astype(bf16)], axis=1)
+    def in_order(mine, other, axis):
+        first = jnp.where(core == 0, mine, other)
+        return jnp.concatenate([first, jnp.where(core == 0, other, mine)], axis=axis)
+
+    got = lax.all_gather(tokens, "seq", axis=0, tiled=False)
+
+    low_qkv = qkv_weight.astype(bf16).reshape(3, own_rows, CORES, feats)
+    pick = partial(lax.dynamic_index_in_dim, low_qkv, axis=2, keepdims=False)
+    by_rows = lambda part: jnp.transpose(part, (1, 0, 2)).reshape(own_rows, 3 * feats)
+    qkv_mine, qkv_give = by_rows(pick(core)), by_rows(pick(1 - core))
+    chip_rows = in_order(qkv_mine, core_swap(qkv_give), 0)
+    qkv_all = lax.all_gather(
+        chip_rows, "seq", axis=0, tiled=True, axis_index_groups=planes_of
+    )
+    second_send = jnp.concatenate(
+        [up_weight.astype(bf16), down_weight.T.astype(bf16), out_weight.T.astype(bf16)], axis=1
+    )
     second_send, unused = lax.optimization_barrier((second_send, got[0, 0, 0:1]))
     ff_all = lax.all_gather(second_send, "seq", axis=0, tiled=True)
 
@@ -581,61 +606,67 @@
     )
     scale = sharpness / math.sqrt(head_dim)
     signs = scale * (2 * own_planes - 1).astype(f32)
-    sign_w = jnp.pad(
-        jnp.transpose(signs, (2, 0, 1, 3)), ((0, 0), (0, 0), (0, 8 - bits), (0, 0))
-    ).astype(bf16)
     bit_w = jnp.pad(
         jnp.transpose(signs, (2, 1, 0, 3)), ((0, 0), (0, 0), (0, rows - hashes), (0, 0))
     )
     bit_w = bit_w.reshape(heads, bits * rows, head_dim).astype(bf16)
-
-    num_parts, q_unit, k_unit, values, inverses, tables, counts, w_cols = pl.pallas_call(
-        partial(forward_kernel, hashes, bits, rows, tile, chips, heads, group_feats),
-        grid=(heads,),
+    bit_wt = jnp.transpose(bit_w, (0, 2, 1))
+
+    def resident(*dims):
+        return pl.BlockSpec(dims, lambda p, i: (0,) * len(dims), pipeline_mode=pl.Buffered(1))
+
+    def stepped(phase, *dims):
+        def place(p, i):
+            rest = steps - 1 if phase == 0 else 0
+            return (jnp.where(p == phase, i, rest),) + (0,) * (len(dims) - 1)
+
+        return pl.BlockSpec(dims, place)
+
+    hash_params = pltpu.CompilerParams(
+        dimension_semantics=("arbitrary", "arbitrary"), vmem_limit_bytes=VMEM_LIMIT
+    )
+    num_parts, q_unit, k_unit, values, inverses, tables, counts = pl.pallas_call(
+        partial(forward_kernel, hashes, bits, rows, work, steps, heads),
+        grid=(2, steps),
         in_specs=[
             smem,
-            whole(*got.shape),
-            whole(*qk_all.shape),
-            whole(*vo_all.shape),
-            by_head(hashes, 8, head_dim),
-            by_head(bits * rows, head_dim),
+            stepped(0, CORES * blocks, tok_rows, width),
+            resident(*qkv_all.shape),
+            resident(*bit_w.shape),
         ],
         out_specs=[
-            pl.BlockSpec((chips, head_dim, tile), lambda h: (0, h, 0)),
-            head_rows(total),
-            head_rows(total),
-            head_rows(total + 256),
-            by_head(8, total),
-            by_head(code_rows, 2 * head_dim),
-            by_head(8, code_rows),
-            whole(width, 3 * feats),
+            stepped(1, blocks, feats, tile),
+            resident(feats, total),
+            resident(feats, total),
+            resident(feats, total + 256),
+            resident(16, total),
+            resident(heads, code_rows, 2 * head_dim),
+            resident(heads, 8, code_rows),
         ],
         out_shape=[
             shape((chips, feats, tile), bf16),
             shape((feats, total), bf16),
             shape((feats, total), bf16),
             shape((feats, total + 256), bf16),
-            shape((heads, 8, total), f32),
+            shape((16, total), f32),
             shape((heads, code_rows, 2 * head_dim), bf16),
             shape((heads, 8, code_rows), f32),
-            shape((width, 3 * feats), bf16),
         ],
         scratch_shapes=[
-            pltpu.VMEM((code_rows, 2 * head_dim + 16), f32),
-            pltpu.VMEM((code_rows, tile), bf16),
-            pltpu.VMEM((code_rows, head_dim), bf16),
-            pltpu.VMEM((heads, 3 * head_dim, width), bf16),
-        ],
-        compiler_params=params,
+            pltpu.VMEM((heads, code_rows, 2 * head_dim + 16), f32),
+            pltpu.VMEM((heads, code_rows, work), bf16),
+            pltpu.VMEM((3 * feats, width), bf16),
+            pltpu.VMEM((heads, 2 * head_dim, code_rows), bf16),
+        ],
+        compiler_params=hash_params,
         name="hash_forward",
-    )(spots, got, qk_all, vo_all, sign_w, bit_w)
+    )(spots, got, qkv_all, bit_w)
     num_got = across(num_parts)
 
     own_taps = lax.dynamic_slice(conv_taps, (core * heads, 0), (heads, taps))
     lead = tile + 128 - rim
-    bases = jnp.zeros((heads, 16, tile + 256), f32)
+    bases = jnp.zeros((heads, 8, tile + 256), f32)
     bases = bases.at[:, 0, lead : lead + taps].set(own_taps[:, ::-1])
-    bases = bases.at[:, 8, lead : lead + taps].set(own_taps)
     window = [
         pl.BlockSpec((head_dim, tile), lambda h, s: (h, s[1])),
         pl.BlockSpec((head_dim, tile), lambda h, s: (h, s[1] + 1)),
@@ -658,8 +689,8 @@
     count_rows = -(-2 * hashes * heads * chip_buckets // tile)
     sum_rows = 4 * width // tile
     extra_rows = -(-(sum_rows + count_rows) // 16) * 16
-    count_send = counts[:, 0:2].reshape(heads, 2, hashes, chips, chip_buckets)
-    count_send = jnp.transpose(count_send, (3, 1, 2, 0, 4)).reshape(chips, -1)
+    count_send = counts[:, 0:2].reshape(heads, 2, chips, chip_buckets, rows)[..., :hashes]
+    count_send = jnp.transpose(count_send, (2, 1, 4, 0, 3)).reshape(chips, -1)
     count_send = jnp.pad(
         count_send, ((0, 0), (0, (extra_rows - sum_rows) * tile - count_send.shape[1]))
     ).reshape(chips, extra_rows - sum_rows, tile)
@@ -672,8 +703,8 @@
     context, mixer_part = once(
         mixer_kernel, "mixer",
         [shape((tok_rows, group_feats), bf16), shape((tok_rows, width), bf16)],
-        [spots, keep, core_swap(give), vo_all],
-        [None, None, None, columns(group_feats, 1)],
+        [spots, keep, core_swap(give), ff_all],
+        [None, None, None, columns(group_feats, 2 * ff // group_feats)],
     )
     first_hat, first_inverse, hidden, active, feed_part = once(
         hidden_kernel, "feed_forward",
@@ -711,9 +742,9 @@
         ],
         [
             spots, grad_second, first_part, head_swap(first_part), first_hat, first_inverse,
-            norm_params, vo_all, second_sums,
-        ],
-        [None, None, None, None, None, None, None, columns(group_feats, 1), None],
+            norm_params, ff_all, second_sums,
+        ],
+        [None, None, None, None, None, None, None, columns(group_feats, 2 * ff // group_feats), None],
     )
     gnum_send, grad_low, grad_high = once(
         partial(attention_back_kernel, heads), "attention_back",
@@ -726,6 +757,7 @@
     )
     gnum_got = across(gnum_send)
 
+    mixer_low, unused = lax.optimization_barrier((mixer_low, grad_low[0:1, 0:1]))
     (big_grad,) = once(
         big_grad_kernel, "weight_grads",
         [shape((width, group_feats + 2 * ff), bf16)],
@@ -733,50 +765,46 @@
     )
     big_owned = lax.psum_scatter(big_grad, "seq", scatter_dimension=0, tiled=True).astype(f32)
 
-    up_moves = [(i, i + CORES) for i in range(seq_count - CORES)]
-    down_moves = [(j, i) for i, j in up_moves]
-    before = lax.ppermute(grad_high, "seq", up_moves)
-    after = lax.ppermute(grad_low, "seq", down_moves)
     conv_grad, tap_parts = pl.pallas_call(
         partial(conv_back_kernel, tile, taps),
         grid_spec=pltpu.PrefetchScalarGridSpec(
             num_scalar_prefetch=1,
             grid=(heads,),
             in_specs=window
-            + [half_rows] * 4
-            + [pl.BlockSpec((1, 8, tile + 256), lambda h, s: (h, 1, 0))],
+            + [half_rows] * 2
+            + [pl.BlockSpec((1, 8, tile + 256), lambda h, s: (h, 0, 0))],
             out_specs=[
-                pl.BlockSpec((head_dim, tile), lambda h, s: (h, 0)),
+                pl.BlockSpec((head_dim, 3 * tile), lambda h, s: (h, 0)),
                 pl.BlockSpec((1, 8, 128), lambda h, s: (h, 0, 0)),
             ],
         ),
-        out_shape=[shape((feats, tile), f32), shape((heads, 8, 128), f32)],
+        out_shape=[shape((feats, 3 * tile), f32), shape((heads, 8, 128), f32)],
         compiler_params=params,
         name="conv_backward",
-    )(spots, values, values, before, grad_low, grad_high, after, bases)
+    )(spots, values, values, grad_low, grad_high, bases)
 
     qkv_send, back_keep, back_give = pl.pallas_call(
-        partial(backward_kernel, hashes, bits, rows, tile, chips, heads, own_rows),
-        grid=(heads,),
+        partial(backward_kernel, hashes, bits, rows, work, steps, heads, own_rows),
+        grid=(2, steps),
         in_specs=[
             smem,
-            whole(*got.shape),
-            whole(*w_cols.shape),
-            by_head(hashes, 8, head_dim),
-            by_head(bits * rows, head_dim),
-            head_rows(total),
-            head_rows(total),
-            head_rows(total + 256),
-            by_head(8, total),
-            by_head(code_rows, 2 * head_dim),
-            pl.BlockSpec((chips, head_dim, tile), lambda h: (0, h, 0)),
-            head_rows(tile),
-            whole(*tap_parts.shape),
+            stepped(1, CORES * blocks, tok_rows, width),
+            resident(*qkv_all.shape),
+            resident(*bit_w.shape),
+            resident(*bit_wt.shape),
+            resident(feats, total),
+            resident(feats, total),
+            resident(feats, total + 256),
+            resident(16, total),
+            resident(heads, code_rows, 2 * head_dim),
+            stepped(0, blocks, feats, tile),
+            resident(feats, 3 * tile),
+            resident(*tap_parts.shape),
         ],
         out_specs=[
-            whole(chips, CORES * own_rows, 3 * feats + 64),
-            whole(chips, width, tok_rows),
-            whole(chips, width, tok_rows),
+            resident(chips, CORES * own_rows, 3 * feats + 64),
+            stepped(1, blocks, width, tok_rows),
+            stepped(1, blocks, width, tok_rows),
         ],
         out_shape=[
             shape((chips, CORES * own_rows, 3 * feats + 64), bf16),
@@ -784,18 +812,17 @@
             shape((chips, width, tok_rows), bf16),
         ],
         scratch_shapes=[
-            pltpu.VMEM((code_rows, 2 * head_dim), f32),
-            pltpu.VMEM((code_rows, tile), bf16),
-            pltpu.VMEM((code_rows, tile), bf16),
-            pltpu.VMEM((heads, 3 * head_dim, total), bf16),
-            pltpu.VMEM((code_rows, head_dim), bf16),
-            pltpu.VMEM((head_dim, code_rows), bf16),
-            pltpu.VMEM((heads, 3 * head_dim, width), f32),
-        ],
-        compiler_params=params,
+            pltpu.VMEM((heads, code_rows, 2 * head_dim), f32),
+            pltpu.VMEM((heads, code_rows, work), bf16),
+            pltpu.VMEM((feats, total), bf16),
+            pltpu.VMEM((3 * feats, width), f32),
+            pltpu.VMEM((heads, 2 * head_dim, code_rows), bf16),
+            pltpu.VMEM((heads, code_rows, 2 * head_dim), bf16),
+        ],
+        compiler_params=hash_params,
         name="hash_backward",
     )(
-        spots, got, w_cols, sign_w, bit_w,
+        spots, got, qkv_all, bit_w, bit_wt,
         q_unit, k_unit, values, inverses, tables, gnum_got, conv_grad, tap_parts,
     )
 
@@ -824,10 +851,6 @@
         jnp.concatenate([norm_half.reshape(-1), count_give.reshape(-1), tap_half.reshape(-1)])
     )
     norm_size, count_size = norm_half.size, count_give.size
-
-    def in_order(mine, other, axis):
-        first = jnp.where(core == 0, mine, other)
-        return jnp.concatenate([first, jnp.where(core == 0, other, mine)], axis=axis)
 
     norm_grad = norm_half + swapped[:norm_size].reshape(norm_half.shape)
     norm_grad = jnp.transpose(
@@ -841,9 +864,7 @@
     conv_tap_grad = in_order(tap_half, swapped[norm_size + count_size :].reshape(heads, taps), 0)
 
     def weight_order(part):
-        return jnp.transpose(part.reshape(own_rows, heads, 3, head_dim), (2, 0, 1, 3)).reshape(
-            3, own_rows, feats
-        )
+        return jnp.transpose(part.reshape(own_rows, 3, feats), (1, 0, 2))
 
     qkv_owned = in_order(weight_order(qkv_mine), weight_order(qkv_other), 2)
     back_low = lax.optimization_barrier(back_half.astype(bf16))
@@ -852,9 +873,9 @@
     lower = jnp.where(side == 0, back_other, back_low)
     tokens_grad = grad_mixer + jnp.concatenate([upper, lower], axis=0).T.astype(f32)
 
-    out_owned = big_owned[:, :group_feats].T
-    up_owned = big_owned[:, group_feats : group_feats + ff]
-    down_owned = big_owned[:, group_feats + ff :].T
+    up_owned = big_owned[:, :ff]
+    down_owned = big_owned[:, ff : 2 * ff].T
+    out_owned = big_owned[:, 2 * ff :].T
     qkv_new, qkv_first_new, qkv_second_new = adam_step(
         qkv_weight, qkv_first, qkv_second, qkv_owned, D ** (-0.5)
     )

time: 382 us -> 322 us (0.84)
  Pallas kernels: 145 us -> 82.2 us
  blocking collectives: 0 us -> 37.9 us
  starting transfers between devices: 45 us -> 26.7 us
  waiting for transfers between devices: 124 us -> 110 us
    pallas_call x2, Pallas kernels: 95.9 us -> 49.1 us  [the longest x1 32.4 us: on_device(): pl.pallas_call(partial(backward_kernel, hashes, bits, rows, work, steps,...]
    all_gather x1, waiting for transfers between devices: 57.4 us -> 11.4 us  [on_device(): got = lax.all_gather(tokens, 'seq', axis=0, tiled=False)]
    all_gather x0 -> x1, blocking collectives: none -> 37.9 us  [on_device(): lax.all_gather(chip_rows, 'seq', axis=0, tiled=True, axis_index_groups=pl...]
    all_to_all x1, waiting for transfers between devices: 0.01 us -> 17.5 us  [on_device(): gnum_got = across(gnum_send)]
    pallas_call x1, Pallas kernels: 21.1 us -> 4.54 us  [on_device(): pl.pallas_call(partial(conv_back_kernel, tile, taps), grid_spec=pltpu.Pre...]
    all_to_all x1, starting transfers between devices: 20.2 us -> 7.82 us  [on_device(): qkv_half = jnp.sum(across(qkv_send).astype(f32), axis=0)]
    all_to_all x1, waiting for transfers between devices: 12.9 us -> 23.3 us  [on_device(): num_got = across(num_parts)]
    all_gather x1, waiting for transfers between devices: 0.01 us -> 8.59 us  [on_device(): ff_all = lax.all_gather(second_send, 'seq', axis=0, tiled=True)]
  transfers between devices with their start and end apart: 19 -> 18, of which waited for: 11 -> 11; matrix products, arithmetic and copies ran while one was open for 9% -> 12% of each run, Pallas kernels for 33% -> 19%
where the time goes in v3:
time: 322 us; the launch traced here: 321 us
  waiting for transfers between devices  110 us (34%)
  Pallas kernels  82.2 us (26%)
  blocking collectives  37.9 us (12%)
  starting transfers between devices  26.7 us (8%)
  other arithmetic  26.3 us (8%)
  local copies, waits for them, and re-layouts  23.4 us (7%)
  between operations  14.3 us (4%)
    all_gather x1, blocking collectives, on_device(): lax.all_gather(chip_rows, 'seq', axis=0, tiled=True, axis_index_groups=pl...  37.9 us
    pallas_call x1, Pallas kernels, on_device(): pl.pallas_call(partial(backward_kernel, hashes, bits, rows, work, steps,...  32.4 us
    pallas_call x7, Pallas kernels, once(): pl.pallas_call(kernel, grid=(1,), in_specs=specs, out_specs=[full(o) for...  24.9 us
    all_to_all x1, waiting for transfers between devices, on_device(): num_got = across(num_parts)  23.3 us
    all_to_all x1, waiting for transfers between devices, on_device(): gnum_got = across(gnum_send)  17.5 us
    pallas_call x1, Pallas kernels, on_device(): pl.pallas_call(partial(forward_kernel, hashes, bits, rows, work, steps, h...  16.7 us
    all_to_all x1, waiting for transfers between devices, on_device(): qkv_half = jnp.sum(across(qkv_send).astype(f32), axis=0)  16.4 us
    all_to_all x1, waiting for transfers between devices, on_device(): back_half = jnp.sum(across(pair_sum.astype(bf16)).astype(f32), axis=0)  14.2 us
  transfers between devices with their start and end apart: 18, of which 11 were waited for; matrix products, arithmetic and copies ran while one was open for 12% of the time, Pallas kernels for 19%

profile of v3, /device:TPU:0, one launch (start us, length us, event | category | flops | bytes accessed | tf_op | source)
XLA Modules:
  0.0 320.8 jit_solution(10797612424812529071)
XLA Ops:
  14.5 37.9 %all_gather.14.w_ref = bf16[768,576]{1,0:T(8,128)(2,1)} all-gather(bf16[96,576]{1,0:T(8,128)(2,1)S(1)} %pad_maximum_fusion.2), channel_id=1, replica_groups={{0,4,8,12,16,20,24,28},{2,6,10,14,18,22,26,30},{1,5,9,13,17,21,25,29},{..., dimensions={0}, use_global_device_ids=true | all-gather | bytes 995328 | tf_op jit(solution)/shard_map/all_gather | solution.py:595
  52.3 11.4 %all-gather.6.cloned.1.call-done = bf16[2048,768]{1,0:T(8,128)(2,1)} async-done(((bf16[128,768]{1,0:T(8,128)(2,1)}), bf16[2048,768]{1,0:T(8,128)(2,1)}) %all-gather.6.cloned.1.call-update) | async-done | bytes 3145744 | tf_op jit(solution)/shard_map/all_gather | solution.py:588
  63.7 16.7 %hash_forward.1 = (bf16[8,192,256]{2,1,0:T(8,128)(2,1)}, bf16[192,2048]{1,0:T(8,128)(2,1)}, bf16[192,2048]{1,0:T(8,128)(2,1)}, bf16[192,2304]{1,0:T(8,128)(2,1)}...) custom-call(s32[3]{0:T(128)} %pad_add_fusion.spots_ref, ...), custom_call_target="tpu_custom_call" | custom-call | tf_op jit(solution)/shard_map/hash_forward/pallas_call | solution.py:628
  80.5 4.0 %all-to-all-start = ((bf16[8,192,256]{2,1,0:T(8,128)(2,1)}), bf16[8,192,256]{2,1,0:T(8,128)(2,1)S(1)}, u32[]{:S(2)}, u32[]{:S(2)}) async-start(bf16[8,192,256]{2,1,0:T(8,128)(2,1)} %get-tuple-element.73), calls=%async_computation | async-start | bytes 1572864 | tf_op jit(solution)/shard_map/all_to_all | solution.py:664
  86.7 1.9 scatter.4.base_ref
  89.3 3.7 %conv_forward.1.conv_ref = f32[192,256]{1,0:T(8,128)} custom-call(s32[3]{0:T(128)} %pad_add_fusion.spots_ref, bf16[192,2304]{1,0:T(8,128)(2,1)} %get-tuple-element.74.left_ref.right_ref.v_ref, bf16[192,2304]{1,0:T(8,128)(2,1)} %get-tuple-element.74.left_ref.right_ref.v_ref, f32[3,8,512]{2,1,0:T(8,128)} %copy-done.9), custom_call_target="tpu_custom_call" | custom-call | tf_op jit(solution)/shard_map/conv_forward/pallas_call | solution.py:675
  92.9 23.3 %all-to-all-done.got_ref = bf16[8,192,256]{2,1,0:T(8,128)(2,1)S(1)} async-done(((bf16[8,192,256]{2,1,0:T(8,128)(2,1)}), bf16[8,192,256]{2,1,0:T(8,128)(2,1)S(1)}, u32[]{:S(2)}, u32[]{:S(2)}) %all-to-all-start) | async-done | bytes 786464 | tf_op jit(solution)/shard_map/all_to_all | solution.py:664
  117.1 2.2 context.1
  120.8 8.6 %all-gather.4.cloned.1.call-done.out_ref.up_ref.down_ref = bf16[768,3456]{1,0:T(8,128)(2,1)} async-done(((bf16[48,3456]{1,0:T(8,128)(2,1)}), bf16[768,3456]{1,0:T(8,128)(2,1)}) %all-gather.4.cloned.1.call-update) | async-done | bytes 5308432 | tf_op jit(solution)/shard_map/all_gather | solution.py:602
  129.4 2.2 mixer.1
  131.6 1.5 collective-permute-start.2
  133.1 5.8 %collective-permute-done.2.other_ref = bf16[128,768]{1,0:T(8,128)(2,1)S(1)} collective-permute-done((bf16[128,768]{1,0:T(8,128)(2,1)}, bf16[128,768]{1,0:T(8,128)(2,1)S(1)}, u32[]{:S(2)}, u32[]{:S(2)}) %collective-permute-start.2) | collective-permute-done | bytes 196640 | tf_op jit(solution)/shard_map/ppermute | solution.py:718
  139.5 4.8 %feed_forward.1 = (f32[128,768]{1,0:T(8,128)}, f32[128,1]{1,0:T(8,128)}, f32[128,1536]{1,0:T(8,128)}, bf16[128,1536]{1,0:T(8,128)(2,1)}, bf16[128,768]{1,0:T(8,128)(2,1)}) custom-call(bf16[128,768]{1,0:T(8,128)(2,1)} %tok_ref.1, bf16[128,768]{1,0:T(8,128)(2,1)} %get-tuple-element.77.own_ref, bf16[128,768]{1,0:T(8,128)(2,1)} %copy-done.19, ...), custom_call_target="tpu_custom_call" | custom-call | tf_op jit(solution)/shard_map/feed_forward/pallas_call | solution.py:574
  144.3 1.5 collective-permute-start.3
  145.8 5.0 %collective-permute-done.3.other_ref = bf16[128,768]{1,0:T(8,128)(2,1)S(1)} collective-permute-done((bf16[128,768]{1,0:T(8,128)(2,1)}, bf16[128,768]{1,0:T(8,128)(2,1)S(1)}, u32[]{:S(2)}, u32[]{:S(2)}) %collective-permute-start.3) | collective-permute-done | bytes 196640 | tf_op jit(solution)/shard_map/ppermute | solution.py:731
  151.5 5.2 %feed_back.1 = (f32[128,768]{1,0:T(8,128)}, f32[128,768]{1,0:T(8,128)}, bf16[128,768]{1,0:T(8,128)(2,1)}, bf16[128,1536]{1,0:T(8,128)(2,1)}, bf16[128,768]{1,0:T(8,128)(2,1)}, /*index=5*/f32[2,768]{1,0:T(2,128)}) custom-call(f32[128,768]{1,0:T(8,128)} %get-tuple-element.78.hat_ref, f32[128,1536]{1,0:T(8,128)} %get-tuple-element.79.hidden_ref, ...), custom_call_target="tpu_custom_call" | custom-call | tf_op jit(solution)/shard_map/feed_back/pallas_call | solution.py:574
  158.2 4.4 %collective-permute-done.4.other_ref = bf16[128,768]{1,0:T(8,128)(2,1)S(1)} collective-permute-done((bf16[128,768]{1,0:T(8,128)(2,1)}, bf16[128,768]{1,0:T(8,128)(2,1)S(1)}, u32[]{:S(2)}, u32[]{:S(2)}) %collective-permute-start.4) | collective-permute-done | bytes 196640 | tf_op jit(solution)/shard_map/ppermute | solution.py:744
  163.3 2.8 mixer_back.1
  166.1 5.5 %weight_grads.1 = bf16[768,3456]{1,0:T(8,128)(2,1)} custom-call(bf16[128,768]{1,0:T(8,128)(2,1)} %get-tuple-element.104.mixer_ref, bf16[128,384]{1,0:T(8,128)(2,1)} %get-tuple-element.105.context_ref, f32[128,768]{1,0:T(8,128)} %get-tuple-element.78.hat_ref, f32[4,768]{1,0:T(4,128)} %norm_ref.7, bf16[128,1536]{1,0:T(8,128)(2,1)} %get-tuple-element.106.slope_ref, ...), custom_call_target="tpu_custom_call" | custom-call | tf_op jit(solution)/shard_map/weight_grads/pallas_call | solution.py:574
  175.3 2.2 attention_back.1
  177.5 3.8 %all-to-all-start.1 = ((bf16[8,208,256]{2,1,0:T(8,128)(2,1)}), bf16[8,208,256]{2,1,0:T(8,128)(2,1)S(1)}, u32[]{:S(2)}, u32[]{:S(2)}) async-start(bf16[8,208,256]{2,1,0:T(8,128)(2,1)} %get-tuple-element.96), calls=%async_computation.1 | async-start | bytes 1703936 | tf_op jit(solution)/shard_map/all_to_all | solution.py:758
  182.0 4.5 %conv_backward.1 = (f32[192,768]{1,0:T(8,128)}, f32[3,8,128]{2,1,0:T(8,128)}) custom-call(s32[3]{0:T(128)} %pad_add_fusion.spots_ref, bf16[192,2304]{1,0:T(8,128)(2,1)} %get-tuple-element.74.left_ref.right_ref.v_ref, bf16[192,2304]{1,0:T(8,128)(2,1)} %get-tuple-element.74.left_ref.right_ref.v_ref, bf16[192,128]{1,0:T(8,128)(2,1)} %get-tuple-element.97.low_ref, ...), custom_call_target="tpu_custom_call" | custom-call | tf_op jit(solution)/shard_map/conv_backward/pallas_call | solution.py:768
  186.6 17.5 %all-to-all-done.1.gnum_ref = bf16[8,208,256]{2,1,0:T(8,128)(2,1)S(1)} async-done(((bf16[8,208,256]{2,1,0:T(8,128)(2,1)}), bf16[8,208,256]{2,1,0:T(8,128)(2,1)S(1)}, u32[]{:S(2)}, u32[]{:S(2)}) %all-to-all-start.1) | async-done | bytes 852000 | tf_op jit(solution)/shard_map/all_to_all | solution.py:758
  205.0 32.4 %hash_backward.1 = (bf16[8,96,640]{2,1,0:T(8,128)(2,1)}, bf16[8,768,128]{2,1,0:T(8,128)(2,1)}, bf16[8,768,128]{2,1,0:T(8,128)(2,1)}) custom-call(s32[3]{0:T(128)} %pad_add_fusion.spots_ref, bf16[16,128,768]{2,1,0:T(8,128)(2,1)} %bitcast.83, bf16[768,576]{1,0:T(8,128)(2,1)} %all_gather.14.w_ref, bf16[3,56,64]{2,1,0:T(8,128)(2,1)} %fusion.12.bit_ref, ...), custom_call_target="tpu_custom_call" | custom-call | tf_op jit(solution)/shard_map/hash_backward/pallas_call | solution.py:786
  237.5 7.8 %all-to-all-start.3 = ((bf16[8,96,640]{2,1,0:T(8,128)(2,1)}), bf16[8,96,640]{2,1,0:T(8,128)(2,1)}, u32[]{:S(2)}, u32[]{:S(2)}) async-start(bf16[8,96,640]{2,1,0:T(8,128)(2,1)} %get-tuple-element.103), calls=%async_computation.3 | async-start | bytes 1966080 | tf_op jit(solution)/shard_map/all_to_all | solution.py:836
  247.3 2.3 add_convert_fusion
  254.6 16.4 %all-to-all-done.3 = bf16[8,96,640]{2,1,0:T(8,128)(2,1)} async-done(((bf16[8,96,640]{2,1,0:T(8,128)(2,1)}), bf16[8,96,640]{2,1,0:T(8,128)(2,1)}, u32[]{:S(2)}, u32[]{:S(2)}) %all-to-all-start.3) | async-done | bytes 983072 | tf_op jit(solution)/shard_map/all_to_all | solution.py:836
  277.0 2.2 fusion
  279.2 3.9 %all-to-all-start.2 = ((bf16[8,384,128]{2,1,0:T(8,128)(2,1)}), bf16[8,384,128]{2,1,0:T(8,128)(2,1)S(1)}, u32[]{:S(2)}, u32[]{:S(2)}) async-start(bf16[8,384,128]{2,1,0:T(8,128)(2,1)} %fusion), calls=%async_computation.2 | async-start | bytes 1572864 | tf_op jit(solution)/shard_map/all_to_all | solution.py:837
  289.4 14.2 %all-to-all-done.2 = bf16[8,384,128]{2,1,0:T(8,128)(2,1)S(1)} async-done(((bf16[8,384,128]{2,1,0:T(8,128)(2,1)}), bf16[8,384,128]{2,1,0:T(8,128)(2,1)S(1)}, u32[]{:S(2)}, u32[]{:S(2)}) %all-to-all-start.2) | async-done | bytes 786464 | tf_op jit(solution)/shard_map/all_to_all | solution.py:837
  305.1 2.1 fusion.23
  310.4 1.7 fusion.21
  (150 shorter events, 47.0 us)
Async XLA Ops:
  7.2 5.7 %copy-start = (s32[64,7,6,64]{3,0,2,1:T(8,128)S(1)}, s32[64,7,6,64]{3,0,2,1:T(8,128)}, u32[]{:S(2)}) copy-start(s32[64,7,6,64]{3,0,2,1:T(8,128)} %param.27) | copy-start | bytes 2064388
  7.2 4.5 %copy-start.6 = (f32[3,48,384]{2,1,0:T(8,128)S(1)}, f32[3,48,384]{2,1,0:T(8,128)}, u32[]{:S(2)}) copy-start(f32[3,48,384]{2,1,0:T(8,128)} %param.28) | copy-start | bytes 663556
  7.2 56.5 %all-gather.6.cloned.1.call-start = ((), (), s32[]{:S(2)}) async-start(), calls=%async_computation.7 | async-start | bytes 3342336 | tf_op jit(solution)/shard_map/all_gather | solution.py:588
  8.0 121.4 %all-gather.4.cloned.1.call-start = ((), (), s32[]{:S(2)}) async-start(), calls=%async_computation.5 | async-start | bytes 5640192 | tf_op jit(solution)/shard_map/all_gather | solution.py:602
  9.9 3.7 %copy-start.25 = (s32[2]{0:T(128)S(1)}, s32[2]{0:T(128)}, u32[]{:S(2)}) copy-start(s32[2]{0:T(128)} %param.26) | copy-start | bytes 28
  12.4 2.0 collective-permute-start
  80.5 4.1 %copy-start.24 = (f32[6,33]{1,0:T(8,128)S(1)}, f32[6,33]{1,0:T(8,128)}, u32[]{:S(2)}) copy-start(f32[6,33]{1,0:T(8,128)} %param.43) | copy-start | bytes 2380
  80.5 4.2 %copy-start.26 = (s32[3]{0:T(128)S(1)}, s32[3]{0:T(128)}, u32[]{:S(2)}) copy-start(s32[3]{0:T(128)} %constant.169.clone.1) | copy-start | bytes 40
  80.5 35.8 %all-to-all-start = ((bf16[8,192,256]{2,1,0:T(8,128)(2,1)}), bf16[8,192,256]{2,1,0:T(8,128)(2,1)S(1)}, u32[]{:S(2)}, u32[]{:S(2)}) async-start(bf16[8,192,256]{2,1,0:T(8,128)(2,1)} %get-tuple-element.73), calls=%async_computation | async-start | bytes 1572864 | tf_op jit(solution)/shard_map/all_to_all | solution.py:664
  84.5 224.8 %reduce-scatter.2.cloned.1.call-start = ((), (), s32[]{:S(2)}) async-start(), calls=%async_computation.6 | async-start | bytes 5640192 | tf_op jit(solution)/shard_map/reduce_scatter | solution.py:766
  119.4 1.4 collective-permute-start.1
  120.8 8.6 %copy-start.21 = (bf16[192,128]{1,0:T(8,128)(2,1)}, bf16[192,128]{1,0:T(8,128)(2,1)S(1)}, u32[]{:S(2)}) copy-start(bf16[192,128]{1,0:T(8,128)(2,1)S(1)} %collective-permute-done.1.other_ref) | copy-start | bytes 147460
  131.6 7.3 %collective-permute-start.2 = (bf16[128,768]{1,0:T(8,128)(2,1)}, bf16[128,768]{1,0:T(8,128)(2,1)S(1)}, u32[]{:S(2)}, u32[]{:S(2)}) collective-permute-start(bf16[128,768]{1,0:T(8,128)(2,1)} %get-tuple-element.77.own_ref), channel_id=1, source_target_pairs={{0,1},{1,0},{2,3},{3,2},{4,5},{5,4},{6,7},{7,6},{8,9},{9,8},{10,11... | collective-permute-start | bytes 589832 | tf_op jit(solution)/shard_map/ppermute | solution.py:718
  144.3 6.5 %collective-permute-start.3 = (bf16[128,768]{1,0:T(8,128)(2,1)}, bf16[128,768]{1,0:T(8,128)(2,1)S(1)}, u32[]{:S(2)}, u32[]{:S(2)}) collective-permute-start(bf16[128,768]{1,0:T(8,128)(2,1)} %get-tuple-element.80.own_ref), channel_id=1, source_target_pairs={{0,1},{1,0},{2,3},{3,2},{4,5},{5,4},{6,7},{7,6},{8,9},{9,8},{10,11... | collective-permute-start | bytes 589832 | tf_op jit(solution)/shard_map/ppermute | solution.py:731
  156.7 5.9 %collective-permute-start.4 = (bf16[128,768]{1,0:T(8,128)(2,1)}, bf16[128,768]{1,0:T(8,128)(2,1)S(1)}, u32[]{:S(2)}, u32[]{:S(2)}) collective-permute-start(bf16[128,768]{1,0:T(8,128)(2,1)} %get-tuple-element.83.own_ref), channel_id=1, source_target_pairs={{0,1},{1,0},{2,3},{3,2},{4,5},{5,4},{6,7},{7,6},{8,9},{9,8},{10,11... | collective-permute-start | bytes 589832 | tf_op jit(solution)/shard_map/ppermute | solution.py:744
  172.4 2.2 collective-permute-start.5
  173.6 7.7 %copy-start.8 = (bf16[3,56,64]{2,1,0:T(8,128)(2,1)S(1)}, bf16[3,56,64]{2,1,0:T(8,128)(2,1)}, u32[]{:S(2)}) copy-start(bf16[3,56,64]{2,1,0:T(8,128)(2,1)} %fusion.12.bit_ref) | copy-start | bytes 64516
  177.5 26.6 %all-to-all-start.1 = ((bf16[8,208,256]{2,1,0:T(8,128)(2,1)}), bf16[8,208,256]{2,1,0:T(8,128)(2,1)S(1)}, u32[]{:S(2)}, u32[]{:S(2)}) async-start(bf16[8,208,256]{2,1,0:T(8,128)(2,1)} %get-tuple-element.96), calls=%async_computation.1 | async-start | bytes 1703936 | tf_op jit(solution)/shard_map/all_to_all | solution.py:758
  237.4 8.8 %collective-permute-start.6 = (bf16[8,768,128]{2,1,0:T(8,128)(2,1)}, bf16[8,768,128]{2,1,0:T(8,128)(2,1)S(1)}, u32[]{:S(2)}, u32[]{:S(2)}) collective-permute-start(bf16[8,768,128]{2,1,0:T(8,128)(2,1)} %get-tuple-element.102), channel_id=1, source_target_pairs={{0,2},{2,0},{4,6},{6,4},{8,10},{10,8},{12,14},{14,12},{16,18},{18,... | collective-permute-start | bytes 4718600 | tf_op jit(solution)/shard_map/ppermute | solution.py:829
  237.5 33.4 %all-to-all-start.3 = ((bf16[8,96,640]{2,1,0:T(8,128)(2,1)}), bf16[8,96,640]{2,1,0:T(8,128)(2,1)}, u32[]{:S(2)}, u32[]{:S(2)}) async-start(bf16[8,96,640]{2,1,0:T(8,128)(2,1)} %get-tuple-element.103), calls=%async_computation.3 | async-start | bytes 1966080 | tf_op jit(solution)/shard_map/all_to_all | solution.py:836
  250.6 26.4 %collective-permute-start.7 = (bf16[8,384,128]{2,1,0:T(8,128)(2,1)}, bf16[8,384,128]{2,1,0:T(8,128)(2,1)}, u32[]{:S(2)}, u32[]{:S(2)}) collective-permute-start(bf16[8,384,128]{2,1,0:T(8,128)(2,1)} %dynamic-slice_bitcast_fusion), channel_id=1, source_target_pairs={{0,1},{1,0},{2,3},{3,2},{4,5},{5,4},{6,7},{7,6},{8,9},{9,8},{10,11... | collective-permute-start | bytes 2359304 | tf_op jit(solution)/shard_map/ppermute | solution.py:834
  273.2 1.2 collective-permute-start.9
  273.8 14.3 %collective-permute-start.10 = (f32[48,576]{1,0:T(8,128)}, f32[48,576]{1,0:T(8,128)}, u32[]{:S(2)}, u32[]{:S(2)}) collective-permute-start(f32[48,576]{1,0:T(8,128)} %bitcast.81), channel_id=1, source_target_pairs={{0,2},{2,0},{4,6},{6,4},{8,10},{10,8},{12,14},{14,12},{16,18},{18,... | collective-permute-start | bytes 331784 | tf_op jit(solution)/shard_map/ppermute | solution.py:841
  277.0 8.5 %copy-start.11 = (f32[4,768]{1,0:T(4,128)S(1)}, f32[4,768]{1,0:T(4,128)}, u32[]{:S(2)}) copy-start(f32[4,768]{1,0:T(4,128)} %norm_ref.7) | copy-start | bytes 36868
  279.2 4.7 %copy-start.22 = (f32[3072]{0:T(1024)S(1)}, f32[3072]{0:T(1024)}, u32[]{:S(2)}) copy-start(f32[3072]{0:T(1024)} %get-tuple-element.222) | copy-start | bytes 36868
  279.2 24.4 %all-to-all-start.2 = ((bf16[8,384,128]{2,1,0:T(8,128)(2,1)}), bf16[8,384,128]{2,1,0:T(8,128)(2,1)S(1)}, u32[]{:S(2)}, u32[]{:S(2)}) async-start(bf16[8,384,128]{2,1,0:T(8,128)(2,1)} %fusion), calls=%async_computation.2 | async-start | bytes 1572864 | tf_op jit(solution)/shard_map/all_to_all | solution.py:837
  287.3 17.8 %copy-start.7 = (f32[3,48,384]{2,1,0:T(8,128)S(1)}, f32[3,48,384]{2,1,0:T(8,128)}, u32[]{:S(2)}) copy-start(f32[3,48,384]{2,1,0:T(8,128)} %param.28) | copy-start | bytes 663556
  289.4 19.2 %copy-start.10 = (f32[128,768]{1,0:T(8,128)S(1)}, f32[128,768]{1,0:T(8,128)}, u32[]{:S(2)}) copy-start(f32[128,768]{1,0:T(8,128)} %get-tuple-element.86) | copy-start | bytes 1179652
  303.8 4.7 %collective-permute-start.8 = (bf16[384,128]{0,1:T(8,128)(2,1)S(1)}, bf16[384,128]{0,1:T(8,128)(2,1)S(1)}, u32[]{:S(2)}, u32[]{:S(2)}) collective-permute-start(bf16[384,128]{0,1:T(8,128)(2,1)S(1)} %copy.116), channel_id=1, source_target_pairs={{0,1},{1,0},{2,3},{3,2},{4,5},{5,4},{6,7},{7,6},{8,9},{9,8},{10,11... | collective-permute-start | bytes 294920 | tf_op jit(solution)/shard_map/ppermute | solution.py:871
  307.2 4.9 %copy-start.4 = (f32[1536,48]{0,1:T(8,128)S(1)}, f32[1536,48]{0,1:T(8,128)}, u32[]{:S(2)}) copy-start(f32[1536,48]{0,1:T(8,128)} %param.37) | copy-start | bytes 884740
  307.2 4.9 %copy-start.12 = (f32[1536,48]{0,1:T(8,128)S(1)}, f32[1536,48]{0,1:T(8,128)}, u32[]{:S(2)}) copy-start(f32[1536,48]{0,1:T(8,128)} %param.38) | copy-start | bytes 884740
  307.2 4.9 %copy-start.13 = (f32[1536,48]{0,1:T(8,128)S(1)}, f32[1536,48]{0,1:T(8,128)}, u32[]{:S(2)}) copy-start(f32[1536,48]{0,1:T(8,128)} %param.39) | copy-start | bytes 884740
  (14 other events, 19.4 us)
Sparse Core Ops, SparseCore 0:
  10.3 53.3 all-gather.5
  66.5 62.8 all-gather.3
  171.7 79.4 reduce-scatter.1

commit v4 on v3

--- a/solution.py
+++ b/solution.py
@@ -3,6 +3,7 @@
 
 import jax
 import jax.numpy as jnp
+import numpy as np
 from jax import lax
 from jax.experimental import pallas as pl
 from jax.experimental.pallas import tpu as pltpu
@@ -25,7 +26,10 @@
 f32 = jnp.float32
 bf16 = jnp.bfloat16
 VMEM_LIMIT = 56 * 1024 * 1024
+SMALL_LIMIT = 16 * 1024 * 1024
 WORK = 2
+SPOTS = 4
+RING = (0, 2, 4, 6, 7, 5, 3, 1)
 
 
 def nn(a, b):
@@ -118,12 +122,24 @@
             codes_ref[head, spot : spot + 2 * rows, :] = pair.astype(bf16)
 
 
+def token_copies(spots_ref, part_refs, tok_ref, sem_ref):
+    return [
+        pltpu.make_async_copy(
+            ref.at[:, pl.ds(0, tok_ref.shape[1])],
+            tok_ref.at[pl.ds(spots_ref[SPOTS + i], ref.shape[0])],
+            sem_ref.at[i],
+        )
+        for i, ref in enumerate(part_refs)
+    ]
+
+
 def forward_kernel(
-    hashes, bits, rows, tile, steps, heads,
-    spots_ref, got_ref, w_ref, bit_ref,
-    num_ref, qu_ref, ku_ref, v_ref, inv_ref, table_ref, count_ref,
-    acc_ref, codes_ref, wt_ref, table_t_ref,
+    hashes, bits, rows, tile, steps, heads, parts, weight_parts, weight_row, spots_ref, *refs
 ):
+    part_refs, refs = refs[:parts], refs[parts:]
+    weight_refs, refs = refs[:weight_parts], refs[weight_parts:]
+    bit_ref, num_ref, qu_ref, ku_ref, v_ref, inv_ref, table_ref, count_ref, w_ref = refs[:9]
+    acc_ref, codes_ref, wt_ref, table_t_ref, tok_ref, got_ref, sem_ref = refs[9:]
     limit = spots_ref[0]
     phase, i = pl.program_id(0), pl.program_id(1)
     feats = heads * 64
@@ -135,15 +151,35 @@
 
     @pl.when((phase == 0) & (i == 0))
     def _():
-        wt_ref[...] = flip(w_ref[...])
+        copies = token_copies(spots_ref, part_refs, tok_ref, sem_ref)
+        loads = [
+            pltpu.make_async_copy(
+                ref.at[:, pl.ds(weight_row, got_ref.shape[1])],
+                got_ref.at[pl.ds(spots_ref[SPOTS + parts + i], ref.shape[0])],
+                sem_ref.at[parts + i],
+            )
+            for i, ref in enumerate(weight_refs)
+        ]
+        for copy in loads + copies:
+            copy.start()
         acc_ref[...] = jnp.zeros_like(acc_ref)
         v_ref[:, 0:128] = jnp.zeros((feats, 128), bf16)
         v_ref[:, 128 + steps * tile :] = jnp.zeros((feats, 128), bf16)
         inv_ref[...] = jnp.zeros_like(inv_ref)
+        for copy in loads:
+            copy.wait()
+        got = got_ref[...]
+        got = got.reshape(got.shape[0] * got.shape[1], got.shape[2])[:, : 3 * feats]
+        w_ref[...] = got
+        wt_ref[...] = flip(got)
+        for copy in copies:
+            copy.wait()
 
     @pl.when(phase == 0)
     def _():
-        proj = nt(wt_ref[...], got_ref[...].reshape(tile, got_ref.shape[2]))
+        devices, tok_rows, width = tok_ref.shape
+        here = pl.ds(i * (devices // steps), devices // steps)
+        proj = nt(wt_ref[...], tok_ref[here].reshape(tile, width))
         values = proj[2 * feats :].astype(bf16)
         v_ref[:, pl.ds(pl.multiple_of(start + 128, 128), tile)] = values
         marks = jnp.concatenate([early, late, jnp.zeros((14, tile), f32)], axis=0).astype(bf16)
@@ -219,18 +255,17 @@
     return inverse * (grad - unit * inner)
 
 
-def backward_kernel(
-    hashes, bits, rows, tile, steps, heads, own_rows,
-    spots_ref, got_ref, w_ref, bit_ref, bit_t_ref,
-    qu_ref, ku_ref, v_ref, inv_ref, table_ref, gnum_ref, conv_ref, tap_ref,
-    grad_ref, keep_ref, give_ref,
-    acc_ref, codes_ref, proj_ref, sum_ref, table_t_ref, table_g_ref,
-):
+def backward_kernel(hashes, bits, rows, tile, steps, heads, own_rows, parts, spots_ref, *refs):
+    part_refs, refs = refs[:parts], refs[parts:]
+    w_ref, bit_ref, bit_t_ref, qu_ref, ku_ref, v_ref, inv_ref, table_ref = refs[:8]
+    gnum_ref, conv_ref, tap_ref, grad_ref, keep_ref, give_ref = refs[8:14]
+    acc_ref, codes_ref, proj_ref, sum_ref, table_t_ref, table_g_ref, tok_ref, sem_ref = refs[14:]
     limit = spots_ref[0]
     spot = spots_ref[1]
     core = spots_ref[2]
     phase, i = pl.program_id(0), pl.program_id(1)
-    width = got_ref.shape[2]
+    devices, unused, width = tok_ref.shape
+    copies = token_copies(spots_ref, part_refs, tok_ref, sem_ref)
     feats = heads * 64
     blocks = keep_ref.shape[0]
     block = tile // blocks
@@ -241,6 +276,8 @@
 
     @pl.when((phase == 0) & (i == 0))
     def _():
+        for copy in copies:
+            copy.start()
         acc_ref[...] = jnp.zeros_like(acc_ref)
         sum_ref[...] = jnp.zeros_like(sum_ref)
 
@@ -267,6 +304,8 @@
 
     @pl.when((phase == 1) & (i == 0))
     def _():
+        for copy in copies:
+            copy.wait()
         for h in range(heads):
             table_g_ref[h] = acc_ref[h].astype(bf16)
             table_t_ref[h] = flip(table_g_ref[h])
@@ -300,7 +339,8 @@
         full = jnp.concatenate(
             [proj_ref[:, span]] + [part[0] for part in parts] + [part[1] for part in parts], axis=0
         )
-        sum_ref[...] += nn(full, got_ref[...].reshape(tile, width))
+        here = pl.ds(i * (devices // steps), devices // steps)
+        sum_ref[...] += nn(full, tok_ref[here].reshape(tile, width))
         part = nn(w_ref[...], full)
         for c in range(blocks):
             first = part[:, c * block : c * block + tok_rows]
@@ -386,35 +426,36 @@
         give_ref[...] = first
 
 
-def mixer_kernel(spots_ref, keep_ref, other_ref, out_ref, context_ref, part_ref):
+def mixer_kernel(spots_ref, keep_ref, other_ref, w_ref, context_ref, part_ref):
     keep, other = keep_ref[...].astype(f32), other_ref[...].astype(f32)
     zero = spots_ref[2] == 0
     pair = jnp.concatenate([jnp.where(zero, keep, other), jnp.where(zero, other, keep)], axis=0)
     context = jnp.transpose(pair).astype(bf16)
     context_ref[...] = context
-    part_ref[...] = nt(context, out_ref[...]).astype(bf16)
+    part_ref[...] = nt(context, w_ref[:, w_ref.shape[1] - context.shape[1] :]).astype(bf16)
 
 
 def hidden_kernel(
-    tok_ref, own_ref, other_ref, norm_ref, up_ref, down_ref,
-    hat_ref, inv_ref, hidden_ref, active_ref, part_ref,
+    tok_ref, own_ref, other_ref, norm_ref, w_ref, hat_ref, inv_ref, hidden_ref, active_ref, part_ref
 ):
+    ff = hidden_ref.shape[1]
     mixed = own_ref[...].astype(f32) + other_ref[...].astype(f32)
     hat, inverse = normalize(tok_ref[...].astype(f32) + mixed)
     hat_ref[...] = hat
     inv_ref[...] = inverse
     low = (hat * norm_ref[0:1] + norm_ref[1:2]).astype(bf16)
-    hidden = nn(low, up_ref[...])
+    hidden = nn(low, w_ref[:, :ff])
     hidden_ref[...] = hidden
     active = (0.5 * hidden * (1.0 + lax.erf(hidden * math.sqrt(0.5)))).astype(bf16)
     active_ref[...] = active
-    part_ref[...] = nt(active, down_ref[...]).astype(bf16)
+    part_ref[...] = nt(active, w_ref[:, ff : 2 * ff]).astype(bf16)
 
 
 def feed_kernel(
-    hat_ref, hidden_ref, own_ref, other_ref, cot_ref, norm_ref, up_ref, down_ref,
+    hat_ref, hidden_ref, own_ref, other_ref, cot_ref, norm_ref, w_ref,
     out_ref, second_ref, feed_ref, slope_ref, part_ref, sums_ref,
 ):
+    ff = hidden_ref.shape[1]
     first_out = hat_ref[...] * norm_ref[0:1] + norm_ref[1:2]
     fed = own_ref[...].astype(f32) + other_ref[...].astype(f32)
     hat, inverse = normalize(first_out + fed)
@@ -425,17 +466,17 @@
     sums_ref[1:2] = offsets
     low = grad.astype(bf16)
     feed_ref[...] = low
-    active_grad = nn(low, down_ref[...])
+    active_grad = nn(low, w_ref[:, ff : 2 * ff])
     hidden = hidden_ref[...]
     cdf = 0.5 * (1.0 + lax.erf(hidden * math.sqrt(0.5)))
     density = jnp.exp(-0.5 * hidden * hidden) * (1.0 / math.sqrt(2.0 * math.pi))
     slope = (active_grad * (cdf + hidden * density)).astype(bf16)
     slope_ref[...] = slope
-    part_ref[...] = nt(slope, up_ref[...]).astype(bf16)
+    part_ref[...] = nt(slope, w_ref[:, :ff]).astype(bf16)
 
 
 def mixer_back_kernel(
-    spots_ref, second_ref, own_ref, other_ref, hat_ref, inv_ref, norm_ref, out_ref, sums_ref,
+    spots_ref, second_ref, own_ref, other_ref, hat_ref, inv_ref, norm_ref, w_ref, sums_ref,
     grad_ref, low_ref, keep_ref, give_ref, all_sums_ref,
 ):
     first = second_ref[...] + (own_ref[...].astype(f32) + other_ref[...].astype(f32))
@@ -446,7 +487,8 @@
     all_sums_ref[2:4] = sums_ref[...]
     low = grad.astype(bf16)
     low_ref[...] = low
-    context = jnp.transpose(nn(low, out_ref[...]))
+    half = keep_ref.shape[0]
+    context = jnp.transpose(nn(low, w_ref[:, w_ref.shape[1] - CORES * half :]))
     half = context.shape[0] // CORES
     zero = spots_ref[2] == 0
     keep_ref[...] = jnp.where(zero, context[:half], context[half:])
@@ -474,24 +516,96 @@
     tile = gnum.shape[1]
     feats = 64 * heads
     pieces = sums_ref.shape[1] // tile
+    chips = send_ref.shape[0]
+    piece = count_ref.shape[2] // chips
+    blank = jnp.zeros((1, tile // 2 - piece), f32)
+    spare = jnp.zeros((send_ref.shape[1] - feats - 4 * pieces - heads, tile), f32)
     sums = sums_ref[...].astype(bf16).astype(f32)
     sums = jnp.concatenate(
         [sums[:, tile * i : tile * (i + 1)] for i in range(pieces)], axis=0
     )
-    for c in range(send_ref.shape[0]):
+    for c in range(chips):
         send_ref[c, 0:feats, :] = gnum
-        extra = jnp.concatenate([sums, count_ref[c]], axis=0)
+        counts = []
+        for h in range(heads):
+            row = [count_ref[h, d : d + 1, c * piece : (c + 1) * piece] for d in range(2)]
+            counts.append(
+                jnp.concatenate([row[0], blank, row[1], blank], axis=1)
+                if blank.shape[1]
+                else jnp.concatenate(row, axis=1)
+            )
+        extra = jnp.concatenate([sums] + counts + [spare], axis=0)
         send_ref[c, feats:, :] = extra.astype(bf16)
 
 
-def big_grad_kernel(
-    mixer_ref, context_ref, hat_ref, norm_ref, slope_ref, feed_ref, active_ref, out_ref
-):
+def feed_grad_kernel(hat_ref, norm_ref, slope_ref, feed_ref, active_ref, out_ref):
+    ff = slope_ref.shape[1]
     low = hat_ref[...] * norm_ref[0:1] + norm_ref[1:2]
-    ff = slope_ref.shape[1]
     out_ref[:, :ff] = nn(flip(low.astype(bf16)), slope_ref[...]).astype(bf16)
     out_ref[:, ff : 2 * ff] = nn(flip(feed_ref[...]), active_ref[...]).astype(bf16)
-    out_ref[:, 2 * ff :] = nn(flip(mixer_ref[...]), context_ref[...]).astype(bf16)
+
+
+def out_grad_kernel(mixer_ref, context_ref, all_ref, out_ref):
+    out_ref[...] = nn(flip(mixer_ref[...]), context_ref[...]).astype(bf16)
+
+
+def pack_kernel(spots_ref, up_ref, down_ref, out_ref, after_ref, bit_ref, all_ref):
+    ff = up_ref.shape[1]
+    all_ref[:, :ff] = up_ref[...].astype(bf16)
+    all_ref[:, ff : 2 * ff] = down_ref[...].astype(bf16)
+    all_ref[:, 2 * ff :] = out_ref[...].astype(bf16)
+
+
+def chip_sum_kernel(spots_ref, own_ref, other_ref, keep_ref, give_ref):
+    total = own_ref[...].astype(f32) + other_ref[...].astype(f32)
+    half = total.shape[1] // 2
+    first, second = total[:, :half], total[:, half:]
+    zero = spots_ref[3] == 0
+    keep_ref[...] = jnp.where(zero, first, second).astype(bf16)
+    give_ref[...] = jnp.where(zero, second, first).astype(bf16)
+
+
+def pair_sum_kernel(own_ref, other_ref, out_ref):
+    out_ref[...] = (own_ref[...].astype(f32) + other_ref[...].astype(f32)).astype(bf16)
+
+
+def weight_sum_kernel(spots_ref, got_ref, after_ref, keep_ref, give_ref):
+    total = jnp.sum(got_ref[...].astype(f32), axis=0)
+    half = total.shape[0] // CORES
+    zero = spots_ref[2] == 0
+    keep_ref[...] = jnp.where(zero, total[:half], total[half:])
+    give_ref[...] = jnp.where(zero, total[half:], total[:half])
+
+
+def adam_refs(grad, ins, outs, rate):
+    new, first, second = adam_step(ins[0], ins[1], ins[2], grad, rate)
+    outs[0][...] = new
+    outs[1][...] = first
+    outs[2][...] = second
+    outs[3][...] = new.astype(bf16)
+
+
+def big_adam_kernel(grad_ref, *refs):
+    ins, outs = refs[:9], refs[9:]
+    ff = ins[0].shape[1]
+    spans = (slice(0, ff), slice(ff, 2 * ff), slice(2 * ff, grad_ref.shape[1]))
+    for k, (span, rate) in enumerate(zip(spans, (D ** (-0.5), FF ** (-0.5), D ** (-0.5)))):
+        state = [ref[...] for ref in ins[3 * k : 3 * k + 3]]
+        adam_refs(grad_ref[:, span].astype(f32), state, outs[4 * k : 4 * k + 4], rate)
+
+
+def qkv_adam_kernel(spots_ref, mine_ref, other_ref, *refs):
+    zero = spots_ref[2] == 0
+    feats = refs[0].shape[2] // CORES
+    for p in range(3):
+        span = slice(p * feats, (p + 1) * feats)
+        mine, other = mine_ref[:, span], other_ref[:, span]
+        grad = jnp.concatenate([jnp.where(zero, mine, other), jnp.where(zero, other, mine)], axis=1)
+        adam_refs(grad, [ref[p] for ref in refs[:3]], [ref.at[p] for ref in refs[3:]], D ** (-0.5))
+
+
+def back_sum_kernel(got_ref, *refs):
+    refs[-1][...] = jnp.sum(got_ref[...].astype(f32), axis=0).astype(bf16)
 
 
 def on_device(
@@ -550,9 +664,65 @@
         lax.ppermute, axis_name="seq", perm=[(i, i ^ 1) for i in range(seq_count)]
     )
     head_swap = partial(lax.ppermute, axis_name="head", perm=[(0, 1), (1, 0)])
-    spots = jnp.stack([doc_lengths[0], spot.astype(jnp.int32), core.astype(jnp.int32)])
+    def in_order(mine, other, axis):
+        first = jnp.where(core == 0, mine, other)
+        return jnp.concatenate([first, jnp.where(core == 0, other, mine)], axis=axis)
+
+    low_qkv = qkv_weight.astype(bf16).reshape(3, own_rows, CORES, feats)
+    pick = partial(lax.dynamic_index_in_dim, low_qkv, axis=2, keepdims=False)
+    by_rows = lambda part: jnp.transpose(part, (1, 0, 2)).reshape(own_rows, 3 * feats)
+    qkv_mine, qkv_give = by_rows(pick(core)), by_rows(pick(1 - core))
+    chip_rows = in_order(qkv_mine, core_swap(qkv_give), 0)
+    chip_rows = jnp.pad(chip_rows, ((0, 0), (0, width - 3 * feats)))
+
+    if chips == len(RING):
+        order = np.array(RING)
+        seats = np.argsort(order)
+        ahead = [
+            (CORES * order[i] + k, CORES * order[(i + 1) % chips] + k)
+            for i in range(chips)
+            for k in range(CORES)
+        ]
+        behind = [(b, a) for a, b in ahead]
+        block = jnp.concatenate([tokens, chip_rows], axis=0)
+        block_parts, turns, moved = [block], [0], [block, block]
+        for step in range(1, chips // 2 + 1):
+            moved[0] = lax.ppermute(moved[0], "seq", ahead)
+            block_parts.append(moved[0])
+            turns.append(chips - step)
+            if 2 * step < chips:
+                moved[1] = lax.ppermute(moved[1], "seq", behind)
+                moved = list(lax.optimization_barrier(tuple(moved)))
+                block_parts[-1] = moved[0]
+                block_parts.append(moved[1])
+                turns.append(step)
+                last_part = moved[1]
+        token_parts = [p[None] for p in block_parts + [core_swap(part) for part in block_parts]]
+        weight_parts, weight_row = token_parts[:chips], tok_rows
+        spot_of = np.array([[order[(seats[c] + t) % chips] for t in turns] for c in range(chips)])
+        spot_of = np.repeat(spot_of, CORES, axis=0)
+        core_of = np.arange(seq_count)[:, None] % CORES
+        place_of = [CORES * spot_of + core_of, CORES * spot_of + 1 - core_of, spot_of]
+    else:
+        token_parts = [lax.all_gather(tokens, "seq", axis=0, tiled=False)]
+        weight_parts = [
+            lax.all_gather(chip_rows, "seq", axis=0, tiled=False, axis_index_groups=planes_of)
+        ]
+        weight_row = 0
+        place_of = [np.zeros((seq_count, 2))]
+        last_part = token_parts[0]
+    parts = len(token_parts)
+    weight_count = len(weight_parts)
+    device = np.arange(seq_count)[:, None]
+    facts = np.concatenate([device // CORES, device % CORES, 0 * device] + place_of, axis=1)
+    facts = np.stack([facts + k * (np.arange(facts.shape[1]) == 2) for k in range(2)])
+    facts = lax.dynamic_slice(
+        jnp.asarray(facts.astype(np.int32)), (side, place, 0), (1, 1, facts.shape[2])
+    )
+    spots = jnp.concatenate([doc_lengths[0:1], facts.reshape(-1)])
 
     smem = pl.BlockSpec(memory_space=pltpu.SMEM)
+    anywhere = pl.BlockSpec(memory_space=pl.ANY)
     params = pltpu.CompilerParams(
         dimension_semantics=("arbitrary",), vmem_limit_bytes=VMEM_LIMIT
     )
@@ -561,10 +731,7 @@
     def full(value):
         return pl.BlockSpec(value.shape, lambda i: (0,) * value.ndim)
 
-    def columns(block, which):
-        return pl.BlockSpec((width, block), lambda i: (0, which))
-
-    def once(kernel, name, outs, args, specs=None):
+    def piped(kernel, name, outs, args, specs=None):
         if specs is None:
             specs = [None] * len(args)
         specs = [
@@ -581,25 +748,28 @@
             name=name,
         )(*args)
 
-    def in_order(mine, other, axis):
-        first = jnp.where(core == 0, mine, other)
-        return jnp.concatenate([first, jnp.where(core == 0, other, mine)], axis=axis)
-
-    got = lax.all_gather(tokens, "seq", axis=0, tiled=False)
-
-    low_qkv = qkv_weight.astype(bf16).reshape(3, own_rows, CORES, feats)
-    pick = partial(lax.dynamic_index_in_dim, low_qkv, axis=2, keepdims=False)
-    by_rows = lambda part: jnp.transpose(part, (1, 0, 2)).reshape(own_rows, 3 * feats)
-    qkv_mine, qkv_give = by_rows(pick(core)), by_rows(pick(1 - core))
-    chip_rows = in_order(qkv_mine, core_swap(qkv_give), 0)
-    qkv_all = lax.all_gather(
-        chip_rows, "seq", axis=0, tiled=True, axis_index_groups=planes_of
-    )
-    second_send = jnp.concatenate(
-        [up_weight.astype(bf16), down_weight.T.astype(bf16), out_weight.T.astype(bf16)], axis=1
-    )
-    second_send, unused = lax.optimization_barrier((second_send, got[0, 0, 0:1]))
-    ff_all = lax.all_gather(second_send, "seq", axis=0, tiled=True)
+    inside = pl.BlockSpec(memory_space=pltpu.VMEM)
+
+    def once(kernel, name, outs, args, after=(), outside=(), aliases=None, limit=SMALL_LIMIT):
+        specs, values = [], []
+        for arg in args:
+            specs.append(smem if arg is spots else inside)
+            values.append(
+                arg if arg is spots else pltpu.with_memory_space_constraint(arg, pltpu.VMEM)
+            )
+        for arg in after:
+            specs.append(anywhere)
+            values.append(arg)
+        return pl.pallas_call(
+            kernel,
+            in_specs=specs,
+            out_specs=[inside] * len(outs),
+            out_shape=[
+                o if i in outside else pltpu.VMEM(o.shape, o.dtype) for i, o in enumerate(outs)
+            ],
+            compiler_params=pltpu.CompilerParams(vmem_limit_bytes=limit),
+            name=name,
+        )(*values)
 
     own_planes = lax.dynamic_slice(
         plane_bits, (spot * hashes, 0, core * heads, 0), (hashes, bits, heads, head_dim)
@@ -612,6 +782,14 @@
     bit_w = bit_w.reshape(heads, bits * rows, head_dim).astype(bf16)
     bit_wt = jnp.transpose(bit_w, (0, 2, 1))
 
+    (second_send,) = piped(
+        pack_kernel, "pack",
+        [shape((own_rows, 2 * ff + group_feats), bf16)],
+        [spots, up_weight, down_weight.T, out_weight.T, last_part, bit_w],
+        [None] * 4 + [anywhere] * 2,
+    )
+    ff_all = lax.all_gather(second_send, "seq", axis=0, tiled=True)
+
     def resident(*dims):
         return pl.BlockSpec(dims, lambda p, i: (0,) * len(dims), pipeline_mode=pl.Buffered(1))
 
@@ -625,13 +803,12 @@
     hash_params = pltpu.CompilerParams(
         dimension_semantics=("arbitrary", "arbitrary"), vmem_limit_bytes=VMEM_LIMIT
     )
-    num_parts, q_unit, k_unit, values, inverses, tables, counts = pl.pallas_call(
-        partial(forward_kernel, hashes, bits, rows, work, steps, heads),
+    num_parts, q_unit, k_unit, values, inverses, tables, counts, qkv_all = pl.pallas_call(
+        partial(forward_kernel, hashes, bits, rows, work, steps, heads, parts, weight_count, weight_row),
         grid=(2, steps),
         in_specs=[
             smem,
-            stepped(0, CORES * blocks, tok_rows, width),
-            resident(*qkv_all.shape),
+            *[anywhere] * (parts + weight_count),
             resident(*bit_w.shape),
         ],
         out_specs=[
@@ -642,6 +819,7 @@
             resident(16, total),
             resident(heads, code_rows, 2 * head_dim),
             resident(heads, 8, code_rows),
+            resident(width, 3 * feats),
         ],
         out_shape=[
             shape((chips, feats, tile), bf16),
@@ -651,16 +829,20 @@
             shape((16, total), f32),
             shape((heads, code_rows, 2 * head_dim), bf16),
             shape((heads, 8, code_rows), f32),
+            shape((width, 3 * feats), bf16),
         ],
         scratch_shapes=[
             pltpu.VMEM((heads, code_rows, 2 * head_dim + 16), f32),
             pltpu.VMEM((heads, code_rows, work), bf16),
             pltpu.VMEM((3 * feats, width), bf16),
             pltpu.VMEM((heads, 2 * head_dim, code_rows), bf16),
+            pltpu.VMEM((seq_count, tok_rows, width), bf16),
+            pltpu.VMEM((chips, CORES * own_rows, width), bf16),
+            pltpu.SemaphoreType.DMA((parts + weight_count,)),
         ],
         compiler_params=hash_params,
         name="hash_forward",
-    )(spots, got, qkv_all, bit_w)
+    )(spots, *token_parts, *weight_parts, bit_w)
     num_got = across(num_parts)
 
     own_taps = lax.dynamic_slice(conv_taps, (core * heads, 0), (heads, taps))
@@ -686,14 +868,8 @@
     )(spots, values, values, bases)
 
     chip_buckets = buckets // chips
-    count_rows = -(-2 * hashes * heads * chip_buckets // tile)
     sum_rows = 4 * width // tile
-    extra_rows = -(-(sum_rows + count_rows) // 16) * 16
-    count_send = counts[:, 0:2].reshape(heads, 2, chips, chip_buckets, rows)[..., :hashes]
-    count_send = jnp.transpose(count_send, (2, 1, 4, 0, 3)).reshape(chips, -1)
-    count_send = jnp.pad(
-        count_send, ((0, 0), (0, (extra_rows - sum_rows) * tile - count_send.shape[1]))
-    ).reshape(chips, extra_rows - sum_rows, tile)
+    extra_rows = -(-(sum_rows + heads) // 16) * 16
 
     keep, give, numerator = once(
         partial(context_kernel, heads), "context",
@@ -704,7 +880,6 @@
         mixer_kernel, "mixer",
         [shape((tok_rows, group_feats), bf16), shape((tok_rows, width), bf16)],
         [spots, keep, core_swap(give), ff_all],
-        [None, None, None, columns(group_feats, 2 * ff // group_feats)],
     )
     first_hat, first_inverse, hidden, active, feed_part = once(
         hidden_kernel, "feed_forward",
@@ -715,8 +890,7 @@
             shape((tok_rows, ff), bf16),
             shape((tok_rows, width), bf16),
         ],
-        [tokens, mixer_part, head_swap(mixer_part), norm_params, ff_all, ff_all],
-        [None, None, None, None, columns(ff, 0), columns(ff, 1)],
+        [tokens, mixer_part, head_swap(mixer_part), norm_params, ff_all],
     )
     block_out, grad_second, feed_low, slope_low, first_part, second_sums = once(
         feed_kernel, "feed_back",
@@ -728,8 +902,8 @@
             shape((tok_rows, width), bf16),
             shape((2, width), f32),
         ],
-        [first_hat, hidden, feed_part, head_swap(feed_part), cotangent, norm_params, ff_all, ff_all],
-        [None, None, None, None, None, None, columns(ff, 0), columns(ff, 1)],
+        [first_hat, hidden, feed_part, head_swap(feed_part), cotangent, norm_params, ff_all],
+        outside=(0,),
     )
     grad_mixer, mixer_low, keep, give, norm_sums = once(
         mixer_back_kernel, "mixer_back",
@@ -744,7 +918,7 @@
             spots, grad_second, first_part, head_swap(first_part), first_hat, first_inverse,
             norm_params, ff_all, second_sums,
         ],
-        [None, None, None, None, None, None, None, columns(group_feats, 2 * ff // group_feats), None],
+        outside=(0,),
     )
     gnum_send, grad_low, grad_high = once(
         partial(attention_back_kernel, heads), "attention_back",
@@ -753,17 +927,32 @@
             shape((feats, tok_rows), bf16),
             shape((feats, tok_rows), bf16),
         ],
-        [spots, keep, core_swap(give), numerator, norm_sums, count_send],
+        [spots, keep, core_swap(give), numerator, norm_sums, counts],
+        outside=(0, 1, 2),
     )
     gnum_got = across(gnum_send)
 
-    mixer_low, unused = lax.optimization_barrier((mixer_low, grad_low[0:1, 0:1]))
-    (big_grad,) = once(
-        big_grad_kernel, "weight_grads",
-        [shape((width, group_feats + 2 * ff), bf16)],
-        [mixer_low, context, first_hat, norm_params, slope_low, feed_low, active],
-    )
-    big_owned = lax.psum_scatter(big_grad, "seq", scatter_dimension=0, tiled=True).astype(f32)
+    columns = 2 * ff + group_feats
+    feed_grads = pl.pallas_call(
+        feed_grad_kernel,
+        grid=(1,),
+        in_specs=[full(v) for v in (first_hat, norm_params, slope_low, feed_low, active)],
+        out_specs=pl.BlockSpec((width, 2 * ff), lambda i: (0, 0)),
+        out_shape=shape((width, columns), bf16),
+        compiler_params=params,
+        name="feed_grads",
+    )(first_hat, norm_params, slope_low, feed_low, active)
+    big_grad = pl.pallas_call(
+        out_grad_kernel,
+        grid=(1,),
+        in_specs=[full(mixer_low), full(context), anywhere],
+        out_specs=pl.BlockSpec((width, group_feats), lambda i: (0, 2 * ff // group_feats)),
+        out_shape=shape((width, columns), bf16),
+        input_output_aliases={2: 0},
+        compiler_params=params,
+        name="out_grads",
+    )(mixer_low, context, feed_grads)
+    big_owned = lax.psum_scatter(big_grad, "seq", scatter_dimension=0, tiled=True)
 
     conv_grad, tap_parts = pl.pallas_call(
         partial(conv_back_kernel, tile, taps),
@@ -784,11 +973,11 @@
     )(spots, values, values, grad_low, grad_high, bases)
 
     qkv_send, back_keep, back_give = pl.pallas_call(
-        partial(backward_kernel, hashes, bits, rows, work, steps, heads, own_rows),
+        partial(backward_kernel, hashes, bits, rows, work, steps, heads, own_rows, parts),
         grid=(2, steps),
         in_specs=[
             smem,
-            stepped(1, CORES * blocks, tok_rows, width),
+            *[anywhere] * parts,
             resident(*qkv_all.shape),
             resident(*bit_w.shape),
             resident(*bit_wt.shape),
@@ -818,35 +1007,57 @@
             pltpu.VMEM((3 * feats, width), f32),
             pltpu.VMEM((heads, 2 * head_dim, code_rows), bf16),
             pltpu.VMEM((heads, code_rows, 2 * head_dim), bf16),
+            pltpu.VMEM((seq_count, tok_rows, width), bf16),
+            pltpu.SemaphoreType.DMA((parts,)),
         ],
         compiler_params=hash_params,
         name="hash_backward",
     )(
-        spots, got, qkv_all, bit_w, bit_wt,
+        spots, *token_parts, qkv_all, bit_w, bit_wt,
         q_unit, k_unit, values, inverses, tables, gnum_got, conv_grad, tap_parts,
     )
 
-    chip_sum = back_keep.astype(f32) + core_swap(back_give).astype(f32)
     half = width // 2
-    chip_sum = chip_sum.astype(bf16).reshape(chips, 2, half, tok_rows)
-    keep = lax.dynamic_index_in_dim(chip_sum, side, 1, keepdims=False)
-    give = lax.dynamic_index_in_dim(chip_sum, 1 - side, 1, keepdims=False)
-    pair_sum = keep.astype(f32) + head_swap(give).astype(f32)
-
-    qkv_half = jnp.sum(across(qkv_send).astype(f32), axis=0)
-    back_half = jnp.sum(across(pair_sum.astype(bf16)).astype(f32), axis=0)
-    by_core = qkv_half.reshape(CORES, own_rows, 3 * feats + 64)
-    qkv_mine = lax.dynamic_index_in_dim(by_core, core, 0, keepdims=False)[:, : 3 * feats]
-    qkv_give = lax.dynamic_index_in_dim(by_core, 1 - core, 0, keepdims=False)[:, : 3 * feats]
+    group = chips // 2
+    per_chip = lambda *dims: pl.BlockSpec((group,) + dims, lambda i: (i, 0, 0))
+    keep, give = pl.pallas_call(
+        chip_sum_kernel,
+        grid=(2,),
+        in_specs=[smem, per_chip(width, tok_rows), per_chip(width, tok_rows)],
+        out_specs=[per_chip(half, tok_rows), per_chip(half, tok_rows)],
+        out_shape=[shape((chips, half, tok_rows), bf16)] * 2,
+        compiler_params=params,
+        name="chip_sum",
+    )(spots, back_keep, core_swap(back_give))
+    pair_sum = pl.pallas_call(
+        pair_sum_kernel,
+        grid=(2,),
+        in_specs=[per_chip(half, tok_rows), per_chip(half, tok_rows)],
+        out_specs=per_chip(half, tok_rows),
+        out_shape=shape((chips, half, tok_rows), bf16),
+        compiler_params=params,
+        name="pair_sum",
+    )(keep, head_swap(give))
+
+    qkv_mine, qkv_give = piped(
+        weight_sum_kernel, "weight_sum",
+        [shape((own_rows, 3 * feats + 64), f32)] * 2,
+        [spots, across(qkv_send), pair_sum],
+        [None, None, anywhere],
+    )
     qkv_other = core_swap(qkv_give)
+    back_got = across(pair_sum)
 
     extras = gnum_got[:, feats:].astype(f32)
     norm_half = jnp.sum(extras[:, :sum_rows], axis=0)
-    count_half = extras[:, sum_rows:].reshape(chips, -1)[:, : 2 * hashes * heads * chip_buckets]
-    count_half = count_half.reshape(chips, 2, hashes, heads, CORES, chip_buckets // CORES)
-    count_mine = lax.dynamic_index_in_dim(count_half, core, 4, keepdims=False)
-    count_give = lax.dynamic_index_in_dim(count_half, 1 - core, 4, keepdims=False)
-    tap_half = qkv_half[:heads, 3 * feats : 3 * feats + taps]
+    count_half = extras[:, sum_rows : sum_rows + heads].reshape(chips, heads, 2, tile // 2)
+    count_half = count_half[..., : chip_buckets * rows]
+    count_half = count_half.reshape(chips, heads, 2, CORES, chip_buckets // CORES, rows)
+    count_half = jnp.transpose(count_half[..., :hashes], (3, 0, 2, 5, 1, 4))
+    count_mine = lax.dynamic_index_in_dim(count_half, core, 0, keepdims=False)
+    count_give = lax.dynamic_index_in_dim(count_half, 1 - core, 0, keepdims=False)
+    tap_first = jnp.where(core == 0, qkv_mine[:heads], qkv_give[:heads])
+    tap_half = tap_first[:, 3 * feats : 3 * feats + taps]
     swapped = core_swap(
         jnp.concatenate([norm_half.reshape(-1), count_give.reshape(-1), tap_half.reshape(-1)])
     )
@@ -863,37 +1074,40 @@
     occupancy = occupancy * (buckets / (tok_rows * seq_count))
     conv_tap_grad = in_order(tap_half, swapped[norm_size + count_size :].reshape(heads, taps), 0)
 
-    def weight_order(part):
-        return jnp.transpose(part.reshape(own_rows, 3, feats), (1, 0, 2))
-
-    qkv_owned = in_order(weight_order(qkv_mine), weight_order(qkv_other), 2)
-    back_low = lax.optimization_barrier(back_half.astype(bf16))
+    matrix = lambda value: [shape(value.shape, f32)] * 3 + [shape(value.shape, bf16)]
+    (
+        up_new, up_first_new, up_second_new, up_copy,
+        down_new, down_first_new, down_second_new, down_copy,
+        out_new, out_first_new, out_second_new, out_copy,
+    ) = piped(
+        big_adam_kernel, "big_adam",
+        matrix(up_weight) + matrix(down_weight.T) + matrix(out_weight.T),
+        [
+            big_owned, up_weight, up_first, up_second,
+            down_weight.T, down_first.T, down_second.T,
+            out_weight.T, out_first.T, out_second.T,
+        ],
+    )
+    qkv_new, qkv_first_new, qkv_second_new, qkv_copy = piped(
+        qkv_adam_kernel, "qkv_adam", matrix(qkv_weight),
+        [spots, qkv_mine, qkv_other, qkv_weight, qkv_first, qkv_second],
+    )
+    norm_new, norm_first_new, norm_second_new = adam_step(
+        norm_params, norm_first, norm_second, norm_grad, 0.3
+    )
+    conv_new, conv_first_new, conv_second_new = adam_step(
+        conv_taps, conv_first, conv_second, conv_tap_grad, CONV ** (-0.5)
+    )
+    (back_low,) = piped(
+        back_sum_kernel, "back_sum",
+        [shape((half, tok_rows), bf16)],
+        [back_got, up_new, down_new, out_new],
+        [None] + [anywhere] * 3,
+    )
     back_other = head_swap(back_low)
     upper = jnp.where(side == 0, back_low, back_other)
     lower = jnp.where(side == 0, back_other, back_low)
     tokens_grad = grad_mixer + jnp.concatenate([upper, lower], axis=0).T.astype(f32)
-
-    up_owned = big_owned[:, :ff]
-    down_owned = big_owned[:, ff : 2 * ff].T
-    out_owned = big_owned[:, 2 * ff :].T
-    qkv_new, qkv_first_new, qkv_second_new = adam_step(
-        qkv_weight, qkv_first, qkv_second, qkv_owned, D ** (-0.5)
-    )
-    out_new, out_first_new, out_second_new = adam_step(
-        out_weight, out_first, out_second, out_owned, D ** (-0.5)
-    )
-    up_new, up_first_new, up_second_new = adam_step(
-        up_weight, up_first, up_second, up_owned, D ** (-0.5)
-    )
-    down_new, down_first_new, down_second_new = adam_step(
-        down_weight, down_first, down_second, down_owned, FF ** (-0.5)
-    )
-    norm_new, norm_first_new, norm_second_new = adam_step(
-        norm_params, norm_first, norm_second, norm_grad, 0.3
-    )
-    conv_new, conv_first_new, conv_second_new = adam_step(
-        conv_taps, conv_first, conv_second, conv_tap_grad, CONV ** (-0.5)
-    )
     return (
         block_out,
         tokens_grad,
@@ -901,19 +1115,19 @@
         qkv_new,
         qkv_first_new,
         qkv_second_new,
-        qkv_new.astype(jnp.bfloat16),
-        out_new,
-        out_first_new,
-        out_second_new,
-        out_new.astype(jnp.bfloat16),
+        qkv_copy,
+        out_new.T,
+        out_first_new.T,
+        out_second_new.T,
+        out_copy.T,
         up_new,
         up_first_new,
         up_second_new,
-        up_new.astype(jnp.bfloat16),
-        down_new,
-        down_first_new,
-        down_second_new,
-        down_new.astype(jnp.bfloat16),
+        up_copy,
+        down_new.T,
+        down_first_new.T,
+        down_second_new.T,
+        down_copy.T,
         norm_new,
         norm_first_new,
         norm_second_new,

time: 322 us -> 291 us (0.904)
  blocking collectives: 37.9 us -> 0 us
  other arithmetic: 26.3 us -> 6.91 us
  Pallas kernels: 82.2 us -> 91 us
  starting transfers between devices: 26.7 us -> 35.1 us
  waiting for transfers between devices: 110 us -> 118 us
    ppermute x2 -> x17, waiting for transfers between devices: 0.01 us -> 51.9 us  [the longest x4 29.5 us: on_device(): moved[0] = lax.ppermute(moved[0], 'seq', ahead)]
    all_gather x1 -> x0, blocking collectives: 37.9 us -> none  [on_device(): lax.all_gather(chip_rows, 'seq', axis=0, tiled=True, axis_index_groups=pl...]
    all_to_all x2, waiting for transfers between devices: 30.6 us -> 14.4 us  [the longest x1 10.3 us: on_device(): back_got = across(pair_sum)]
    convert_element_type x10 -> x0, other arithmetic: 14.4 us -> none  [the longest x1 2.3 us: on_device(): chip_sum = chip_sum.astype(bf16).reshape(chips, 2, half, tok_rows)]
    all_gather x1 -> x0, waiting for transfers between devices: 11.4 us -> none  [on_device(): got = lax.all_gather(tokens, 'seq', axis=0, tiled=False)]
    ppermute x2 -> x17, starting transfers between devices: 0.17 us -> 10.2 us  [the longest x4 7.57 us: on_device(): moved[0] = lax.ppermute(moved[0], 'seq', ahead)]
    all_gather x1, waiting for transfers between devices: 8.59 us -> 0.01 us  [on_device(): ff_all = lax.all_gather(second_send, 'seq', axis=0, tiled=True)]
    pallas_call x7 -> x15, Pallas kernels: 24.9 us -> 31.9 us  [the longest x5 11.3 us: piped(): pl.pallas_call(kernel, grid=(1,), in_specs=specs, out_specs=[full(o) for...]
  transfers between devices with their start and end apart: 18 -> 32, of which waited for: 11 -> 19; matrix products, arithmetic and copies ran while one was open for 12% -> 5% of each run, Pallas kernels for 19% -> 28%
where the time goes in v4:
time: 291 us; the launch traced here: 290 us
  waiting for transfers between devices  118 us (41%)
  Pallas kernels  91 us (31%)
  starting transfers between devices  35.1 us (12%)
  local copies, waits for them, and re-layouts  24.7 us (8%)
  between operations  14.8 us (5%)
  other arithmetic  6.91 us (2%)
    pallas_call x1, Pallas kernels, on_device(): pl.pallas_call(partial(backward_kernel, hashes, bits, rows, work, steps,...  32.3 us
    ppermute x4, waiting for transfers between devices, on_device(): moved[0] = lax.ppermute(moved[0], 'seq', ahead)  29.5 us
    all_to_all x1, waiting for transfers between devices, on_device(): num_got = across(num_parts)  20.9 us
    pallas_call x1, Pallas kernels, on_device(): pl.pallas_call(partial(forward_kernel, hashes, bits, rows, work, steps, h...  18.5 us
    ppermute x1, waiting for transfers between devices, on_device(): head_swap(give)  16.8 us
    all_to_all x1, waiting for transfers between devices, on_device(): gnum_got = across(gnum_send)  16.6 us
    unnamed x97, local copies, waits for them, and re-layouts  14.5 us
    pallas_call x5, Pallas kernels, piped(): pl.pallas_call(kernel, grid=(1,), in_specs=specs, out_specs=[full(o) for...  11.3 us
  transfers between devices with their start and end apart: 32, of which 19 were waited for; matrix products, arithmetic and copies ran while one was open for 5% of the time, Pallas kernels for 28%

profile of v4, /device:TPU:0, one launch (start us, length us, event | category | flops | bytes accessed | tf_op | source)
XLA Modules:
  0.0 290.1 jit_solution(16432238790002948966)
XLA Ops:
  11.3 2.9 %collective-permute-start.1 = (bf16[224,768]{1,0:T(8,128)(2,1)S(1)}, bf16[224,768]{1,0:T(8,128)(2,1)S(1)}, u32[]{:S(2)}, u32[]{:S(2)}) collective-permute-start(bf16[224,768]{1,0:T(8,128)(2,1)S(1)} %get-tuple-element.246), channel_id=1, source_target_pairs={{0,8},{2,10},{8,16},{10,18},{16,24},{18,26},{24,28},{26,30},{28,20... | collective-permute-start | bytes 1032200 | tf_op jit(solution)/shard_map/ppermute | solution.py:690
  14.2 8.3 %collective-permute-done.1 = bf16[224,768]{1,0:T(8,128)(2,1)S(1)} collective-permute-done((bf16[224,768]{1,0:T(8,128)(2,1)S(1)}, bf16[224,768]{1,0:T(8,128)(2,1)S(1)}, u32[]{:S(2)}, u32[]{:S(2)}) %collective-permute-start.1) | collective-permute-done | bytes 344096 | tf_op jit(solution)/shard_map/ppermute | solution.py:690
  26.1 7.0 %collective-permute-done.3 = bf16[224,768]{1,0:T(8,128)(2,1)S(1)} collective-permute-done((bf16[224,768]{1,0:T(8,128)(2,1)S(1)}, bf16[224,768]{1,0:T(8,128)(2,1)S(1)}, u32[]{:S(2)}, u32[]{:S(2)}) %collective-permute-start.3) | collective-permute-done | bytes 344096 | tf_op jit(solution)/shard_map/ppermute | solution.py:690
  38.4 3.8 %collective-permute-done.5 = bf16[224,768]{1,0:T(8,128)(2,1)} collective-permute-done((bf16[224,768]{1,0:T(8,128)(2,1)S(1)}, bf16[224,768]{1,0:T(8,128)(2,1)}, u32[]{:S(2)}, u32[]{:S(2)}) %collective-permute-start.5) | collective-permute-done | bytes 344096 | tf_op jit(solution)/shard_map/ppermute | solution.py:690
  49.2 10.4 %collective-permute-done.7 = bf16[224,768]{1,0:T(8,128)(2,1)S(1)} collective-permute-done((bf16[224,768]{1,0:T(8,128)(2,1)}, bf16[224,768]{1,0:T(8,128)(2,1)S(1)}, u32[]{:S(2)}, u32[]{:S(2)}) %collective-permute-start.7) | collective-permute-done | bytes 344096 | tf_op jit(solution)/shard_map/ppermute | solution.py:690
  62.0 18.5 %hash_forward.1 = (bf16[8,192,256]{2,1,0:T(8,128)(2,1)}, bf16[192,2048]{1,0:T(8,128)(2,1)}, bf16[192,2048]{1,0:T(8,128)(2,1)}, bf16[192,2304]{1,0:T(8,128)(2,1)}...) custom-call(s32[28]{0:T(128)} %pad_add_fusion.spots_ref, ...), custom_call_target="tpu_custom_call" | custom-call | tf_op jit(solution)/shard_map/hash_forward/pallas_call | solution.py:806
  80.5 4.8 %all-to-all-start = ((bf16[8,192,256]{2,1,0:T(8,128)(2,1)}), bf16[8,192,256]{2,1,0:T(8,128)(2,1)S(1)}, u32[]{:S(2)}, u32[]{:S(2)}) async-start(bf16[8,192,256]{2,1,0:T(8,128)(2,1)} %get-tuple-element.106), calls=%async_computation | async-start | bytes 1572864 | tf_op jit(solution)/shard_map/all_to_all | solution.py:846
  87.4 1.9 scatter.4.base_ref
  90.0 3.7 %conv_forward.1.conv_ref = f32[192,256]{1,0:T(8,128)} custom-call(s32[28]{0:T(128)} %pad_add_fusion.spots_ref, bf16[192,2304]{1,0:T(8,128)(2,1)} %get-tuple-element.107.left_ref.right_ref.refs_21_, bf16[192,2304]{1,0:T(8,128)(2,1)} %get-tuple-element.107.left_ref.right_ref.refs_21_, f32[3,8,512]{2,1,0:T(8,128)} %copy-done.37), custom_call_target="tpu_custom_call" | custom-call | tf_op jit(solution)/shard_map/conv_forward/pallas_call | solution.py:857
  93.6 20.9 %all-to-all-done.got_ref = bf16[8,192,256]{2,1,0:T(8,128)(2,1)S(1)} async-done(((bf16[8,192,256]{2,1,0:T(8,128)(2,1)}), bf16[8,192,256]{2,1,0:T(8,128)(2,1)S(1)}, u32[]{:S(2)}, u32[]{:S(2)}) %all-to-all-start) | async-done | bytes 786464 | tf_op jit(solution)/shard_map/all_to_all | solution.py:846
  117.6 2.5 copy-done.1
  123.2 5.4 %collective-permute-done.17.other_ref = bf16[128,768]{1,0:T(8,128)(2,1)S(1)} collective-permute-done((bf16[128,768]{1,0:T(8,128)(2,1)S(1)}, bf16[128,768]{1,0:T(8,128)(2,1)S(1)}, u32[]{:S(2)}, u32[]{:S(2)}) %collective-permute-start.17) | collective-permute-done | bytes 196640 | tf_op jit(solution)/shard_map/ppermute | solution.py:893
  131.7 4.6 %collective-permute-done.18.other_ref = bf16[128,768]{1,0:T(8,128)(2,1)S(1)} collective-permute-done((bf16[128,768]{1,0:T(8,128)(2,1)S(1)}, bf16[128,768]{1,0:T(8,128)(2,1)S(1)}, u32[]{:S(2)}, u32[]{:S(2)}) %collective-permute-start.18) | collective-permute-done | bytes 196640 | tf_op jit(solution)/shard_map/ppermute | solution.py:905
  136.3 2.2 feed_back.1
  141.5 5.0 %feed_grads.1.all_ref = bf16[768,3456]{1,0:T(8,128)(2,1)} custom-call(f32[128,768]{1,0:T(8,128)} %copy-done.4, f32[4,768]{1,0:T(4,128)} %norm_ref.7, bf16[128,1536]{1,0:T(8,128)(2,1)} %copy-done.9, bf16[128,768]{1,0:T(8,128)(2,1)} %copy-done.12, bf16[128,1536]{1,0:T(8,128)(2,1)} %copy-done.8), custom_call_target="tpu_custom_call" | custom-call | tf_op jit(solution)/shard_map/feed_grads/pallas_call | solution.py:936
  146.6 2.5 copy-done.3
  150.9 2.2 out_grads.1
  157.4 3.8 %all-to-all-start.1 = ((bf16[8,208,256]{2,1,0:T(8,128)(2,1)}), bf16[8,208,256]{2,1,0:T(8,128)(2,1)S(1)}, u32[]{:S(2)}, u32[]{:S(2)}) async-start(bf16[8,208,256]{2,1,0:T(8,128)(2,1)} %get-tuple-element.130), calls=%async_computation.1 | async-start | bytes 1703936 | tf_op jit(solution)/shard_map/all_to_all | solution.py:933
  161.9 4.5 %conv_backward.1 = (f32[192,768]{1,0:T(8,128)}, f32[3,8,128]{2,1,0:T(8,128)}) custom-call(s32[28]{0:T(128)} %pad_add_fusion.spots_ref, bf16[192,2304]{1,0:T(8,128)(2,1)} %get-tuple-element.107.left_ref.right_ref.refs_21_, bf16[192,2304]{1,0:T(8,128)(2,1)} %get-tuple-element.107.left_ref.right_ref.refs_21_, bf16[192,128]{1,0:T(8,128)(2,1)} %copy-done.18, ...), custom_call_target="tpu_custom_call" | custom-call | tf_op jit(solution)/shard_map/conv_backward/pallas_call | solution.py:957
  166.5 16.6 %all-to-all-done.1.refs_24_ = bf16[8,208,256]{2,1,0:T(8,128)(2,1)S(1)} async-done(((bf16[8,208,256]{2,1,0:T(8,128)(2,1)}), bf16[8,208,256]{2,1,0:T(8,128)(2,1)S(1)}, u32[]{:S(2)}, u32[]{:S(2)}) %all-to-all-start.1) | async-done | bytes 852000 | tf_op jit(solution)/shard_map/all_to_all | solution.py:933
  184.0 32.3 %hash_backward.1 = (bf16[8,96,640]{2,1,0:T(8,128)(2,1)}, bf16[8,768,128]{2,1,0:T(8,128)(2,1)}, bf16[8,768,128]{2,1,0:T(8,128)(2,1)}) custom-call(s32[28]{0:T(128)} %pad_add_fusion.spots_ref, bf16[1,224,768]{2,1,0:T(8,128)(2,1)} %get-tuple-element.247.refs_0_.refs_16_, bf16[1,224,768]{2,1,0:T(8,128)(2,1)} %bitcast.78, bf16[1,224,768]{2,1,0:T(8,128)(2,1)} %bitcast.81, ...), custom_call_target="tpu_custom_call" | custom-call | tf_op jit(solution)/shard_map/hash_backward/pallas_call | solution.py:975
  216.5 4.6 %all-to-all-start.3 = ((bf16[8,96,640]{2,1,0:T(8,128)(2,1)}), bf16[8,96,640]{2,1,0:T(8,128)(2,1)S(1)}, u32[]{:S(2)}, u32[]{:S(2)}) async-start(bf16[8,96,640]{2,1,0:T(8,128)(2,1)} %get-tuple-element.147), calls=%async_computation.4 | async-start | bytes 1966080 | tf_op jit(solution)/shard_map/all_to_all | solution.py:1045
  221.1 3.1 %chip_sum.1 = (bf16[8,384,128]{2,1,0:T(8,128)(2,1)}, bf16[8,384,128]{2,1,0:T(8,128)(2,1)}) custom-call(s32[28]{0:T(128)} %pad_add_fusion.spots_ref, bf16[8,768,128]{2,1,0:T(8,128)(2,1)} %get-tuple-element.135.own_ref, bf16[8,768,128]{2,1,0:T(8,128)(2,1)} %collective-permute-done.21.other_ref), custom_call_target="tpu_custom_call" | custom-call | tf_op jit(solution)/shard_map/chip_sum/pallas_call | solution.py:1023
  227.3 16.8 %collective-permute-done.22.other_ref = bf16[8,384,128]{2,1,0:T(8,128)(2,1)} collective-permute-done((bf16[8,384,128]{2,1,0:T(8,128)(2,1)}, bf16[8,384,128]{2,1,0:T(8,128)(2,1)}, u32[]{:S(2)}, u32[]{:S(2)}) %collective-permute-start.22) | collective-permute-done | bytes 786464 | tf_op jit(solution)/shard_map/ppermute | solution.py:1040
  244.1 2.2 pair_sum.1.after_ref
  246.3 4.1 %all-to-all-done.3.got_ref = bf16[8,96,640]{2,1,0:T(8,128)(2,1)S(1)} async-done(((bf16[8,96,640]{2,1,0:T(8,128)(2,1)}), bf16[8,96,640]{2,1,0:T(8,128)(2,1)S(1)}, u32[]{:S(2)}, u32[]{:S(2)}) %all-to-all-start.3) | async-done | bytes 983072 | tf_op jit(solution)/shard_map/all_to_all | solution.py:1045
  250.4 4.5 %all-to-all-start.2 = ((bf16[8,384,128]{2,1,0:T(8,128)(2,1)}), bf16[8,384,128]{2,1,0:T(8,128)(2,1)}, u32[]{:S(2)}, u32[]{:S(2)}) async-start(bf16[8,384,128]{2,1,0:T(8,128)(2,1)} %pair_sum.1.after_ref), calls=%async_computation.2 | async-start | bytes 1572864 | tf_op jit(solution)/shard_map/all_to_all | solution.py:1049
  254.9 2.0 weight_sum.1
  261.6 3.2 %big_adam.1 = (f32[48,1536]{1,0:T(8,128)}, f32[48,1536]{1,0:T(8,128)}, f32[48,1536]{1,0:T(8,128)}, bf16[48,1536]{1,0:T(8,128)(2,1)}, f32[48,1536]{1,0:T(8,128)},...) custom-call(bf16[48,3456]{1,0:T(8,128)(2,1)} %reduce-scatter.2.clone, ...), custom_call_target="tpu_custom_call" | custom-call | tf_op jit(solution)/shard_map/big_adam/pallas_call | solution.py:741
  264.8 10.3 %all-to-all-done.2.got_ref = bf16[8,384,128]{2,1,0:T(8,128)(2,1)} async-done(((bf16[8,384,128]{2,1,0:T(8,128)(2,1)}), bf16[8,384,128]{2,1,0:T(8,128)(2,1)}, u32[]{:S(2)}, u32[]{:S(2)}) %all-to-all-start.2) | async-done | bytes 786464 | tf_op jit(solution)/shard_map/all_to_all | solution.py:1049
  275.1 1.9 back_sum.1
  279.9 2.3 qkv_adam.1
  (205 shorter events, 56.3 us)
Async XLA Ops:
  7.2 110.4 %all-gather.2.cloned.1.call-start = ((), (), s32[]{:S(2)}) async-start(), calls=%async_computation.5 | async-start | bytes 5640192 | tf_op jit(solution)/shard_map/all_gather | solution.py:791
  9.1 1.4 collective-permute-start
  11.3 11.2 %collective-permute-start.1 = (bf16[224,768]{1,0:T(8,128)(2,1)S(1)}, bf16[224,768]{1,0:T(8,128)(2,1)S(1)}, u32[]{:S(2)}, u32[]{:S(2)}) collective-permute-start(bf16[224,768]{1,0:T(8,128)(2,1)S(1)} %get-tuple-element.246), channel_id=1, source_target_pairs={{0,8},{2,10},{8,16},{10,18},{16,24},{18,26},{24,28},{26,30},{28,20... | collective-permute-start | bytes 1032200 | tf_op jit(solution)/shard_map/ppermute | solution.py:690
  14.2 9.8 %collective-permute-start.2 = (bf16[224,768]{1,0:T(8,128)(2,1)S(1)}, bf16[224,768]{1,0:T(8,128)(2,1)S(1)}, u32[]{:S(2)}, u32[]{:S(2)}) collective-permute-start(bf16[224,768]{1,0:T(8,128)(2,1)S(1)} %get-tuple-element.246), channel_id=1, source_target_pairs={{8,0},{10,2},{16,8},{18,10},{24,16},{26,18},{28,24},{30,26},{20,28... | collective-permute-start | bytes 1032200 | tf_op jit(solution)/shard_map/ppermute | solution.py:694
  24.1 9.0 %collective-permute-start.3 = (bf16[224,768]{1,0:T(8,128)(2,1)S(1)}, bf16[224,768]{1,0:T(8,128)(2,1)S(1)}, u32[]{:S(2)}, u32[]{:S(2)}) collective-permute-start(bf16[224,768]{1,0:T(8,128)(2,1)S(1)} %collective-permute-done.1), channel_id=1, source_target_pairs={{0,8},{2,10},{8,16},{10,18},{16,24},{18,26},{24,28},{26,30},{28,20... | collective-permute-start | bytes 1032200 | tf_op jit(solution)/shard_map/ppermute | solution.py:690
  25.7 8.7 %collective-permute-start.4 = (bf16[224,768]{1,0:T(8,128)(2,1)S(1)}, bf16[224,768]{1,0:T(8,128)(2,1)S(1)}, u32[]{:S(2)}, u32[]{:S(2)}) collective-permute-start(bf16[224,768]{1,0:T(8,128)(2,1)S(1)} %collective-permute-done.2), channel_id=1, source_target_pairs={{8,0},{10,2},{16,8},{18,10},{24,16},{26,18},{28,24},{30,26},{20,28... | collective-permute-start | bytes 1032200 | tf_op jit(solution)/shard_map/ppermute | solution.py:694
  34.4 7.9 %collective-permute-start.5 = (bf16[224,768]{1,0:T(8,128)(2,1)S(1)}, bf16[224,768]{1,0:T(8,128)(2,1)}, u32[]{:S(2)}, u32[]{:S(2)}) collective-permute-start(bf16[224,768]{1,0:T(8,128)(2,1)S(1)} %collective-permute-done.3), channel_id=1, source_target_pairs={{0,8},{2,10},{8,16},{10,18},{16,24},{18,26},{24,28},{26,30},{28,20... | collective-permute-start | bytes 1032200 | tf_op jit(solution)/shard_map/ppermute | solution.py:690
  36.0 7.5 %collective-permute-start.6 = (bf16[224,768]{1,0:T(8,128)(2,1)S(1)}, bf16[224,768]{1,0:T(8,128)(2,1)S(1)}, u32[]{:S(2)}, u32[]{:S(2)}) collective-permute-start(bf16[224,768]{1,0:T(8,128)(2,1)S(1)} %collective-permute-done.4), channel_id=1, source_target_pairs={{8,0},{10,2},{16,8},{18,10},{24,16},{26,18},{28,24},{30,26},{20,28... | collective-permute-start | bytes 1032200 | tf_op jit(solution)/shard_map/ppermute | solution.py:694
  46.0 2.3 collective-permute-start.8
  46.1 2.6 collective-permute-start.9
  46.6 2.3 collective-permute-start.10
  46.7 12.9 %collective-permute-start.7 = (bf16[224,768]{1,0:T(8,128)(2,1)}, bf16[224,768]{1,0:T(8,128)(2,1)S(1)}, u32[]{:S(2)}, u32[]{:S(2)}) collective-permute-start(bf16[224,768]{1,0:T(8,128)(2,1)} %collective-permute-done.5), channel_id=1, source_target_pairs={{0,8},{2,10},{8,16},{10,18},{16,24},{18,26},{24,28},{26,30},{28,20... | collective-permute-start | bytes 1032200 | tf_op jit(solution)/shard_map/ppermute | solution.py:690
  48.2 11.4 %collective-permute-start.11 = (bf16[224,768]{1,0:T(8,128)(2,1)S(1)}, bf16[224,768]{1,0:T(8,128)(2,1)S(1)}, u32[]{:S(2)}, u32[]{:S(2)}) collective-permute-start(bf16[224,768]{1,0:T(8,128)(2,1)S(1)} %collective-permute-done.3), channel_id=1, source_target_pairs={{0,2},{2,0},{4,6},{6,4},{8,10},{10,8},{12,14},{14,12},{16,18},{18,... | collective-permute-start | bytes 1032200 | tf_op jit(solution)/shard_map/ppermute | solution.py:700
  48.3 11.3 %collective-permute-start.12 = (bf16[224,768]{1,0:T(8,128)(2,1)S(1)}, bf16[224,768]{1,0:T(8,128)(2,1)S(1)}, u32[]{:S(2)}, u32[]{:S(2)}) collective-permute-start(bf16[224,768]{1,0:T(8,128)(2,1)S(1)} %collective-permute-done.4), channel_id=1, source_target_pairs={{0,2},{2,0},{4,6},{6,4},{8,10},{10,8},{12,14},{14,12},{16,18},{18,... | collective-permute-start | bytes 1032200 | tf_op jit(solution)/shard_map/ppermute | solution.py:700
  48.7 10.9 %collective-permute-start.13 = (bf16[224,768]{1,0:T(8,128)(2,1)}, bf16[224,768]{1,0:T(8,128)(2,1)S(1)}, u32[]{:S(2)}, u32[]{:S(2)}) collective-permute-start(bf16[224,768]{1,0:T(8,128)(2,1)} %collective-permute-done.5), channel_id=1, source_target_pairs={{0,2},{2,0},{4,6},{6,4},{8,10},{10,8},{12,14},{14,12},{16,18},{18,... | collective-permute-start | bytes 1032200 | tf_op jit(solution)/shard_map/ppermute | solution.py:700
  48.9 10.8 %collective-permute-start.14 = (bf16[224,768]{1,0:T(8,128)(2,1)}, bf16[224,768]{1,0:T(8,128)(2,1)S(1)}, u32[]{:S(2)}, u32[]{:S(2)}) collective-permute-start(bf16[224,768]{1,0:T(8,128)(2,1)} %copy-done.20), channel_id=1, source_target_pairs={{0,2},{2,0},{4,6},{6,4},{8,10},{10,8},{12,14},{14,12},{16,18},{18,... | collective-permute-start | bytes 1032200 | tf_op jit(solution)/shard_map/ppermute | solution.py:700
  59.6 1.7 collective-permute-start.15
  80.5 34.0 %all-to-all-start = ((bf16[8,192,256]{2,1,0:T(8,128)(2,1)}), bf16[8,192,256]{2,1,0:T(8,128)(2,1)S(1)}, u32[]{:S(2)}, u32[]{:S(2)}) async-start(bf16[8,192,256]{2,1,0:T(8,128)(2,1)} %get-tuple-element.106), calls=%async_computation | async-start | bytes 1572864 | tf_op jit(solution)/shard_map/all_to_all | solution.py:846
  85.3 176.3 %reduce-scatter.2.cloned.1.call-start = ((), (), s32[]{:S(2)}) async-start(), calls=%async_computation.6 | async-start | bytes 5640192 | tf_op jit(solution)/shard_map/reduce_scatter | solution.py:955
  116.3 1.3 collective-permute-start.16
  121.7 7.0 %collective-permute-start.17 = (bf16[128,768]{1,0:T(8,128)(2,1)S(1)}, bf16[128,768]{1,0:T(8,128)(2,1)S(1)}, u32[]{:S(2)}, u32[]{:S(2)}) collective-permute-start(bf16[128,768]{1,0:T(8,128)(2,1)S(1)} %get-tuple-element.110.own_ref), channel_id=1, source_target_pairs={{0,1},{1,0},{2,3},{3,2},{4,5},{5,4},{6,7},{7,6},{8,9},{9,8},{10,11... | collective-permute-start | bytes 589832 | tf_op jit(solution)/shard_map/ppermute | solution.py:893
  130.1 6.2 %collective-permute-start.18 = (bf16[128,768]{1,0:T(8,128)(2,1)S(1)}, bf16[128,768]{1,0:T(8,128)(2,1)S(1)}, u32[]{:S(2)}, u32[]{:S(2)}) collective-permute-start(bf16[128,768]{1,0:T(8,128)(2,1)S(1)} %get-tuple-element.113.own_ref), channel_id=1, source_target_pairs={{0,1},{1,0},{2,3},{3,2},{4,5},{5,4},{6,7},{7,6},{8,9},{9,8},{10,11... | collective-permute-start | bytes 589832 | tf_op jit(solution)/shard_map/ppermute | solution.py:905
  140.0 6.6 %collective-permute-start.19 = (bf16[128,768]{1,0:T(8,128)(2,1)S(1)}, bf16[128,768]{1,0:T(8,128)(2,1)S(1)}, u32[]{:S(2)}, u32[]{:S(2)}) collective-permute-start(bf16[128,768]{1,0:T(8,128)(2,1)S(1)} %get-tuple-element.116.own_ref), channel_id=1, source_target_pairs={{0,1},{1,0},{2,3},{3,2},{4,5},{5,4},{6,7},{7,6},{8,9},{9,8},{10,11... | collective-permute-start | bytes 589832 | tf_op jit(solution)/shard_map/ppermute | solution.py:918
  153.2 1.4 collective-permute-start.20
  157.4 25.7 %all-to-all-start.1 = ((bf16[8,208,256]{2,1,0:T(8,128)(2,1)}), bf16[8,208,256]{2,1,0:T(8,128)(2,1)S(1)}, u32[]{:S(2)}, u32[]{:S(2)}) async-start(bf16[8,208,256]{2,1,0:T(8,128)(2,1)} %get-tuple-element.130), calls=%async_computation.1 | async-start | bytes 1703936 | tf_op jit(solution)/shard_map/all_to_all | solution.py:933
  216.4 4.7 %collective-permute-start.21 = (bf16[8,768,128]{2,1,0:T(8,128)(2,1)}, bf16[8,768,128]{2,1,0:T(8,128)(2,1)}, u32[]{:S(2)}, u32[]{:S(2)}) collective-permute-start(bf16[8,768,128]{2,1,0:T(8,128)(2,1)} %get-tuple-element.136), channel_id=1, source_target_pairs={{0,2},{2,0},{4,6},{6,4},{8,10},{10,8},{12,14},{14,12},{16,18},{18,... | collective-permute-start | bytes 4718600 | tf_op jit(solution)/shard_map/ppermute | solution.py:1031
  216.5 33.9 %all-to-all-start.3 = ((bf16[8,96,640]{2,1,0:T(8,128)(2,1)}), bf16[8,96,640]{2,1,0:T(8,128)(2,1)S(1)}, u32[]{:S(2)}, u32[]{:S(2)}) async-start(bf16[8,96,640]{2,1,0:T(8,128)(2,1)} %get-tuple-element.147), calls=%async_computation.4 | async-start | bytes 1966080 | tf_op jit(solution)/shard_map/all_to_all | solution.py:1045
  224.1 20.0 %collective-permute-start.22 = (bf16[8,384,128]{2,1,0:T(8,128)(2,1)}, bf16[8,384,128]{2,1,0:T(8,128)(2,1)}, u32[]{:S(2)}, u32[]{:S(2)}) collective-permute-start(bf16[8,384,128]{2,1,0:T(8,128)(2,1)} %get-tuple-element.138), channel_id=1, source_target_pairs={{0,1},{1,0},{2,3},{3,2},{4,5},{5,4},{6,7},{7,6},{8,9},{9,8},{10,11... | collective-permute-start | bytes 2359304 | tf_op jit(solution)/shard_map/ppermute | solution.py:1040
  250.4 24.7 %all-to-all-start.2 = ((bf16[8,384,128]{2,1,0:T(8,128)(2,1)}), bf16[8,384,128]{2,1,0:T(8,128)(2,1)}, u32[]{:S(2)}, u32[]{:S(2)}) async-start(bf16[8,384,128]{2,1,0:T(8,128)(2,1)} %pair_sum.1.after_ref), calls=%async_computation.2 | async-start | bytes 1572864 | tf_op jit(solution)/shard_map/all_to_all | solution.py:1049
  258.6 1.2 collective-permute-start.24
  258.8 20.5 %collective-permute-start.25 = (f32[48,640]{1,0:T(8,128)}, f32[48,640]{1,0:T(8,128)S(1)}, u32[]{:S(2)}, u32[]{:S(2)}) collective-permute-start(f32[48,640]{1,0:T(8,128)} %get-tuple-element.149), channel_id=1, source_target_pairs={{0,2},{2,0},{4,6},{6,4},{8,10},{10,8},{12,14},{14,12},{16,18},{18,... | collective-permute-start | bytes 368648 | tf_op jit(solution)/shard_map/ppermute | solution.py:1048
  277.0 5.3 %collective-permute-start.23 = (bf16[384,128]{1,0:T(8,128)(2,1)}, bf16[384,128]{1,0:T(8,128)(2,1)S(1)}, u32[]{:S(2)}, u32[]{:S(2)}) collective-permute-start(bf16[384,128]{1,0:T(8,128)(2,1)} %back_sum.1), channel_id=1, source_target_pairs={{0,1},{1,0},{2,3},{3,2},{4,5},{5,4},{6,7},{7,6},{8,9},{9,8},{10,11... | collective-permute-start | bytes 294920 | tf_op jit(solution)/shard_map/ppermute | solution.py:1107
  (48 other events, 421.1 us)
Sparse Core Ops, SparseCore 0:
  46.1 68.8 all-gather.1
  153.3 79.6 reduce-scatter.1

commit v5 on v4

--- a/solution.py
+++ b/solution.py
@@ -134,10 +134,10 @@
 
 
 def forward_kernel(
-    hashes, bits, rows, tile, steps, heads, parts, weight_parts, weight_row, spots_ref, *refs
+    hashes, bits, rows, tile, steps, heads, parts, weight_spots, spots_ref, *refs
 ):
     part_refs, refs = refs[:parts], refs[parts:]
-    weight_refs, refs = refs[:weight_parts], refs[weight_parts:]
+    weight_refs, refs = refs[: len(weight_spots)], refs[len(weight_spots) :]
     bit_ref, num_ref, qu_ref, ku_ref, v_ref, inv_ref, table_ref, count_ref, w_ref = refs[:9]
     acc_ref, codes_ref, wt_ref, table_t_ref, tok_ref, got_ref, sem_ref = refs[9:]
     limit = spots_ref[0]
@@ -154,7 +154,7 @@
         copies = token_copies(spots_ref, part_refs, tok_ref, sem_ref)
         loads = [
             pltpu.make_async_copy(
-                ref.at[:, pl.ds(weight_row, got_ref.shape[1])],
+                ref.at[:, pl.ds(weight_spots[i], got_ref.shape[1])],
                 got_ref.at[pl.ds(spots_ref[SPOTS + parts + i], ref.shape[0])],
                 sem_ref.at[parts + i],
             )
@@ -168,8 +168,12 @@
         inv_ref[...] = jnp.zeros_like(inv_ref)
         for copy in loads:
             copy.wait()
-        got = got_ref[...]
-        got = got.reshape(got.shape[0] * got.shape[1], got.shape[2])[:, : 3 * feats]
+        got = got_ref[...].astype(f32)
+        if len(weight_refs) > 1:
+            quarter = got.shape[1] // 3
+            rest = [got[:, quarter * j : quarter * (j + 1), 3 * feats :] for j in range(3)]
+            got = jnp.concatenate([got[:, :, : 3 * feats], jnp.concatenate(rest, axis=2)], axis=1)
+        got = got.reshape(got.shape[0] * got.shape[1], got.shape[2])[:, : 3 * feats].astype(bf16)
         w_ref[...] = got
         wt_ref[...] = flip(got)
         for copy in copies:
@@ -255,17 +259,25 @@
     return inverse * (grad - unit * inner)
 
 
-def backward_kernel(hashes, bits, rows, tile, steps, heads, own_rows, parts, spots_ref, *refs):
+def backward_kernel(
+    hashes, bits, rows, tile, steps, heads, own_rows, parts, gnum_parts, spots_ref, *refs
+):
     part_refs, refs = refs[:parts], refs[parts:]
+    gnum_refs, refs = refs[:gnum_parts], refs[gnum_parts:]
     w_ref, bit_ref, bit_t_ref, qu_ref, ku_ref, v_ref, inv_ref, table_ref = refs[:8]
-    gnum_ref, conv_ref, tap_ref, grad_ref, keep_ref, give_ref = refs[8:14]
-    acc_ref, codes_ref, proj_ref, sum_ref, table_t_ref, table_g_ref, tok_ref, sem_ref = refs[14:]
+    conv_ref, tap_ref, grad_ref, keep_ref, give_ref, extra_ref = refs[8:14]
+    acc_ref, codes_ref, proj_ref, sum_ref, table_t_ref, table_g_ref = refs[14:20]
+    tok_ref, gnum_ref, sem_ref = refs[20:]
     limit = spots_ref[0]
     spot = spots_ref[1]
     core = spots_ref[2]
     phase, i = pl.program_id(0), pl.program_id(1)
     devices, unused, width = tok_ref.shape
     copies = token_copies(spots_ref, part_refs, tok_ref, sem_ref)
+    loads = [
+        (ref, pl.ds(spots_ref[SPOTS + parts + j], ref.shape[0]))
+        for j, ref in enumerate(gnum_refs)
+    ]
     feats = heads * 64
     blocks = keep_ref.shape[0]
     block = tile // blocks
@@ -280,13 +292,16 @@
             copy.start()
         acc_ref[...] = jnp.zeros_like(acc_ref)
         sum_ref[...] = jnp.zeros_like(sum_ref)
+        for ref, where in loads:
+            gnum_ref[where] = ref[:, :feats]
+            extra_ref[where] = ref[:, feats:]
 
     @pl.when(phase == 0)
     def _():
         spans = [slice(64 * h, 64 * (h + 1)) for h in range(heads)]
         pairs, grads, slopes = [], [], []
         for mine in spans:
-            gnum = jnp.concatenate([gnum_ref[c, mine, :] for c in range(blocks)], axis=1)
+            gnum = jnp.concatenate([gnum_ref[i * blocks + c, mine, :] for c in range(blocks)], axis=1)
             pairs.append(masked_pair(gnum.astype(f32), early, late))
         for h, mine in enumerate(spans):
             slopes.append(
@@ -378,33 +393,41 @@
     return upper, (matrix - upper.astype(f32)).astype(bf16)
 
 
-def conv_kernel(tile, spots_ref, left_ref, right_ref, base_ref, out_ref):
-    upper, lower = banded(base_ref[0, 0:1], window_same(spots_ref, tile), tile)
-    window = jnp.concatenate([left_ref[...], right_ref[...]], axis=1)
-    out_ref[...] = nn(window, upper) + nn(window, lower)
+def conv_kernel(tile, heads, spots_ref, values_ref, base_ref, out_ref, window_ref):
+    same = window_same(spots_ref, tile)
+    first = pl.multiple_of(spots_ref[1] * tile, tile)
+    window = values_ref[:, pl.ds(first, tile + 256)]
+    window_ref[...] = window
+    for h in range(heads):
+        mine = slice(64 * h, 64 * (h + 1))
+        upper, lower = banded(base_ref[h, 0:1], same, tile)
+        out_ref[mine] = nn(window[mine], upper) + nn(window[mine], lower)
 
 
 def conv_back_kernel(
-    tile, taps, spots_ref, left_ref, right_ref, low_ref, high_ref, base_ref, out_ref, tap_ref
+    tile, taps, heads, spots_ref, window_ref, low_ref, high_ref, base_ref, out_ref, tap_ref
 ):
-    upper, lower = banded(base_ref[0, 0:1], window_same(spots_ref, tile), tile)
-    own = jnp.concatenate([low_ref[...], high_ref[...]], axis=1)
-    out_ref[...] = jnp.zeros_like(out_ref)
-    out_ref[:, 128 : 128 + tile + 256] = nt(own, upper) + nt(own, lower)
+    same = window_same(spots_ref, tile)
     width = tile + 256
     rim = taps // 2
-    values = jnp.concatenate([left_ref[...], right_ref[...]], axis=1).astype(f32)
-    own = own.astype(f32)
-    sums = []
-    for o in range(taps):
-        moved = pltpu.roll(values, width - (128 - rim) - o, 1)[:, :tile]
-        sums.append(jnp.sum(moved * own, axis=0, keepdims=True))
-    sums = jnp.concatenate(sums + [jnp.zeros((128 - taps, tile), f32)], axis=0)
+    out_ref[...] = jnp.zeros_like(out_ref)
     pos = lax.broadcasted_iota(jnp.int32, (128, tile), 1) + spots_ref[1] * tile
     other = pos + lax.broadcasted_iota(jnp.int32, (128, tile), 0) - rim
-    same = (pos >= spots_ref[0]) == (other >= spots_ref[0])
-    total = jnp.sum(jnp.where(same, sums, 0.0), axis=1, keepdims=True)
-    tap_ref[0] = jnp.transpose(jnp.broadcast_to(total, (128, 128)))[0:8]
+    near = (pos >= spots_ref[0]) == (other >= spots_ref[0])
+    for h in range(heads):
+        mine = slice(64 * h, 64 * (h + 1))
+        upper, lower = banded(base_ref[h, 0:1], same, tile)
+        own = jnp.concatenate([low_ref[mine], high_ref[mine]], axis=1)
+        out_ref[mine, 128 : 128 + width] = nt(own, upper) + nt(own, lower)
+        values = window_ref[mine].astype(f32)
+        own = own.astype(f32)
+        sums = []
+        for o in range(taps):
+            moved = pltpu.roll(values, width - (128 - rim) - o, 1)[:, :tile]
+            sums.append(jnp.sum(moved * own, axis=0, keepdims=True))
+        sums = jnp.concatenate(sums + [jnp.zeros((128 - taps, tile), f32)], axis=0)
+        total = jnp.sum(jnp.where(near, sums, 0.0), axis=1, keepdims=True)
+        tap_ref[h] = jnp.transpose(jnp.broadcast_to(total, (128, 128)))[0:8]
 
 
 def context_kernel(heads, spots_ref, got_ref, conv_ref, keep_ref, give_ref, num_ref):
@@ -432,7 +455,7 @@
     pair = jnp.concatenate([jnp.where(zero, keep, other), jnp.where(zero, other, keep)], axis=0)
     context = jnp.transpose(pair).astype(bf16)
     context_ref[...] = context
-    part_ref[...] = nt(context, w_ref[:, w_ref.shape[1] - context.shape[1] :]).astype(bf16)
+    part_ref[...] = nt(context, w_ref[...]).astype(bf16)
 
 
 def hidden_kernel(
@@ -516,26 +539,17 @@
     tile = gnum.shape[1]
     feats = 64 * heads
     pieces = sums_ref.shape[1] // tile
-    chips = send_ref.shape[0]
-    piece = count_ref.shape[2] // chips
-    blank = jnp.zeros((1, tile // 2 - piece), f32)
-    spare = jnp.zeros((send_ref.shape[1] - feats - 4 * pieces - heads, tile), f32)
+    counts = []
+    for h in range(heads):
+        for d in range(2):
+            row = count_ref[h, d : d + 1, :]
+            counts += [row[:, tile * i : tile * (i + 1)] for i in range(row.shape[1] // tile)]
+    used = feats + 4 * pieces + len(counts)
+    spare = jnp.zeros((send_ref.shape[0] - used, tile), f32)
     sums = sums_ref[...].astype(bf16).astype(f32)
-    sums = jnp.concatenate(
-        [sums[:, tile * i : tile * (i + 1)] for i in range(pieces)], axis=0
-    )
-    for c in range(chips):
-        send_ref[c, 0:feats, :] = gnum
-        counts = []
-        for h in range(heads):
-            row = [count_ref[h, d : d + 1, c * piece : (c + 1) * piece] for d in range(2)]
-            counts.append(
-                jnp.concatenate([row[0], blank, row[1], blank], axis=1)
-                if blank.shape[1]
-                else jnp.concatenate(row, axis=1)
-            )
-        extra = jnp.concatenate([sums] + counts + [spare], axis=0)
-        send_ref[c, feats:, :] = extra.astype(bf16)
+    sums = [sums[:, tile * i : tile * (i + 1)] for i in range(pieces)]
+    send_ref[0:feats, :] = gnum
+    send_ref[feats:, :] = jnp.concatenate(sums + counts + [spare], axis=0).astype(bf16)
 
 
 def feed_grad_kernel(hat_ref, norm_ref, slope_ref, feed_ref, active_ref, out_ref):
@@ -565,7 +579,8 @@
     give_ref[...] = jnp.where(zero, second, first).astype(bf16)
 
 
-def pair_sum_kernel(own_ref, other_ref, out_ref):
+def pair_sum_kernel(own_ref, other_ref, out_ref, flag_ref):
+    flag_ref[...] = jnp.zeros_like(flag_ref)
     out_ref[...] = (own_ref[...].astype(f32) + other_ref[...].astype(f32)).astype(bf16)
 
 
@@ -586,7 +601,8 @@
 
 
 def big_adam_kernel(grad_ref, *refs):
-    ins, outs = refs[:9], refs[9:]
+    ins, outs, flag_ref = refs[:9], refs[9:-1], refs[-1]
+    flag_ref[...] = jnp.zeros_like(flag_ref)
     ff = ins[0].shape[1]
     spans = (slice(0, ff), slice(ff, 2 * ff), slice(2 * ff, grad_ref.shape[1]))
     for k, (span, rate) in enumerate(zip(spans, (D ** (-0.5), FF ** (-0.5), D ** (-0.5)))):
@@ -602,6 +618,13 @@
         mine, other = mine_ref[:, span], other_ref[:, span]
         grad = jnp.concatenate([jnp.where(zero, mine, other), jnp.where(zero, other, mine)], axis=1)
         adam_refs(grad, [ref[p] for ref in refs[:3]], [ref.at[p] for ref in refs[3:]], D ** (-0.5))
+
+
+def final_kernel(spots_ref, mine_ref, other_ref, mixer_ref, out_ref):
+    mine, other = mine_ref[...].astype(f32), other_ref[...].astype(f32)
+    zero = spots_ref[3] == 0
+    total = jnp.concatenate([jnp.where(zero, mine, other), jnp.where(zero, other, mine)], axis=0)
+    out_ref[...] = mixer_ref[...] + jnp.transpose(total)
 
 
 def back_sum_kernel(got_ref, *refs):
@@ -673,9 +696,19 @@
     by_rows = lambda part: jnp.transpose(part, (1, 0, 2)).reshape(own_rows, 3 * feats)
     qkv_mine, qkv_give = by_rows(pick(core)), by_rows(pick(1 - core))
     chip_rows = in_order(qkv_mine, core_swap(qkv_give), 0)
-    chip_rows = jnp.pad(chip_rows, ((0, 0), (0, width - 3 * feats)))
-
-    if chips == len(RING):
+
+    def ring(value, steps, hold):
+        moved, found, turns = [value, value], [value], [0]
+        for step in range(1, steps + 1):
+            moved = [lax.ppermute(v, "seq", p) for v, p in zip(moved, (ahead, behind))]
+            if hold:
+                moved = list(lax.optimization_barrier(tuple(moved)))
+            found += moved
+            turns += [chips - step, step]
+        return moved, found, turns
+
+    ringed = chips == len(RING)
+    if ringed:
         order = np.array(RING)
         seats = np.argsort(order)
         ahead = [
@@ -684,31 +717,36 @@
             for k in range(CORES)
         ]
         behind = [(b, a) for a, b in ahead]
-        block = jnp.concatenate([tokens, chip_rows], axis=0)
-        block_parts, turns, moved = [block], [0], [block, block]
-        for step in range(1, chips // 2 + 1):
-            moved[0] = lax.ppermute(moved[0], "seq", ahead)
-            block_parts.append(moved[0])
-            turns.append(chips - step)
-            if 2 * step < chips:
-                moved[1] = lax.ppermute(moved[1], "seq", behind)
-                moved = list(lax.optimization_barrier(tuple(moved)))
-                block_parts[-1] = moved[0]
-                block_parts.append(moved[1])
-                turns.append(step)
-                last_part = moved[1]
-        token_parts = [p[None] for p in block_parts + [core_swap(part) for part in block_parts]]
-        weight_parts, weight_row = token_parts[:chips], tok_rows
+        quarter = CORES * own_rows // 4
+        third = feats
+        rest = chip_rows[3 * quarter :]
+        rest = jnp.concatenate([rest[:, third * j : third * (j + 1)] for j in range(3)], axis=0)
+        packed = jnp.concatenate([chip_rows[: 3 * quarter], rest], axis=1)
+        block = jnp.concatenate([tokens, packed], axis=0)
+        moved, block_parts, turns = ring(block, chips // 2 - 1, True)
+        last_part = block_parts[2][0:8, 0:128]
+        far_tokens, far_rows = lax.optimization_barrier(
+            (moved[0][:tok_rows], moved[1][tok_rows:])
+        )
+        across_tokens = lax.ppermute(far_tokens, "seq", ahead)
+        across_rows = lax.ppermute(far_rows, "seq", behind)
+        across_tokens, across_rows = lax.optimization_barrier((across_tokens, across_rows))
+        turns.append(chips // 2)
+        token_parts = block_parts + [across_tokens]
+        token_parts = [p[None] for p in token_parts + [core_swap(part) for part in token_parts]]
+        weight_parts = [p[None] for p in block_parts + [across_rows]]
+        weight_spots = [tok_rows] * (chips - 1) + [0]
         spot_of = np.array([[order[(seats[c] + t) % chips] for t in turns] for c in range(chips)])
         spot_of = np.repeat(spot_of, CORES, axis=0)
         core_of = np.arange(seq_count)[:, None] % CORES
         place_of = [CORES * spot_of + core_of, CORES * spot_of + 1 - core_of, spot_of]
     else:
         token_parts = [lax.all_gather(tokens, "seq", axis=0, tiled=False)]
+        chip_rows = jnp.pad(chip_rows, ((0, 0), (0, width - 3 * feats)))
         weight_parts = [
             lax.all_gather(chip_rows, "seq", axis=0, tiled=False, axis_index_groups=planes_of)
         ]
-        weight_row = 0
+        weight_spots = [0]
         place_of = [np.zeros((seq_count, 2))]
         last_part = token_parts[0]
     parts = len(token_parts)
@@ -729,7 +767,7 @@
     shape = jax.ShapeDtypeStruct
 
     def full(value):
-        return pl.BlockSpec(value.shape, lambda i: (0,) * value.ndim)
+        return pl.BlockSpec(value.shape, lambda i: (0,) * len(value.shape))
 
     def piped(kernel, name, outs, args, specs=None):
         if specs is None:
@@ -749,23 +787,28 @@
         )(*args)
 
     inside = pl.BlockSpec(memory_space=pltpu.VMEM)
-
-    def once(kernel, name, outs, args, after=(), outside=(), aliases=None, limit=SMALL_LIMIT):
+    in_vmem = lambda value: pltpu.with_memory_space_constraint(value, pltpu.VMEM)
+    small = pltpu.CompilerParams(
+        dimension_semantics=("arbitrary",), vmem_limit_bytes=SMALL_LIMIT
+    )
+
+    def once(kernel, name, outs, args, after=(), outside=(), blocks={}, limit=SMALL_LIMIT):
         specs, values = [], []
-        for arg in args:
-            specs.append(smem if arg is spots else inside)
-            values.append(
-                arg if arg is spots else pltpu.with_memory_space_constraint(arg, pltpu.VMEM)
-            )
+        for i, arg in enumerate(args):
+            plain = arg is spots or i in blocks
+            specs.append(smem if arg is spots else blocks.get(i, inside))
+            values.append(arg if plain else in_vmem(arg))
         for arg in after:
             specs.append(anywhere)
             values.append(arg)
         return pl.pallas_call(
             kernel,
+            grid=(1,) if blocks else (),
             in_specs=specs,
             out_specs=[inside] * len(outs),
             out_shape=[
-                o if i in outside else pltpu.VMEM(o.shape, o.dtype) for i, o in enumerate(outs)
+                (pltpu.HBM if i in outside else pltpu.VMEM)(o.shape, o.dtype)
+                for i, o in enumerate(outs)
             ],
             compiler_params=pltpu.CompilerParams(vmem_limit_bytes=limit),
             name=name,
@@ -804,7 +847,7 @@
         dimension_semantics=("arbitrary", "arbitrary"), vmem_limit_bytes=VMEM_LIMIT
     )
     num_parts, q_unit, k_unit, values, inverses, tables, counts, qkv_all = pl.pallas_call(
-        partial(forward_kernel, hashes, bits, rows, work, steps, heads, parts, weight_count, weight_row),
+        partial(forward_kernel, hashes, bits, rows, work, steps, heads, parts, weight_spots),
         grid=(2, steps),
         in_specs=[
             smem,
@@ -837,7 +880,7 @@
             pltpu.VMEM((3 * feats, width), bf16),
             pltpu.VMEM((heads, 2 * head_dim, code_rows), bf16),
             pltpu.VMEM((seq_count, tok_rows, width), bf16),
-            pltpu.VMEM((chips, CORES * own_rows, width), bf16),
+            pltpu.VMEM((chips, weight_parts[-1].shape[1], width), bf16),
             pltpu.SemaphoreType.DMA((parts + weight_count,)),
         ],
         compiler_params=hash_params,
@@ -849,27 +892,16 @@
     lead = tile + 128 - rim
     bases = jnp.zeros((heads, 8, tile + 256), f32)
     bases = bases.at[:, 0, lead : lead + taps].set(own_taps[:, ::-1])
-    window = [
-        pl.BlockSpec((head_dim, tile), lambda h, s: (h, s[1])),
-        pl.BlockSpec((head_dim, tile), lambda h, s: (h, s[1] + 1)),
-    ]
-    half_rows = pl.BlockSpec((head_dim, tok_rows), lambda h, s: (h, 0))
-    conv = pl.pallas_call(
-        partial(conv_kernel, tile),
-        grid_spec=pltpu.PrefetchScalarGridSpec(
-            num_scalar_prefetch=1,
-            grid=(heads,),
-            in_specs=window + [pl.BlockSpec((1, 8, tile + 256), lambda h, s: (h, 0, 0))],
-            out_specs=pl.BlockSpec((head_dim, tile), lambda h, s: (h, 0)),
-        ),
-        out_shape=shape((feats, tile), f32),
-        compiler_params=params,
-        name="conv_forward",
-    )(spots, values, values, bases)
+    conv, window_values = once(
+        partial(conv_kernel, tile, heads), "conv_forward",
+        [shape((feats, tile), f32), shape((feats, tile + 256), bf16)],
+        [spots, values, bases],
+    )
 
     chip_buckets = buckets // chips
     sum_rows = 4 * width // tile
-    extra_rows = -(-(sum_rows + heads) // 16) * 16
+    count_rows = 2 * heads * code_rows // tile
+    extra_rows = -(-(sum_rows + count_rows) // 16) * 16
 
     keep, give, numerator = once(
         partial(context_kernel, heads), "context",
@@ -880,7 +912,9 @@
         mixer_kernel, "mixer",
         [shape((tok_rows, group_feats), bf16), shape((tok_rows, width), bf16)],
         [spots, keep, core_swap(give), ff_all],
-    )
+        blocks={3: pl.BlockSpec((width, group_feats), lambda i: (0, 2 * ff // group_feats))},
+    )
+    ff_all, mixer_part = lax.optimization_barrier((ff_all, mixer_part))
     first_hat, first_inverse, hidden, active, feed_part = once(
         hidden_kernel, "feed_forward",
         [
@@ -918,66 +952,68 @@
             spots, grad_second, first_part, head_swap(first_part), first_hat, first_inverse,
             norm_params, ff_all, second_sums,
         ],
-        outside=(0,),
     )
     gnum_send, grad_low, grad_high = once(
         partial(attention_back_kernel, heads), "attention_back",
         [
-            shape((chips, feats + extra_rows, tile), bf16),
+            shape((feats + extra_rows, tile), bf16),
             shape((feats, tok_rows), bf16),
             shape((feats, tok_rows), bf16),
         ],
         [spots, keep, core_swap(give), numerator, norm_sums, counts],
-        outside=(0, 1, 2),
-    )
-    gnum_got = across(gnum_send)
+    )
+    conv_grad, tap_parts = once(
+        partial(conv_back_kernel, tile, taps, heads), "conv_backward",
+        [shape((feats, 3 * tile), f32), shape((heads, 8, 128), f32)],
+        [spots, window_values, grad_low, grad_high, bases],
+    )
+    if ringed:
+        moved, gnum_parts, unused = ring(gnum_send, 1, False)
+        *moved, tap_parts = lax.optimization_barrier((*moved, tap_parts))
+        gnum_parts = [gnum_send]
+        for step in range(2, chips // 2 + 1):
+            gnum_parts += moved
+            moved = [
+                lax.ppermute(v, "seq", p)
+                for v, p in zip(moved, (ahead, behind))
+                if p is ahead or 2 * step < chips
+            ]
+        gnum_parts = [p[None] for p in gnum_parts + moved]
+    else:
+        gnum_parts = [
+            lax.all_gather(gnum_send, "seq", axis=0, tiled=False, axis_index_groups=planes_of)
+        ]
+    gnum_count = len(gnum_parts)
 
     columns = 2 * ff + group_feats
     feed_grads = pl.pallas_call(
         feed_grad_kernel,
         grid=(1,),
-        in_specs=[full(v) for v in (first_hat, norm_params, slope_low, feed_low, active)],
+        in_specs=[inside] * 5,
         out_specs=pl.BlockSpec((width, 2 * ff), lambda i: (0, 0)),
-        out_shape=shape((width, columns), bf16),
-        compiler_params=params,
+        out_shape=pltpu.HBM((width, columns), bf16),
+        compiler_params=small,
         name="feed_grads",
-    )(first_hat, norm_params, slope_low, feed_low, active)
+    )(*[in_vmem(v) for v in (first_hat, norm_params, slope_low, feed_low, active)])
     big_grad = pl.pallas_call(
         out_grad_kernel,
         grid=(1,),
-        in_specs=[full(mixer_low), full(context), anywhere],
+        in_specs=[inside, inside, anywhere],
         out_specs=pl.BlockSpec((width, group_feats), lambda i: (0, 2 * ff // group_feats)),
-        out_shape=shape((width, columns), bf16),
+        out_shape=pltpu.HBM((width, columns), bf16),
         input_output_aliases={2: 0},
-        compiler_params=params,
+        compiler_params=small,
         name="out_grads",
-    )(mixer_low, context, feed_grads)
+    )(in_vmem(mixer_low), in_vmem(context), feed_grads)
     big_owned = lax.psum_scatter(big_grad, "seq", scatter_dimension=0, tiled=True)
 
-    conv_grad, tap_parts = pl.pallas_call(
-        partial(conv_back_kernel, tile, taps),
-        grid_spec=pltpu.PrefetchScalarGridSpec(
-            num_scalar_prefetch=1,
-            grid=(heads,),
-            in_specs=window
-            + [half_rows] * 2
-            + [pl.BlockSpec((1, 8, tile + 256), lambda h, s: (h, 0, 0))],
-            out_specs=[
-                pl.BlockSpec((head_dim, 3 * tile), lambda h, s: (h, 0)),
-                pl.BlockSpec((1, 8, 128), lambda h, s: (h, 0, 0)),
-            ],
-        ),
-        out_shape=[shape((feats, 3 * tile), f32), shape((heads, 8, 128), f32)],
-        compiler_params=params,
-        name="conv_backward",
-    )(spots, values, values, grad_low, grad_high, bases)
-
-    qkv_send, back_keep, back_give = pl.pallas_call(
-        partial(backward_kernel, hashes, bits, rows, work, steps, heads, own_rows, parts),
+    qkv_send, back_keep, back_give, extras = pl.pallas_call(
+        partial(backward_kernel, hashes, bits, rows, work, steps, heads, own_rows, parts, gnum_count),
         grid=(2, steps),
         in_specs=[
             smem,
             *[anywhere] * parts,
+            *[inside] * gnum_count,
             resident(*qkv_all.shape),
             resident(*bit_w.shape),
             resident(*bit_wt.shape),
@@ -986,7 +1022,6 @@
             resident(feats, total + 256),
             resident(16, total),
             resident(heads, code_rows, 2 * head_dim),
-            stepped(0, blocks, feats, tile),
             resident(feats, 3 * tile),
             resident(*tap_parts.shape),
         ],
@@ -994,11 +1029,13 @@
             resident(chips, CORES * own_rows, 3 * feats + 64),
             stepped(1, blocks, width, tok_rows),
             stepped(1, blocks, width, tok_rows),
+            resident(chips, extra_rows, tile),
         ],
         out_shape=[
             shape((chips, CORES * own_rows, 3 * feats + 64), bf16),
             shape((chips, width, tok_rows), bf16),
             shape((chips, width, tok_rows), bf16),
+            shape((chips, extra_rows, tile), bf16),
         ],
         scratch_shapes=[
             pltpu.VMEM((heads, code_rows, 2 * head_dim), f32),
@@ -1008,13 +1045,14 @@
             pltpu.VMEM((heads, 2 * head_dim, code_rows), bf16),
             pltpu.VMEM((heads, code_rows, 2 * head_dim), bf16),
             pltpu.VMEM((seq_count, tok_rows, width), bf16),
+            pltpu.VMEM((chips, feats, tile), bf16),
             pltpu.SemaphoreType.DMA((parts,)),
         ],
         compiler_params=hash_params,
         name="hash_backward",
     )(
-        spots, *token_parts, qkv_all, bit_w, bit_wt,
-        q_unit, k_unit, values, inverses, tables, gnum_got, conv_grad, tap_parts,
+        spots, *token_parts, *[in_vmem(p) for p in gnum_parts], qkv_all, bit_w, bit_wt,
+        q_unit, k_unit, values, inverses, tables, conv_grad, tap_parts,
     )
 
     half = width // 2
@@ -1029,30 +1067,30 @@
         compiler_params=params,
         name="chip_sum",
     )(spots, back_keep, core_swap(back_give))
-    pair_sum = pl.pallas_call(
+    pair_sum, pair_done = pl.pallas_call(
         pair_sum_kernel,
         grid=(2,),
         in_specs=[per_chip(half, tok_rows), per_chip(half, tok_rows)],
-        out_specs=per_chip(half, tok_rows),
-        out_shape=shape((chips, half, tok_rows), bf16),
+        out_specs=[per_chip(half, tok_rows), pl.BlockSpec((8, 128), lambda i: (0, 0))],
+        out_shape=[shape((chips, half, tok_rows), bf16), shape((8, 128), f32)],
         compiler_params=params,
         name="pair_sum",
     )(keep, head_swap(give))
 
-    qkv_mine, qkv_give = piped(
+    qkv_mine, qkv_give = once(
         weight_sum_kernel, "weight_sum",
         [shape((own_rows, 3 * feats + 64), f32)] * 2,
-        [spots, across(qkv_send), pair_sum],
-        [None, None, anywhere],
+        [spots, across(qkv_send)],
+        after=[pair_done],
     )
     qkv_other = core_swap(qkv_give)
     back_got = across(pair_sum)
 
-    extras = gnum_got[:, feats:].astype(f32)
+    extras = extras.astype(f32)
     norm_half = jnp.sum(extras[:, :sum_rows], axis=0)
-    count_half = extras[:, sum_rows : sum_rows + heads].reshape(chips, heads, 2, tile // 2)
-    count_half = count_half[..., : chip_buckets * rows]
-    count_half = count_half.reshape(chips, heads, 2, CORES, chip_buckets // CORES, rows)
+    count_half = extras[:, sum_rows : sum_rows + count_rows]
+    count_half = count_half.reshape(chips, heads, 2, chips, CORES, chip_buckets // CORES, rows)
+    count_half = lax.dynamic_index_in_dim(count_half, spot, 3, keepdims=False)
     count_half = jnp.transpose(count_half[..., :hashes], (3, 0, 2, 5, 1, 4))
     count_mine = lax.dynamic_index_in_dim(count_half, core, 0, keepdims=False)
     count_give = lax.dynamic_index_in_dim(count_half, 1 - core, 0, keepdims=False)
@@ -1074,14 +1112,15 @@
     occupancy = occupancy * (buckets / (tok_rows * seq_count))
     conv_tap_grad = in_order(tap_half, swapped[norm_size + count_size :].reshape(heads, taps), 0)
 
-    matrix = lambda value: [shape(value.shape, f32)] * 3 + [shape(value.shape, bf16)]
+    flag = shape((8, 128), f32)
+    matrix = lambda value: [pltpu.HBM(value.shape, f32)] * 3 + [pltpu.HBM(value.shape, bf16)]
     (
         up_new, up_first_new, up_second_new, up_copy,
         down_new, down_first_new, down_second_new, down_copy,
-        out_new, out_first_new, out_second_new, out_copy,
+        out_new, out_first_new, out_second_new, out_copy, big_done,
     ) = piped(
         big_adam_kernel, "big_adam",
-        matrix(up_weight) + matrix(down_weight.T) + matrix(out_weight.T),
+        matrix(up_weight) + matrix(down_weight.T) + matrix(out_weight.T) + [flag],
         [
             big_owned, up_weight, up_first, up_second,
             down_weight.T, down_first.T, down_second.T,
@@ -1098,16 +1137,18 @@
     conv_new, conv_first_new, conv_second_new = adam_step(
         conv_taps, conv_first, conv_second, conv_tap_grad, CONV ** (-0.5)
     )
-    (back_low,) = piped(
+    (back_low,) = once(
         back_sum_kernel, "back_sum",
         [shape((half, tok_rows), bf16)],
-        [back_got, up_new, down_new, out_new],
-        [None] + [anywhere] * 3,
-    )
-    back_other = head_swap(back_low)
-    upper = jnp.where(side == 0, back_low, back_other)
-    lower = jnp.where(side == 0, back_other, back_low)
-    tokens_grad = grad_mixer + jnp.concatenate([upper, lower], axis=0).T.astype(f32)
+        [back_got],
+        after=[big_done],
+    )
+    (tokens_grad,) = once(
+        final_kernel, "tokens_grad",
+        [shape((tok_rows, width), f32)],
+        [spots, back_low, head_swap(back_low), grad_mixer],
+        outside=(0,),
+    )
     return (
         block_out,
         tokens_grad,

time: 291 us -> 272 us (0.935)
  Pallas kernels: 91 us -> 81.3 us
  waiting for transfers between devices: 118 us -> 109 us
  local copies, waits for them, and re-layouts: 24.7 us -> 18.5 us
  other arithmetic: 6.91 us -> 10 us
    all_to_all x1 -> x0, waiting for transfers between devices: 16.6 us -> none  [on_device(): gnum_got = across(gnum_send)]
    ppermute x8 -> x16, waiting for transfers between devices: 33.5 us -> 43.8 us  [the longest x8 30.1 us: ring(): moved = [lax.ppermute(v, 'seq', p) for v, p in zip(moved, (ahead, behind))]]
    unnamed x97 -> x84, local copies, waits for them, and re-layouts: 14.5 us -> 6.58 us
    ppermute x8 -> x16, starting transfers between devices: 9.78 us -> 17.1 us  [the longest x8 9.16 us: ring(): moved = [lax.ppermute(v, 'seq', p) for v, p in zip(moved, (ahead, behind))]]
    all_to_all x1, waiting for transfers between devices: 20.9 us -> 14 us  [on_device(): num_got = across(num_parts)]
    all_to_all x1, waiting for transfers between devices: 4.08 us -> 10.5 us  [on_device(): across(qkv_send)]
    pallas_call x10 -> x13, Pallas kernels: 23.7 us -> 18.2 us  [the longest x11 13.3 us: once(): pl.pallas_call(kernel, grid=(1,) if blocks else (), in_specs=specs, out_s...]
    ppermute x1, waiting for transfers between devices: 16.8 us -> 12 us  [on_device(): head_swap(give)]
  transfers between devices with their start and end apart: 32 -> 39, of which waited for: 19 -> 24; matrix products, arithmetic and copies ran while one was open for 5% -> 7% of each run, Pallas kernels for 28% -> 26%
where the time goes in v5:
time: 272 us; the launch traced here: 271 us
  waiting for transfers between devices  109 us (40%)
  Pallas kernels  81.3 us (30%)
  starting transfers between devices  38 us (14%)
  local copies, waits for them, and re-layouts  18.5 us (7%)
  between operations  14.7 us (5%)
  other arithmetic  10 us (4%)
    pallas_call x1, Pallas kernels, on_device(): pl.pallas_call(partial(backward_kernel, hashes, bits, rows, work, steps,...  32.2 us
    ppermute x8, waiting for transfers between devices, ring(): moved = [lax.ppermute(v, 'seq', p) for v, p in zip(moved, (ahead, behind))]  30.1 us
    pallas_call x1, Pallas kernels, on_device(): pl.pallas_call(partial(forward_kernel, hashes, bits, rows, work, steps, h...  18.4 us
    all_to_all x1, waiting for transfers between devices, on_device(): num_got = across(num_parts)  14 us
    pallas_call x11, Pallas kernels, once(): pl.pallas_call(kernel, grid=(1,) if blocks else (), in_specs=specs, out_s...  13.3 us
    all_to_all x1, waiting for transfers between devices, on_device(): back_got = across(pair_sum)  12.3 us
    ppermute x1, waiting for transfers between devices, on_device(): head_swap(give)  12 us
    all_to_all x1, waiting for transfers between devices, on_device(): across(qkv_send)  10.5 us
  transfers between devices with their start and end apart: 39, of which 24 were waited for; matrix products, arithmetic and copies ran while one was open for 7% of the time, Pallas kernels for 26%

profile of v5, /device:TPU:0, one launch (start us, length us, event | category | flops | bytes accessed | tf_op | source)
XLA Modules:
  0.0 271.5 jit_solution(1714213760064234553)
XLA Ops:
  11.6 3.0 %collective-permute-start.1 = (bf16[200,768]{1,0:T(8,128)(2,1)S(1)}, bf16[200,768]{1,0:T(8,128)(2,1)S(1)}, u32[]{:S(2)}, u32[]{:S(2)}) collective-permute-start(bf16[200,768]{1,0:T(8,128)(2,1)S(1)} %fusion.2), channel_id=1, source_target_pairs={{0,8},{2,10},{8,16},{10,18},{16,24},{18,26},{24,28},{26,30},{28,20... | collective-permute-start | bytes 921608 | tf_op jit(solution)/shard_map/ppermute | solution.py:703
  17.1 4.9 %collective-permute-done.1 = bf16[200,768]{1,0:T(8,128)(2,1)S(1)} collective-permute-done((bf16[200,768]{1,0:T(8,128)(2,1)S(1)}, bf16[200,768]{1,0:T(8,128)(2,1)S(1)}, u32[]{:S(2)}, u32[]{:S(2)}) %collective-permute-start.1) | collective-permute-done | bytes 307232 | tf_op jit(solution)/shard_map/ppermute | solution.py:703
  24.2 1.8 pack.1
  28.1 6.2 %collective-permute-done.3 = bf16[200,768]{1,0:T(8,128)(2,1)S(1)} collective-permute-done((bf16[200,768]{1,0:T(8,128)(2,1)S(1)}, bf16[200,768]{1,0:T(8,128)(2,1)S(1)}, u32[]{:S(2)}, u32[]{:S(2)}) %collective-permute-start.3) | collective-permute-done | bytes 307232 | tf_op jit(solution)/shard_map/ppermute | solution.py:703
  38.1 12.2 %collective-permute-done.5 = bf16[200,768]{1,0:T(8,128)(2,1)S(1)} collective-permute-done((bf16[200,768]{1,0:T(8,128)(2,1)S(1)}, bf16[200,768]{1,0:T(8,128)(2,1)S(1)}, u32[]{:S(2)}, u32[]{:S(2)}) %collective-permute-start.5) | collective-permute-done | bytes 307232 | tf_op jit(solution)/shard_map/ppermute | solution.py:703
  50.3 4.0 %collective-permute-done.6 = bf16[200,768]{1,0:T(8,128)(2,1)S(1)} collective-permute-done((bf16[200,768]{1,0:T(8,128)(2,1)S(1)}, bf16[200,768]{1,0:T(8,128)(2,1)S(1)}, u32[]{:S(2)}, u32[]{:S(2)}) %collective-permute-start.6) | collective-permute-done | bytes 307232 | tf_op jit(solution)/shard_map/ppermute | solution.py:703
  54.4 1.8 collective-permute-start.7
  57.0 4.0 %collective-permute-done.8 = bf16[72,768]{1,0:T(8,128)(2,1)S(1)} collective-permute-done((bf16[72,768]{1,0:T(8,128)(2,1)S(1)}, bf16[72,768]{1,0:T(8,128)(2,1)S(1)}, u32[]{:S(2)}, u32[]{:S(2)}) %collective-permute-start.8) | collective-permute-done | bytes 110624 | tf_op jit(solution)/shard_map/ppermute | solution.py:732
  63.9 18.4 %hash_forward.1 = (bf16[8,192,256]{2,1,0:T(8,128)(2,1)}, bf16[192,2048]{1,0:T(8,128)(2,1)}, bf16[192,2048]{1,0:T(8,128)(2,1)}, bf16[192,2304]{1,0:T(8,128)(2,1)}...) custom-call(s32[28]{0:T(128)} %pad_add_fusion.spots_ref, ...), custom_call_target="tpu_custom_call" | custom-call | tf_op jit(solution)/shard_map/hash_forward/pallas_call | solution.py:849
  82.3 3.7 %all-to-all-start = ((bf16[8,192,256]{2,1,0:T(8,128)(2,1)}), bf16[8,192,256]{2,1,0:T(8,128)(2,1)S(1)}, u32[]{:S(2)}, u32[]{:S(2)}) async-start(bf16[8,192,256]{2,1,0:T(8,128)(2,1)} %get-tuple-element.125), calls=%async_computation | async-start | bytes 1572864 | tf_op jit(solution)/shard_map/all_to_all | solution.py:889
  88.2 1.9 scatter.4.base_ref
  92.6 14.0 %all-to-all-done.got_ref = bf16[8,192,256]{2,1,0:T(8,128)(2,1)S(1)} async-done(((bf16[8,192,256]{2,1,0:T(8,128)(2,1)}), bf16[8,192,256]{2,1,0:T(8,128)(2,1)S(1)}, u32[]{:S(2)}, u32[]{:S(2)}) %all-to-all-start) | async-done | bytes 786464 | tf_op jit(solution)/shard_map/all_to_all | solution.py:889
  108.8 2.5 copy-done.1
  113.8 5.5 %collective-permute-done.18.other_ref = bf16[128,768]{1,0:T(8,128)(2,1)S(1)} collective-permute-done((bf16[128,768]{1,0:T(8,128)(2,1)S(1)}, bf16[128,768]{1,0:T(8,128)(2,1)S(1)}, u32[]{:S(2)}, u32[]{:S(2)}) %collective-permute-start.18) | collective-permute-done | bytes 196640 | tf_op jit(solution)/shard_map/ppermute | solution.py:927
  122.2 4.7 %collective-permute-done.19.other_ref = bf16[128,768]{1,0:T(8,128)(2,1)S(1)} collective-permute-done((bf16[128,768]{1,0:T(8,128)(2,1)S(1)}, bf16[128,768]{1,0:T(8,128)(2,1)S(1)}, u32[]{:S(2)}, u32[]{:S(2)}) %collective-permute-start.19) | collective-permute-done | bytes 196640 | tf_op jit(solution)/shard_map/ppermute | solution.py:939
  126.9 2.2 feed_back.1
  130.6 3.6 %feed_grads.1.all_ref = bf16[768,3456]{1,0:T(8,128)(2,1)} custom-call(f32[128,768]{1,0:T(8,128)S(1)} %get-tuple-element.133.hat_ref, f32[4,768]{1,0:T(4,128)S(1)} %copy-done.6, bf16[128,1536]{1,0:T(8,128)(2,1)S(1)} %get-tuple-element.167.slope_ref, bf16[128,768]{1,0:T(8,128)(2,1)S(1)} %get-tuple-element.168.feed_ref, ...), custom_call_target="tpu_custom_call" | custom-call | tf_op jit(solution)/shard_map/feed_grads/pallas_call | solution.py:989
  141.3 2.7 conv_backward.1
  146.9 2.9 %collective-permute-done.24 = bf16[240,256]{1,0:T(8,128)(2,1)S(1)} collective-permute-done((bf16[240,256]{1,0:T(8,128)(2,1)S(1)}, bf16[240,256]{1,0:T(8,128)(2,1)S(1)}, u32[]{:S(2)}, u32[]{:S(2)}) %collective-permute-start.24) | collective-permute-done | bytes 122912 | tf_op jit(solution)/shard_map/ppermute | solution.py:977
  151.8 2.9 %collective-permute-done.26 = bf16[240,256]{1,0:T(8,128)(2,1)S(1)} collective-permute-done((bf16[240,256]{1,0:T(8,128)(2,1)S(1)}, bf16[240,256]{1,0:T(8,128)(2,1)S(1)}, u32[]{:S(2)}, u32[]{:S(2)}) %collective-permute-start.26) | collective-permute-done | bytes 122912 | tf_op jit(solution)/shard_map/ppermute | solution.py:977
  155.7 3.9 %collective-permute-done.28 = bf16[240,256]{1,0:T(8,128)(2,1)S(1)} collective-permute-done((bf16[240,256]{1,0:T(8,128)(2,1)S(1)}, bf16[240,256]{1,0:T(8,128)(2,1)S(1)}, u32[]{:S(2)}, u32[]{:S(2)}) %collective-permute-start.28) | collective-permute-done | bytes 122912 | tf_op jit(solution)/shard_map/ppermute | solution.py:977
  159.6 32.2 %hash_backward.1 = (bf16[8,96,640]{2,1,0:T(8,128)(2,1)}, bf16[8,768,128]{2,1,0:T(8,128)(2,1)}, bf16[8,768,128]{2,1,0:T(8,128)(2,1)}, bf16[8,48,256]{2,1,0:T(8,128)(2,1)}) custom-call(s32[28]{0:T(128)} %pad_add_fusion.spots_ref, bf16[1,200,768]{2,1,0:T(8,128)(2,1)} %bitcast.92, bf16[1,200,768]{2,1,0:T(8,128)(2,1)} %bitcast.104, ...), custom_call_target="tpu_custom_call" | custom-call | tf_op jit(solution)/shard_map/hash_backward/pallas_call | solution.py:1010
  191.9 4.4 %all-to-all-start.2 = ((bf16[8,96,640]{2,1,0:T(8,128)(2,1)}), bf16[8,96,640]{2,1,0:T(8,128)(2,1)S(1)}, u32[]{:S(2)}, u32[]{:S(2)}) async-start(bf16[8,96,640]{2,1,0:T(8,128)(2,1)} %get-tuple-element.173), calls=%async_computation.3 | async-start | bytes 1966080 | tf_op jit(solution)/shard_map/all_to_all | solution.py:1083
  196.3 3.0 %chip_sum.1 = (bf16[8,384,128]{2,1,0:T(8,128)(2,1)}, bf16[8,384,128]{2,1,0:T(8,128)(2,1)}) custom-call(s32[28]{0:T(128)} %pad_add_fusion.spots_ref, bf16[8,768,128]{2,1,0:T(8,128)(2,1)} %get-tuple-element.160.own_ref, bf16[8,768,128]{2,1,0:T(8,128)(2,1)} %collective-permute-done.29.other_ref), custom_call_target="tpu_custom_call" | custom-call | tf_op jit(solution)/shard_map/chip_sum/pallas_call | solution.py:1061
  201.6 3.4 %reshape.152 = f32[8,3,2,8,2,8,8]{6,5,4,3,2,1,0:T(8,128)} reshape(f32[8,24,256]{2,1,0:T(8,128)S(1)} %slice.102) | data formatting | bytes 393216 | tf_op jit(solution)/shard_map/reshape | solution.py:1092
  207.3 12.0 %collective-permute-done.30.other_ref = bf16[8,384,128]{2,1,0:T(8,128)(2,1)} collective-permute-done((bf16[8,384,128]{2,1,0:T(8,128)(2,1)}, bf16[8,384,128]{2,1,0:T(8,128)(2,1)}, u32[]{:S(2)}, u32[]{:S(2)}) %collective-permute-start.30) | collective-permute-done | bytes 786464 | tf_op jit(solution)/shard_map/ppermute | solution.py:1078
  219.2 2.2 pair_sum.1
  221.4 10.5 %all-to-all-done.2.got_ref = bf16[8,96,640]{2,1,0:T(8,128)(2,1)S(1)} async-done(((bf16[8,96,640]{2,1,0:T(8,128)(2,1)}), bf16[8,96,640]{2,1,0:T(8,128)(2,1)S(1)}, u32[]{:S(2)}, u32[]{:S(2)}) %all-to-all-start.2) | async-done | bytes 983072 | tf_op jit(solution)/shard_map/all_to_all | solution.py:1083
  233.4 3.8 %all-to-all-start.1 = ((bf16[8,384,128]{2,1,0:T(8,128)(2,1)}), bf16[8,384,128]{2,1,0:T(8,128)(2,1)S(1)}, u32[]{:S(2)}, u32[]{:S(2)}) async-start(bf16[8,384,128]{2,1,0:T(8,128)(2,1)} %get-tuple-element.164), calls=%async_computation.1 | async-start | bytes 1572864 | tf_op jit(solution)/shard_map/all_to_all | solution.py:1087
  242.0 3.2 %big_adam.1 = (f32[48,1536]{1,0:T(8,128)}, f32[48,1536]{1,0:T(8,128)}, f32[48,1536]{1,0:T(8,128)}, bf16[48,1536]{1,0:T(8,128)(2,1)}, f32[48,1536]{1,0:T(8,128)},...) custom-call(bf16[48,3456]{1,0:T(8,128)(2,1)} %reduce-scatter.2.clone, ...), custom_call_target="tpu_custom_call" | custom-call | tf_op jit(solution)/shard_map/big_adam/pallas_call | solution.py:779
  245.2 12.3 %all-to-all-done.1.got_ref = bf16[8,384,128]{2,1,0:T(8,128)(2,1)S(1)} async-done(((bf16[8,384,128]{2,1,0:T(8,128)(2,1)}), bf16[8,384,128]{2,1,0:T(8,128)(2,1)S(1)}, u32[]{:S(2)}, u32[]{:S(2)}) %all-to-all-start.1) | async-done | bytes 786464 | tf_op jit(solution)/shard_map/all_to_all | solution.py:1087
  260.9 2.3 qkv_adam.1
  (206 shorter events, 60.6 us)
Async XLA Ops:
  7.2 101.6 %all-gather.2.cloned.1.call-start = ((), (), s32[]{:S(2)}) async-start(), calls=%async_computation.4 | async-start | bytes 5640192 | tf_op jit(solution)/shard_map/all_gather | solution.py:834
  11.6 10.5 %collective-permute-start.1 = (bf16[200,768]{1,0:T(8,128)(2,1)S(1)}, bf16[200,768]{1,0:T(8,128)(2,1)S(1)}, u32[]{:S(2)}, u32[]{:S(2)}) collective-permute-start(bf16[200,768]{1,0:T(8,128)(2,1)S(1)} %fusion.2), channel_id=1, source_target_pairs={{0,8},{2,10},{8,16},{10,18},{16,24},{18,26},{24,28},{26,30},{28,20... | collective-permute-start | bytes 921608 | tf_op jit(solution)/shard_map/ppermute | solution.py:703
  14.5 9.1 %collective-permute-start.2 = (bf16[200,768]{1,0:T(8,128)(2,1)S(1)}, bf16[200,768]{1,0:T(8,128)(2,1)S(1)}, u32[]{:S(2)}, u32[]{:S(2)}) collective-permute-start(bf16[200,768]{1,0:T(8,128)(2,1)S(1)} %fusion.2), channel_id=1, source_target_pairs={{8,0},{10,2},{16,8},{18,10},{24,16},{26,18},{28,24},{30,26},{20,28... | collective-permute-start | bytes 921608 | tf_op jit(solution)/shard_map/ppermute | solution.py:703
  26.0 8.2 %collective-permute-start.3 = (bf16[200,768]{1,0:T(8,128)(2,1)S(1)}, bf16[200,768]{1,0:T(8,128)(2,1)S(1)}, u32[]{:S(2)}, u32[]{:S(2)}) collective-permute-start(bf16[200,768]{1,0:T(8,128)(2,1)S(1)} %collective-permute-done.1), channel_id=1, source_target_pairs={{0,8},{2,10},{8,16},{10,18},{16,24},{18,26},{24,28},{26,30},{28,20... | collective-permute-start | bytes 921608 | tf_op jit(solution)/shard_map/ppermute | solution.py:703
  27.7 7.9 %collective-permute-start.4 = (bf16[200,768]{1,0:T(8,128)(2,1)S(1)}, bf16[200,768]{1,0:T(8,128)(2,1)S(1)}, u32[]{:S(2)}, u32[]{:S(2)}) collective-permute-start(bf16[200,768]{1,0:T(8,128)(2,1)S(1)} %collective-permute-done.2), channel_id=1, source_target_pairs={{8,0},{10,2},{16,8},{18,10},{24,16},{26,18},{28,24},{30,26},{20,28... | collective-permute-start | bytes 921608 | tf_op jit(solution)/shard_map/ppermute | solution.py:703
  35.6 14.7 %collective-permute-start.5 = (bf16[200,768]{1,0:T(8,128)(2,1)S(1)}, bf16[200,768]{1,0:T(8,128)(2,1)S(1)}, u32[]{:S(2)}, u32[]{:S(2)}) collective-permute-start(bf16[200,768]{1,0:T(8,128)(2,1)S(1)} %collective-permute-done.3), channel_id=1, source_target_pairs={{0,8},{2,10},{8,16},{10,18},{16,24},{18,26},{24,28},{26,30},{28,20... | collective-permute-start | bytes 921608 | tf_op jit(solution)/shard_map/ppermute | solution.py:703
  37.2 17.2 %collective-permute-start.6 = (bf16[200,768]{1,0:T(8,128)(2,1)S(1)}, bf16[200,768]{1,0:T(8,128)(2,1)S(1)}, u32[]{:S(2)}, u32[]{:S(2)}) collective-permute-start(bf16[200,768]{1,0:T(8,128)(2,1)S(1)} %collective-permute-done.4), channel_id=1, source_target_pairs={{8,0},{10,2},{16,8},{18,10},{24,16},{26,18},{28,24},{30,26},{20,28... | collective-permute-start | bytes 921608 | tf_op jit(solution)/shard_map/ppermute | solution.py:703
  37.6 18.8 %collective-permute-start.9 = (bf16[200,768]{1,0:T(8,128)(2,1)S(1)}, bf16[200,768]{1,0:T(8,128)(2,1)S(1)}, u32[]{:S(2)}, u32[]{:S(2)}) collective-permute-start(bf16[200,768]{1,0:T(8,128)(2,1)S(1)} %fusion.2), channel_id=1, source_target_pairs={{0,2},{2,0},{4,6},{6,4},{8,10},{10,8},{12,14},{14,12},{16,18},{18,... | collective-permute-start | bytes 921608 | tf_op jit(solution)/shard_map/ppermute | solution.py:736
  37.6 18.8 %collective-permute-start.10 = (bf16[200,768]{1,0:T(8,128)(2,1)S(1)}, bf16[200,768]{1,0:T(8,128)(2,1)S(1)}, u32[]{:S(2)}, u32[]{:S(2)}) collective-permute-start(bf16[200,768]{1,0:T(8,128)(2,1)S(1)} %collective-permute-done.1), channel_id=1, source_target_pairs={{0,2},{2,0},{4,6},{6,4},{8,10},{10,8},{12,14},{14,12},{16,18},{18,... | collective-permute-start | bytes 921608 | tf_op jit(solution)/shard_map/ppermute | solution.py:736
  38.1 23.3 %collective-permute-start.11 = (bf16[200,768]{1,0:T(8,128)(2,1)S(1)}, bf16[200,768]{1,0:T(8,128)(2,1)S(1)}, u32[]{:S(2)}, u32[]{:S(2)}) collective-permute-start(bf16[200,768]{1,0:T(8,128)(2,1)S(1)} %collective-permute-done.2), channel_id=1, source_target_pairs={{0,2},{2,0},{4,6},{6,4},{8,10},{10,8},{12,14},{14,12},{16,18},{18,... | collective-permute-start | bytes 921608 | tf_op jit(solution)/shard_map/ppermute | solution.py:736
  54.4 6.6 %collective-permute-start.7 = (bf16[128,768]{1,0:T(8,128)(2,1)S(1)}, bf16[128,768]{1,0:T(8,128)(2,1)S(1)}, u32[]{:S(2)}, u32[]{:S(2)}) collective-permute-start(bf16[128,768]{1,0:T(8,128)(2,1)S(1)} %slice.87), channel_id=1, source_target_pairs={{0,8},{2,10},{8,16},{10,18},{16,24},{18,26},{24,28},{26,30},{28,20... | collective-permute-start | bytes 589832 | tf_op jit(solution)/shard_map/ppermute | solution.py:731
  56.2 4.7 %collective-permute-start.8 = (bf16[72,768]{1,0:T(8,128)(2,1)S(1)}, bf16[72,768]{1,0:T(8,128)(2,1)S(1)}, u32[]{:S(2)}, u32[]{:S(2)}) collective-permute-start(bf16[72,768]{1,0:T(8,128)(2,1)S(1)} %slice.88), channel_id=1, source_target_pairs={{8,0},{10,2},{16,8},{18,10},{24,16},{26,18},{28,24},{30,26},{20,28... | collective-permute-start | bytes 331784 | tf_op jit(solution)/shard_map/ppermute | solution.py:732
  56.4 5.1 %collective-permute-start.12 = (bf16[200,768]{1,0:T(8,128)(2,1)S(1)}, bf16[200,768]{1,0:T(8,128)(2,1)S(1)}, u32[]{:S(2)}, u32[]{:S(2)}) collective-permute-start(bf16[200,768]{1,0:T(8,128)(2,1)S(1)} %collective-permute-done.3), channel_id=1, source_target_pairs={{0,2},{2,0},{4,6},{6,4},{8,10},{10,8},{12,14},{14,12},{16,18},{18,... | collective-permute-start | bytes 921608 | tf_op jit(solution)/shard_map/ppermute | solution.py:736
  56.5 5.1 %collective-permute-start.13 = (bf16[200,768]{1,0:T(8,128)(2,1)S(1)}, bf16[200,768]{1,0:T(8,128)(2,1)S(1)}, u32[]{:S(2)}, u32[]{:S(2)}) collective-permute-start(bf16[200,768]{1,0:T(8,128)(2,1)S(1)} %collective-permute-done.4), channel_id=1, source_target_pairs={{0,2},{2,0},{4,6},{6,4},{8,10},{10,8},{12,14},{14,12},{16,18},{18,... | collective-permute-start | bytes 921608 | tf_op jit(solution)/shard_map/ppermute | solution.py:736
  82.3 24.3 %all-to-all-start = ((bf16[8,192,256]{2,1,0:T(8,128)(2,1)}), bf16[8,192,256]{2,1,0:T(8,128)(2,1)S(1)}, u32[]{:S(2)}, u32[]{:S(2)}) async-start(bf16[8,192,256]{2,1,0:T(8,128)(2,1)} %get-tuple-element.125), calls=%async_computation | async-start | bytes 1572864 | tf_op jit(solution)/shard_map/all_to_all | solution.py:889
  86.0 155.9 %reduce-scatter.2.cloned.1.call-start = ((), (), s32[]{:S(2)}) async-start(), calls=%async_computation.5 | async-start | bytes 5640192 | tf_op jit(solution)/shard_map/reduce_scatter | solution.py:1008
  112.2 7.0 %collective-permute-start.18 = (bf16[128,768]{1,0:T(8,128)(2,1)S(1)}, bf16[128,768]{1,0:T(8,128)(2,1)S(1)}, u32[]{:S(2)}, u32[]{:S(2)}) collective-permute-start(bf16[128,768]{1,0:T(8,128)(2,1)S(1)} %get-tuple-element.131.own_ref), channel_id=1, source_target_pairs={{0,1},{1,0},{2,3},{3,2},{4,5},{5,4},{6,7},{7,6},{8,9},{9,8},{10,11... | collective-permute-start | bytes 589832 | tf_op jit(solution)/shard_map/ppermute | solution.py:927
  120.7 6.2 %collective-permute-start.19 = (bf16[128,768]{1,0:T(8,128)(2,1)S(1)}, bf16[128,768]{1,0:T(8,128)(2,1)S(1)}, u32[]{:S(2)}, u32[]{:S(2)}) collective-permute-start(bf16[128,768]{1,0:T(8,128)(2,1)S(1)} %get-tuple-element.135.own_ref), channel_id=1, source_target_pairs={{0,1},{1,0},{2,3},{3,2},{4,5},{5,4},{6,7},{7,6},{8,9},{9,8},{10,11... | collective-permute-start | bytes 589832 | tf_op jit(solution)/shard_map/ppermute | solution.py:939
  129.1 5.7 %collective-permute-start.20 = (bf16[128,768]{1,0:T(8,128)(2,1)S(1)}, bf16[128,768]{1,0:T(8,128)(2,1)S(1)}, u32[]{:S(2)}, u32[]{:S(2)}) collective-permute-start(bf16[128,768]{1,0:T(8,128)(2,1)S(1)} %get-tuple-element.138.own_ref), channel_id=1, source_target_pairs={{0,1},{1,0},{2,3},{3,2},{4,5},{5,4},{6,7},{7,6},{8,9},{9,8},{10,11... | collective-permute-start | bytes 589832 | tf_op jit(solution)/shard_map/ppermute | solution.py:952
  139.2 5.6 %collective-permute-start.22 = (bf16[240,256]{1,0:T(8,128)(2,1)S(1)}, bf16[240,256]{1,0:T(8,128)(2,1)S(1)}, u32[]{:S(2)}, u32[]{:S(2)}) collective-permute-start(bf16[240,256]{1,0:T(8,128)(2,1)S(1)} %get-tuple-element.146), channel_id=1, source_target_pairs={{0,8},{2,10},{8,16},{10,18},{16,24},{18,26},{24,28},{26,30},{28,20... | collective-permute-start | bytes 368648 | tf_op jit(solution)/shard_map/ppermute | solution.py:703
  139.5 5.3 %collective-permute-start.23 = (bf16[240,256]{1,0:T(8,128)(2,1)S(1)}, bf16[240,256]{1,0:T(8,128)(2,1)S(1)}, u32[]{:S(2)}, u32[]{:S(2)}) collective-permute-start(bf16[240,256]{1,0:T(8,128)(2,1)S(1)} %get-tuple-element.146), channel_id=1, source_target_pairs={{8,0},{10,2},{16,8},{18,10},{24,16},{26,18},{28,24},{30,26},{20,28... | collective-permute-start | bytes 368648 | tf_op jit(solution)/shard_map/ppermute | solution.py:703
  144.8 4.9 %collective-permute-start.24 = (bf16[240,256]{1,0:T(8,128)(2,1)S(1)}, bf16[240,256]{1,0:T(8,128)(2,1)S(1)}, u32[]{:S(2)}, u32[]{:S(2)}) collective-permute-start(bf16[240,256]{1,0:T(8,128)(2,1)S(1)} %collective-permute-done.22), channel_id=1, source_target_pairs={{0,8},{2,10},{8,16},{10,18},{16,24},{18,26},{24,28},{26,30},{28,20... | collective-permute-start | bytes 368648 | tf_op jit(solution)/shard_map/ppermute | solution.py:977
  145.1 4.9 %collective-permute-start.25 = (bf16[240,256]{1,0:T(8,128)(2,1)S(1)}, bf16[240,256]{1,0:T(8,128)(2,1)S(1)}, u32[]{:S(2)}, u32[]{:S(2)}) collective-permute-start(bf16[240,256]{1,0:T(8,128)(2,1)S(1)} %collective-permute-done.23), channel_id=1, source_target_pairs={{8,0},{10,2},{16,8},{18,10},{24,16},{26,18},{28,24},{30,26},{20,28... | collective-permute-start | bytes 368648 | tf_op jit(solution)/shard_map/ppermute | solution.py:977
  149.8 5.0 %collective-permute-start.26 = (bf16[240,256]{1,0:T(8,128)(2,1)S(1)}, bf16[240,256]{1,0:T(8,128)(2,1)S(1)}, u32[]{:S(2)}, u32[]{:S(2)}) collective-permute-start(bf16[240,256]{1,0:T(8,128)(2,1)S(1)} %collective-permute-done.24), channel_id=1, source_target_pairs={{0,8},{2,10},{8,16},{10,18},{16,24},{18,26},{24,28},{26,30},{28,20... | collective-permute-start | bytes 368648 | tf_op jit(solution)/shard_map/ppermute | solution.py:977
  150.0 5.6 %collective-permute-start.27 = (bf16[240,256]{1,0:T(8,128)(2,1)S(1)}, bf16[240,256]{1,0:T(8,128)(2,1)S(1)}, u32[]{:S(2)}, u32[]{:S(2)}) collective-permute-start(bf16[240,256]{1,0:T(8,128)(2,1)S(1)} %collective-permute-done.25), channel_id=1, source_target_pairs={{8,0},{10,2},{16,8},{18,10},{24,16},{26,18},{28,24},{30,26},{20,28... | collective-permute-start | bytes 368648 | tf_op jit(solution)/shard_map/ppermute | solution.py:977
  154.7 4.9 %collective-permute-start.28 = (bf16[240,256]{1,0:T(8,128)(2,1)S(1)}, bf16[240,256]{1,0:T(8,128)(2,1)S(1)}, u32[]{:S(2)}, u32[]{:S(2)}) collective-permute-start(bf16[240,256]{1,0:T(8,128)(2,1)S(1)} %collective-permute-done.26), channel_id=1, source_target_pairs={{0,8},{2,10},{8,16},{10,18},{16,24},{18,26},{24,28},{26,30},{28,20... | collective-permute-start | bytes 368648 | tf_op jit(solution)/shard_map/ppermute | solution.py:977
  191.8 4.5 %collective-permute-start.29 = (bf16[8,768,128]{2,1,0:T(8,128)(2,1)}, bf16[8,768,128]{2,1,0:T(8,128)(2,1)}, u32[]{:S(2)}, u32[]{:S(2)}) collective-permute-start(bf16[8,768,128]{2,1,0:T(8,128)(2,1)} %get-tuple-element.161), channel_id=1, source_target_pairs={{0,2},{2,0},{4,6},{6,4},{8,10},{10,8},{12,14},{14,12},{16,18},{18,... | collective-permute-start | bytes 4718600 | tf_op jit(solution)/shard_map/ppermute | solution.py:1069
  191.9 40.1 %all-to-all-start.2 = ((bf16[8,96,640]{2,1,0:T(8,128)(2,1)}), bf16[8,96,640]{2,1,0:T(8,128)(2,1)S(1)}, u32[]{:S(2)}, u32[]{:S(2)}) async-start(bf16[8,96,640]{2,1,0:T(8,128)(2,1)} %get-tuple-element.173), calls=%async_computation.3 | async-start | bytes 1966080 | tf_op jit(solution)/shard_map/all_to_all | solution.py:1083
  199.3 20.0 %collective-permute-start.30 = (bf16[8,384,128]{2,1,0:T(8,128)(2,1)}, bf16[8,384,128]{2,1,0:T(8,128)(2,1)}, u32[]{:S(2)}, u32[]{:S(2)}) collective-permute-start(bf16[8,384,128]{2,1,0:T(8,128)(2,1)} %get-tuple-element.163), channel_id=1, source_target_pairs={{0,1},{1,0},{2,3},{3,2},{4,5},{5,4},{6,7},{7,6},{8,9},{9,8},{10,11... | collective-permute-start | bytes 2359304 | tf_op jit(solution)/shard_map/ppermute | solution.py:1078
  233.4 24.1 %all-to-all-start.1 = ((bf16[8,384,128]{2,1,0:T(8,128)(2,1)}), bf16[8,384,128]{2,1,0:T(8,128)(2,1)S(1)}, u32[]{:S(2)}, u32[]{:S(2)}) async-start(bf16[8,384,128]{2,1,0:T(8,128)(2,1)} %get-tuple-element.164), calls=%async_computation.1 | async-start | bytes 1572864 | tf_op jit(solution)/shard_map/all_to_all | solution.py:1087
  237.4 23.4 %collective-permute-start.33 = (f32[48,640]{1,0:T(8,128)S(1)}, f32[48,640]{1,0:T(8,128)}, u32[]{:S(2)}, u32[]{:S(2)}) collective-permute-start(f32[48,640]{1,0:T(8,128)S(1)} %get-tuple-element.176), channel_id=1, source_target_pairs={{0,2},{2,0},{4,6},{6,4},{8,10},{10,8},{12,14},{14,12},{16,18},{18,... | collective-permute-start | bytes 368648 | tf_op jit(solution)/shard_map/ppermute | solution.py:1086
  258.2 4.9 %collective-permute-start.31 = (bf16[384,128]{1,0:T(8,128)(2,1)S(1)}, bf16[384,128]{1,0:T(8,128)(2,1)S(1)}, u32[]{:S(2)}, u32[]{:S(2)}) collective-permute-start(bf16[384,128]{1,0:T(8,128)(2,1)S(1)} %back_sum.1.mine_ref), channel_id=1, source_target_pairs={{0,1},{1,0},{2,3},{3,2},{4,5},{5,4},{6,7},{7,6},{8,9},{9,8},{10,11... | collective-permute-start | bytes 294920 | tf_op jit(solution)/shard_map/ppermute | solution.py:1149
  (49 other events, 656.9 us)
Sparse Core Ops, SparseCore 0:
  26.2 61.5 all-gather.1
  137.3 93.2 reduce-scatter.1

commit v6 on v5

--- a/solution.py
+++ b/solution.py
@@ -579,9 +579,16 @@
     give_ref[...] = jnp.where(zero, second, first).astype(bf16)
 
 
-def pair_sum_kernel(own_ref, other_ref, out_ref, flag_ref):
+def pair_sum_kernel(spots_ref, own_ref, other_ref, *refs):
+    out_refs, flag_ref = refs[:-1], refs[-1]
     flag_ref[...] = jnp.zeros_like(flag_ref)
-    out_ref[...] = (own_ref[...].astype(f32) + other_ref[...].astype(f32)).astype(bf16)
+    for d, out_ref in enumerate(out_refs):
+        if len(out_refs) == 1:
+            total = own_ref[...].astype(f32) + other_ref[...].astype(f32)
+        else:
+            chip = spots_ref[1] ^ d
+            total = own_ref[chip].astype(f32) + other_ref[chip].astype(f32)
+        out_ref[...] = total.astype(bf16)
 
 
 def weight_sum_kernel(spots_ref, got_ref, after_ref, keep_ref, give_ref):
@@ -627,8 +634,11 @@
     out_ref[...] = mixer_ref[...] + jnp.transpose(total)
 
 
-def back_sum_kernel(got_ref, *refs):
-    refs[-1][...] = jnp.sum(got_ref[...].astype(f32), axis=0).astype(bf16)
+def back_sum_kernel(*refs):
+    total = jnp.sum(refs[0][...].astype(f32), axis=0)
+    for ref in refs[1:-2]:
+        total = total + jnp.sum(ref[...].astype(f32), axis=0)
+    refs[-1][...] = total.astype(bf16)
 
 
 def on_device(
@@ -1067,24 +1077,33 @@
         compiler_params=params,
         name="chip_sum",
     )(spots, back_keep, core_swap(back_give))
-    pair_sum, pair_done = pl.pallas_call(
-        pair_sum_kernel,
-        grid=(2,),
-        in_specs=[per_chip(half, tok_rows), per_chip(half, tok_rows)],
-        out_specs=[per_chip(half, tok_rows), pl.BlockSpec((8, 128), lambda i: (0, 0))],
-        out_shape=[shape((chips, half, tok_rows), bf16), shape((8, 128), f32)],
-        compiler_params=params,
-        name="pair_sum",
-    )(keep, head_swap(give))
+    *pair_sums, pair_done = once(
+        pair_sum_kernel, "pair_sum",
+        [shape((half, tok_rows) if ringed else (chips, half, tok_rows), bf16)]
+        * (chips if ringed else 1)
+        + [shape((8, 128), f32)],
+        [spots, keep, head_swap(give)],
+        outside=tuple(range(1, chips)) if ringed else (),
+    )
+    qkv_got = across(qkv_send)
+    if ringed:
+        back_got = [pair_sums[0]]
+        for d in range(1, chips):
+            perm = [(CORES * c + k, CORES * (c ^ d) + k) for c in range(chips) for k in range(CORES)]
+            back_got.append(lax.ppermute(pair_sums[d], "seq", perm))
+        qkv_got, *tied = lax.optimization_barrier((qkv_got, *back_got[1:5]))
+        back_got = [back_got[0]] + tied + back_got[1 + len(tied) :]
+        back_got = [p[None] for p in back_got]
+    else:
+        back_got = [across(pair_sums[0])]
 
     qkv_mine, qkv_give = once(
         weight_sum_kernel, "weight_sum",
         [shape((own_rows, 3 * feats + 64), f32)] * 2,
-        [spots, across(qkv_send)],
+        [spots, qkv_got],
         after=[pair_done],
     )
     qkv_other = core_swap(qkv_give)
-    back_got = across(pair_sum)
 
     extras = extras.astype(f32)
     norm_half = jnp.sum(extras[:, :sum_rows], axis=0)
@@ -1140,7 +1159,7 @@
     (back_low,) = once(
         back_sum_kernel, "back_sum",
         [shape((half, tok_rows), bf16)],
-        [back_got],
+        back_got,
         after=[big_done],
     )
     (tokens_grad,) = once(

time: 272 us -> 270 us (level)
  waiting for transfers between devices: 109 us -> 87.5 us
  starting transfers between devices: 38 us -> 46 us
  local copies, waits for them, and re-layouts: 18.5 us -> 25.5 us
    all_to_all x2 -> x1, waiting for transfers between devices: 22.8 us -> 5.78 us  [on_device(): qkv_got = across(qkv_send)]
    ppermute x0 -> x7, starting transfers between devices: none -> 12.3 us  [on_device(): back_got.append(lax.ppermute(pair_sums[d], 'seq', perm))]
    ppermute x1, waiting for transfers between devices: 12 us -> 6.32 us  [on_device(): head_swap(give)]
    all_to_all x2 -> x1, starting transfers between devices: 8.21 us -> 4.4 us  [on_device(): qkv_got = across(qkv_send)]
    pallas_call x11 -> x12, Pallas kernels: 13.3 us -> 16.2 us  [once(): pl.pallas_call(kernel, grid=(1,) if blocks else (), in_specs=specs, out_s...]
    unnamed x84 -> x80, local copies, waits for them, and re-layouts: 6.58 us -> 7.19 us
  transfers between devices with their start and end apart: 39 -> 45, of which waited for: 24 -> 24; matrix products, arithmetic and copies ran while one was open for 7% -> 10% of each run, Pallas kernels for 26% -> 27%
where the time goes in v6:
time: 270 us; the launch traced here: 268 us
  waiting for transfers between devices  87.5 us (32%)
  Pallas kernels  81.9 us (30%)
  starting transfers between devices  46 us (17%)
  local copies, waits for them, and re-layouts  25.5 us (9%)
  between operations  14.7 us (5%)
  other arithmetic  12.5 us (5%)
    pallas_call x1, Pallas kernels, on_device(): pl.pallas_call(partial(backward_kernel, hashes, bits, rows, work, steps,...  32.2 us
    ppermute x8, waiting for transfers between devices, ring(): moved = [lax.ppermute(v, 'seq', p) for v, p in zip(moved, (ahead, behind))]  30.1 us
    pallas_call x1, Pallas kernels, on_device(): pl.pallas_call(partial(forward_kernel, hashes, bits, rows, work, steps, h...  18.3 us
    pallas_call x12, Pallas kernels, once(): pl.pallas_call(kernel, grid=(1,) if blocks else (), in_specs=specs, out_s...  16.2 us
    all_to_all x1, waiting for transfers between devices, on_device(): num_got = across(num_parts)  14 us
    ppermute x7, starting transfers between devices, on_device(): back_got.append(lax.ppermute(pair_sums[d], 'seq', perm))  12.3 us
    ppermute x5, waiting for transfers between devices, on_device(): lax.ppermute(v, 'seq', p)  9.73 us
    ppermute x8, starting transfers between devices, ring(): moved = [lax.ppermute(v, 'seq', p) for v, p in zip(moved, (ahead, behind))]  9.16 us
  transfers between devices with their start and end apart: 45, of which 24 were waited for; matrix products, arithmetic and copies ran while one was open for 10% of the time, Pallas kernels for 27%

profile of v6, /device:TPU:0, one launch (start us, length us, event | category | flops | bytes accessed | tf_op | source)
XLA Modules:
  0.0 268.0 jit_solution(1313438947342167458)
XLA Ops:
  11.6 3.0 %collective-permute-start.1 = (bf16[200,768]{1,0:T(8,128)(2,1)S(1)}, bf16[200,768]{1,0:T(8,128)(2,1)S(1)}, u32[]{:S(2)}, u32[]{:S(2)}) collective-permute-start(bf16[200,768]{1,0:T(8,128)(2,1)S(1)} %fusion.2), channel_id=1, source_target_pairs={{0,8},{2,10},{8,16},{10,18},{16,24},{18,26},{24,28},{26,30},{28,20... | collective-permute-start | bytes 921608 | tf_op jit(solution)/shard_map/ppermute | solution.py:713
  17.1 4.9 %collective-permute-done.1 = bf16[200,768]{1,0:T(8,128)(2,1)S(1)} collective-permute-done((bf16[200,768]{1,0:T(8,128)(2,1)S(1)}, bf16[200,768]{1,0:T(8,128)(2,1)S(1)}, u32[]{:S(2)}, u32[]{:S(2)}) %collective-permute-start.1) | collective-permute-done | bytes 307232 | tf_op jit(solution)/shard_map/ppermute | solution.py:713
  24.2 1.8 pack.1
  28.1 6.2 %collective-permute-done.3 = bf16[200,768]{1,0:T(8,128)(2,1)S(1)} collective-permute-done((bf16[200,768]{1,0:T(8,128)(2,1)S(1)}, bf16[200,768]{1,0:T(8,128)(2,1)S(1)}, u32[]{:S(2)}, u32[]{:S(2)}) %collective-permute-start.3) | collective-permute-done | bytes 307232 | tf_op jit(solution)/shard_map/ppermute | solution.py:713
  38.1 12.2 %collective-permute-done.5 = bf16[200,768]{1,0:T(8,128)(2,1)S(1)} collective-permute-done((bf16[200,768]{1,0:T(8,128)(2,1)S(1)}, bf16[200,768]{1,0:T(8,128)(2,1)S(1)}, u32[]{:S(2)}, u32[]{:S(2)}) %collective-permute-start.5) | collective-permute-done | bytes 307232 | tf_op jit(solution)/shard_map/ppermute | solution.py:713
  50.3 4.0 %collective-permute-done.6 = bf16[200,768]{1,0:T(8,128)(2,1)S(1)} collective-permute-done((bf16[200,768]{1,0:T(8,128)(2,1)S(1)}, bf16[200,768]{1,0:T(8,128)(2,1)S(1)}, u32[]{:S(2)}, u32[]{:S(2)}) %collective-permute-start.6) | collective-permute-done | bytes 307232 | tf_op jit(solution)/shard_map/ppermute | solution.py:713
  54.4 1.8 collective-permute-start.7
  57.0 4.0 %collective-permute-done.8 = bf16[72,768]{1,0:T(8,128)(2,1)S(1)} collective-permute-done((bf16[72,768]{1,0:T(8,128)(2,1)S(1)}, bf16[72,768]{1,0:T(8,128)(2,1)S(1)}, u32[]{:S(2)}, u32[]{:S(2)}) %collective-permute-start.8) | collective-permute-done | bytes 110624 | tf_op jit(solution)/shard_map/ppermute | solution.py:742
  64.0 18.3 %hash_forward.1 = (bf16[8,192,256]{2,1,0:T(8,128)(2,1)}, bf16[192,2048]{1,0:T(8,128)(2,1)}, bf16[192,2048]{1,0:T(8,128)(2,1)}, bf16[192,2304]{1,0:T(8,128)(2,1)}...) custom-call(s32[28]{0:T(128)} %pad_add_fusion.spots_ref, ...), custom_call_target="tpu_custom_call" | custom-call | tf_op jit(solution)/shard_map/hash_forward/pallas_call | solution.py:859
  82.3 3.7 %all-to-all-start = ((bf16[8,192,256]{2,1,0:T(8,128)(2,1)}), bf16[8,192,256]{2,1,0:T(8,128)(2,1)S(1)}, u32[]{:S(2)}, u32[]{:S(2)}) async-start(bf16[8,192,256]{2,1,0:T(8,128)(2,1)} %get-tuple-element.137), calls=%async_computation | async-start | bytes 1572864 | tf_op jit(solution)/shard_map/all_to_all | solution.py:899
  88.2 1.9 scatter.4.base_ref
  92.5 14.0 %all-to-all-done.got_ref = bf16[8,192,256]{2,1,0:T(8,128)(2,1)S(1)} async-done(((bf16[8,192,256]{2,1,0:T(8,128)(2,1)}), bf16[8,192,256]{2,1,0:T(8,128)(2,1)S(1)}, u32[]{:S(2)}, u32[]{:S(2)}) %all-to-all-start) | async-done | bytes 786464 | tf_op jit(solution)/shard_map/all_to_all | solution.py:899
  108.8 2.5 copy-done.1
  113.7 5.5 %collective-permute-done.18.other_ref = bf16[128,768]{1,0:T(8,128)(2,1)S(1)} collective-permute-done((bf16[128,768]{1,0:T(8,128)(2,1)S(1)}, bf16[128,768]{1,0:T(8,128)(2,1)S(1)}, u32[]{:S(2)}, u32[]{:S(2)}) %collective-permute-start.18) | collective-permute-done | bytes 196640 | tf_op jit(solution)/shard_map/ppermute | solution.py:937
  122.2 4.7 %collective-permute-done.19.other_ref = bf16[128,768]{1,0:T(8,128)(2,1)S(1)} collective-permute-done((bf16[128,768]{1,0:T(8,128)(2,1)S(1)}, bf16[128,768]{1,0:T(8,128)(2,1)S(1)}, u32[]{:S(2)}, u32[]{:S(2)}) %collective-permute-start.19) | collective-permute-done | bytes 196640 | tf_op jit(solution)/shard_map/ppermute | solution.py:949
  126.9 2.3 feed_back.1
  130.6 3.6 %feed_grads.1.all_ref = bf16[768,3456]{1,0:T(8,128)(2,1)} custom-call(f32[128,768]{1,0:T(8,128)S(1)} %get-tuple-element.145.hat_ref, f32[4,768]{1,0:T(4,128)S(1)} %copy-done.7, bf16[128,1536]{1,0:T(8,128)(2,1)S(1)} %get-tuple-element.191.slope_ref, bf16[128,768]{1,0:T(8,128)(2,1)S(1)} %get-tuple-element.192.feed_ref, ...), custom_call_target="tpu_custom_call" | custom-call | tf_op jit(solution)/shard_map/feed_grads/pallas_call | solution.py:999
  141.4 2.7 conv_backward.1
  147.0 2.9 %collective-permute-done.24 = bf16[240,256]{1,0:T(8,128)(2,1)S(1)} collective-permute-done((bf16[240,256]{1,0:T(8,128)(2,1)S(1)}, bf16[240,256]{1,0:T(8,128)(2,1)S(1)}, u32[]{:S(2)}, u32[]{:S(2)}) %collective-permute-start.24) | collective-permute-done | bytes 122912 | tf_op jit(solution)/shard_map/ppermute | solution.py:987
  151.9 2.9 %collective-permute-done.26 = bf16[240,256]{1,0:T(8,128)(2,1)S(1)} collective-permute-done((bf16[240,256]{1,0:T(8,128)(2,1)S(1)}, bf16[240,256]{1,0:T(8,128)(2,1)S(1)}, u32[]{:S(2)}, u32[]{:S(2)}) %collective-permute-start.26) | collective-permute-done | bytes 122912 | tf_op jit(solution)/shard_map/ppermute | solution.py:987
  155.8 3.9 %collective-permute-done.28 = bf16[240,256]{1,0:T(8,128)(2,1)S(1)} collective-permute-done((bf16[240,256]{1,0:T(8,128)(2,1)S(1)}, bf16[240,256]{1,0:T(8,128)(2,1)S(1)}, u32[]{:S(2)}, u32[]{:S(2)}) %collective-permute-start.28) | collective-permute-done | bytes 122912 | tf_op jit(solution)/shard_map/ppermute | solution.py:987
  159.7 32.2 %hash_backward.1 = (bf16[8,96,640]{2,1,0:T(8,128)(2,1)}, bf16[8,768,128]{2,1,0:T(8,128)(2,1)}, bf16[8,768,128]{2,1,0:T(8,128)(2,1)}, bf16[8,48,256]{2,1,0:T(8,128)(2,1)}) custom-call(s32[28]{0:T(128)} %pad_add_fusion.spots_ref, bf16[1,200,768]{2,1,0:T(8,128)(2,1)} %bitcast.108, bf16[1,200,768]{2,1,0:T(8,128)(2,1)} %bitcast.120, ...), custom_call_target="tpu_custom_call" | custom-call | tf_op jit(solution)/shard_map/hash_backward/pallas_call | solution.py:1020
  192.0 4.4 %all-to-all-start.1 = ((bf16[8,96,640]{2,1,0:T(8,128)(2,1)}), bf16[8,96,640]{2,1,0:T(8,128)(2,1)S(1)}, u32[]{:S(2)}, u32[]{:S(2)}) async-start(bf16[8,96,640]{2,1,0:T(8,128)(2,1)} %get-tuple-element.177), calls=%async_computation.1 | async-start | bytes 1966080 | tf_op jit(solution)/shard_map/all_to_all | solution.py:1088
  196.4 3.0 %chip_sum.1 = (bf16[8,384,128]{2,1,0:T(8,128)(2,1)}, bf16[8,384,128]{2,1,0:T(8,128)(2,1)}) custom-call(s32[28]{0:T(128)} %pad_add_fusion.spots_ref, bf16[8,768,128]{2,1,0:T(8,128)(2,1)} %get-tuple-element.172.own_ref, bf16[8,768,128]{2,1,0:T(8,128)(2,1)} %collective-permute-done.29.other_ref), custom_call_target="tpu_custom_call" | custom-call | tf_op jit(solution)/shard_map/chip_sum/pallas_call | solution.py:1071
  204.2 3.8 %reshape.152 = f32[8,3,2,8,2,8,8]{6,5,4,3,2,1,0:T(8,128)} reshape(f32[8,24,256]{2,1,0:T(8,128)} %slice.102) | data formatting | bytes 393216 | tf_op jit(solution)/shard_map/reshape | solution.py:1111
  213.1 6.3 %collective-permute-done.30.other_ref = bf16[8,384,128]{2,1,0:T(8,128)(2,1)} collective-permute-done((bf16[8,384,128]{2,1,0:T(8,128)(2,1)}, bf16[8,384,128]{2,1,0:T(8,128)(2,1)}, u32[]{:S(2)}, u32[]{:S(2)}) %collective-permute-start.30) | collective-permute-done | bytes 786464 | tf_op jit(solution)/shard_map/ppermute | solution.py:1085
  219.4 2.1 pair_sum.1
  225.6 2.6 collective-permute-start.34
  229.2 5.8 %all-to-all-done.1.got_ref = bf16[8,96,640]{2,1,0:T(8,128)(2,1)S(1)} async-done(((bf16[8,96,640]{2,1,0:T(8,128)(2,1)}), bf16[8,96,640]{2,1,0:T(8,128)(2,1)S(1)}, u32[]{:S(2)}, u32[]{:S(2)}) %all-to-all-start.1) | async-done | bytes 983072 | tf_op jit(solution)/shard_map/all_to_all | solution.py:1088
  242.0 4.1 %collective-permute-start.37 = (bf16[384,128]{1,0:T(8,128)(2,1)}, bf16[384,128]{1,0:T(8,128)(2,1)S(1)}, u32[]{:S(2)}, u32[]{:S(2)}) collective-permute-start(bf16[384,128]{1,0:T(8,128)(2,1)} %get-tuple-element.188), channel_id=1, source_target_pairs={{0,28},{2,30},{4,24},{6,26},{8,20},{10,22},{12,16},{14,18},{16,12}... | collective-permute-start | bytes 294920 | tf_op jit(solution)/shard_map/ppermute | solution.py:1093
  250.2 3.2 %big_adam.1 = (f32[48,1536]{1,0:T(8,128)}, f32[48,1536]{1,0:T(8,128)}, f32[48,1536]{1,0:T(8,128)}, bf16[48,1536]{1,0:T(8,128)(2,1)}, f32[48,1536]{1,0:T(8,128)},...) custom-call(bf16[48,3456]{1,0:T(8,128)(2,1)} %reduce-scatter.2.clone, ...), custom_call_target="tpu_custom_call" | custom-call | tf_op jit(solution)/shard_map/big_adam/pallas_call | solution.py:789
  257.4 2.3 qkv_adam.1
  (214 shorter events, 76.7 us)
Async XLA Ops:
  7.2 101.5 %all-gather.2.cloned.1.call-start = ((), (), s32[]{:S(2)}) async-start(), calls=%async_computation.3 | async-start | bytes 5640192 | tf_op jit(solution)/shard_map/all_gather | solution.py:844
  11.6 10.5 %collective-permute-start.1 = (bf16[200,768]{1,0:T(8,128)(2,1)S(1)}, bf16[200,768]{1,0:T(8,128)(2,1)S(1)}, u32[]{:S(2)}, u32[]{:S(2)}) collective-permute-start(bf16[200,768]{1,0:T(8,128)(2,1)S(1)} %fusion.2), channel_id=1, source_target_pairs={{0,8},{2,10},{8,16},{10,18},{16,24},{18,26},{24,28},{26,30},{28,20... | collective-permute-start | bytes 921608 | tf_op jit(solution)/shard_map/ppermute | solution.py:713
  14.5 9.1 %collective-permute-start.2 = (bf16[200,768]{1,0:T(8,128)(2,1)S(1)}, bf16[200,768]{1,0:T(8,128)(2,1)S(1)}, u32[]{:S(2)}, u32[]{:S(2)}) collective-permute-start(bf16[200,768]{1,0:T(8,128)(2,1)S(1)} %fusion.2), channel_id=1, source_target_pairs={{8,0},{10,2},{16,8},{18,10},{24,16},{26,18},{28,24},{30,26},{20,28... | collective-permute-start | bytes 921608 | tf_op jit(solution)/shard_map/ppermute | solution.py:713
  26.1 8.2 %collective-permute-start.3 = (bf16[200,768]{1,0:T(8,128)(2,1)S(1)}, bf16[200,768]{1,0:T(8,128)(2,1)S(1)}, u32[]{:S(2)}, u32[]{:S(2)}) collective-permute-start(bf16[200,768]{1,0:T(8,128)(2,1)S(1)} %collective-permute-done.1), channel_id=1, source_target_pairs={{0,8},{2,10},{8,16},{10,18},{16,24},{18,26},{24,28},{26,30},{28,20... | collective-permute-start | bytes 921608 | tf_op jit(solution)/shard_map/ppermute | solution.py:713
  27.7 7.9 %collective-permute-start.4 = (bf16[200,768]{1,0:T(8,128)(2,1)S(1)}, bf16[200,768]{1,0:T(8,128)(2,1)S(1)}, u32[]{:S(2)}, u32[]{:S(2)}) collective-permute-start(bf16[200,768]{1,0:T(8,128)(2,1)S(1)} %collective-permute-done.2), channel_id=1, source_target_pairs={{8,0},{10,2},{16,8},{18,10},{24,16},{26,18},{28,24},{30,26},{20,28... | collective-permute-start | bytes 921608 | tf_op jit(solution)/shard_map/ppermute | solution.py:713
  35.6 14.7 %collective-permute-start.5 = (bf16[200,768]{1,0:T(8,128)(2,1)S(1)}, bf16[200,768]{1,0:T(8,128)(2,1)S(1)}, u32[]{:S(2)}, u32[]{:S(2)}) collective-permute-start(bf16[200,768]{1,0:T(8,128)(2,1)S(1)} %collective-permute-done.3), channel_id=1, source_target_pairs={{0,8},{2,10},{8,16},{10,18},{16,24},{18,26},{24,28},{26,30},{28,20... | collective-permute-start | bytes 921608 | tf_op jit(solution)/shard_map/ppermute | solution.py:713
  37.2 17.2 %collective-permute-start.6 = (bf16[200,768]{1,0:T(8,128)(2,1)S(1)}, bf16[200,768]{1,0:T(8,128)(2,1)S(1)}, u32[]{:S(2)}, u32[]{:S(2)}) collective-permute-start(bf16[200,768]{1,0:T(8,128)(2,1)S(1)} %collective-permute-done.4), channel_id=1, source_target_pairs={{8,0},{10,2},{16,8},{18,10},{24,16},{26,18},{28,24},{30,26},{20,28... | collective-permute-start | bytes 921608 | tf_op jit(solution)/shard_map/ppermute | solution.py:713
  37.6 18.8 %collective-permute-start.9 = (bf16[200,768]{1,0:T(8,128)(2,1)S(1)}, bf16[200,768]{1,0:T(8,128)(2,1)S(1)}, u32[]{:S(2)}, u32[]{:S(2)}) collective-permute-start(bf16[200,768]{1,0:T(8,128)(2,1)S(1)} %fusion.2), channel_id=1, source_target_pairs={{0,2},{2,0},{4,6},{6,4},{8,10},{10,8},{12,14},{14,12},{16,18},{18,... | collective-permute-start | bytes 921608 | tf_op jit(solution)/shard_map/ppermute | solution.py:746
  37.6 18.8 %collective-permute-start.10 = (bf16[200,768]{1,0:T(8,128)(2,1)S(1)}, bf16[200,768]{1,0:T(8,128)(2,1)S(1)}, u32[]{:S(2)}, u32[]{:S(2)}) collective-permute-start(bf16[200,768]{1,0:T(8,128)(2,1)S(1)} %collective-permute-done.1), channel_id=1, source_target_pairs={{0,2},{2,0},{4,6},{6,4},{8,10},{10,8},{12,14},{14,12},{16,18},{18,... | collective-permute-start | bytes 921608 | tf_op jit(solution)/shard_map/ppermute | solution.py:746
  38.1 23.3 %collective-permute-start.11 = (bf16[200,768]{1,0:T(8,128)(2,1)S(1)}, bf16[200,768]{1,0:T(8,128)(2,1)S(1)}, u32[]{:S(2)}, u32[]{:S(2)}) collective-permute-start(bf16[200,768]{1,0:T(8,128)(2,1)S(1)} %collective-permute-done.2), channel_id=1, source_target_pairs={{0,2},{2,0},{4,6},{6,4},{8,10},{10,8},{12,14},{14,12},{16,18},{18,... | collective-permute-start | bytes 921608 | tf_op jit(solution)/shard_map/ppermute | solution.py:746
  54.4 6.6 %collective-permute-start.7 = (bf16[128,768]{1,0:T(8,128)(2,1)S(1)}, bf16[128,768]{1,0:T(8,128)(2,1)S(1)}, u32[]{:S(2)}, u32[]{:S(2)}) collective-permute-start(bf16[128,768]{1,0:T(8,128)(2,1)S(1)} %slice.87), channel_id=1, source_target_pairs={{0,8},{2,10},{8,16},{10,18},{16,24},{18,26},{24,28},{26,30},{28,20... | collective-permute-start | bytes 589832 | tf_op jit(solution)/shard_map/ppermute | solution.py:741
  56.4 5.1 %collective-permute-start.12 = (bf16[200,768]{1,0:T(8,128)(2,1)S(1)}, bf16[200,768]{1,0:T(8,128)(2,1)S(1)}, u32[]{:S(2)}, u32[]{:S(2)}) collective-permute-start(bf16[200,768]{1,0:T(8,128)(2,1)S(1)} %collective-permute-done.3), channel_id=1, source_target_pairs={{0,2},{2,0},{4,6},{6,4},{8,10},{10,8},{12,14},{14,12},{16,18},{18,... | collective-permute-start | bytes 921608 | tf_op jit(solution)/shard_map/ppermute | solution.py:746
  56.5 5.1 %collective-permute-start.13 = (bf16[200,768]{1,0:T(8,128)(2,1)S(1)}, bf16[200,768]{1,0:T(8,128)(2,1)S(1)}, u32[]{:S(2)}, u32[]{:S(2)}) collective-permute-start(bf16[200,768]{1,0:T(8,128)(2,1)S(1)} %collective-permute-done.4), channel_id=1, source_target_pairs={{0,2},{2,0},{4,6},{6,4},{8,10},{10,8},{12,14},{14,12},{16,18},{18,... | collective-permute-start | bytes 921608 | tf_op jit(solution)/shard_map/ppermute | solution.py:746
  82.3 24.3 %all-to-all-start = ((bf16[8,192,256]{2,1,0:T(8,128)(2,1)}), bf16[8,192,256]{2,1,0:T(8,128)(2,1)S(1)}, u32[]{:S(2)}, u32[]{:S(2)}) async-start(bf16[8,192,256]{2,1,0:T(8,128)(2,1)} %get-tuple-element.137), calls=%async_computation | async-start | bytes 1572864 | tf_op jit(solution)/shard_map/all_to_all | solution.py:899
  86.0 164.2 %reduce-scatter.2.cloned.1.call-start = ((), (), s32[]{:S(2)}) async-start(), calls=%async_computation.4 | async-start | bytes 5640192 | tf_op jit(solution)/shard_map/reduce_scatter | solution.py:1018
  112.2 7.0 %collective-permute-start.18 = (bf16[128,768]{1,0:T(8,128)(2,1)S(1)}, bf16[128,768]{1,0:T(8,128)(2,1)S(1)}, u32[]{:S(2)}, u32[]{:S(2)}) collective-permute-start(bf16[128,768]{1,0:T(8,128)(2,1)S(1)} %get-tuple-element.143.own_ref), channel_id=1, source_target_pairs={{0,1},{1,0},{2,3},{3,2},{4,5},{5,4},{6,7},{7,6},{8,9},{9,8},{10,11... | collective-permute-start | bytes 589832 | tf_op jit(solution)/shard_map/ppermute | solution.py:937
  120.7 6.2 %collective-permute-start.19 = (bf16[128,768]{1,0:T(8,128)(2,1)S(1)}, bf16[128,768]{1,0:T(8,128)(2,1)S(1)}, u32[]{:S(2)}, u32[]{:S(2)}) collective-permute-start(bf16[128,768]{1,0:T(8,128)(2,1)S(1)} %get-tuple-element.147.own_ref), channel_id=1, source_target_pairs={{0,1},{1,0},{2,3},{3,2},{4,5},{5,4},{6,7},{7,6},{8,9},{9,8},{10,11... | collective-permute-start | bytes 589832 | tf_op jit(solution)/shard_map/ppermute | solution.py:949
  129.2 5.7 %collective-permute-start.20 = (bf16[128,768]{1,0:T(8,128)(2,1)S(1)}, bf16[128,768]{1,0:T(8,128)(2,1)S(1)}, u32[]{:S(2)}, u32[]{:S(2)}) collective-permute-start(bf16[128,768]{1,0:T(8,128)(2,1)S(1)} %get-tuple-element.150.own_ref), channel_id=1, source_target_pairs={{0,1},{1,0},{2,3},{3,2},{4,5},{5,4},{6,7},{7,6},{8,9},{9,8},{10,11... | collective-permute-start | bytes 589832 | tf_op jit(solution)/shard_map/ppermute | solution.py:962
  139.3 5.6 %collective-permute-start.22 = (bf16[240,256]{1,0:T(8,128)(2,1)S(1)}, bf16[240,256]{1,0:T(8,128)(2,1)S(1)}, u32[]{:S(2)}, u32[]{:S(2)}) collective-permute-start(bf16[240,256]{1,0:T(8,128)(2,1)S(1)} %get-tuple-element.158), channel_id=1, source_target_pairs={{0,8},{2,10},{8,16},{10,18},{16,24},{18,26},{24,28},{26,30},{28,20... | collective-permute-start | bytes 368648 | tf_op jit(solution)/shard_map/ppermute | solution.py:713
  139.7 5.3 %collective-permute-start.23 = (bf16[240,256]{1,0:T(8,128)(2,1)S(1)}, bf16[240,256]{1,0:T(8,128)(2,1)S(1)}, u32[]{:S(2)}, u32[]{:S(2)}) collective-permute-start(bf16[240,256]{1,0:T(8,128)(2,1)S(1)} %get-tuple-element.158), channel_id=1, source_target_pairs={{8,0},{10,2},{16,8},{18,10},{24,16},{26,18},{28,24},{30,26},{20,28... | collective-permute-start | bytes 368648 | tf_op jit(solution)/shard_map/ppermute | solution.py:713
  150.1 5.6 %collective-permute-start.27 = (bf16[240,256]{1,0:T(8,128)(2,1)S(1)}, bf16[240,256]{1,0:T(8,128)(2,1)S(1)}, u32[]{:S(2)}, u32[]{:S(2)}) collective-permute-start(bf16[240,256]{1,0:T(8,128)(2,1)S(1)} %collective-permute-done.25), channel_id=1, source_target_pairs={{8,0},{10,2},{16,8},{18,10},{24,16},{26,18},{28,24},{30,26},{20,28... | collective-permute-start | bytes 368648 | tf_op jit(solution)/shard_map/ppermute | solution.py:987
  192.0 43.0 %all-to-all-start.1 = ((bf16[8,96,640]{2,1,0:T(8,128)(2,1)}), bf16[8,96,640]{2,1,0:T(8,128)(2,1)S(1)}, u32[]{:S(2)}, u32[]{:S(2)}) async-start(bf16[8,96,640]{2,1,0:T(8,128)(2,1)} %get-tuple-element.177), calls=%async_computation.1 | async-start | bytes 1966080 | tf_op jit(solution)/shard_map/all_to_all | solution.py:1088
  199.4 20.0 %collective-permute-start.30 = (bf16[8,384,128]{2,1,0:T(8,128)(2,1)}, bf16[8,384,128]{2,1,0:T(8,128)(2,1)}, u32[]{:S(2)}, u32[]{:S(2)}) collective-permute-start(bf16[8,384,128]{2,1,0:T(8,128)(2,1)} %get-tuple-element.175), channel_id=1, source_target_pairs={{0,1},{1,0},{2,3},{3,2},{4,5},{5,4},{6,7},{7,6},{8,9},{9,8},{10,11... | collective-permute-start | bytes 2359304 | tf_op jit(solution)/shard_map/ppermute | solution.py:1085
  222.1 12.8 %collective-permute-start.31 = (bf16[384,128]{1,0:T(8,128)(2,1)}, bf16[384,128]{1,0:T(8,128)(2,1)S(1)}, u32[]{:S(2)}, u32[]{:S(2)}) collective-permute-start(bf16[384,128]{1,0:T(8,128)(2,1)} %get-tuple-element.178), channel_id=1, source_target_pairs={{0,4},{2,6},{4,0},{6,2},{8,12},{10,14},{12,8},{14,10},{16,20},{18,... | collective-permute-start | bytes 294920 | tf_op jit(solution)/shard_map/ppermute | solution.py:1093
  223.8 11.1 %collective-permute-start.32 = (bf16[384,128]{1,0:T(8,128)(2,1)}, bf16[384,128]{1,0:T(8,128)(2,1)S(1)}, u32[]{:S(2)}, u32[]{:S(2)}) collective-permute-start(bf16[384,128]{1,0:T(8,128)(2,1)} %get-tuple-element.179), channel_id=1, source_target_pairs={{0,8},{2,10},{4,12},{6,14},{8,0},{10,2},{12,4},{14,6},{16,24},{18,... | collective-permute-start | bytes 294920 | tf_op jit(solution)/shard_map/ppermute | solution.py:1093
  225.4 9.5 %collective-permute-start.33 = (bf16[384,128]{1,0:T(8,128)(2,1)}, bf16[384,128]{1,0:T(8,128)(2,1)S(1)}, u32[]{:S(2)}, u32[]{:S(2)}) collective-permute-start(bf16[384,128]{1,0:T(8,128)(2,1)} %get-tuple-element.180), channel_id=1, source_target_pairs={{0,12},{2,14},{4,8},{6,10},{8,4},{10,6},{12,0},{14,2},{16,28},{18,... | collective-permute-start | bytes 294920 | tf_op jit(solution)/shard_map/ppermute | solution.py:1093
  225.6 10.7 %collective-permute-start.34 = (bf16[384,128]{1,0:T(8,128)(2,1)}, bf16[384,128]{1,0:T(8,128)(2,1)S(1)}, u32[]{:S(2)}, u32[]{:S(2)}) collective-permute-start(bf16[384,128]{1,0:T(8,128)(2,1)} %get-tuple-element.181), channel_id=1, source_target_pairs={{0,16},{2,18},{4,20},{6,22},{8,24},{10,26},{12,28},{14,30},{16,0},... | collective-permute-start | bytes 294920 | tf_op jit(solution)/shard_map/ppermute | solution.py:1093
  239.9 6.2 %collective-permute-start.39 = (f32[6243]{0:T(1024)S(1)}, f32[6243]{0:T(1024)S(1)}, u32[]{:S(2)}, u32[]{:S(2)}) collective-permute-start(f32[6243]{0:T(1024)S(1)} %pad_maximum_fusion.1), channel_id=1, source_target_pairs={{0,2},{2,0},{4,6},{6,4},{8,10},{10,8},{12,14},{14,12},{16,18},{18,... | collective-permute-start | bytes 74924 | tf_op jit(solution)/shard_map/ppermute | solution.py:1118
  239.9 14.0 %collective-permute-start.35 = (bf16[384,128]{1,0:T(8,128)(2,1)}, bf16[384,128]{1,0:T(8,128)(2,1)S(1)}, u32[]{:S(2)}, u32[]{:S(2)}) collective-permute-start(bf16[384,128]{1,0:T(8,128)(2,1)} %get-tuple-element.186), channel_id=1, source_target_pairs={{0,20},{2,22},{4,16},{6,18},{8,28},{10,30},{12,24},{14,26},{16,4},... | collective-permute-start | bytes 294920 | tf_op jit(solution)/shard_map/ppermute | solution.py:1093
  240.5 13.5 %collective-permute-start.36 = (bf16[384,128]{1,0:T(8,128)(2,1)}, bf16[384,128]{1,0:T(8,128)(2,1)S(1)}, u32[]{:S(2)}, u32[]{:S(2)}) collective-permute-start(bf16[384,128]{1,0:T(8,128)(2,1)} %get-tuple-element.187), channel_id=1, source_target_pairs={{0,24},{2,26},{4,28},{6,30},{8,16},{10,18},{12,20},{14,22},{16,8},... | collective-permute-start | bytes 294920 | tf_op jit(solution)/shard_map/ppermute | solution.py:1093
  242.0 11.9 %collective-permute-start.37 = (bf16[384,128]{1,0:T(8,128)(2,1)}, bf16[384,128]{1,0:T(8,128)(2,1)S(1)}, u32[]{:S(2)}, u32[]{:S(2)}) collective-permute-start(bf16[384,128]{1,0:T(8,128)(2,1)} %get-tuple-element.188), channel_id=1, source_target_pairs={{0,28},{2,30},{4,24},{6,26},{8,20},{10,22},{12,16},{14,18},{16,12}... | collective-permute-start | bytes 294920 | tf_op jit(solution)/shard_map/ppermute | solution.py:1093
  246.1 11.2 %collective-permute-start.40 = (f32[48,640]{1,0:T(8,128)}, f32[48,640]{1,0:T(8,128)}, u32[]{:S(2)}, u32[]{:S(2)}) collective-permute-start(f32[48,640]{1,0:T(8,128)} %get-tuple-element.200), channel_id=1, source_target_pairs={{0,2},{2,0},{4,6},{6,4},{8,10},{10,8},{12,14},{14,12},{16,18},{18,... | collective-permute-start | bytes 368648 | tf_op jit(solution)/shard_map/ppermute | solution.py:1106
  (53 other events, 553.8 us)
Sparse Core Ops, SparseCore 0:
  26.2 61.4 all-gather.1
  137.4 93.3 reduce-scatter.1

commit v7 on v6

--- a/solution.py
+++ b/solution.py
@@ -807,6 +807,8 @@
         for i, arg in enumerate(args):
             plain = arg is spots or i in blocks
             specs.append(smem if arg is spots else blocks.get(i, inside))
+            if i in blocks:
+                arg = pltpu.with_memory_space_constraint(arg, pltpu.HBM)
             values.append(arg if plain else in_vmem(arg))
         for arg in after:
             specs.append(anywhere)

time: 270 us -> 269 us (level)
    unnamed x80 -> x78, local copies, waits for them, and re-layouts: 7.19 us -> 4.68 us
where the time goes in v7:
time: 269 us; the launch traced here: 266 us
  waiting for transfers between devices  87.4 us (32%)
  Pallas kernels  82.6 us (31%)
  starting transfers between devices  46 us (17%)
  local copies, waits for them, and re-layouts  23 us (9%)
  between operations  14.7 us (5%)
  other arithmetic  12.5 us (5%)
    pallas_call x1, Pallas kernels, on_device(): pl.pallas_call(partial(backward_kernel, hashes, bits, rows, work, steps,...  32.2 us
    ppermute x8, waiting for transfers between devices, ring(): moved = [lax.ppermute(v, 'seq', p) for v, p in zip(moved, (ahead, behind))]  30.1 us
    pallas_call x1, Pallas kernels, on_device(): pl.pallas_call(partial(forward_kernel, hashes, bits, rows, work, steps, h...  18.3 us
    pallas_call x12, Pallas kernels, once(): pl.pallas_call(kernel, grid=(1,) if blocks else (), in_specs=specs, out_s...  16.8 us
    all_to_all x1, waiting for transfers between devices, on_device(): num_got = across(num_parts)  14 us
    ppermute x7, starting transfers between devices, on_device(): back_got.append(lax.ppermute(pair_sums[d], 'seq', perm))  12.3 us
    ppermute x5, waiting for transfers between devices, on_device(): lax.ppermute(v, 'seq', p)  9.73 us
    ppermute x8, starting transfers between devices, ring(): moved = [lax.ppermute(v, 'seq', p) for v, p in zip(moved, (ahead, behind))]  9.16 us
  transfers between devices with their start and end apart: 45, of which 24 were waited for; matrix products, arithmetic and copies ran while one was open for 10% of the time, Pallas kernels for 27%

profile of v7, /device:TPU:0, one launch (start us, length us, event | category | flops | bytes accessed | tf_op | source)
XLA Modules:
  0.0 266.2 jit_solution(10634368958532284960)
XLA Ops:
  11.6 3.0 %collective-permute-start.1 = (bf16[200,768]{1,0:T(8,128)(2,1)S(1)}, bf16[200,768]{1,0:T(8,128)(2,1)S(1)}, u32[]{:S(2)}, u32[]{:S(2)}) collective-permute-start(bf16[200,768]{1,0:T(8,128)(2,1)S(1)} %fusion.2), channel_id=1, source_target_pairs={{0,8},{2,10},{8,16},{10,18},{16,24},{18,26},{24,28},{26,30},{28,20... | collective-permute-start | bytes 921608 | tf_op jit(solution)/shard_map/ppermute | solution.py:713
  17.1 4.9 %collective-permute-done.1 = bf16[200,768]{1,0:T(8,128)(2,1)S(1)} collective-permute-done((bf16[200,768]{1,0:T(8,128)(2,1)S(1)}, bf16[200,768]{1,0:T(8,128)(2,1)S(1)}, u32[]{:S(2)}, u32[]{:S(2)}) %collective-permute-start.1) | collective-permute-done | bytes 307232 | tf_op jit(solution)/shard_map/ppermute | solution.py:713
  24.2 1.8 pack.1
  28.1 6.2 %collective-permute-done.3 = bf16[200,768]{1,0:T(8,128)(2,1)S(1)} collective-permute-done((bf16[200,768]{1,0:T(8,128)(2,1)S(1)}, bf16[200,768]{1,0:T(8,128)(2,1)S(1)}, u32[]{:S(2)}, u32[]{:S(2)}) %collective-permute-start.3) | collective-permute-done | bytes 307232 | tf_op jit(solution)/shard_map/ppermute | solution.py:713
  38.1 12.2 %collective-permute-done.5 = bf16[200,768]{1,0:T(8,128)(2,1)S(1)} collective-permute-done((bf16[200,768]{1,0:T(8,128)(2,1)S(1)}, bf16[200,768]{1,0:T(8,128)(2,1)S(1)}, u32[]{:S(2)}, u32[]{:S(2)}) %collective-permute-start.5) | collective-permute-done | bytes 307232 | tf_op jit(solution)/shard_map/ppermute | solution.py:713
  50.3 4.0 %collective-permute-done.6 = bf16[200,768]{1,0:T(8,128)(2,1)S(1)} collective-permute-done((bf16[200,768]{1,0:T(8,128)(2,1)S(1)}, bf16[200,768]{1,0:T(8,128)(2,1)S(1)}, u32[]{:S(2)}, u32[]{:S(2)}) %collective-permute-start.6) | collective-permute-done | bytes 307232 | tf_op jit(solution)/shard_map/ppermute | solution.py:713
  54.4 1.8 collective-permute-start.7
  57.0 4.0 %collective-permute-done.8 = bf16[72,768]{1,0:T(8,128)(2,1)S(1)} collective-permute-done((bf16[72,768]{1,0:T(8,128)(2,1)S(1)}, bf16[72,768]{1,0:T(8,128)(2,1)S(1)}, u32[]{:S(2)}, u32[]{:S(2)}) %collective-permute-start.8) | collective-permute-done | bytes 110624 | tf_op jit(solution)/shard_map/ppermute | solution.py:742
  64.0 18.3 %hash_forward.1 = (bf16[8,192,256]{2,1,0:T(8,128)(2,1)}, bf16[192,2048]{1,0:T(8,128)(2,1)}, bf16[192,2048]{1,0:T(8,128)(2,1)}, bf16[192,2304]{1,0:T(8,128)(2,1)}...) custom-call(s32[28]{0:T(128)} %pad_add_fusion.spots_ref, ...), custom_call_target="tpu_custom_call" | custom-call | tf_op jit(solution)/shard_map/hash_forward/pallas_call | solution.py:861
  82.3 3.7 %all-to-all-start = ((bf16[8,192,256]{2,1,0:T(8,128)(2,1)}), bf16[8,192,256]{2,1,0:T(8,128)(2,1)S(1)}, u32[]{:S(2)}, u32[]{:S(2)}) async-start(bf16[8,192,256]{2,1,0:T(8,128)(2,1)} %get-tuple-element.137), calls=%async_computation | async-start | bytes 1572864 | tf_op jit(solution)/shard_map/all_to_all | solution.py:901
  88.2 1.9 scatter.4.base_ref
  92.6 14.0 %all-to-all-done.got_ref = bf16[8,192,256]{2,1,0:T(8,128)(2,1)S(1)} async-done(((bf16[8,192,256]{2,1,0:T(8,128)(2,1)}), bf16[8,192,256]{2,1,0:T(8,128)(2,1)S(1)}, u32[]{:S(2)}, u32[]{:S(2)}) %all-to-all-start) | async-done | bytes 786464 | tf_op jit(solution)/shard_map/all_to_all | solution.py:901
  111.9 5.5 %collective-permute-done.18.other_ref = bf16[128,768]{1,0:T(8,128)(2,1)S(1)} collective-permute-done((bf16[128,768]{1,0:T(8,128)(2,1)S(1)}, bf16[128,768]{1,0:T(8,128)(2,1)S(1)}, u32[]{:S(2)}, u32[]{:S(2)}) %collective-permute-start.18) | collective-permute-done | bytes 196640 | tf_op jit(solution)/shard_map/ppermute | solution.py:939
  120.4 4.7 %collective-permute-done.19.other_ref = bf16[128,768]{1,0:T(8,128)(2,1)S(1)} collective-permute-done((bf16[128,768]{1,0:T(8,128)(2,1)S(1)}, bf16[128,768]{1,0:T(8,128)(2,1)S(1)}, u32[]{:S(2)}, u32[]{:S(2)}) %collective-permute-start.19) | collective-permute-done | bytes 196640 | tf_op jit(solution)/shard_map/ppermute | solution.py:951
  125.1 2.3 feed_back.1
  128.8 3.7 %feed_grads.1.all_ref = bf16[768,3456]{1,0:T(8,128)(2,1)} custom-call(f32[128,768]{1,0:T(8,128)S(1)} %get-tuple-element.145.hat_ref, f32[4,768]{1,0:T(4,128)S(1)} %copy-done.6, bf16[128,1536]{1,0:T(8,128)(2,1)S(1)} %get-tuple-element.191.slope_ref, bf16[128,768]{1,0:T(8,128)(2,1)S(1)} %get-tuple-element.192.feed_ref, ...), custom_call_target="tpu_custom_call" | custom-call | tf_op jit(solution)/shard_map/feed_grads/pallas_call | solution.py:1001
  139.6 2.7 conv_backward.1
  145.2 2.9 %collective-permute-done.24 = bf16[240,256]{1,0:T(8,128)(2,1)S(1)} collective-permute-done((bf16[240,256]{1,0:T(8,128)(2,1)S(1)}, bf16[240,256]{1,0:T(8,128)(2,1)S(1)}, u32[]{:S(2)}, u32[]{:S(2)}) %collective-permute-start.24) | collective-permute-done | bytes 122912 | tf_op jit(solution)/shard_map/ppermute | solution.py:989
  150.1 2.9 %collective-permute-done.26 = bf16[240,256]{1,0:T(8,128)(2,1)S(1)} collective-permute-done((bf16[240,256]{1,0:T(8,128)(2,1)S(1)}, bf16[240,256]{1,0:T(8,128)(2,1)S(1)}, u32[]{:S(2)}, u32[]{:S(2)}) %collective-permute-start.26) | collective-permute-done | bytes 122912 | tf_op jit(solution)/shard_map/ppermute | solution.py:989
  154.0 3.9 %collective-permute-done.28 = bf16[240,256]{1,0:T(8,128)(2,1)S(1)} collective-permute-done((bf16[240,256]{1,0:T(8,128)(2,1)S(1)}, bf16[240,256]{1,0:T(8,128)(2,1)S(1)}, u32[]{:S(2)}, u32[]{:S(2)}) %collective-permute-start.28) | collective-permute-done | bytes 122912 | tf_op jit(solution)/shard_map/ppermute | solution.py:989
  157.9 32.2 %hash_backward.1 = (bf16[8,96,640]{2,1,0:T(8,128)(2,1)}, bf16[8,768,128]{2,1,0:T(8,128)(2,1)}, bf16[8,768,128]{2,1,0:T(8,128)(2,1)}, bf16[8,48,256]{2,1,0:T(8,128)(2,1)}) custom-call(s32[28]{0:T(128)} %pad_add_fusion.spots_ref, bf16[1,200,768]{2,1,0:T(8,128)(2,1)} %bitcast.108, bf16[1,200,768]{2,1,0:T(8,128)(2,1)} %bitcast.120, ...), custom_call_target="tpu_custom_call" | custom-call | tf_op jit(solution)/shard_map/hash_backward/pallas_call | solution.py:1022
  190.2 4.4 %all-to-all-start.1 = ((bf16[8,96,640]{2,1,0:T(8,128)(2,1)}), bf16[8,96,640]{2,1,0:T(8,128)(2,1)S(1)}, u32[]{:S(2)}, u32[]{:S(2)}) async-start(bf16[8,96,640]{2,1,0:T(8,128)(2,1)} %get-tuple-element.177), calls=%async_computation.1 | async-start | bytes 1966080 | tf_op jit(solution)/shard_map/all_to_all | solution.py:1090
  194.6 3.0 %chip_sum.1 = (bf16[8,384,128]{2,1,0:T(8,128)(2,1)}, bf16[8,384,128]{2,1,0:T(8,128)(2,1)}) custom-call(s32[28]{0:T(128)} %pad_add_fusion.spots_ref, bf16[8,768,128]{2,1,0:T(8,128)(2,1)} %get-tuple-element.172.own_ref, bf16[8,768,128]{2,1,0:T(8,128)(2,1)} %collective-permute-done.29.other_ref), custom_call_target="tpu_custom_call" | custom-call | tf_op jit(solution)/shard_map/chip_sum/pallas_call | solution.py:1073
  202.4 3.7 %reshape.152 = f32[8,3,2,8,2,8,8]{6,5,4,3,2,1,0:T(8,128)} reshape(f32[8,24,256]{2,1,0:T(8,128)} %slice.102) | data formatting | bytes 393216 | tf_op jit(solution)/shard_map/reshape | solution.py:1113
  207.8 1.8 copy.71
  211.2 6.3 %collective-permute-done.30.other_ref = bf16[8,384,128]{2,1,0:T(8,128)(2,1)} collective-permute-done((bf16[8,384,128]{2,1,0:T(8,128)(2,1)}, bf16[8,384,128]{2,1,0:T(8,128)(2,1)}, u32[]{:S(2)}, u32[]{:S(2)}) %collective-permute-start.30) | collective-permute-done | bytes 786464 | tf_op jit(solution)/shard_map/ppermute | solution.py:1087
  217.6 2.1 pair_sum.1
  223.8 2.6 collective-permute-start.34
  227.3 5.8 %all-to-all-done.1.got_ref = bf16[8,96,640]{2,1,0:T(8,128)(2,1)S(1)} async-done(((bf16[8,96,640]{2,1,0:T(8,128)(2,1)}), bf16[8,96,640]{2,1,0:T(8,128)(2,1)S(1)}, u32[]{:S(2)}, u32[]{:S(2)}) %all-to-all-start.1) | async-done | bytes 983072 | tf_op jit(solution)/shard_map/all_to_all | solution.py:1090
  240.2 4.1 %collective-permute-start.37 = (bf16[384,128]{1,0:T(8,128)(2,1)}, bf16[384,128]{1,0:T(8,128)(2,1)S(1)}, u32[]{:S(2)}, u32[]{:S(2)}) collective-permute-start(bf16[384,128]{1,0:T(8,128)(2,1)} %get-tuple-element.188), channel_id=1, source_target_pairs={{0,28},{2,30},{4,24},{6,26},{8,20},{10,22},{12,16},{14,18},{16,12}... | collective-permute-start | bytes 294920 | tf_op jit(solution)/shard_map/ppermute | solution.py:1095
  248.4 3.2 %big_adam.1 = (f32[48,1536]{1,0:T(8,128)}, f32[48,1536]{1,0:T(8,128)}, f32[48,1536]{1,0:T(8,128)}, bf16[48,1536]{1,0:T(8,128)(2,1)}, f32[48,1536]{1,0:T(8,128)},...) custom-call(bf16[48,3456]{1,0:T(8,128)(2,1)} %reduce-scatter.2.clone, ...), custom_call_target="tpu_custom_call" | custom-call | tf_op jit(solution)/shard_map/big_adam/pallas_call | solution.py:789
  255.6 2.3 qkv_adam.1
  (212 shorter events, 75.7 us)
Async XLA Ops:
  7.2 101.6 %all-gather.2.cloned.1.call-start = ((), (), s32[]{:S(2)}) async-start(), calls=%async_computation.3 | async-start | bytes 5640192 | tf_op jit(solution)/shard_map/all_gather | solution.py:846
  11.6 10.5 %collective-permute-start.1 = (bf16[200,768]{1,0:T(8,128)(2,1)S(1)}, bf16[200,768]{1,0:T(8,128)(2,1)S(1)}, u32[]{:S(2)}, u32[]{:S(2)}) collective-permute-start(bf16[200,768]{1,0:T(8,128)(2,1)S(1)} %fusion.2), channel_id=1, source_target_pairs={{0,8},{2,10},{8,16},{10,18},{16,24},{18,26},{24,28},{26,30},{28,20... | collective-permute-start | bytes 921608 | tf_op jit(solution)/shard_map/ppermute | solution.py:713
  14.5 9.1 %collective-permute-start.2 = (bf16[200,768]{1,0:T(8,128)(2,1)S(1)}, bf16[200,768]{1,0:T(8,128)(2,1)S(1)}, u32[]{:S(2)}, u32[]{:S(2)}) collective-permute-start(bf16[200,768]{1,0:T(8,128)(2,1)S(1)} %fusion.2), channel_id=1, source_target_pairs={{8,0},{10,2},{16,8},{18,10},{24,16},{26,18},{28,24},{30,26},{20,28... | collective-permute-start | bytes 921608 | tf_op jit(solution)/shard_map/ppermute | solution.py:713
  26.1 8.2 %collective-permute-start.3 = (bf16[200,768]{1,0:T(8,128)(2,1)S(1)}, bf16[200,768]{1,0:T(8,128)(2,1)S(1)}, u32[]{:S(2)}, u32[]{:S(2)}) collective-permute-start(bf16[200,768]{1,0:T(8,128)(2,1)S(1)} %collective-permute-done.1), channel_id=1, source_target_pairs={{0,8},{2,10},{8,16},{10,18},{16,24},{18,26},{24,28},{26,30},{28,20... | collective-permute-start | bytes 921608 | tf_op jit(solution)/shard_map/ppermute | solution.py:713
  27.7 7.9 %collective-permute-start.4 = (bf16[200,768]{1,0:T(8,128)(2,1)S(1)}, bf16[200,768]{1,0:T(8,128)(2,1)S(1)}, u32[]{:S(2)}, u32[]{:S(2)}) collective-permute-start(bf16[200,768]{1,0:T(8,128)(2,1)S(1)} %collective-permute-done.2), channel_id=1, source_target_pairs={{8,0},{10,2},{16,8},{18,10},{24,16},{26,18},{28,24},{30,26},{20,28... | collective-permute-start | bytes 921608 | tf_op jit(solution)/shard_map/ppermute | solution.py:713
  35.6 14.7 %collective-permute-start.5 = (bf16[200,768]{1,0:T(8,128)(2,1)S(1)}, bf16[200,768]{1,0:T(8,128)(2,1)S(1)}, u32[]{:S(2)}, u32[]{:S(2)}) collective-permute-start(bf16[200,768]{1,0:T(8,128)(2,1)S(1)} %collective-permute-done.3), channel_id=1, source_target_pairs={{0,8},{2,10},{8,16},{10,18},{16,24},{18,26},{24,28},{26,30},{28,20... | collective-permute-start | bytes 921608 | tf_op jit(solution)/shard_map/ppermute | solution.py:713
  37.2 17.2 %collective-permute-start.6 = (bf16[200,768]{1,0:T(8,128)(2,1)S(1)}, bf16[200,768]{1,0:T(8,128)(2,1)S(1)}, u32[]{:S(2)}, u32[]{:S(2)}) collective-permute-start(bf16[200,768]{1,0:T(8,128)(2,1)S(1)} %collective-permute-done.4), channel_id=1, source_target_pairs={{8,0},{10,2},{16,8},{18,10},{24,16},{26,18},{28,24},{30,26},{20,28... | collective-permute-start | bytes 921608 | tf_op jit(solution)/shard_map/ppermute | solution.py:713
  37.6 18.8 %collective-permute-start.9 = (bf16[200,768]{1,0:T(8,128)(2,1)S(1)}, bf16[200,768]{1,0:T(8,128)(2,1)S(1)}, u32[]{:S(2)}, u32[]{:S(2)}) collective-permute-start(bf16[200,768]{1,0:T(8,128)(2,1)S(1)} %fusion.2), channel_id=1, source_target_pairs={{0,2},{2,0},{4,6},{6,4},{8,10},{10,8},{12,14},{14,12},{16,18},{18,... | collective-permute-start | bytes 921608 | tf_op jit(solution)/shard_map/ppermute | solution.py:746
  37.6 18.8 %collective-permute-start.10 = (bf16[200,768]{1,0:T(8,128)(2,1)S(1)}, bf16[200,768]{1,0:T(8,128)(2,1)S(1)}, u32[]{:S(2)}, u32[]{:S(2)}) collective-permute-start(bf16[200,768]{1,0:T(8,128)(2,1)S(1)} %collective-permute-done.1), channel_id=1, source_target_pairs={{0,2},{2,0},{4,6},{6,4},{8,10},{10,8},{12,14},{14,12},{16,18},{18,... | collective-permute-start | bytes 921608 | tf_op jit(solution)/shard_map/ppermute | solution.py:746
  38.1 23.3 %collective-permute-start.11 = (bf16[200,768]{1,0:T(8,128)(2,1)S(1)}, bf16[200,768]{1,0:T(8,128)(2,1)S(1)}, u32[]{:S(2)}, u32[]{:S(2)}) collective-permute-start(bf16[200,768]{1,0:T(8,128)(2,1)S(1)} %collective-permute-done.2), channel_id=1, source_target_pairs={{0,2},{2,0},{4,6},{6,4},{8,10},{10,8},{12,14},{14,12},{16,18},{18,... | collective-permute-start | bytes 921608 | tf_op jit(solution)/shard_map/ppermute | solution.py:746
  54.4 6.6 %collective-permute-start.7 = (bf16[128,768]{1,0:T(8,128)(2,1)S(1)}, bf16[128,768]{1,0:T(8,128)(2,1)S(1)}, u32[]{:S(2)}, u32[]{:S(2)}) collective-permute-start(bf16[128,768]{1,0:T(8,128)(2,1)S(1)} %slice.87), channel_id=1, source_target_pairs={{0,8},{2,10},{8,16},{10,18},{16,24},{18,26},{24,28},{26,30},{28,20... | collective-permute-start | bytes 589832 | tf_op jit(solution)/shard_map/ppermute | solution.py:741
  56.4 5.1 %collective-permute-start.12 = (bf16[200,768]{1,0:T(8,128)(2,1)S(1)}, bf16[200,768]{1,0:T(8,128)(2,1)S(1)}, u32[]{:S(2)}, u32[]{:S(2)}) collective-permute-start(bf16[200,768]{1,0:T(8,128)(2,1)S(1)} %collective-permute-done.3), channel_id=1, source_target_pairs={{0,2},{2,0},{4,6},{6,4},{8,10},{10,8},{12,14},{14,12},{16,18},{18,... | collective-permute-start | bytes 921608 | tf_op jit(solution)/shard_map/ppermute | solution.py:746
  56.5 5.1 %collective-permute-start.13 = (bf16[200,768]{1,0:T(8,128)(2,1)S(1)}, bf16[200,768]{1,0:T(8,128)(2,1)S(1)}, u32[]{:S(2)}, u32[]{:S(2)}) collective-permute-start(bf16[200,768]{1,0:T(8,128)(2,1)S(1)} %collective-permute-done.4), channel_id=1, source_target_pairs={{0,2},{2,0},{4,6},{6,4},{8,10},{10,8},{12,14},{14,12},{16,18},{18,... | collective-permute-start | bytes 921608 | tf_op jit(solution)/shard_map/ppermute | solution.py:746
  82.3 24.3 %all-to-all-start = ((bf16[8,192,256]{2,1,0:T(8,128)(2,1)}), bf16[8,192,256]{2,1,0:T(8,128)(2,1)S(1)}, u32[]{:S(2)}, u32[]{:S(2)}) async-start(bf16[8,192,256]{2,1,0:T(8,128)(2,1)} %get-tuple-element.137), calls=%async_computation | async-start | bytes 1572864 | tf_op jit(solution)/shard_map/all_to_all | solution.py:901
  86.0 162.4 %reduce-scatter.2.cloned.1.call-start = ((), (), s32[]{:S(2)}) async-start(), calls=%async_computation.4 | async-start | bytes 5640192 | tf_op jit(solution)/shard_map/reduce_scatter | solution.py:1020
  110.4 7.0 %collective-permute-start.18 = (bf16[128,768]{1,0:T(8,128)(2,1)S(1)}, bf16[128,768]{1,0:T(8,128)(2,1)S(1)}, u32[]{:S(2)}, u32[]{:S(2)}) collective-permute-start(bf16[128,768]{1,0:T(8,128)(2,1)S(1)} %get-tuple-element.143.own_ref), channel_id=1, source_target_pairs={{0,1},{1,0},{2,3},{3,2},{4,5},{5,4},{6,7},{7,6},{8,9},{9,8},{10,11... | collective-permute-start | bytes 589832 | tf_op jit(solution)/shard_map/ppermute | solution.py:939
  118.9 6.2 %collective-permute-start.19 = (bf16[128,768]{1,0:T(8,128)(2,1)S(1)}, bf16[128,768]{1,0:T(8,128)(2,1)S(1)}, u32[]{:S(2)}, u32[]{:S(2)}) collective-permute-start(bf16[128,768]{1,0:T(8,128)(2,1)S(1)} %get-tuple-element.147.own_ref), channel_id=1, source_target_pairs={{0,1},{1,0},{2,3},{3,2},{4,5},{5,4},{6,7},{7,6},{8,9},{9,8},{10,11... | collective-permute-start | bytes 589832 | tf_op jit(solution)/shard_map/ppermute | solution.py:951
  127.3 5.7 %collective-permute-start.20 = (bf16[128,768]{1,0:T(8,128)(2,1)S(1)}, bf16[128,768]{1,0:T(8,128)(2,1)S(1)}, u32[]{:S(2)}, u32[]{:S(2)}) collective-permute-start(bf16[128,768]{1,0:T(8,128)(2,1)S(1)} %get-tuple-element.150.own_ref), channel_id=1, source_target_pairs={{0,1},{1,0},{2,3},{3,2},{4,5},{5,4},{6,7},{7,6},{8,9},{9,8},{10,11... | collective-permute-start | bytes 589832 | tf_op jit(solution)/shard_map/ppermute | solution.py:964
  137.5 5.6 %collective-permute-start.22 = (bf16[240,256]{1,0:T(8,128)(2,1)S(1)}, bf16[240,256]{1,0:T(8,128)(2,1)S(1)}, u32[]{:S(2)}, u32[]{:S(2)}) collective-permute-start(bf16[240,256]{1,0:T(8,128)(2,1)S(1)} %get-tuple-element.158), channel_id=1, source_target_pairs={{0,8},{2,10},{8,16},{10,18},{16,24},{18,26},{24,28},{26,30},{28,20... | collective-permute-start | bytes 368648 | tf_op jit(solution)/shard_map/ppermute | solution.py:713
  137.9 5.3 %collective-permute-start.23 = (bf16[240,256]{1,0:T(8,128)(2,1)S(1)}, bf16[240,256]{1,0:T(8,128)(2,1)S(1)}, u32[]{:S(2)}, u32[]{:S(2)}) collective-permute-start(bf16[240,256]{1,0:T(8,128)(2,1)S(1)} %get-tuple-element.158), channel_id=1, source_target_pairs={{8,0},{10,2},{16,8},{18,10},{24,16},{26,18},{28,24},{30,26},{20,28... | collective-permute-start | bytes 368648 | tf_op jit(solution)/shard_map/ppermute | solution.py:713
  148.3 5.6 %collective-permute-start.27 = (bf16[240,256]{1,0:T(8,128)(2,1)S(1)}, bf16[240,256]{1,0:T(8,128)(2,1)S(1)}, u32[]{:S(2)}, u32[]{:S(2)}) collective-permute-start(bf16[240,256]{1,0:T(8,128)(2,1)S(1)} %collective-permute-done.25), channel_id=1, source_target_pairs={{8,0},{10,2},{16,8},{18,10},{24,16},{26,18},{28,24},{30,26},{20,28... | collective-permute-start | bytes 368648 | tf_op jit(solution)/shard_map/ppermute | solution.py:989
  190.2 43.0 %all-to-all-start.1 = ((bf16[8,96,640]{2,1,0:T(8,128)(2,1)}), bf16[8,96,640]{2,1,0:T(8,128)(2,1)S(1)}, u32[]{:S(2)}, u32[]{:S(2)}) async-start(bf16[8,96,640]{2,1,0:T(8,128)(2,1)} %get-tuple-element.177), calls=%async_computation.1 | async-start | bytes 1966080 | tf_op jit(solution)/shard_map/all_to_all | solution.py:1090
  197.6 20.0 %collective-permute-start.30 = (bf16[8,384,128]{2,1,0:T(8,128)(2,1)}, bf16[8,384,128]{2,1,0:T(8,128)(2,1)}, u32[]{:S(2)}, u32[]{:S(2)}) collective-permute-start(bf16[8,384,128]{2,1,0:T(8,128)(2,1)} %get-tuple-element.175), channel_id=1, source_target_pairs={{0,1},{1,0},{2,3},{3,2},{4,5},{5,4},{6,7},{7,6},{8,9},{9,8},{10,11... | collective-permute-start | bytes 2359304 | tf_op jit(solution)/shard_map/ppermute | solution.py:1087
  220.3 12.9 %collective-permute-start.31 = (bf16[384,128]{1,0:T(8,128)(2,1)}, bf16[384,128]{1,0:T(8,128)(2,1)S(1)}, u32[]{:S(2)}, u32[]{:S(2)}) collective-permute-start(bf16[384,128]{1,0:T(8,128)(2,1)} %get-tuple-element.178), channel_id=1, source_target_pairs={{0,4},{2,6},{4,0},{6,2},{8,12},{10,14},{12,8},{14,10},{16,20},{18,... | collective-permute-start | bytes 294920 | tf_op jit(solution)/shard_map/ppermute | solution.py:1095
  222.0 11.1 %collective-permute-start.32 = (bf16[384,128]{1,0:T(8,128)(2,1)}, bf16[384,128]{1,0:T(8,128)(2,1)S(1)}, u32[]{:S(2)}, u32[]{:S(2)}) collective-permute-start(bf16[384,128]{1,0:T(8,128)(2,1)} %get-tuple-element.179), channel_id=1, source_target_pairs={{0,8},{2,10},{4,12},{6,14},{8,0},{10,2},{12,4},{14,6},{16,24},{18,... | collective-permute-start | bytes 294920 | tf_op jit(solution)/shard_map/ppermute | solution.py:1095
  223.6 9.6 %collective-permute-start.33 = (bf16[384,128]{1,0:T(8,128)(2,1)}, bf16[384,128]{1,0:T(8,128)(2,1)S(1)}, u32[]{:S(2)}, u32[]{:S(2)}) collective-permute-start(bf16[384,128]{1,0:T(8,128)(2,1)} %get-tuple-element.180), channel_id=1, source_target_pairs={{0,12},{2,14},{4,8},{6,10},{8,4},{10,6},{12,0},{14,2},{16,28},{18,... | collective-permute-start | bytes 294920 | tf_op jit(solution)/shard_map/ppermute | solution.py:1095
  223.8 10.7 %collective-permute-start.34 = (bf16[384,128]{1,0:T(8,128)(2,1)}, bf16[384,128]{1,0:T(8,128)(2,1)S(1)}, u32[]{:S(2)}, u32[]{:S(2)}) collective-permute-start(bf16[384,128]{1,0:T(8,128)(2,1)} %get-tuple-element.181), channel_id=1, source_target_pairs={{0,16},{2,18},{4,20},{6,22},{8,24},{10,26},{12,28},{14,30},{16,0},... | collective-permute-start | bytes 294920 | tf_op jit(solution)/shard_map/ppermute | solution.py:1095
  238.1 6.2 %collective-permute-start.39 = (f32[6243]{0:T(1024)S(1)}, f32[6243]{0:T(1024)S(1)}, u32[]{:S(2)}, u32[]{:S(2)}) collective-permute-start(f32[6243]{0:T(1024)S(1)} %pad_maximum_fusion.1), channel_id=1, source_target_pairs={{0,2},{2,0},{4,6},{6,4},{8,10},{10,8},{12,14},{14,12},{16,18},{18,... | collective-permute-start | bytes 74924 | tf_op jit(solution)/shard_map/ppermute | solution.py:1120
  238.1 14.0 %collective-permute-start.35 = (bf16[384,128]{1,0:T(8,128)(2,1)}, bf16[384,128]{1,0:T(8,128)(2,1)S(1)}, u32[]{:S(2)}, u32[]{:S(2)}) collective-permute-start(bf16[384,128]{1,0:T(8,128)(2,1)} %get-tuple-element.186), channel_id=1, source_target_pairs={{0,20},{2,22},{4,16},{6,18},{8,28},{10,30},{12,24},{14,26},{16,4},... | collective-permute-start | bytes 294920 | tf_op jit(solution)/shard_map/ppermute | solution.py:1095
  238.7 13.5 %collective-permute-start.36 = (bf16[384,128]{1,0:T(8,128)(2,1)}, bf16[384,128]{1,0:T(8,128)(2,1)S(1)}, u32[]{:S(2)}, u32[]{:S(2)}) collective-permute-start(bf16[384,128]{1,0:T(8,128)(2,1)} %get-tuple-element.187), channel_id=1, source_target_pairs={{0,24},{2,26},{4,28},{6,30},{8,16},{10,18},{12,20},{14,22},{16,8},... | collective-permute-start | bytes 294920 | tf_op jit(solution)/shard_map/ppermute | solution.py:1095
  240.2 11.9 %collective-permute-start.37 = (bf16[384,128]{1,0:T(8,128)(2,1)}, bf16[384,128]{1,0:T(8,128)(2,1)S(1)}, u32[]{:S(2)}, u32[]{:S(2)}) collective-permute-start(bf16[384,128]{1,0:T(8,128)(2,1)} %get-tuple-element.188), channel_id=1, source_target_pairs={{0,28},{2,30},{4,24},{6,26},{8,20},{10,22},{12,16},{14,18},{16,12}... | collective-permute-start | bytes 294920 | tf_op jit(solution)/shard_map/ppermute | solution.py:1095
  244.3 11.2 %collective-permute-start.40 = (f32[48,640]{1,0:T(8,128)}, f32[48,640]{1,0:T(8,128)}, u32[]{:S(2)}, u32[]{:S(2)}) collective-permute-start(f32[48,640]{1,0:T(8,128)} %get-tuple-element.200), channel_id=1, source_target_pairs={{0,2},{2,0},{4,6},{6,4},{8,10},{10,8},{12,14},{14,12},{16,18},{18,... | collective-permute-start | bytes 368648 | tf_op jit(solution)/shard_map/ppermute | solution.py:1108
  (52 other events, 548.3 us)
Sparse Core Ops, SparseCore 0:
  26.2 61.4 all-gather.1
  135.6 93.3 reduce-scatter.1

commit v8 on v7

--- a/solution.py
+++ b/solution.py
@@ -414,12 +414,13 @@
     pos = lax.broadcasted_iota(jnp.int32, (128, tile), 1) + spots_ref[1] * tile
     other = pos + lax.broadcasted_iota(jnp.int32, (128, tile), 0) - rim
     near = (pos >= spots_ref[0]) == (other >= spots_ref[0])
-    for h in range(heads):
-        mine = slice(64 * h, 64 * (h + 1))
+
+    def one(h, carry):
+        mine = pl.ds(pl.multiple_of(h * 64, 64), 64)
         upper, lower = banded(base_ref[h, 0:1], same, tile)
-        own = jnp.concatenate([low_ref[mine], high_ref[mine]], axis=1)
+        own = jnp.concatenate([low_ref[mine, :], high_ref[mine, :]], axis=1)
         out_ref[mine, 128 : 128 + width] = nt(own, upper) + nt(own, lower)
-        values = window_ref[mine].astype(f32)
+        values = window_ref[mine, :].astype(f32)
         own = own.astype(f32)
         sums = []
         for o in range(taps):
@@ -428,6 +429,9 @@
         sums = jnp.concatenate(sums + [jnp.zeros((128 - taps, tile), f32)], axis=0)
         total = jnp.sum(jnp.where(near, sums, 0.0), axis=1, keepdims=True)
         tap_ref[h] = jnp.transpose(jnp.broadcast_to(total, (128, 128)))[0:8]
+        return carry
+
+    lax.fori_loop(0, heads, one, 0)
 
 
 def context_kernel(heads, spots_ref, got_ref, conv_ref, keep_ref, give_ref, num_ref):
@@ -688,6 +692,7 @@
     blocks = WORK if chips % WORK == 0 else 1
     steps = chips // blocks
     work = blocks * tile
+    wide = 2 * blocks if chips % (2 * blocks) == 0 else blocks
     planes_of = [[CORES * c + k for c in range(chips)] for k in range(CORES)]
     across = partial(
         lax.all_to_all, axis_name="seq", split_axis=0, concat_axis=0, tiled=True,
@@ -859,15 +864,15 @@
         dimension_semantics=("arbitrary", "arbitrary"), vmem_limit_bytes=VMEM_LIMIT
     )
     num_parts, q_unit, k_unit, values, inverses, tables, counts, qkv_all = pl.pallas_call(
-        partial(forward_kernel, hashes, bits, rows, work, steps, heads, parts, weight_spots),
-        grid=(2, steps),
+        partial(forward_kernel, hashes, bits, rows, wide * tile, chips // wide, heads, parts, weight_spots),
+        grid=(2, chips // wide),
         in_specs=[
             smem,
             *[anywhere] * (parts + weight_count),
             resident(*bit_w.shape),
         ],
         out_specs=[
-            stepped(1, blocks, feats, tile),
+            stepped(1, wide, feats, tile),
             resident(feats, total),
             resident(feats, total),
             resident(feats, total + 256),
@@ -888,7 +893,7 @@
         ],
         scratch_shapes=[
             pltpu.VMEM((heads, code_rows, 2 * head_dim + 16), f32),
-            pltpu.VMEM((heads, code_rows, work), bf16),
+            pltpu.VMEM((heads, code_rows, wide * tile), bf16),
             pltpu.VMEM((3 * feats, width), bf16),
             pltpu.VMEM((heads, 2 * head_dim, code_rows), bf16),
             pltpu.VMEM((seq_count, tok_rows, width), bf16),

time: 269 us -> 267 us (level)
  no operation moved by 1% of the time
where the time goes in v8:
time: 267 us; the launch traced here: 264 us
  waiting for transfers between devices  87.3 us (33%)
  Pallas kernels  81.1 us (30%)
  starting transfers between devices  45.8 us (17%)
  local copies, waits for them, and re-layouts  23 us (9%)
  between operations  14.7 us (6%)
  other arithmetic  12.5 us (5%)
    pallas_call x1, Pallas kernels, on_device(): pl.pallas_call(partial(backward_kernel, hashes, bits, rows, work, steps,...  32.2 us
    ppermute x8, waiting for transfers between devices, ring(): moved = [lax.ppermute(v, 'seq', p) for v, p in zip(moved, (ahead, behind))]  30.1 us
    pallas_call x12, Pallas kernels, once(): pl.pallas_call(kernel, grid=(1,) if blocks else (), in_specs=specs, out_s...  17.1 us
    pallas_call x1, Pallas kernels, on_device(): pl.pallas_call(partial(forward_kernel, hashes, bits, rows, wide * tile, c...  16.6 us
    all_to_all x1, waiting for transfers between devices, on_device(): num_got = across(num_parts)  14 us
    ppermute x7, starting transfers between devices, on_device(): back_got.append(lax.ppermute(pair_sums[d], 'seq', perm))  12.3 us
    ppermute x5, waiting for transfers between devices, on_device(): lax.ppermute(v, 'seq', p)  9.73 us
    ppermute x8, starting transfers between devices, ring(): moved = [lax.ppermute(v, 'seq', p) for v, p in zip(moved, (ahead, behind))]  9.16 us
  transfers between devices with their start and end apart: 45, of which 24 were waited for; matrix products, arithmetic and copies ran while one was open for 10% of the time, Pallas kernels for 27%

profile of v8, /device:TPU:0, one launch (start us, length us, event | category | flops | bytes accessed | tf_op | source)
XLA Modules:
  0.0 264.4 jit_solution(745298724204168849)
XLA Ops:
  11.6 3.0 %collective-permute-start.1 = (bf16[200,768]{1,0:T(8,128)(2,1)S(1)}, bf16[200,768]{1,0:T(8,128)(2,1)S(1)}, u32[]{:S(2)}, u32[]{:S(2)}) collective-permute-start(bf16[200,768]{1,0:T(8,128)(2,1)S(1)} %fusion.2), channel_id=1, source_target_pairs={{0,8},{2,10},{8,16},{10,18},{16,24},{18,26},{24,28},{26,30},{28,20... | collective-permute-start | bytes 921608 | tf_op jit(solution)/shard_map/ppermute | solution.py:718
  17.1 4.9 %collective-permute-done.1 = bf16[200,768]{1,0:T(8,128)(2,1)S(1)} collective-permute-done((bf16[200,768]{1,0:T(8,128)(2,1)S(1)}, bf16[200,768]{1,0:T(8,128)(2,1)S(1)}, u32[]{:S(2)}, u32[]{:S(2)}) %collective-permute-start.1) | collective-permute-done | bytes 307232 | tf_op jit(solution)/shard_map/ppermute | solution.py:718
  24.2 1.8 pack.1
  28.1 6.2 %collective-permute-done.3 = bf16[200,768]{1,0:T(8,128)(2,1)S(1)} collective-permute-done((bf16[200,768]{1,0:T(8,128)(2,1)S(1)}, bf16[200,768]{1,0:T(8,128)(2,1)S(1)}, u32[]{:S(2)}, u32[]{:S(2)}) %collective-permute-start.3) | collective-permute-done | bytes 307232 | tf_op jit(solution)/shard_map/ppermute | solution.py:718
  38.1 12.2 %collective-permute-done.5 = bf16[200,768]{1,0:T(8,128)(2,1)S(1)} collective-permute-done((bf16[200,768]{1,0:T(8,128)(2,1)S(1)}, bf16[200,768]{1,0:T(8,128)(2,1)S(1)}, u32[]{:S(2)}, u32[]{:S(2)}) %collective-permute-start.5) | collective-permute-done | bytes 307232 | tf_op jit(solution)/shard_map/ppermute | solution.py:718
  50.3 4.0 %collective-permute-done.6 = bf16[200,768]{1,0:T(8,128)(2,1)S(1)} collective-permute-done((bf16[200,768]{1,0:T(8,128)(2,1)S(1)}, bf16[200,768]{1,0:T(8,128)(2,1)S(1)}, u32[]{:S(2)}, u32[]{:S(2)}) %collective-permute-start.6) | collective-permute-done | bytes 307232 | tf_op jit(solution)/shard_map/ppermute | solution.py:718
  54.4 1.8 collective-permute-start.7
  57.0 4.0 %collective-permute-done.8 = bf16[72,768]{1,0:T(8,128)(2,1)S(1)} collective-permute-done((bf16[72,768]{1,0:T(8,128)(2,1)S(1)}, bf16[72,768]{1,0:T(8,128)(2,1)S(1)}, u32[]{:S(2)}, u32[]{:S(2)}) %collective-permute-start.8) | collective-permute-done | bytes 110624 | tf_op jit(solution)/shard_map/ppermute | solution.py:747
  64.0 16.6 %hash_forward.1 = (bf16[8,192,256]{2,1,0:T(8,128)(2,1)}, bf16[192,2048]{1,0:T(8,128)(2,1)}, bf16[192,2048]{1,0:T(8,128)(2,1)}, bf16[192,2304]{1,0:T(8,128)(2,1)}...) custom-call(s32[28]{0:T(128)} %pad_add_fusion.spots_ref, ...), custom_call_target="tpu_custom_call" | custom-call | tf_op jit(solution)/shard_map/hash_forward/pallas_call | solution.py:866
  80.5 3.7 %all-to-all-start = ((bf16[8,192,256]{2,1,0:T(8,128)(2,1)}), bf16[8,192,256]{2,1,0:T(8,128)(2,1)S(1)}, u32[]{:S(2)}, u32[]{:S(2)}) async-start(bf16[8,192,256]{2,1,0:T(8,128)(2,1)} %get-tuple-element.137), calls=%async_computation | async-start | bytes 1572864 | tf_op jit(solution)/shard_map/all_to_all | solution.py:906
  86.4 1.9 scatter.4.base_ref
  90.8 14.0 %all-to-all-done.got_ref = bf16[8,192,256]{2,1,0:T(8,128)(2,1)S(1)} async-done(((bf16[8,192,256]{2,1,0:T(8,128)(2,1)}), bf16[8,192,256]{2,1,0:T(8,128)(2,1)S(1)}, u32[]{:S(2)}, u32[]{:S(2)}) %all-to-all-start) | async-done | bytes 786464 | tf_op jit(solution)/shard_map/all_to_all | solution.py:906
  110.2 5.5 %collective-permute-done.18.other_ref = bf16[128,768]{1,0:T(8,128)(2,1)S(1)} collective-permute-done((bf16[128,768]{1,0:T(8,128)(2,1)S(1)}, bf16[128,768]{1,0:T(8,128)(2,1)S(1)}, u32[]{:S(2)}, u32[]{:S(2)}) %collective-permute-start.18) | collective-permute-done | bytes 196640 | tf_op jit(solution)/shard_map/ppermute | solution.py:944
  118.7 4.6 %collective-permute-done.19.other_ref = bf16[128,768]{1,0:T(8,128)(2,1)S(1)} collective-permute-done((bf16[128,768]{1,0:T(8,128)(2,1)S(1)}, bf16[128,768]{1,0:T(8,128)(2,1)S(1)}, u32[]{:S(2)}, u32[]{:S(2)}) %collective-permute-start.19) | collective-permute-done | bytes 196640 | tf_op jit(solution)/shard_map/ppermute | solution.py:956
  123.3 2.3 feed_back.1
  127.1 3.7 %feed_grads.1.all_ref = bf16[768,3456]{1,0:T(8,128)(2,1)} custom-call(f32[128,768]{1,0:T(8,128)S(1)} %get-tuple-element.145.hat_ref, f32[4,768]{1,0:T(4,128)S(1)} %copy-done.6, bf16[128,1536]{1,0:T(8,128)(2,1)S(1)} %get-tuple-element.191.slope_ref, bf16[128,768]{1,0:T(8,128)(2,1)S(1)} %get-tuple-element.192.feed_ref, ...), custom_call_target="tpu_custom_call" | custom-call | tf_op jit(solution)/shard_map/feed_grads/pallas_call | solution.py:1006
  137.8 2.9 %conv_backward.1 = (f32[192,768]{1,0:T(8,128)S(1)}, f32[3,8,128]{2,1,0:T(8,128)S(1)}) custom-call(s32[28]{0:T(128)S(1)} %copy-done.9, bf16[192,512]{1,0:T(8,128)(2,1)S(1)} %get-tuple-element.159.window_ref, bf16[192,128]{1,0:T(8,128)(2,1)S(1)} %get-tuple-element.160.low_ref, bf16[192,128]{1,0:T(8,128)(2,1)S(1)} %get-tuple-element.161.high_ref, ...), custom_call_target="tpu_custom_call" | custom-call | tf_op jit(solution)/shard_map/conv_backward/pallas_call | solution.py:821
  143.7 2.9 %collective-permute-done.24 = bf16[240,256]{1,0:T(8,128)(2,1)S(1)} collective-permute-done((bf16[240,256]{1,0:T(8,128)(2,1)S(1)}, bf16[240,256]{1,0:T(8,128)(2,1)S(1)}, u32[]{:S(2)}, u32[]{:S(2)}) %collective-permute-start.24) | collective-permute-done | bytes 122912 | tf_op jit(solution)/shard_map/ppermute | solution.py:994
  148.6 2.9 %collective-permute-done.26 = bf16[240,256]{1,0:T(8,128)(2,1)S(1)} collective-permute-done((bf16[240,256]{1,0:T(8,128)(2,1)S(1)}, bf16[240,256]{1,0:T(8,128)(2,1)S(1)}, u32[]{:S(2)}, u32[]{:S(2)}) %collective-permute-start.26) | collective-permute-done | bytes 122912 | tf_op jit(solution)/shard_map/ppermute | solution.py:994
  152.4 3.9 %collective-permute-done.28 = bf16[240,256]{1,0:T(8,128)(2,1)S(1)} collective-permute-done((bf16[240,256]{1,0:T(8,128)(2,1)S(1)}, bf16[240,256]{1,0:T(8,128)(2,1)S(1)}, u32[]{:S(2)}, u32[]{:S(2)}) %collective-permute-start.28) | collective-permute-done | bytes 122912 | tf_op jit(solution)/shard_map/ppermute | solution.py:994
  156.4 32.2 %hash_backward.1 = (bf16[8,96,640]{2,1,0:T(8,128)(2,1)}, bf16[8,768,128]{2,1,0:T(8,128)(2,1)}, bf16[8,768,128]{2,1,0:T(8,128)(2,1)}, bf16[8,48,256]{2,1,0:T(8,128)(2,1)}) custom-call(s32[28]{0:T(128)} %pad_add_fusion.spots_ref, bf16[1,200,768]{2,1,0:T(8,128)(2,1)} %bitcast.108, bf16[1,200,768]{2,1,0:T(8,128)(2,1)} %bitcast.120, ...), custom_call_target="tpu_custom_call" | custom-call | tf_op jit(solution)/shard_map/hash_backward/pallas_call | solution.py:1027
  188.7 4.1 %all-to-all-start.1 = ((bf16[8,96,640]{2,1,0:T(8,128)(2,1)}), bf16[8,96,640]{2,1,0:T(8,128)(2,1)S(1)}, u32[]{:S(2)}, u32[]{:S(2)}) async-start(bf16[8,96,640]{2,1,0:T(8,128)(2,1)} %get-tuple-element.177), calls=%async_computation.1 | async-start | bytes 1966080 | tf_op jit(solution)/shard_map/all_to_all | solution.py:1095
  192.8 3.0 %chip_sum.1 = (bf16[8,384,128]{2,1,0:T(8,128)(2,1)}, bf16[8,384,128]{2,1,0:T(8,128)(2,1)}) custom-call(s32[28]{0:T(128)} %pad_add_fusion.spots_ref, bf16[8,768,128]{2,1,0:T(8,128)(2,1)} %get-tuple-element.172.own_ref, bf16[8,768,128]{2,1,0:T(8,128)(2,1)} %collective-permute-done.29.other_ref), custom_call_target="tpu_custom_call" | custom-call | tf_op jit(solution)/shard_map/chip_sum/pallas_call | solution.py:1078
  200.6 3.7 %reshape.152 = f32[8,3,2,8,2,8,8]{6,5,4,3,2,1,0:T(8,128)} reshape(f32[8,24,256]{2,1,0:T(8,128)} %slice.102) | data formatting | bytes 393216 | tf_op jit(solution)/shard_map/reshape | solution.py:1118
  206.0 1.8 copy.71
  209.5 6.3 %collective-permute-done.30.other_ref = bf16[8,384,128]{2,1,0:T(8,128)(2,1)} collective-permute-done((bf16[8,384,128]{2,1,0:T(8,128)(2,1)}, bf16[8,384,128]{2,1,0:T(8,128)(2,1)}, u32[]{:S(2)}, u32[]{:S(2)}) %collective-permute-start.30) | collective-permute-done | bytes 786464 | tf_op jit(solution)/shard_map/ppermute | solution.py:1092
  215.8 2.1 pair_sum.1
  222.0 2.6 collective-permute-start.34
  225.6 5.8 %all-to-all-done.1.got_ref = bf16[8,96,640]{2,1,0:T(8,128)(2,1)S(1)} async-done(((bf16[8,96,640]{2,1,0:T(8,128)(2,1)}), bf16[8,96,640]{2,1,0:T(8,128)(2,1)S(1)}, u32[]{:S(2)}, u32[]{:S(2)}) %all-to-all-start.1) | async-done | bytes 983072 | tf_op jit(solution)/shard_map/all_to_all | solution.py:1095
  238.4 4.1 %collective-permute-start.37 = (bf16[384,128]{1,0:T(8,128)(2,1)}, bf16[384,128]{1,0:T(8,128)(2,1)S(1)}, u32[]{:S(2)}, u32[]{:S(2)}) collective-permute-start(bf16[384,128]{1,0:T(8,128)(2,1)} %get-tuple-element.188), channel_id=1, source_target_pairs={{0,28},{2,30},{4,24},{6,26},{8,20},{10,22},{12,16},{14,18},{16,12}... | collective-permute-start | bytes 294920 | tf_op jit(solution)/shard_map/ppermute | solution.py:1100
  246.7 3.2 %big_adam.1 = (f32[48,1536]{1,0:T(8,128)}, f32[48,1536]{1,0:T(8,128)}, f32[48,1536]{1,0:T(8,128)}, bf16[48,1536]{1,0:T(8,128)(2,1)}, f32[48,1536]{1,0:T(8,128)},...) custom-call(bf16[48,3456]{1,0:T(8,128)(2,1)} %reduce-scatter.2.clone, ...), custom_call_target="tpu_custom_call" | custom-call | tf_op jit(solution)/shard_map/big_adam/pallas_call | solution.py:794
  253.8 2.3 qkv_adam.1
  (212 shorter events, 75.7 us)
Async XLA Ops:
  7.2 99.8 %all-gather.2.cloned.1.call-start = ((), (), s32[]{:S(2)}) async-start(), calls=%async_computation.3 | async-start | bytes 5640192 | tf_op jit(solution)/shard_map/all_gather | solution.py:851
  11.6 10.5 %collective-permute-start.1 = (bf16[200,768]{1,0:T(8,128)(2,1)S(1)}, bf16[200,768]{1,0:T(8,128)(2,1)S(1)}, u32[]{:S(2)}, u32[]{:S(2)}) collective-permute-start(bf16[200,768]{1,0:T(8,128)(2,1)S(1)} %fusion.2), channel_id=1, source_target_pairs={{0,8},{2,10},{8,16},{10,18},{16,24},{18,26},{24,28},{26,30},{28,20... | collective-permute-start | bytes 921608 | tf_op jit(solution)/shard_map/ppermute | solution.py:718
  14.5 9.1 %collective-permute-start.2 = (bf16[200,768]{1,0:T(8,128)(2,1)S(1)}, bf16[200,768]{1,0:T(8,128)(2,1)S(1)}, u32[]{:S(2)}, u32[]{:S(2)}) collective-permute-start(bf16[200,768]{1,0:T(8,128)(2,1)S(1)} %fusion.2), channel_id=1, source_target_pairs={{8,0},{10,2},{16,8},{18,10},{24,16},{26,18},{28,24},{30,26},{20,28... | collective-permute-start | bytes 921608 | tf_op jit(solution)/shard_map/ppermute | solution.py:718
  26.1 8.2 %collective-permute-start.3 = (bf16[200,768]{1,0:T(8,128)(2,1)S(1)}, bf16[200,768]{1,0:T(8,128)(2,1)S(1)}, u32[]{:S(2)}, u32[]{:S(2)}) collective-permute-start(bf16[200,768]{1,0:T(8,128)(2,1)S(1)} %collective-permute-done.1), channel_id=1, source_target_pairs={{0,8},{2,10},{8,16},{10,18},{16,24},{18,26},{24,28},{26,30},{28,20... | collective-permute-start | bytes 921608 | tf_op jit(solution)/shard_map/ppermute | solution.py:718
  27.7 7.9 %collective-permute-start.4 = (bf16[200,768]{1,0:T(8,128)(2,1)S(1)}, bf16[200,768]{1,0:T(8,128)(2,1)S(1)}, u32[]{:S(2)}, u32[]{:S(2)}) collective-permute-start(bf16[200,768]{1,0:T(8,128)(2,1)S(1)} %collective-permute-done.2), channel_id=1, source_target_pairs={{8,0},{10,2},{16,8},{18,10},{24,16},{26,18},{28,24},{30,26},{20,28... | collective-permute-start | bytes 921608 | tf_op jit(solution)/shard_map/ppermute | solution.py:718
  35.6 14.7 %collective-permute-start.5 = (bf16[200,768]{1,0:T(8,128)(2,1)S(1)}, bf16[200,768]{1,0:T(8,128)(2,1)S(1)}, u32[]{:S(2)}, u32[]{:S(2)}) collective-permute-start(bf16[200,768]{1,0:T(8,128)(2,1)S(1)} %collective-permute-done.3), channel_id=1, source_target_pairs={{0,8},{2,10},{8,16},{10,18},{16,24},{18,26},{24,28},{26,30},{28,20... | collective-permute-start | bytes 921608 | tf_op jit(solution)/shard_map/ppermute | solution.py:718
  37.2 17.2 %collective-permute-start.6 = (bf16[200,768]{1,0:T(8,128)(2,1)S(1)}, bf16[200,768]{1,0:T(8,128)(2,1)S(1)}, u32[]{:S(2)}, u32[]{:S(2)}) collective-permute-start(bf16[200,768]{1,0:T(8,128)(2,1)S(1)} %collective-permute-done.4), channel_id=1, source_target_pairs={{8,0},{10,2},{16,8},{18,10},{24,16},{26,18},{28,24},{30,26},{20,28... | collective-permute-start | bytes 921608 | tf_op jit(solution)/shard_map/ppermute | solution.py:718
  37.6 18.8 %collective-permute-start.9 = (bf16[200,768]{1,0:T(8,128)(2,1)S(1)}, bf16[200,768]{1,0:T(8,128)(2,1)S(1)}, u32[]{:S(2)}, u32[]{:S(2)}) collective-permute-start(bf16[200,768]{1,0:T(8,128)(2,1)S(1)} %fusion.2), channel_id=1, source_target_pairs={{0,2},{2,0},{4,6},{6,4},{8,10},{10,8},{12,14},{14,12},{16,18},{18,... | collective-permute-start | bytes 921608 | tf_op jit(solution)/shard_map/ppermute | solution.py:751
  37.6 18.8 %collective-permute-start.10 = (bf16[200,768]{1,0:T(8,128)(2,1)S(1)}, bf16[200,768]{1,0:T(8,128)(2,1)S(1)}, u32[]{:S(2)}, u32[]{:S(2)}) collective-permute-start(bf16[200,768]{1,0:T(8,128)(2,1)S(1)} %collective-permute-done.1), channel_id=1, source_target_pairs={{0,2},{2,0},{4,6},{6,4},{8,10},{10,8},{12,14},{14,12},{16,18},{18,... | collective-permute-start | bytes 921608 | tf_op jit(solution)/shard_map/ppermute | solution.py:751
  38.1 23.3 %collective-permute-start.11 = (bf16[200,768]{1,0:T(8,128)(2,1)S(1)}, bf16[200,768]{1,0:T(8,128)(2,1)S(1)}, u32[]{:S(2)}, u32[]{:S(2)}) collective-permute-start(bf16[200,768]{1,0:T(8,128)(2,1)S(1)} %collective-permute-done.2), channel_id=1, source_target_pairs={{0,2},{2,0},{4,6},{6,4},{8,10},{10,8},{12,14},{14,12},{16,18},{18,... | collective-permute-start | bytes 921608 | tf_op jit(solution)/shard_map/ppermute | solution.py:751
  54.4 6.6 %collective-permute-start.7 = (bf16[128,768]{1,0:T(8,128)(2,1)S(1)}, bf16[128,768]{1,0:T(8,128)(2,1)S(1)}, u32[]{:S(2)}, u32[]{:S(2)}) collective-permute-start(bf16[128,768]{1,0:T(8,128)(2,1)S(1)} %slice.87), channel_id=1, source_target_pairs={{0,8},{2,10},{8,16},{10,18},{16,24},{18,26},{24,28},{26,30},{28,20... | collective-permute-start | bytes 589832 | tf_op jit(solution)/shard_map/ppermute | solution.py:746
  56.4 5.1 %collective-permute-start.12 = (bf16[200,768]{1,0:T(8,128)(2,1)S(1)}, bf16[200,768]{1,0:T(8,128)(2,1)S(1)}, u32[]{:S(2)}, u32[]{:S(2)}) collective-permute-start(bf16[200,768]{1,0:T(8,128)(2,1)S(1)} %collective-permute-done.3), channel_id=1, source_target_pairs={{0,2},{2,0},{4,6},{6,4},{8,10},{10,8},{12,14},{14,12},{16,18},{18,... | collective-permute-start | bytes 921608 | tf_op jit(solution)/shard_map/ppermute | solution.py:751
  56.5 5.1 %collective-permute-start.13 = (bf16[200,768]{1,0:T(8,128)(2,1)S(1)}, bf16[200,768]{1,0:T(8,128)(2,1)S(1)}, u32[]{:S(2)}, u32[]{:S(2)}) collective-permute-start(bf16[200,768]{1,0:T(8,128)(2,1)S(1)} %collective-permute-done.4), channel_id=1, source_target_pairs={{0,2},{2,0},{4,6},{6,4},{8,10},{10,8},{12,14},{14,12},{16,18},{18,... | collective-permute-start | bytes 921608 | tf_op jit(solution)/shard_map/ppermute | solution.py:751
  80.5 24.3 %all-to-all-start = ((bf16[8,192,256]{2,1,0:T(8,128)(2,1)}), bf16[8,192,256]{2,1,0:T(8,128)(2,1)S(1)}, u32[]{:S(2)}, u32[]{:S(2)}) async-start(bf16[8,192,256]{2,1,0:T(8,128)(2,1)} %get-tuple-element.137), calls=%async_computation | async-start | bytes 1572864 | tf_op jit(solution)/shard_map/all_to_all | solution.py:906
  84.3 162.4 %reduce-scatter.2.cloned.1.call-start = ((), (), s32[]{:S(2)}) async-start(), calls=%async_computation.4 | async-start | bytes 5640192 | tf_op jit(solution)/shard_map/reduce_scatter | solution.py:1025
  108.6 7.0 %collective-permute-start.18 = (bf16[128,768]{1,0:T(8,128)(2,1)S(1)}, bf16[128,768]{1,0:T(8,128)(2,1)S(1)}, u32[]{:S(2)}, u32[]{:S(2)}) collective-permute-start(bf16[128,768]{1,0:T(8,128)(2,1)S(1)} %get-tuple-element.143.own_ref), channel_id=1, source_target_pairs={{0,1},{1,0},{2,3},{3,2},{4,5},{5,4},{6,7},{7,6},{8,9},{9,8},{10,11... | collective-permute-start | bytes 589832 | tf_op jit(solution)/shard_map/ppermute | solution.py:944
  117.1 6.2 %collective-permute-start.19 = (bf16[128,768]{1,0:T(8,128)(2,1)S(1)}, bf16[128,768]{1,0:T(8,128)(2,1)S(1)}, u32[]{:S(2)}, u32[]{:S(2)}) collective-permute-start(bf16[128,768]{1,0:T(8,128)(2,1)S(1)} %get-tuple-element.147.own_ref), channel_id=1, source_target_pairs={{0,1},{1,0},{2,3},{3,2},{4,5},{5,4},{6,7},{7,6},{8,9},{9,8},{10,11... | collective-permute-start | bytes 589832 | tf_op jit(solution)/shard_map/ppermute | solution.py:956
  125.6 5.7 %collective-permute-start.20 = (bf16[128,768]{1,0:T(8,128)(2,1)S(1)}, bf16[128,768]{1,0:T(8,128)(2,1)S(1)}, u32[]{:S(2)}, u32[]{:S(2)}) collective-permute-start(bf16[128,768]{1,0:T(8,128)(2,1)S(1)} %get-tuple-element.150.own_ref), channel_id=1, source_target_pairs={{0,1},{1,0},{2,3},{3,2},{4,5},{5,4},{6,7},{7,6},{8,9},{9,8},{10,11... | collective-permute-start | bytes 589832 | tf_op jit(solution)/shard_map/ppermute | solution.py:969
  135.8 5.9 %collective-permute-start.22 = (bf16[240,256]{1,0:T(8,128)(2,1)S(1)}, bf16[240,256]{1,0:T(8,128)(2,1)S(1)}, u32[]{:S(2)}, u32[]{:S(2)}) collective-permute-start(bf16[240,256]{1,0:T(8,128)(2,1)S(1)} %get-tuple-element.158), channel_id=1, source_target_pairs={{0,8},{2,10},{8,16},{10,18},{16,24},{18,26},{24,28},{26,30},{28,20... | collective-permute-start | bytes 368648 | tf_op jit(solution)/shard_map/ppermute | solution.py:718
  136.1 5.5 %collective-permute-start.23 = (bf16[240,256]{1,0:T(8,128)(2,1)S(1)}, bf16[240,256]{1,0:T(8,128)(2,1)S(1)}, u32[]{:S(2)}, u32[]{:S(2)}) collective-permute-start(bf16[240,256]{1,0:T(8,128)(2,1)S(1)} %get-tuple-element.158), channel_id=1, source_target_pairs={{8,0},{10,2},{16,8},{18,10},{24,16},{26,18},{28,24},{30,26},{20,28... | collective-permute-start | bytes 368648 | tf_op jit(solution)/shard_map/ppermute | solution.py:718
  146.8 5.6 %collective-permute-start.27 = (bf16[240,256]{1,0:T(8,128)(2,1)S(1)}, bf16[240,256]{1,0:T(8,128)(2,1)S(1)}, u32[]{:S(2)}, u32[]{:S(2)}) collective-permute-start(bf16[240,256]{1,0:T(8,128)(2,1)S(1)} %collective-permute-done.25), channel_id=1, source_target_pairs={{8,0},{10,2},{16,8},{18,10},{24,16},{26,18},{28,24},{30,26},{20,28... | collective-permute-start | bytes 368648 | tf_op jit(solution)/shard_map/ppermute | solution.py:994
  188.7 42.7 %all-to-all-start.1 = ((bf16[8,96,640]{2,1,0:T(8,128)(2,1)}), bf16[8,96,640]{2,1,0:T(8,128)(2,1)S(1)}, u32[]{:S(2)}, u32[]{:S(2)}) async-start(bf16[8,96,640]{2,1,0:T(8,128)(2,1)} %get-tuple-element.177), calls=%async_computation.1 | async-start | bytes 1966080 | tf_op jit(solution)/shard_map/all_to_all | solution.py:1095
  195.8 20.0 %collective-permute-start.30 = (bf16[8,384,128]{2,1,0:T(8,128)(2,1)}, bf16[8,384,128]{2,1,0:T(8,128)(2,1)}, u32[]{:S(2)}, u32[]{:S(2)}) collective-permute-start(bf16[8,384,128]{2,1,0:T(8,128)(2,1)} %get-tuple-element.175), channel_id=1, source_target_pairs={{0,1},{1,0},{2,3},{3,2},{4,5},{5,4},{6,7},{7,6},{8,9},{9,8},{10,11... | collective-permute-start | bytes 2359304 | tf_op jit(solution)/shard_map/ppermute | solution.py:1092
  218.5 12.9 %collective-permute-start.31 = (bf16[384,128]{1,0:T(8,128)(2,1)}, bf16[384,128]{1,0:T(8,128)(2,1)S(1)}, u32[]{:S(2)}, u32[]{:S(2)}) collective-permute-start(bf16[384,128]{1,0:T(8,128)(2,1)} %get-tuple-element.178), channel_id=1, source_target_pairs={{0,4},{2,6},{4,0},{6,2},{8,12},{10,14},{12,8},{14,10},{16,20},{18,... | collective-permute-start | bytes 294920 | tf_op jit(solution)/shard_map/ppermute | solution.py:1100
  220.3 11.1 %collective-permute-start.32 = (bf16[384,128]{1,0:T(8,128)(2,1)}, bf16[384,128]{1,0:T(8,128)(2,1)S(1)}, u32[]{:S(2)}, u32[]{:S(2)}) collective-permute-start(bf16[384,128]{1,0:T(8,128)(2,1)} %get-tuple-element.179), channel_id=1, source_target_pairs={{0,8},{2,10},{4,12},{6,14},{8,0},{10,2},{12,4},{14,6},{16,24},{18,... | collective-permute-start | bytes 294920 | tf_op jit(solution)/shard_map/ppermute | solution.py:1100
  221.8 9.6 %collective-permute-start.33 = (bf16[384,128]{1,0:T(8,128)(2,1)}, bf16[384,128]{1,0:T(8,128)(2,1)S(1)}, u32[]{:S(2)}, u32[]{:S(2)}) collective-permute-start(bf16[384,128]{1,0:T(8,128)(2,1)} %get-tuple-element.180), channel_id=1, source_target_pairs={{0,12},{2,14},{4,8},{6,10},{8,4},{10,6},{12,0},{14,2},{16,28},{18,... | collective-permute-start | bytes 294920 | tf_op jit(solution)/shard_map/ppermute | solution.py:1100
  222.0 10.7 %collective-permute-start.34 = (bf16[384,128]{1,0:T(8,128)(2,1)}, bf16[384,128]{1,0:T(8,128)(2,1)S(1)}, u32[]{:S(2)}, u32[]{:S(2)}) collective-permute-start(bf16[384,128]{1,0:T(8,128)(2,1)} %get-tuple-element.181), channel_id=1, source_target_pairs={{0,16},{2,18},{4,20},{6,22},{8,24},{10,26},{12,28},{14,30},{16,0},... | collective-permute-start | bytes 294920 | tf_op jit(solution)/shard_map/ppermute | solution.py:1100
  236.4 6.2 %collective-permute-start.39 = (f32[6243]{0:T(1024)S(1)}, f32[6243]{0:T(1024)S(1)}, u32[]{:S(2)}, u32[]{:S(2)}) collective-permute-start(f32[6243]{0:T(1024)S(1)} %pad_maximum_fusion.1), channel_id=1, source_target_pairs={{0,2},{2,0},{4,6},{6,4},{8,10},{10,8},{12,14},{14,12},{16,18},{18,... | collective-permute-start | bytes 74924 | tf_op jit(solution)/shard_map/ppermute | solution.py:1125
  236.4 14.0 %collective-permute-start.35 = (bf16[384,128]{1,0:T(8,128)(2,1)}, bf16[384,128]{1,0:T(8,128)(2,1)S(1)}, u32[]{:S(2)}, u32[]{:S(2)}) collective-permute-start(bf16[384,128]{1,0:T(8,128)(2,1)} %get-tuple-element.186), channel_id=1, source_target_pairs={{0,20},{2,22},{4,16},{6,18},{8,28},{10,30},{12,24},{14,26},{16,4},... | collective-permute-start | bytes 294920 | tf_op jit(solution)/shard_map/ppermute | solution.py:1100
  236.9 13.5 %collective-permute-start.36 = (bf16[384,128]{1,0:T(8,128)(2,1)}, bf16[384,128]{1,0:T(8,128)(2,1)S(1)}, u32[]{:S(2)}, u32[]{:S(2)}) collective-permute-start(bf16[384,128]{1,0:T(8,128)(2,1)} %get-tuple-element.187), channel_id=1, source_target_pairs={{0,24},{2,26},{4,28},{6,30},{8,16},{10,18},{12,20},{14,22},{16,8},... | collective-permute-start | bytes 294920 | tf_op jit(solution)/shard_map/ppermute | solution.py:1100
  238.4 12.0 %collective-permute-start.37 = (bf16[384,128]{1,0:T(8,128)(2,1)}, bf16[384,128]{1,0:T(8,128)(2,1)S(1)}, u32[]{:S(2)}, u32[]{:S(2)}) collective-permute-start(bf16[384,128]{1,0:T(8,128)(2,1)} %get-tuple-element.188), channel_id=1, source_target_pairs={{0,28},{2,30},{4,24},{6,26},{8,20},{10,22},{12,16},{14,18},{16,12}... | collective-permute-start | bytes 294920 | tf_op jit(solution)/shard_map/ppermute | solution.py:1100
  242.6 11.3 %collective-permute-start.40 = (f32[48,640]{1,0:T(8,128)}, f32[48,640]{1,0:T(8,128)}, u32[]{:S(2)}, u32[]{:S(2)}) collective-permute-start(f32[48,640]{1,0:T(8,128)} %get-tuple-element.200), channel_id=1, source_target_pairs={{0,2},{2,0},{4,6},{6,4},{8,10},{10,8},{12,14},{14,12},{16,18},{18,... | collective-permute-start | bytes 368648 | tf_op jit(solution)/shard_map/ppermute | solution.py:1113
  (52 other events, 543.1 us)
Sparse Core Ops, SparseCore 0:
  26.2 61.4 all-gather.1
  133.8 93.4 reduce-scatter.1

commit v9 on v8

--- a/solution.py
+++ b/solution.py
@@ -1073,11 +1073,11 @@
     )
 
     half = width // 2
-    group = chips // 2
+    group = chips // 4
     per_chip = lambda *dims: pl.BlockSpec((group,) + dims, lambda i: (i, 0, 0))
     keep, give = pl.pallas_call(
         chip_sum_kernel,
-        grid=(2,),
+        grid=(4,),
         in_specs=[smem, per_chip(width, tok_rows), per_chip(width, tok_rows)],
         out_specs=[per_chip(half, tok_rows), per_chip(half, tok_rows)],
         out_shape=[shape((chips, half, tok_rows), bf16)] * 2,

time: 267 us -> 267 us (level)
  transfers between devices with their start and end apart: 45 -> 45, of which waited for: 24 -> 25; matrix products, arithmetic and copies ran while one was open for 10% -> 10% of each run, Pallas kernels for 27% -> 27%
where the time goes in v9:
time: 267 us; the launch traced here: 265 us
  waiting for transfers between devices  86.5 us (32%)
  Pallas kernels  82.2 us (31%)
  starting transfers between devices  45.7 us (17%)
  local copies, waits for them, and re-layouts  23 us (9%)
  between operations  14.7 us (6%)
  other arithmetic  12.5 us (5%)
    pallas_call x1, Pallas kernels, on_device(): pl.pallas_call(partial(backward_kernel, hashes, bits, rows, work, steps,...  32.2 us
    ppermute x8, waiting for transfers between devices, ring(): moved = [lax.ppermute(v, 'seq', p) for v, p in zip(moved, (ahead, behind))]  30.1 us
    pallas_call x12, Pallas kernels, once(): pl.pallas_call(kernel, grid=(1,) if blocks else (), in_specs=specs, out_s...  17.1 us
    pallas_call x1, Pallas kernels, on_device(): pl.pallas_call(partial(forward_kernel, hashes, bits, rows, wide * tile, c...  16.6 us
    all_to_all x1, waiting for transfers between devices, on_device(): num_got = across(num_parts)  14 us
    ppermute x7, starting transfers between devices, on_device(): back_got.append(lax.ppermute(pair_sums[d], 'seq', perm))  12.2 us
    ppermute x5, waiting for transfers between devices, on_device(): lax.ppermute(v, 'seq', p)  9.73 us
    ppermute x8, starting transfers between devices, ring(): moved = [lax.ppermute(v, 'seq', p) for v, p in zip(moved, (ahead, behind))]  9.16 us
  transfers between devices with their start and end apart: 45, of which 25 were waited for; matrix products, arithmetic and copies ran while one was open for 10% of the time, Pallas kernels for 27%

profile of v9, /device:TPU:0, one launch (start us, length us, event | category | flops | bytes accessed | tf_op | source)
XLA Modules:
  0.0 264.5 jit_solution(5813764956140084762)
XLA Ops:
  11.6 3.0 %collective-permute-start.1 = (bf16[200,768]{1,0:T(8,128)(2,1)S(1)}, bf16[200,768]{1,0:T(8,128)(2,1)S(1)}, u32[]{:S(2)}, u32[]{:S(2)}) collective-permute-start(bf16[200,768]{1,0:T(8,128)(2,1)S(1)} %fusion.2), channel_id=1, source_target_pairs={{0,8},{2,10},{8,16},{10,18},{16,24},{18,26},{24,28},{26,30},{28,20... | collective-permute-start | bytes 921608 | tf_op jit(solution)/shard_map/ppermute | solution.py:718
  17.1 4.9 %collective-permute-done.1 = bf16[200,768]{1,0:T(8,128)(2,1)S(1)} collective-permute-done((bf16[200,768]{1,0:T(8,128)(2,1)S(1)}, bf16[200,768]{1,0:T(8,128)(2,1)S(1)}, u32[]{:S(2)}, u32[]{:S(2)}) %collective-permute-start.1) | collective-permute-done | bytes 307232 | tf_op jit(solution)/shard_map/ppermute | solution.py:718
  24.2 1.8 pack.1
  28.1 6.2 %collective-permute-done.3 = bf16[200,768]{1,0:T(8,128)(2,1)S(1)} collective-permute-done((bf16[200,768]{1,0:T(8,128)(2,1)S(1)}, bf16[200,768]{1,0:T(8,128)(2,1)S(1)}, u32[]{:S(2)}, u32[]{:S(2)}) %collective-permute-start.3) | collective-permute-done | bytes 307232 | tf_op jit(solution)/shard_map/ppermute | solution.py:718
  38.1 12.2 %collective-permute-done.5 = bf16[200,768]{1,0:T(8,128)(2,1)S(1)} collective-permute-done((bf16[200,768]{1,0:T(8,128)(2,1)S(1)}, bf16[200,768]{1,0:T(8,128)(2,1)S(1)}, u32[]{:S(2)}, u32[]{:S(2)}) %collective-permute-start.5) | collective-permute-done | bytes 307232 | tf_op jit(solution)/shard_map/ppermute | solution.py:718
  50.3 4.0 %collective-permute-done.6 = bf16[200,768]{1,0:T(8,128)(2,1)S(1)} collective-permute-done((bf16[200,768]{1,0:T(8,128)(2,1)S(1)}, bf16[200,768]{1,0:T(8,128)(2,1)S(1)}, u32[]{:S(2)}, u32[]{:S(2)}) %collective-permute-start.6) | collective-permute-done | bytes 307232 | tf_op jit(solution)/shard_map/ppermute | solution.py:718
  54.4 1.8 collective-permute-start.7
  57.0 4.0 %collective-permute-done.8 = bf16[72,768]{1,0:T(8,128)(2,1)S(1)} collective-permute-done((bf16[72,768]{1,0:T(8,128)(2,1)S(1)}, bf16[72,768]{1,0:T(8,128)(2,1)S(1)}, u32[]{:S(2)}, u32[]{:S(2)}) %collective-permute-start.8) | collective-permute-done | bytes 110624 | tf_op jit(solution)/shard_map/ppermute | solution.py:747
  64.0 16.6 %hash_forward.1 = (bf16[8,192,256]{2,1,0:T(8,128)(2,1)}, bf16[192,2048]{1,0:T(8,128)(2,1)}, bf16[192,2048]{1,0:T(8,128)(2,1)}, bf16[192,2304]{1,0:T(8,128)(2,1)}...) custom-call(s32[28]{0:T(128)} %pad_add_fusion.spots_ref, ...), custom_call_target="tpu_custom_call" | custom-call | tf_op jit(solution)/shard_map/hash_forward/pallas_call | solution.py:866
  80.5 3.7 %all-to-all-start = ((bf16[8,192,256]{2,1,0:T(8,128)(2,1)}), bf16[8,192,256]{2,1,0:T(8,128)(2,1)S(1)}, u32[]{:S(2)}, u32[]{:S(2)}) async-start(bf16[8,192,256]{2,1,0:T(8,128)(2,1)} %get-tuple-element.137), calls=%async_computation | async-start | bytes 1572864 | tf_op jit(solution)/shard_map/all_to_all | solution.py:906
  86.4 1.9 scatter.4.base_ref
  90.8 14.0 %all-to-all-done.got_ref = bf16[8,192,256]{2,1,0:T(8,128)(2,1)S(1)} async-done(((bf16[8,192,256]{2,1,0:T(8,128)(2,1)}), bf16[8,192,256]{2,1,0:T(8,128)(2,1)S(1)}, u32[]{:S(2)}, u32[]{:S(2)}) %all-to-all-start) | async-done | bytes 786464 | tf_op jit(solution)/shard_map/all_to_all | solution.py:906
  110.2 5.5 %collective-permute-done.18.other_ref = bf16[128,768]{1,0:T(8,128)(2,1)S(1)} collective-permute-done((bf16[128,768]{1,0:T(8,128)(2,1)S(1)}, bf16[128,768]{1,0:T(8,128)(2,1)S(1)}, u32[]{:S(2)}, u32[]{:S(2)}) %collective-permute-start.18) | collective-permute-done | bytes 196640 | tf_op jit(solution)/shard_map/ppermute | solution.py:944
  118.7 4.6 %collective-permute-done.19.other_ref = bf16[128,768]{1,0:T(8,128)(2,1)S(1)} collective-permute-done((bf16[128,768]{1,0:T(8,128)(2,1)S(1)}, bf16[128,768]{1,0:T(8,128)(2,1)S(1)}, u32[]{:S(2)}, u32[]{:S(2)}) %collective-permute-start.19) | collective-permute-done | bytes 196640 | tf_op jit(solution)/shard_map/ppermute | solution.py:956
  123.3 2.3 feed_back.1
  127.1 3.7 %feed_grads.1.all_ref = bf16[768,3456]{1,0:T(8,128)(2,1)} custom-call(f32[128,768]{1,0:T(8,128)S(1)} %get-tuple-element.145.hat_ref, f32[4,768]{1,0:T(4,128)S(1)} %copy-done.6, bf16[128,1536]{1,0:T(8,128)(2,1)S(1)} %get-tuple-element.191.slope_ref, bf16[128,768]{1,0:T(8,128)(2,1)S(1)} %get-tuple-element.192.feed_ref, ...), custom_call_target="tpu_custom_call" | custom-call | tf_op jit(solution)/shard_map/feed_grads/pallas_call | solution.py:1006
  137.8 2.9 %conv_backward.1 = (f32[192,768]{1,0:T(8,128)S(1)}, f32[3,8,128]{2,1,0:T(8,128)S(1)}) custom-call(s32[28]{0:T(128)S(1)} %copy-done.9, bf16[192,512]{1,0:T(8,128)(2,1)S(1)} %get-tuple-element.159.window_ref, bf16[192,128]{1,0:T(8,128)(2,1)S(1)} %get-tuple-element.160.low_ref, bf16[192,128]{1,0:T(8,128)(2,1)S(1)} %get-tuple-element.161.high_ref, ...), custom_call_target="tpu_custom_call" | custom-call | tf_op jit(solution)/shard_map/conv_backward/pallas_call | solution.py:821
  143.7 2.9 %collective-permute-done.24 = bf16[240,256]{1,0:T(8,128)(2,1)S(1)} collective-permute-done((bf16[240,256]{1,0:T(8,128)(2,1)S(1)}, bf16[240,256]{1,0:T(8,128)(2,1)S(1)}, u32[]{:S(2)}, u32[]{:S(2)}) %collective-permute-start.24) | collective-permute-done | bytes 122912 | tf_op jit(solution)/shard_map/ppermute | solution.py:994
  148.6 2.9 %collective-permute-done.26 = bf16[240,256]{1,0:T(8,128)(2,1)S(1)} collective-permute-done((bf16[240,256]{1,0:T(8,128)(2,1)S(1)}, bf16[240,256]{1,0:T(8,128)(2,1)S(1)}, u32[]{:S(2)}, u32[]{:S(2)}) %collective-permute-start.26) | collective-permute-done | bytes 122912 | tf_op jit(solution)/shard_map/ppermute | solution.py:994
  152.4 3.9 %collective-permute-done.28 = bf16[240,256]{1,0:T(8,128)(2,1)S(1)} collective-permute-done((bf16[240,256]{1,0:T(8,128)(2,1)S(1)}, bf16[240,256]{1,0:T(8,128)(2,1)S(1)}, u32[]{:S(2)}, u32[]{:S(2)}) %collective-permute-start.28) | collective-permute-done | bytes 122912 | tf_op jit(solution)/shard_map/ppermute | solution.py:994
  156.4 32.2 %hash_backward.1 = (bf16[8,96,640]{2,1,0:T(8,128)(2,1)}, bf16[8,768,128]{2,1,0:T(8,128)(2,1)}, bf16[8,768,128]{2,1,0:T(8,128)(2,1)}, bf16[8,48,256]{2,1,0:T(8,128)(2,1)}) custom-call(s32[28]{0:T(128)} %pad_add_fusion.spots_ref, bf16[1,200,768]{2,1,0:T(8,128)(2,1)} %bitcast.108, bf16[1,200,768]{2,1,0:T(8,128)(2,1)} %bitcast.120, ...), custom_call_target="tpu_custom_call" | custom-call | tf_op jit(solution)/shard_map/hash_backward/pallas_call | solution.py:1027
  188.7 4.1 %all-to-all-start.1 = ((bf16[8,96,640]{2,1,0:T(8,128)(2,1)}), bf16[8,96,640]{2,1,0:T(8,128)(2,1)S(1)}, u32[]{:S(2)}, u32[]{:S(2)}) async-start(bf16[8,96,640]{2,1,0:T(8,128)(2,1)} %get-tuple-element.177), calls=%async_computation.1 | async-start | bytes 1966080 | tf_op jit(solution)/shard_map/all_to_all | solution.py:1095
  192.8 4.0 %chip_sum.1 = (bf16[8,384,128]{2,1,0:T(8,128)(2,1)}, bf16[8,384,128]{2,1,0:T(8,128)(2,1)}) custom-call(s32[28]{0:T(128)} %pad_add_fusion.spots_ref, bf16[8,768,128]{2,1,0:T(8,128)(2,1)} %get-tuple-element.172.own_ref, bf16[8,768,128]{2,1,0:T(8,128)(2,1)} %collective-permute-done.29.other_ref), custom_call_target="tpu_custom_call" | custom-call | tf_op jit(solution)/shard_map/chip_sum/pallas_call | solution.py:1078
  201.7 3.7 %reshape.152 = f32[8,3,2,8,2,8,8]{6,5,4,3,2,1,0:T(8,128)} reshape(f32[8,24,256]{2,1,0:T(8,128)} %slice.102) | data formatting | bytes 393216 | tf_op jit(solution)/shard_map/reshape | solution.py:1118
  210.5 6.3 %collective-permute-done.30.other_ref = bf16[8,384,128]{2,1,0:T(8,128)(2,1)} collective-permute-done((bf16[8,384,128]{2,1,0:T(8,128)(2,1)}, bf16[8,384,128]{2,1,0:T(8,128)(2,1)}, u32[]{:S(2)}, u32[]{:S(2)}) %collective-permute-start.30) | collective-permute-done | bytes 786464 | tf_op jit(solution)/shard_map/ppermute | solution.py:1092
  216.9 2.1 pair_sum.1
  223.1 2.6 collective-permute-start.34
  226.6 4.8 %all-to-all-done.1.got_ref = bf16[8,96,640]{2,1,0:T(8,128)(2,1)S(1)} async-done(((bf16[8,96,640]{2,1,0:T(8,128)(2,1)}), bf16[8,96,640]{2,1,0:T(8,128)(2,1)S(1)}, u32[]{:S(2)}, u32[]{:S(2)}) %all-to-all-start.1) | async-done | bytes 983072 | tf_op jit(solution)/shard_map/all_to_all | solution.py:1095
  236.9 2.1 collective-permute-start.36
  239.0 3.5 %collective-permute-start.37 = (bf16[384,128]{1,0:T(8,128)(2,1)}, bf16[384,128]{1,0:T(8,128)(2,1)S(1)}, u32[]{:S(2)}, u32[]{:S(2)}) collective-permute-start(bf16[384,128]{1,0:T(8,128)(2,1)} %get-tuple-element.188), channel_id=1, source_target_pairs={{0,28},{2,30},{4,24},{6,26},{8,20},{10,22},{12,16},{14,18},{16,12}... | collective-permute-start | bytes 294920 | tf_op jit(solution)/shard_map/ppermute | solution.py:1100
  246.7 3.2 %big_adam.1 = (f32[48,1536]{1,0:T(8,128)}, f32[48,1536]{1,0:T(8,128)}, f32[48,1536]{1,0:T(8,128)}, bf16[48,1536]{1,0:T(8,128)(2,1)}, f32[48,1536]{1,0:T(8,128)},...) custom-call(bf16[48,3456]{1,0:T(8,128)(2,1)} %reduce-scatter.2.clone, ...), custom_call_target="tpu_custom_call" | custom-call | tf_op jit(solution)/shard_map/big_adam/pallas_call | solution.py:794
  253.9 2.3 qkv_adam.1
  (212 shorter events, 75.9 us)
Async XLA Ops:
  7.2 99.8 %all-gather.2.cloned.1.call-start = ((), (), s32[]{:S(2)}) async-start(), calls=%async_computation.3 | async-start | bytes 5640192 | tf_op jit(solution)/shard_map/all_gather | solution.py:851
  11.6 10.5 %collective-permute-start.1 = (bf16[200,768]{1,0:T(8,128)(2,1)S(1)}, bf16[200,768]{1,0:T(8,128)(2,1)S(1)}, u32[]{:S(2)}, u32[]{:S(2)}) collective-permute-start(bf16[200,768]{1,0:T(8,128)(2,1)S(1)} %fusion.2), channel_id=1, source_target_pairs={{0,8},{2,10},{8,16},{10,18},{16,24},{18,26},{24,28},{26,30},{28,20... | collective-permute-start | bytes 921608 | tf_op jit(solution)/shard_map/ppermute | solution.py:718
  14.5 9.1 %collective-permute-start.2 = (bf16[200,768]{1,0:T(8,128)(2,1)S(1)}, bf16[200,768]{1,0:T(8,128)(2,1)S(1)}, u32[]{:S(2)}, u32[]{:S(2)}) collective-permute-start(bf16[200,768]{1,0:T(8,128)(2,1)S(1)} %fusion.2), channel_id=1, source_target_pairs={{8,0},{10,2},{16,8},{18,10},{24,16},{26,18},{28,24},{30,26},{20,28... | collective-permute-start | bytes 921608 | tf_op jit(solution)/shard_map/ppermute | solution.py:718
  26.1 8.2 %collective-permute-start.3 = (bf16[200,768]{1,0:T(8,128)(2,1)S(1)}, bf16[200,768]{1,0:T(8,128)(2,1)S(1)}, u32[]{:S(2)}, u32[]{:S(2)}) collective-permute-start(bf16[200,768]{1,0:T(8,128)(2,1)S(1)} %collective-permute-done.1), channel_id=1, source_target_pairs={{0,8},{2,10},{8,16},{10,18},{16,24},{18,26},{24,28},{26,30},{28,20... | collective-permute-start | bytes 921608 | tf_op jit(solution)/shard_map/ppermute | solution.py:718
  27.7 7.9 %collective-permute-start.4 = (bf16[200,768]{1,0:T(8,128)(2,1)S(1)}, bf16[200,768]{1,0:T(8,128)(2,1)S(1)}, u32[]{:S(2)}, u32[]{:S(2)}) collective-permute-start(bf16[200,768]{1,0:T(8,128)(2,1)S(1)} %collective-permute-done.2), channel_id=1, source_target_pairs={{8,0},{10,2},{16,8},{18,10},{24,16},{26,18},{28,24},{30,26},{20,28... | collective-permute-start | bytes 921608 | tf_op jit(solution)/shard_map/ppermute | solution.py:718
  35.6 14.7 %collective-permute-start.5 = (bf16[200,768]{1,0:T(8,128)(2,1)S(1)}, bf16[200,768]{1,0:T(8,128)(2,1)S(1)}, u32[]{:S(2)}, u32[]{:S(2)}) collective-permute-start(bf16[200,768]{1,0:T(8,128)(2,1)S(1)} %collective-permute-done.3), channel_id=1, source_target_pairs={{0,8},{2,10},{8,16},{10,18},{16,24},{18,26},{24,28},{26,30},{28,20... | collective-permute-start | bytes 921608 | tf_op jit(solution)/shard_map/ppermute | solution.py:718
  37.2 17.2 %collective-permute-start.6 = (bf16[200,768]{1,0:T(8,128)(2,1)S(1)}, bf16[200,768]{1,0:T(8,128)(2,1)S(1)}, u32[]{:S(2)}, u32[]{:S(2)}) collective-permute-start(bf16[200,768]{1,0:T(8,128)(2,1)S(1)} %collective-permute-done.4), channel_id=1, source_target_pairs={{8,0},{10,2},{16,8},{18,10},{24,16},{26,18},{28,24},{30,26},{20,28... | collective-permute-start | bytes 921608 | tf_op jit(solution)/shard_map/ppermute | solution.py:718
  37.6 18.8 %collective-permute-start.9 = (bf16[200,768]{1,0:T(8,128)(2,1)S(1)}, bf16[200,768]{1,0:T(8,128)(2,1)S(1)}, u32[]{:S(2)}, u32[]{:S(2)}) collective-permute-start(bf16[200,768]{1,0:T(8,128)(2,1)S(1)} %fusion.2), channel_id=1, source_target_pairs={{0,2},{2,0},{4,6},{6,4},{8,10},{10,8},{12,14},{14,12},{16,18},{18,... | collective-permute-start | bytes 921608 | tf_op jit(solution)/shard_map/ppermute | solution.py:751
  37.6 18.8 %collective-permute-start.10 = (bf16[200,768]{1,0:T(8,128)(2,1)S(1)}, bf16[200,768]{1,0:T(8,128)(2,1)S(1)}, u32[]{:S(2)}, u32[]{:S(2)}) collective-permute-start(bf16[200,768]{1,0:T(8,128)(2,1)S(1)} %collective-permute-done.1), channel_id=1, source_target_pairs={{0,2},{2,0},{4,6},{6,4},{8,10},{10,8},{12,14},{14,12},{16,18},{18,... | collective-permute-start | bytes 921608 | tf_op jit(solution)/shard_map/ppermute | solution.py:751
  38.1 23.3 %collective-permute-start.11 = (bf16[200,768]{1,0:T(8,128)(2,1)S(1)}, bf16[200,768]{1,0:T(8,128)(2,1)S(1)}, u32[]{:S(2)}, u32[]{:S(2)}) collective-permute-start(bf16[200,768]{1,0:T(8,128)(2,1)S(1)} %collective-permute-done.2), channel_id=1, source_target_pairs={{0,2},{2,0},{4,6},{6,4},{8,10},{10,8},{12,14},{14,12},{16,18},{18,... | collective-permute-start | bytes 921608 | tf_op jit(solution)/shard_map/ppermute | solution.py:751
  54.4 6.6 %collective-permute-start.7 = (bf16[128,768]{1,0:T(8,128)(2,1)S(1)}, bf16[128,768]{1,0:T(8,128)(2,1)S(1)}, u32[]{:S(2)}, u32[]{:S(2)}) collective-permute-start(bf16[128,768]{1,0:T(8,128)(2,1)S(1)} %slice.87), channel_id=1, source_target_pairs={{0,8},{2,10},{8,16},{10,18},{16,24},{18,26},{24,28},{26,30},{28,20... | collective-permute-start | bytes 589832 | tf_op jit(solution)/shard_map/ppermute | solution.py:746
  56.4 5.1 %collective-permute-start.12 = (bf16[200,768]{1,0:T(8,128)(2,1)S(1)}, bf16[200,768]{1,0:T(8,128)(2,1)S(1)}, u32[]{:S(2)}, u32[]{:S(2)}) collective-permute-start(bf16[200,768]{1,0:T(8,128)(2,1)S(1)} %collective-permute-done.3), channel_id=1, source_target_pairs={{0,2},{2,0},{4,6},{6,4},{8,10},{10,8},{12,14},{14,12},{16,18},{18,... | collective-permute-start | bytes 921608 | tf_op jit(solution)/shard_map/ppermute | solution.py:751
  56.5 5.1 %collective-permute-start.13 = (bf16[200,768]{1,0:T(8,128)(2,1)S(1)}, bf16[200,768]{1,0:T(8,128)(2,1)S(1)}, u32[]{:S(2)}, u32[]{:S(2)}) collective-permute-start(bf16[200,768]{1,0:T(8,128)(2,1)S(1)} %collective-permute-done.4), channel_id=1, source_target_pairs={{0,2},{2,0},{4,6},{6,4},{8,10},{10,8},{12,14},{14,12},{16,18},{18,... | collective-permute-start | bytes 921608 | tf_op jit(solution)/shard_map/ppermute | solution.py:751
  80.5 24.3 %all-to-all-start = ((bf16[8,192,256]{2,1,0:T(8,128)(2,1)}), bf16[8,192,256]{2,1,0:T(8,128)(2,1)S(1)}, u32[]{:S(2)}, u32[]{:S(2)}) async-start(bf16[8,192,256]{2,1,0:T(8,128)(2,1)} %get-tuple-element.137), calls=%async_computation | async-start | bytes 1572864 | tf_op jit(solution)/shard_map/all_to_all | solution.py:906
  84.3 162.4 %reduce-scatter.2.cloned.1.call-start = ((), (), s32[]{:S(2)}) async-start(), calls=%async_computation.4 | async-start | bytes 5640192 | tf_op jit(solution)/shard_map/reduce_scatter | solution.py:1025
  108.6 7.0 %collective-permute-start.18 = (bf16[128,768]{1,0:T(8,128)(2,1)S(1)}, bf16[128,768]{1,0:T(8,128)(2,1)S(1)}, u32[]{:S(2)}, u32[]{:S(2)}) collective-permute-start(bf16[128,768]{1,0:T(8,128)(2,1)S(1)} %get-tuple-element.143.own_ref), channel_id=1, source_target_pairs={{0,1},{1,0},{2,3},{3,2},{4,5},{5,4},{6,7},{7,6},{8,9},{9,8},{10,11... | collective-permute-start | bytes 589832 | tf_op jit(solution)/shard_map/ppermute | solution.py:944
  117.1 6.2 %collective-permute-start.19 = (bf16[128,768]{1,0:T(8,128)(2,1)S(1)}, bf16[128,768]{1,0:T(8,128)(2,1)S(1)}, u32[]{:S(2)}, u32[]{:S(2)}) collective-permute-start(bf16[128,768]{1,0:T(8,128)(2,1)S(1)} %get-tuple-element.147.own_ref), channel_id=1, source_target_pairs={{0,1},{1,0},{2,3},{3,2},{4,5},{5,4},{6,7},{7,6},{8,9},{9,8},{10,11... | collective-permute-start | bytes 589832 | tf_op jit(solution)/shard_map/ppermute | solution.py:956
  125.6 5.7 %collective-permute-start.20 = (bf16[128,768]{1,0:T(8,128)(2,1)S(1)}, bf16[128,768]{1,0:T(8,128)(2,1)S(1)}, u32[]{:S(2)}, u32[]{:S(2)}) collective-permute-start(bf16[128,768]{1,0:T(8,128)(2,1)S(1)} %get-tuple-element.150.own_ref), channel_id=1, source_target_pairs={{0,1},{1,0},{2,3},{3,2},{4,5},{5,4},{6,7},{7,6},{8,9},{9,8},{10,11... | collective-permute-start | bytes 589832 | tf_op jit(solution)/shard_map/ppermute | solution.py:969
  135.8 5.9 %collective-permute-start.22 = (bf16[240,256]{1,0:T(8,128)(2,1)S(1)}, bf16[240,256]{1,0:T(8,128)(2,1)S(1)}, u32[]{:S(2)}, u32[]{:S(2)}) collective-permute-start(bf16[240,256]{1,0:T(8,128)(2,1)S(1)} %get-tuple-element.158), channel_id=1, source_target_pairs={{0,8},{2,10},{8,16},{10,18},{16,24},{18,26},{24,28},{26,30},{28,20... | collective-permute-start | bytes 368648 | tf_op jit(solution)/shard_map/ppermute | solution.py:718
  136.1 5.5 %collective-permute-start.23 = (bf16[240,256]{1,0:T(8,128)(2,1)S(1)}, bf16[240,256]{1,0:T(8,128)(2,1)S(1)}, u32[]{:S(2)}, u32[]{:S(2)}) collective-permute-start(bf16[240,256]{1,0:T(8,128)(2,1)S(1)} %get-tuple-element.158), channel_id=1, source_target_pairs={{8,0},{10,2},{16,8},{18,10},{24,16},{26,18},{28,24},{30,26},{20,28... | collective-permute-start | bytes 368648 | tf_op jit(solution)/shard_map/ppermute | solution.py:718
  146.8 5.6 %collective-permute-start.27 = (bf16[240,256]{1,0:T(8,128)(2,1)S(1)}, bf16[240,256]{1,0:T(8,128)(2,1)S(1)}, u32[]{:S(2)}, u32[]{:S(2)}) collective-permute-start(bf16[240,256]{1,0:T(8,128)(2,1)S(1)} %collective-permute-done.25), channel_id=1, source_target_pairs={{8,0},{10,2},{16,8},{18,10},{24,16},{26,18},{28,24},{30,26},{20,28... | collective-permute-start | bytes 368648 | tf_op jit(solution)/shard_map/ppermute | solution.py:994
  188.7 42.8 %all-to-all-start.1 = ((bf16[8,96,640]{2,1,0:T(8,128)(2,1)}), bf16[8,96,640]{2,1,0:T(8,128)(2,1)S(1)}, u32[]{:S(2)}, u32[]{:S(2)}) async-start(bf16[8,96,640]{2,1,0:T(8,128)(2,1)} %get-tuple-element.177), calls=%async_computation.1 | async-start | bytes 1966080 | tf_op jit(solution)/shard_map/all_to_all | solution.py:1095
  196.8 20.0 %collective-permute-start.30 = (bf16[8,384,128]{2,1,0:T(8,128)(2,1)}, bf16[8,384,128]{2,1,0:T(8,128)(2,1)}, u32[]{:S(2)}, u32[]{:S(2)}) collective-permute-start(bf16[8,384,128]{2,1,0:T(8,128)(2,1)} %get-tuple-element.175), channel_id=1, source_target_pairs={{0,1},{1,0},{2,3},{3,2},{4,5},{5,4},{6,7},{7,6},{8,9},{9,8},{10,11... | collective-permute-start | bytes 2359304 | tf_op jit(solution)/shard_map/ppermute | solution.py:1092
  219.6 11.9 %collective-permute-start.31 = (bf16[384,128]{1,0:T(8,128)(2,1)}, bf16[384,128]{1,0:T(8,128)(2,1)S(1)}, u32[]{:S(2)}, u32[]{:S(2)}) collective-permute-start(bf16[384,128]{1,0:T(8,128)(2,1)} %get-tuple-element.178), channel_id=1, source_target_pairs={{0,4},{2,6},{4,0},{6,2},{8,12},{10,14},{12,8},{14,10},{16,20},{18,... | collective-permute-start | bytes 294920 | tf_op jit(solution)/shard_map/ppermute | solution.py:1100
  221.3 10.2 %collective-permute-start.32 = (bf16[384,128]{1,0:T(8,128)(2,1)}, bf16[384,128]{1,0:T(8,128)(2,1)S(1)}, u32[]{:S(2)}, u32[]{:S(2)}) collective-permute-start(bf16[384,128]{1,0:T(8,128)(2,1)} %get-tuple-element.179), channel_id=1, source_target_pairs={{0,8},{2,10},{4,12},{6,14},{8,0},{10,2},{12,4},{14,6},{16,24},{18,... | collective-permute-start | bytes 294920 | tf_op jit(solution)/shard_map/ppermute | solution.py:1100
  222.9 8.9 %collective-permute-start.33 = (bf16[384,128]{1,0:T(8,128)(2,1)}, bf16[384,128]{1,0:T(8,128)(2,1)S(1)}, u32[]{:S(2)}, u32[]{:S(2)}) collective-permute-start(bf16[384,128]{1,0:T(8,128)(2,1)} %get-tuple-element.180), channel_id=1, source_target_pairs={{0,12},{2,14},{4,8},{6,10},{8,4},{10,6},{12,0},{14,2},{16,28},{18,... | collective-permute-start | bytes 294920 | tf_op jit(solution)/shard_map/ppermute | solution.py:1100
  223.1 9.8 %collective-permute-start.34 = (bf16[384,128]{1,0:T(8,128)(2,1)}, bf16[384,128]{1,0:T(8,128)(2,1)S(1)}, u32[]{:S(2)}, u32[]{:S(2)}) collective-permute-start(bf16[384,128]{1,0:T(8,128)(2,1)} %get-tuple-element.181), channel_id=1, source_target_pairs={{0,16},{2,18},{4,20},{6,22},{8,24},{10,26},{12,28},{14,30},{16,0},... | collective-permute-start | bytes 294920 | tf_op jit(solution)/shard_map/ppermute | solution.py:1100
  236.5 6.1 %collective-permute-start.39 = (f32[6243]{0:T(1024)S(1)}, f32[6243]{0:T(1024)S(1)}, u32[]{:S(2)}, u32[]{:S(2)}) collective-permute-start(f32[6243]{0:T(1024)S(1)} %pad_maximum_fusion.1), channel_id=1, source_target_pairs={{0,2},{2,0},{4,6},{6,4},{8,10},{10,8},{12,14},{14,12},{16,18},{18,... | collective-permute-start | bytes 74924 | tf_op jit(solution)/shard_map/ppermute | solution.py:1125
  236.5 14.0 %collective-permute-start.35 = (bf16[384,128]{1,0:T(8,128)(2,1)}, bf16[384,128]{1,0:T(8,128)(2,1)S(1)}, u32[]{:S(2)}, u32[]{:S(2)}) collective-permute-start(bf16[384,128]{1,0:T(8,128)(2,1)} %get-tuple-element.186), channel_id=1, source_target_pairs={{0,20},{2,22},{4,16},{6,18},{8,28},{10,30},{12,24},{14,26},{16,4},... | collective-permute-start | bytes 294920 | tf_op jit(solution)/shard_map/ppermute | solution.py:1100
  236.9 13.6 %collective-permute-start.36 = (bf16[384,128]{1,0:T(8,128)(2,1)}, bf16[384,128]{1,0:T(8,128)(2,1)S(1)}, u32[]{:S(2)}, u32[]{:S(2)}) collective-permute-start(bf16[384,128]{1,0:T(8,128)(2,1)} %get-tuple-element.187), channel_id=1, source_target_pairs={{0,24},{2,26},{4,28},{6,30},{8,16},{10,18},{12,20},{14,22},{16,8},... | collective-permute-start | bytes 294920 | tf_op jit(solution)/shard_map/ppermute | solution.py:1100
  239.0 11.5 %collective-permute-start.37 = (bf16[384,128]{1,0:T(8,128)(2,1)}, bf16[384,128]{1,0:T(8,128)(2,1)S(1)}, u32[]{:S(2)}, u32[]{:S(2)}) collective-permute-start(bf16[384,128]{1,0:T(8,128)(2,1)} %get-tuple-element.188), channel_id=1, source_target_pairs={{0,28},{2,30},{4,24},{6,26},{8,20},{10,22},{12,16},{14,18},{16,12}... | collective-permute-start | bytes 294920 | tf_op jit(solution)/shard_map/ppermute | solution.py:1100
  242.6 11.3 %collective-permute-start.40 = (f32[48,640]{1,0:T(8,128)}, f32[48,640]{1,0:T(8,128)}, u32[]{:S(2)}, u32[]{:S(2)}) collective-permute-start(f32[48,640]{1,0:T(8,128)} %get-tuple-element.200), channel_id=1, source_target_pairs={{0,2},{2,0},{4,6},{6,4},{8,10},{10,8},{12,14},{14,12},{16,18},{18,... | collective-permute-start | bytes 368648 | tf_op jit(solution)/shard_map/ppermute | solution.py:1113
  (52 other events, 542.2 us)
Sparse Core Ops, SparseCore 0:
  26.2 61.4 all-gather.1
  133.8 93.4 reduce-scatter.1
